TPU v7x, 32 devices: a whole 2x2x4 slice. The times are simulated.
32 devices in a mesh: dp: 4 (over z), expert: 8 (over y, x, core).
Axes of the slice: x: 2, y: 2, z: 4, core: 2. Of those that a mesh axis runs over, the one named last changes fastest.
Arguments:
- tokens: bfloat16 [8, 512, 1024], P('expert', 'dp'), may hold values from -6 to 6
- qkv_weight: bfloat16 [1024, 3072], P(('dp', 'expert')), may hold values from -0.1875 to 0.1875
- proj_weight: bfloat16 [1024, 1024], P(('dp', 'expert')), may hold values from -0.75 to 0.75
- router_weight: bfloat16 [1024, 8], P(('dp', 'expert')), may hold values from -0.09375 to 0.09375
- norm_gains: bfloat16 [2, 1024], P(None, ('dp', 'expert')), may hold values from 0.5 to 1.5
- biases: bfloat16 [5, 1024], P(None, ('dp', 'expert')), may hold values from -1.1953125 to 1.1953125
- up_weight: bfloat16 [8, 1024, 4096], P('expert', None, 'dp'), may hold values from -0.1875 to 0.1875
- up_bias: bfloat16 [8, 4096], P('expert', 'dp'), may hold values from -1.1953125 to 1.1953125
- down_weight: bfloat16 [8, 4096, 1024], P('expert', 'dp'), may hold values from -0.75 to 0.75
- down_bias: bfloat16 [8, 1024], P('expert', 'dp'), may hold values from -6 to 6
- routes: int32 [8, 512, 1], P('expert', 'dp'), may hold values from 0 to 7
- slot_order: int32 [8, 4, 128], P('expert', 'dp'), may hold values from 0 to 127, each once within a row
- segments: int32 [8, 512], P('expert'), may hold values from 0 to 6, never falling along the last dimension, each value on 1 to 256 neighbouring positions
- parents: int32 [8, 7], P('expert'), may hold values from 0 to 5, as said below
- cotangent: bfloat16 [8, 512, 1024], P('expert', 'dp'), may hold values from -6 to 6
Outputs:
- outputs: bfloat16 [8, 512, 1024], P('expert', 'dp')
- grad_tokens: float32 [8, 512, 1024], P('expert', 'dp')
- grad_qkv: float32 [1024, 3072], P(('dp', 'expert'))
- grad_proj: float32 [1024, 1024], P(('dp', 'expert'))
- grad_router: float32 [1024, 8], P(('dp', 'expert'))
- grad_gains: float32 [2, 1024], P(None, ('dp', 'expert'))
- grad_biases: float32 [5, 1024], P(None, ('dp', 'expert'))
- grad_up: float32 [8, 1024, 4096], P('expert', None, 'dp')
- grad_up_bias: float32 [8, 4096], P('expert', 'dp')
- grad_down: float32 [8, 4096, 1024], P('expert', 'dp')
- grad_down_bias: float32 [8, 1024], P('expert', 'dp')
Inputs may be any that keep to these rules, and one draw needn't show every extreme that they name: Along each tree the segment number never falls, every one of the 7 segments has a token, and the longest has 256. parents[t, 0] = 0, parents[t, s] < s for every other s, and the last segment's parent is segment 7 - 2. `routes`: every expert is the route of some token. `slot_order`: each device's 128 tokens hold every priority once.
All inputs are finite; a program needn't handle non-finite values.
Results may differ from a plain program's by a relative error of at most 0.014.
Values may be sent and summed in bfloat16 or wider, within the bound.
No kernel may reach another device: no remote copies, remote signals or barrier semaphores. Data moves between devices by JAX's collectives and lax.ppermute only.
A program may use at most 192 MiB of HBM per device.

v0:
```python
from functools import partial
import math

import jax
import jax.numpy as jnp
from jax import lax
from jax.sharding import PartitionSpec as P

H = 16
NSEG = 7


EPS = 1e-05
NEG = -1e30
HIGH = lax.Precision.HIGHEST


def layer_norm(values, gain, shift):
    mean = jnp.mean(values, axis=-1, keepdims=True)
    centred = values - mean
    spread = jnp.mean(centred * centred, axis=-1, keepdims=True)
    return centred * lax.rsqrt(spread + EPS) * gain + shift


def ancestry(parents, number):
    labels = jnp.arange(number, dtype=jnp.int32)
    direct = (labels[None, :] == parents[:, None]).astype(jnp.float32)
    reach = jnp.minimum(direct + jnp.eye(number, dtype=jnp.float32), 1.0)
    for step in range(3):
        reach = jnp.minimum(jnp.dot(reach, reach, precision=HIGH), 1.0)
    return reach


def slot_table(route_ids, order, experts, capacity):
    labels = jnp.arange(experts, dtype=jnp.int32)
    expert_hot = route_ids[:, None] == labels[None, :]
    same = route_ids[:, None] == route_ids[None, :]
    before = order[None, :] < order[:, None]
    rank = jnp.sum((same & before).astype(jnp.int32), axis=1)
    slot_hot = rank[:, None] == jnp.arange(capacity, dtype=jnp.int32)[None, :]
    table = expert_hot[:, :, None] & slot_hot[:, None, :]
    return (expert_hot.astype(jnp.float32), table)


def expert_gate(logits, expert_hot):
    return jnp.sum(jax.nn.softmax(logits, axis=-1) * expert_hot, axis=-1)


def tanh_gelu(values):
    return jax.nn.gelu(values, approximate=True)


def shards(
    tokens,
    qkv_weight,
    proj_weight,
    router_weight,
    norm_gains,
    biases,
    up_weight,
    up_bias,
    down_weight,
    down_bias,
    routes,
    slot_order,
    segments,
    parents,
    cotangent,
):
    qkv_full, proj_full, router_full, gain_full, bias_full = (
        lax.all_gather(qkv_weight, ("dp", "expert"), axis=0, tiled=True),
        lax.all_gather(proj_weight, ("dp", "expert"), axis=0, tiled=True),
        lax.all_gather(router_weight, ("dp", "expert"), axis=0, tiled=True),
        lax.all_gather(norm_gains, ("dp", "expert"), axis=1, tiled=True),
        lax.all_gather(biases, ("dp", "expert"), axis=1, tiled=True),
    )
    up_full, up_shift, down_full, down_shift = (
        lax.all_gather(up_weight, "dp", axis=2, tiled=True),
        lax.all_gather(up_bias, "dp", axis=1, tiled=True),
        lax.all_gather(down_weight, "dp", axis=1, tiled=True),
        lax.all_gather(down_bias, "dp", axis=1, tiled=True),
    )
    rows = tokens.shape[1]
    width = tokens.shape[2]
    head_dim = width // H
    scale = head_dim ** (-0.5)
    experts = router_full.shape[1]
    capacity = (9 * rows + 8 * experts - 1) // (8 * experts)
    gain32 = gain_full.astype(jnp.float32)
    bias32 = bias_full.astype(jnp.float32)
    inputs = tokens[0].astype(jnp.float32)
    normed, norm1_back = jax.vjp(layer_norm, inputs, gain32[0], bias32[0])
    normed_low = normed.astype(jnp.bfloat16)
    shift = jnp.concatenate([bias32[1], jnp.zeros((width,), jnp.float32), bias32[2]])
    packed = (jnp.dot(normed_low, qkv_full, preferred_element_type=jnp.float32) + shift).astype(
        jnp.bfloat16
    )
    key_value = lax.all_gather(packed[:, width:], "dp", axis=0, tiled=True)
    length = key_value.shape[0]
    start = lax.axis_index("dp") * rows
    query_pos = start + jnp.arange(rows, dtype=jnp.int32)
    reach = ancestry(parents[0], NSEG)
    labels = jnp.arange(NSEG, dtype=jnp.int32)
    key_hot = (segments[0][:, None] == labels[None, :]).astype(jnp.float32)
    query_reach = jnp.dot(lax.dynamic_slice_in_dim(key_hot, start, rows, 0), reach, precision=HIGH)
    block = math.gcd(length, 512)
    number = length // block
    hot_blocks = key_hot.reshape(number, block, NSEG)
    pos_blocks = jnp.arange(length, dtype=jnp.int32).reshape(number, block)
    query_heads = packed[:, :width].reshape(rows, H, head_dim)

    def block_scores(key_blk, hot_blk, pos_blk):
        allowed = (jnp.dot(query_reach, hot_blk.T, precision=HIGH) > 0.5) & (
            pos_blk[None, :] <= query_pos[:, None]
        )
        raw = (
            jnp.einsum("qhd,khd->hqk", query_heads, key_blk, preferred_element_type=jnp.float32)
            * scale
        )
        return jnp.where(allowed[None], raw, NEG)

    def split_blocks(pairs):
        keys = pairs[:, :width].reshape(number, block, H, head_dim)
        values = pairs[:, width:].reshape(number, block, H, head_dim)
        return (keys, values)

    key_blocks, value_blocks = split_blocks(key_value)

    def total_step(carry, item):
        top, total = carry
        scores = block_scores(item[0], item[1], item[2])
        new_top = jnp.maximum(top, jnp.max(scores, axis=-1))
        total = total * jnp.exp(top - new_top) + jnp.sum(
            jnp.exp(scores - new_top[:, :, None]), axis=-1
        )
        return ((new_top, total), None)

    first_carry = (jnp.full((H, rows), NEG, jnp.float32), jnp.zeros((H, rows), jnp.float32))
    (top, total), unused = lax.scan(total_step, first_carry, (key_blocks, hot_blocks, pos_blocks))
    log_total = top + jnp.log(total)

    def value_step(accum, item):
        scores = block_scores(item[0], item[1], item[2])
        probs = jnp.exp(scores - log_total[:, :, None]).astype(jnp.bfloat16)
        return (
            accum + jnp.einsum("hqk,khd->qhd", probs, item[3], preferred_element_type=jnp.float32),
            None,
        )

    attended32, unused = lax.scan(
        value_step,
        jnp.zeros((rows, H, head_dim), jnp.float32),
        (key_blocks, hot_blocks, pos_blocks, value_blocks),
    )
    attended_low = attended32.reshape(rows, width).astype(jnp.bfloat16)
    mixed = (
        inputs + jnp.dot(attended_low, proj_full, preferred_element_type=jnp.float32) + bias32[3]
    )
    normed2, norm2_back = jax.vjp(layer_norm, mixed, gain32[1], bias32[4])
    normed2_low = normed2.astype(jnp.bfloat16)
    logits = jnp.dot(normed2_low, router_full, preferred_element_type=jnp.float32)
    expert_hot, table = slot_table(routes[0, :, 0], slot_order[0, 0], experts, capacity)
    gate, gate_back = jax.vjp(partial(expert_gate, expert_hot=expert_hot), logits)
    table_low = table.astype(jnp.bfloat16)
    sent = jnp.einsum(
        "tec,td->ecd", table_low, normed2_low, preferred_element_type=jnp.float32
    ).astype(jnp.bfloat16)
    arrived = lax.all_to_all(sent, "expert", split_axis=0, concat_axis=0, tiled=True)
    slots = arrived.reshape(-1, width)
    pre = jnp.dot(slots, up_full[0], preferred_element_type=jnp.float32) + up_shift[0].astype(
        jnp.float32
    )
    act, act_back = jax.vjp(tanh_gelu, pre)
    act_low = act.astype(jnp.bfloat16)
    result = (
        jnp.dot(act_low, down_full[0], preferred_element_type=jnp.float32)
        + down_shift[0].astype(jnp.float32)
    ).astype(jnp.bfloat16)
    returned = lax.all_to_all(
        result.reshape(arrived.shape), "expert", split_axis=0, concat_axis=0, tiled=True
    )
    combined = jnp.einsum("tec,ecd->td", table_low, returned, preferred_element_type=jnp.float32)
    outputs = (mixed + gate[:, None] * combined).astype(jnp.bfloat16)
    qkv_full, proj_full, router_full = (
        lax.all_gather(qkv_weight, ("dp", "expert"), axis=0, tiled=True),
        lax.all_gather(proj_weight, ("dp", "expert"), axis=0, tiled=True),
        lax.all_gather(router_weight, ("dp", "expert"), axis=0, tiled=True),
    )
    up_full, down_full = (
        lax.all_gather(up_weight, "dp", axis=2, tiled=True),
        lax.all_gather(down_weight, "dp", axis=1, tiled=True),
    )
    key_value = lax.all_gather(packed[:, width:], "dp", axis=0, tiled=True)
    key_blocks, value_blocks = split_blocks(key_value)
    upstream = cotangent[0].astype(jnp.float32)
    d_gate = jnp.sum(upstream * combined, axis=-1)
    table32 = table.astype(jnp.float32)
    d_result = jnp.einsum("tec,td->ecd", table32, gate[:, None] * upstream, precision=HIGH).astype(
        jnp.bfloat16
    )
    d_arrived = lax.all_to_all(d_result, "expert", split_axis=0, concat_axis=0, tiled=True)
    d_rows = d_arrived.reshape(-1, width)
    grad_down_bias = jnp.sum(d_rows.astype(jnp.float32), axis=0)
    grad_down = jnp.einsum("rf,rd->fd", act_low, d_rows, preferred_element_type=jnp.float32)
    d_act = jnp.einsum("rd,fd->rf", d_rows, down_full[0], preferred_element_type=jnp.float32)
    d_pre = act_back(d_act)[0]
    grad_up_bias = jnp.sum(d_pre, axis=0)
    d_pre_low = d_pre.astype(jnp.bfloat16)
    grad_up = jnp.einsum("rd,rf->df", slots, d_pre_low, preferred_element_type=jnp.float32)
    d_slots = jnp.einsum(
        "rf,df->rd", d_pre_low, up_full[0], preferred_element_type=jnp.float32
    ).astype(jnp.bfloat16)
    d_sent = lax.all_to_all(
        d_slots.reshape(arrived.shape), "expert", split_axis=0, concat_axis=0, tiled=True
    )
    d_logits = gate_back(d_gate)[0]
    grad_router = jnp.einsum("td,te->de", normed2_low.astype(jnp.float32), d_logits, precision=HIGH)
    d_normed2 = jnp.einsum("tec,ecd->td", table_low, d_sent, preferred_element_type=jnp.float32)
    d_normed2 = d_normed2 + jnp.einsum(
        "te,de->td", d_logits, router_full.astype(jnp.float32), precision=HIGH
    )
    d_mixed_norm, grad_gain_second, grad_shift_norm2 = norm2_back(d_normed2)
    d_mixed = upstream + d_mixed_norm
    grad_shift_proj = jnp.sum(d_mixed, axis=0)
    d_mixed_low = d_mixed.astype(jnp.bfloat16)
    grad_proj = jnp.einsum(
        "tc,td->cd", attended_low, d_mixed_low, preferred_element_type=jnp.float32
    )
    d_attended = jnp.einsum(
        "td,cd->tc", d_mixed_low, proj_full, preferred_element_type=jnp.float32
    ).astype(jnp.bfloat16)
    d_heads = d_attended.reshape(rows, H, head_dim)
    delta = jnp.einsum("qhd,qhd->hq", d_heads.astype(jnp.float32), attended32, precision=HIGH)

    def grad_step(d_query, item):
        scores = block_scores(item[0], item[1], item[2])
        probs = jnp.exp(scores - log_total[:, :, None])
        probs_low = probs.astype(jnp.bfloat16)
        d_value = jnp.einsum("hqk,qhd->khd", probs_low, d_heads, preferred_element_type=jnp.float32)
        d_probs = jnp.einsum("qhd,khd->hqk", d_heads, item[3], preferred_element_type=jnp.float32)
        d_scores = (probs * (d_probs - delta[:, :, None])).astype(jnp.bfloat16)
        d_query = d_query + jnp.einsum(
            "hqk,khd->qhd", d_scores, item[0], preferred_element_type=jnp.float32
        )
        d_key = (
            jnp.einsum("hqk,qhd->khd", d_scores, query_heads, preferred_element_type=jnp.float32)
            * scale
        )
        joined = jnp.concatenate(
            [d_key.reshape(block, width), d_value.reshape(block, width)], axis=1
        )
        return (d_query, joined)

    d_query, joined = lax.scan(
        grad_step,
        jnp.zeros((rows, H, head_dim), jnp.float32),
        (key_blocks, hot_blocks, pos_blocks, value_blocks),
    )
    joined_rows = joined.reshape(length, 2 * width)
    d_key_value = lax.psum_scatter(
        joined_rows.astype(jnp.bfloat16), "dp", scatter_dimension=0, tiled=True
    ).astype(jnp.float32)
    d_packed = jnp.concatenate(
        [(d_query * scale).reshape(rows, width), d_key_value], axis=1
    ).astype(jnp.bfloat16)
    packed_sums = jnp.sum(d_packed.astype(jnp.float32), axis=0)
    grad_qkv = jnp.einsum("tc,te->ce", normed_low, d_packed, preferred_element_type=jnp.float32)
    d_normed = jnp.einsum("te,ce->tc", d_packed, qkv_full, preferred_element_type=jnp.float32)
    d_inputs, grad_gain_first, grad_shift_norm1 = norm1_back(d_normed)
    grad_tokens = d_mixed + d_inputs
    grad_gains = jnp.stack([grad_gain_first, grad_gain_second])
    grad_biases = jnp.stack(
        [
            grad_shift_norm1,
            packed_sums[:width],
            packed_sums[2 * width :],
            grad_shift_proj,
            grad_shift_norm2,
        ]
    )
    owned_qkv, owned_proj, owned_router, owned_gains, owned_biases = (
        lax.psum_scatter(grad_qkv, ("dp", "expert"), scatter_dimension=0, tiled=True),
        lax.psum_scatter(grad_proj, ("dp", "expert"), scatter_dimension=0, tiled=True),
        lax.psum_scatter(grad_router, ("dp", "expert"), scatter_dimension=0, tiled=True),
        lax.psum_scatter(grad_gains, ("dp", "expert"), scatter_dimension=1, tiled=True),
        lax.psum_scatter(grad_biases, ("dp", "expert"), scatter_dimension=1, tiled=True),
    )
    owned_up, owned_up_bias, owned_down, owned_down_bias = (
        lax.psum_scatter(
            grad_up[None].astype(jnp.bfloat16), "dp", scatter_dimension=2, tiled=True
        ).astype(jnp.float32),
        lax.psum_scatter(
            grad_up_bias[None].astype(jnp.bfloat16), "dp", scatter_dimension=1, tiled=True
        ).astype(jnp.float32),
        lax.psum_scatter(
            grad_down[None].astype(jnp.bfloat16), "dp", scatter_dimension=1, tiled=True
        ).astype(jnp.float32),
        lax.psum_scatter(
            grad_down_bias[None].astype(jnp.bfloat16), "dp", scatter_dimension=1, tiled=True
        ).astype(jnp.float32),
    )
    return (
        outputs[None],
        grad_tokens[None],
        owned_qkv,
        owned_proj,
        owned_router,
        owned_gains,
        owned_biases,
        owned_up,
        owned_up_bias,
        owned_down,
        owned_down_bias,
    )


def solution(mesh):
    placed = (
        P("expert", "dp", None),
        P(("dp", "expert"), None),
        P(("dp", "expert"), None),
        P(("dp", "expert"), None),
        P(None, ("dp", "expert")),
        P(None, ("dp", "expert")),
        P("expert", None, "dp"),
        P("expert", "dp"),
        P("expert", "dp", None),
        P("expert", "dp"),
        P("expert", "dp", None),
        P("expert", "dp", None),
        P("expert", None),
        P("expert", None),
        P("expert", "dp", None),
    )
    return jax.shard_map(
        shards,
        mesh=mesh,
        in_specs=placed,
        out_specs=(
            P("expert", "dp", None),
            P("expert", "dp", None),
            P(("dp", "expert"), None),
            P(("dp", "expert"), None),
            P(("dp", "expert"), None),
            P(None, ("dp", "expert")),
            P(None, ("dp", "expert")),
            P("expert", None, "dp"),
            P("expert", "dp"),
            P("expert", "dp", None),
            P("expert", "dp"),
        ),
        check_vma=False,
    )
```

profile of v0, /device:TPU:0, one launch (start us, length us, event | category | flops | bytes accessed | tf_op | source)
XLA Modules:
  0.0 1658.4 jit_solution(5418637222346388384)
XLA Ops:
  8.0 43.2 %all-gather = bf16[32,32,2]{1,2,0:T(2,128)(2,1)S(1)} all-gather(bf16[1,32,2]{1,2,0:T(2,128)(2,1)} %bitcast.257), channel_id=1, replica_groups=mesh['dp'=4,'expert'=8] {'dp','expert'}, dimensions={0}, use_global_device_ids=true | all-gather | bytes 4224 | tf_op jit(solution)/shard_map/all_gather | solution.py:74
  51.3 37.4 %all-gather.1 = bf16[32,32,5]{1,2,0:T(8,128)(2,1)S(1)} all-gather(bf16[1,32,5]{1,2,0:T(8,128)(2,1)} %bitcast.252), channel_id=1, replica_groups=mesh['dp'=4,'expert'=8] {'dp','expert'}, dimensions={0}, use_global_device_ids=true | all-gather | bytes 10560 | tf_op jit(solution)/shard_map/all_gather | solution.py:75
  99.6 40.3 %all-gather.11.cloned.1.call-done = bf16[512,2048]{1,0:T(8,128)(2,1)} async-done(((bf16[128,2048]{1,0:T(8,128)(2,1)}), bf16[512,2048]{1,0:T(8,128)(2,1)}) %all-gather.11.cloned.1.call-update) | async-done | bytes 2097168 | tf_op jit(solution)/shard_map/all_gather | solution.py:98
  147.7 50.2 %all-gather.13.cloned.1.call-done = bf16[1024,1024]{1,0:T(8,128)(2,1)} async-done(((bf16[32,1024]{1,0:T(8,128)(2,1)}), bf16[1024,1024]{1,0:T(8,128)(2,1)}) %all-gather.13.cloned.1.call-update) | async-done | bytes 2097168 | tf_op jit(solution)/shard_map/all_gather | solution.py:72
  205.0 9.8 all_gather.45
  214.8 15.4 all_gather.43
  230.2 41.5 %all-gather.2 = bf16[32,32,8]{1,2,0:T(8,128)(2,1)S(1)} all-gather(bf16[1,32,8]{1,2,0:T(8,128)(2,1)S(1)} %bitcast.255), channel_id=1, replica_groups=mesh['dp'=4,'expert'=8] {'dp','expert'}, dimensions={0}, use_global_device_ids=true | all-gather | bytes 16896 | tf_op jit(solution)/shard_map/all_gather | solution.py:73
  272.2 76.2 %all-gather.15.cloned.1.call-done = bf16[1,1024,4096]{2,1,0:T(8,128)(2,1)} async-done(((bf16[1,1024,1024]{2,1,0:T(8,128)(2,1)}), bf16[1,1024,4096]{2,1,0:T(8,128)(2,1)}) %all-gather.15.cloned.1.call-update) | async-done | bytes 8388624 | tf_op jit(solution)/shard_map/all_gather | solution.py:78
  348.4 6.2 fusion.8
  354.6 143.0 %all-gather.17.cloned.1.call-done = bf16[1,4096,1024]{2,1,0:T(8,128)(2,1)} async-done(((bf16[1,1024,1024]{2,1,0:T(8,128)(2,1)}), bf16[1,4096,1024]{2,1,0:T(8,128)(2,1)}) %all-gather.17.cloned.1.call-update) | async-done | bytes 8388624 | tf_op jit(solution)/shard_map/all_gather | solution.py:80
  497.6 5.8 fusion.26
  508.0 8.3 all-to-all-done.1
  517.3 10.7 all_to_all.20
  528.2 8.0 fusion.114
  537.3 6.3 fusion.29
  548.2 8.0 all-to-all-done.3
  577.1 32.7 %reduce-scatter.31.cloned.1.call-done = bf16[128,2048]{1,0:T(8,128)(2,1)} async-done(((bf16[512,2048]{1,0:T(8,128)(2,1)}), bf16[128,2048]{1,0:T(8,128)(2,1)}) %reduce-scatter.31.cloned.1.call-update) | async-done | bytes 524304
  612.4 5.2 fusion.106
  621.4 7.3 convert_bitcast_fusion
  630.0 5.7 convert_bitcast_fusion.1
  640.3 6.5 fusion.56
  646.9 98.7 %reduce-scatter.33.cloned.1.call-done = f32[32,8]{1,0:T(8,128)} async-done(((f32[1024,8]{1,0:T(8,128)}), f32[32,8]{1,0:T(8,128)}) %reduce-scatter.33.cloned.1.call-update) | async-done | bytes 1040
  746.9 16.5 reduce-scatter.41.cloned.1.call-done
  764.9 26.3 %reduce-scatter.39.cloned.1.call-done = bf16[1024,1]{1,0:T(8,128)(2,1)} async-done(((bf16[4096,1]{1,0:T(8,128)(2,1)}), bf16[1024,1]{1,0:T(8,128)(2,1)}) %reduce-scatter.39.cloned.1.call-update) | async-done | bytes 2064
  792.9 133.7 %reduce-scatter.35.cloned.1.call-done = f32[32,2]{1,0:T(8,128)} async-done(((f32[1024,2]{1,0:T(8,128)}), f32[32,2]{1,0:T(8,128)}) %reduce-scatter.35.cloned.1.call-update) | async-done | bytes 272
  927.9 130.8 %reduce-scatter.37.cloned.1.call-done = f32[32,5]{1,0:T(8,128)} async-done(((f32[1024,5]{1,0:T(8,128)}), f32[32,5]{1,0:T(8,128)}) %reduce-scatter.37.cloned.1.call-update) | async-done | bytes 656
  1060.1 141.2 %reduce-scatter.29.cloned.1.call-done = bf16[1,1024,1024]{2,1,0:T(8,128)(2,1)} async-done(((bf16[1,4096,1024]{2,1,0:T(8,128)(2,1)}), bf16[1,1024,1024]{2,1,0:T(8,128)(2,1)}) %reduce-scatter.29.cloned.1.call-update) | async-done | bytes 2097168 | tf_op jit(solution)/shard_map/reduce_scatter | solution.py:295
  1201.4 4.1 convert_element_type.182
  1205.5 143.5 %reduce-scatter.27.cloned.1.call-done = bf16[1,1024,1024]{2,1,0:T(8,128)(2,1)} async-done(((bf16[1,1024,4096]{2,1,0:T(8,128)(2,1)}), bf16[1,1024,1024]{2,1,0:T(8,128)(2,1)}) %reduce-scatter.27.cloned.1.call-update) | async-done | bytes 2097168 | tf_op jit(solution)/shard_map/reduce_scatter | solution.py:289
  1349.0 4.1 convert_element_type.176
  1353.0 140.4 %reduce-scatter.25.cloned.1.call-done = f32[32,1024]{1,0:T(8,128)} async-done(((f32[1024,1024]{1,0:T(8,128)}), f32[32,1024]{1,0:T(8,128)}) %reduce-scatter.25.cloned.1.call-update) | async-done | bytes 131088 | tf_op jit(solution)/shard_map/reduce_scatter | solution.py:283
  1493.4 158.0 %reduce-scatter.23.cloned.1.call-done = f32[32,3072]{1,0:T(8,128)} async-done(((f32[1024,3072]{1,0:T(8,128)}), f32[32,3072]{1,0:T(8,128)}) %reduce-scatter.23.cloned.1.call-update) | async-done | bytes 393232 | tf_op jit(solution)/shard_map/reduce_scatter | solution.py:282
  (193 shorter events, 78.3 us)
Async XLA Ops:
  7.2 84.0 %all-gather.9.cloned.1.call-start = ((), (), s32[]{:S(2)}) async-start(), calls=%async_computation.14 | async-start | bytes 6488064 | tf_op jit(solution)/shard_map/all_gather | solution.py:71
  7.9 132.0 %all-gather.11.cloned.1.call-start = ((), (), s32[]{:S(2)}) async-start(), calls=%async_computation.15 | async-start | bytes 2621440 | tf_op jit(solution)/shard_map/all_gather | solution.py:98
  96.0 101.9 %all-gather.13.cloned.1.call-start = ((), (), s32[]{:S(2)}) async-start(), calls=%async_computation.16 | async-start | bytes 2162688 | tf_op jit(solution)/shard_map/all_gather | solution.py:72
  96.7 251.6 %all-gather.15.cloned.1.call-start = ((), (), s32[]{:S(2)}) async-start(), calls=%async_computation.17 | async-start | bytes 10485760 | tf_op jit(solution)/shard_map/all_gather | solution.py:78
  97.3 400.3 %all-gather.17.cloned.1.call-start = ((), (), s32[]{:S(2)}) async-start(), calls=%async_computation.18 | async-start | bytes 10485760 | tf_op jit(solution)/shard_map/all_gather | solution.py:80
  99.6 43.1 %copy-start.17 = (bf16[128,1024]{0,1:T(8,128)(2,1)}, bf16[128,1024]{0,1:T(8,128)(2,1)S(1)}, u32[]{:S(2)}) copy-start(bf16[128,1024]{0,1:T(8,128)(2,1)S(1)} %copy.58) | copy-start | bytes 786436
  145.7 52.2 %copy-start.2 = (bf16[1,128,1024]{2,1,0:T(8,128)(2,1)S(1)}, bf16[1,128,1024]{2,1,0:T(8,128)(2,1)}, u32[]{:S(2)}) copy-start(bf16[1,128,1024]{2,1,0:T(8,128)(2,1)} %param.15) | copy-start | bytes 786436
  147.7 52.6 %copy-start.21 = (bf16[128,16,64]{0,2,1:T(8,128)(2,1)}, bf16[128,16,64]{0,2,1:T(8,128)(2,1)S(1)}, u32[]{:S(2)}) copy-start(bf16[128,16,64]{0,2,1:T(8,128)(2,1)S(1)} %get-tuple-element.134) | copy-start | bytes 786436
  197.9 7.1 copy-start.31
  197.9 16.9 %copy-start.27 = (bf16[1,1024]{1,0:T(2,128)(2,1)S(1)}, bf16[1,1024]{1,0:T(2,128)(2,1)}, u32[]{:S(2)}) copy-start(bf16[1,1024]{1,0:T(2,128)(2,1)} %param.22) | copy-start | bytes 6148
  197.9 32.3 %copy-start.29 = (bf16[32,8]{0,1:T(8,128)(2,1)S(1)}, bf16[32,8]{0,1:T(8,128)(2,1)}, u32[]{:S(2)}) copy-start(bf16[32,8]{0,1:T(8,128)(2,1)} %param.18) | copy-start | bytes 1540
  200.5 154.1 %copy-start.12 = (bf16[128,1024]{1,0:T(8,128)(2,1)}, bf16[128,1024]{1,0:T(8,128)(2,1)S(1)}, u32[]{:S(2)}) copy-start(bf16[128,1024]{1,0:T(8,128)(2,1)S(1)} %add_convert_fusion.1) | copy-start | bytes 786436
  201.5 70.6 %all-to-all-start = ((bf16[8,18,1024]{2,1,0:T(8,128)(2,1)}), bf16[8,18,1024]{2,1,0:T(8,128)(2,1)S(1)}, u32[]{:S(2)}, u32[]{:S(2)}) async-start(bf16[8,18,1024]{2,1,0:T(8,128)(2,1)} %convolution_convert_fusion.2), calls=%async_computation | async-start | bytes 786432 | tf_op jit(solution)/shard_map/all_to_all | solution.py:168
  272.2 82.4 %copy-start.13 = (bf16[144,1024]{1,0:T(8,128)(2,1)}, bf16[144,1024]{1,0:T(8,128)(2,1)S(1)}, u32[]{:S(2)}) copy-start(bf16[144,1024]{1,0:T(8,128)(2,1)S(1)} %reshape.239) | copy-start | bytes 884740
  497.6 18.7 %copy-start.8 = (bf16[1,128,1024]{2,1,0:T(8,128)(2,1)S(1)}, bf16[1,128,1024]{2,1,0:T(8,128)(2,1)}, u32[]{:S(2)}) copy-start(bf16[1,128,1024]{2,1,0:T(8,128)(2,1)} %param.29) | copy-start | bytes 786436
  504.3 12.0 all-to-all-start.1
  528.0 8.1 copy-start.15
  528.1 8.0 copy-start.24
  544.4 11.7 all-to-all-start.3
  547.9 61.9 %reduce-scatter.31.cloned.1.call-start = ((), (), s32[]{:S(2)}) async-start(), calls=%async_computation.23 | async-start | bytes 2621440
  569.3 6.2 copy-start.5
  569.3 176.2 %reduce-scatter.33.cloned.1.call-start = ((), (), s32[]{:S(2)}) async-start(), calls=%async_computation.24 | async-start | bytes 540672
  571.7 191.7 %reduce-scatter.41.cloned.1.call-start = ((), (), s32[]{:S(2)}) async-start(), calls=%async_computation.28 | async-start | bytes 327680
  573.8 217.4 %reduce-scatter.39.cloned.1.call-start = ((), (), s32[]{:S(2)}) async-start(), calls=%async_computation.27 | async-start | bytes 1310720
  575.5 351.1 %reduce-scatter.35.cloned.1.call-start = ((), (), s32[]{:S(2)}) async-start(), calls=%async_computation.25 | async-start | bytes 540672
  612.3 6.8 copy-start.7
  612.3 6.8 copy-start.9
  619.0 439.7 %reduce-scatter.37.cloned.1.call-start = ((), (), s32[]{:S(2)}) async-start(), calls=%async_computation.26 | async-start | bytes 540672
  621.3 580.1 %reduce-scatter.29.cloned.1.call-start = ((), (), s32[]{:S(2)}) async-start(), calls=%async_computation.22 | async-start | bytes 10485760 | tf_op jit(solution)/shard_map/reduce_scatter | solution.py:295
  628.7 720.3 %reduce-scatter.27.cloned.1.call-start = ((), (), s32[]{:S(2)}) async-start(), calls=%async_computation.21 | async-start | bytes 10485760 | tf_op jit(solution)/shard_map/reduce_scatter | solution.py:289
  635.7 857.7 %reduce-scatter.25.cloned.1.call-start = ((), (), s32[]{:S(2)}) async-start(), calls=%async_computation.20 | async-start | bytes 4325376 | tf_op jit(solution)/shard_map/reduce_scatter | solution.py:283
  639.4 1012.1 %reduce-scatter.23.cloned.1.call-start = ((), (), s32[]{:S(2)}) async-start(), calls=%async_computation.19 | async-start | bytes 12976128 | tf_op jit(solution)/shard_map/reduce_scatter | solution.py:282
  (19 other events, 37.7 us)
Sparse Core Ops, SparseCore 0:
  10.9 71.9 all-gather.8
  96.1 43.7 all-gather.10
  142.8 55.0 all-gather.12
  199.3 149.0 all-gather.14
  349.8 147.7 all-gather.16
  569.4 40.3 reduce-scatter.30
  612.1 133.3 reduce-scatter.32
  747.8 15.5 reduce-scatter.40
  765.8 25.3 reduce-scatter.38
  793.8 132.6 reduce-scatter.34
  928.9 129.7 reduce-scatter.36
  1061.0 140.3 reduce-scatter.28
  1203.7 145.1 reduce-scatter.26
  1351.7 141.6 reduce-scatter.24
  1499.9 151.5 reduce-scatter.22
where the time goes:
time: 1670 us; the launch traced here: 1660 us
  waiting for transfers between devices  1350 us (81%)
  blocking collectives  158 us (9%)
  matrix products  77.5 us (5%)
  local copies, waits for them, and re-layouts  27.1 us (2%)
  other arithmetic  18.6 us (1%)
    unnamed x21, waiting for transfers between devices  441 us
    reduce_scatter x1, waiting for transfers between devices, shards(): lax.psum_scatter(grad_qkv, ('dp', 'expert'), scatter_dimension=0, tiled=T...  158 us
    reduce_scatter x1, waiting for transfers between devices, shards(): lax.psum_scatter(grad_up[None].astype(jnp.bfloat16), 'dp', scatter_dimens...  144 us
    all_gather x1, waiting for transfers between devices, shards(): lax.all_gather(down_weight, 'dp', axis=1, tiled=True)  143 us
    reduce_scatter x1, waiting for transfers between devices, shards(): lax.psum_scatter(grad_down[None].astype(jnp.bfloat16), 'dp', scatter_dime...  141 us
    reduce_scatter x1, waiting for transfers between devices, shards(): lax.psum_scatter(grad_proj, ('dp', 'expert'), scatter_dimension=0, tiled=...  140 us
    all_gather x1, waiting for transfers between devices, shards(): lax.all_gather(up_weight, 'dp', axis=2, tiled=True)  76.2 us
    all_gather x1, waiting for transfers between devices, shards(): lax.all_gather(proj_weight, ('dp', 'expert'), axis=0, tiled=True)  50.2 us
  transfers between devices with their start and end apart: 18, of which 16 were waited for; matrix products, arithmetic and copies ran while one was open for 5% of the time, Pallas kernels for 0%

commit v1 on v0

v1 whole, which is shorter than its diff:
```python
import jax
import jax.numpy as jnp
from jax import lax
from jax.sharding import PartitionSpec as P

H = 16
NSEG = 7
EPS = 1e-05
NEG = -1e30
BF = jnp.bfloat16
F32 = jnp.float32


def mm(a, b, ca=1, cb=0):
    return lax.dot_general(a, b, (((ca,), (cb,)), ((), ())), preferred_element_type=F32)


def ahead(x, step):
    n = lax.axis_size("dp")
    return lax.ppermute(x, "dp", [(i, (i + step) % n) for i in range(n)])


def flip(x, bits):
    n = lax.axis_size("expert")
    return lax.ppermute(x, "expert", [(i, i ^ bits) for i in range(n)])


def gather_experts(x):
    n = lax.axis_size("expert")
    mine = [x] + [flip(x, 2 * k) for k in range(1, n // 2)]
    out = []
    for block in mine:
        out += [block, flip(block, 1)]
    return out


def in_order(blocks, me):
    n = len(blocks)
    stacked = jnp.stack(blocks)
    return jnp.take(stacked, me ^ jnp.arange(n), axis=0)


def rotated(blocks, me):
    n = len(blocks)
    back = jnp.stack([blocks[0]] + blocks[:0:-1])
    twice = jnp.concatenate([back, back])
    return lax.dynamic_slice_in_dim(twice, (n - me) % n, n, 0)


def pick(x, index):
    return lax.dynamic_index_in_dim(x, index, 0, keepdims=False)


def normalise(values):
    mean = jnp.mean(values, axis=-1, keepdims=True)
    centred = values - mean
    scale = lax.rsqrt(jnp.mean(centred * centred, axis=-1, keepdims=True) + EPS)
    return centred * scale, scale


def norm_back(upstream, gain, unit, scale):
    e = upstream * gain
    return scale * (
        e
        - jnp.mean(e, axis=-1, keepdims=True)
        - unit * jnp.mean(e * unit, axis=-1, keepdims=True)
    )


def ancestry(parents):
    labels = jnp.arange(NSEG, dtype=jnp.int32)
    direct = (labels[None, :] == parents[:, None]).astype(F32)
    reach = jnp.minimum(direct + jnp.eye(NSEG, dtype=F32), 1.0)
    for _ in range(3):
        reach = jnp.minimum(mm(reach, reach), 1.0)
    return reach


def slot_table(route_ids, order, experts, capacity):
    labels = jnp.arange(experts, dtype=jnp.int32)
    expert_hot = route_ids[:, None] == labels[None, :]
    same = route_ids[:, None] == route_ids[None, :]
    before = order[None, :] < order[:, None]
    rank = jnp.sum((same & before).astype(jnp.int32), axis=1)
    slot_hot = rank[:, None] == jnp.arange(capacity, dtype=jnp.int32)[None, :]
    table = expert_hot[:, :, None] & slot_hot[:, None, :]
    return expert_hot.astype(F32), table.reshape(table.shape[0], -1).astype(BF)


def to_experts(x, n_ex):
    blocks = x.reshape(n_ex, -1, x.shape[-1])
    return lax.all_to_all(blocks, "expert", split_axis=0, concat_axis=0, tiled=True).reshape(x.shape)


def owned_sum(payload, me_d, me_e):
    n_ex = payload.shape[1]
    low = payload.astype(BF)
    near = jnp.stack([pick_axis1(low, me_e ^ (2 * q + 1)) for q in range(n_ex // 2)])
    came = flip(near, 1)
    own = [
        pick_axis1(payload, me_e ^ (2 * q)) + came[q].astype(F32) for q in range(n_ex // 2)
    ]
    total = own[0]
    for q in range(1, n_ex // 2):
        total = total + flip(own[q].astype(BF), 2 * q).astype(F32)
    return total


def pick_axis1(x, index):
    return lax.dynamic_index_in_dim(x, index, 1, keepdims=False)


def shards(
    tokens,
    qkv_weight,
    proj_weight,
    router_weight,
    norm_gains,
    biases,
    up_weight,
    up_bias,
    down_weight,
    down_bias,
    routes,
    slot_order,
    segments,
    parents,
    cotangent,
):
    n_dp, n_ex = lax.axis_size("dp"), lax.axis_size("expert")
    me_d, me_e = lax.axis_index("dp"), lax.axis_index("expert")
    rows, width = tokens.shape[1], tokens.shape[2]
    part = width // n_dp
    head_dim = width // H
    heads = part // head_dim
    scale = head_dim ** (-0.5)
    own = qkv_weight.shape[0]
    experts = router_weight.shape[1]
    capacity = (9 * rows + 8 * experts - 1) // (8 * experts)

    by_part = jnp.transpose(qkv_weight.reshape(own, 3, n_dp, part), (2, 0, 1, 3)).reshape(
        n_dp, own, 3 * part
    )
    sliced = [pick(by_part, me_d)]
    for j in range(1, n_dp):
        sliced.append(ahead(pick(by_part, (me_d + j) % n_dp), j))
    line_qkv = rotated(sliced, me_d)
    token_blocks = [tokens[0]] + [ahead(tokens[0], j) for j in range(1, n_dp)]
    small = jnp.concatenate(
        [
            router_weight,
            norm_gains.T,
            biases.T,
            jnp.zeros((own, 128 - experts - 7), BF),
        ],
        axis=1,
    )
    mine = jnp.concatenate([proj_weight, small], axis=1)
    line_proj = rotated([mine] + [ahead(mine, j) for j in range(1, n_dp)], me_d)
    qkv_blocks = gather_experts(line_qkv)
    proj_blocks = gather_experts(line_proj)
    qkv_own = jnp.swapaxes(in_order(qkv_blocks, me_e), 0, 1).reshape(width, 3 * part)
    proj_all = jnp.swapaxes(in_order(proj_blocks, me_e), 0, 1).reshape(width, width + 128)
    proj_full = proj_all[:, :width]
    router_full = proj_all[:, width : width + experts]
    vectors = proj_all[:, width + experts : width + experts + 7].T.astype(F32)
    gain1, gain2 = vectors[0], vectors[1]
    shift1, shift_q, shift_v, shift_proj, shift2 = (vectors[2 + i] for i in range(5))

    expert_hot, table = slot_table(routes[0, :, 0], slot_order[0, 0], experts, capacity)
    upstream = cotangent[0].astype(F32)
    grads_out = mm(table, cotangent[0], 0, 0).astype(BF)
    grads_in = to_experts(grads_out, n_ex)
    grads_all = jnp.concatenate([grads_in] + [ahead(grads_in, j) for j in range(1, n_dp)])

    x_tree = jnp.concatenate(token_blocks).astype(F32)
    unit1, rstd1 = normalise(x_tree)
    normed1 = (unit1 * gain1 + shift1).astype(BF)
    own_q = lax.dynamic_slice_in_dim(shift_q, me_d * part, part)
    own_v = lax.dynamic_slice_in_dim(shift_v, me_d * part, part)
    shift = jnp.concatenate([own_q, jnp.zeros((part,), F32), own_v])
    packed = (mm(normed1, qkv_own) + shift).astype(BF)
    length = n_dp * rows
    seg_blocks = segments[0].reshape(n_dp, rows)
    order_d = [(me_d - j) % n_dp for j in range(n_dp)]
    seg = jnp.concatenate([pick(seg_blocks, d) for d in order_d])
    pos = jnp.concatenate([d * rows + jnp.arange(rows, dtype=jnp.int32) for d in order_d])
    reach = ancestry(parents[0])
    hot = (seg[:, None] == jnp.arange(NSEG, dtype=jnp.int32)[None, :]).astype(F32)
    allowed = (mm(mm(hot, reach), hot, 1, 1) > 0.5) & (pos[None, :] <= pos[:, None])
    q = packed[:, :part].reshape(length, heads, head_dim)
    k = packed[:, part : 2 * part].reshape(length, heads, head_dim)
    v = packed[:, 2 * part :].reshape(length, heads, head_dim)
    scores = jnp.einsum("qhd,khd->hqk", q, k, preferred_element_type=F32) * scale
    scores = jnp.where(allowed[None], scores, NEG)
    top = jnp.max(scores, axis=-1, keepdims=True)
    total = jnp.sum(jnp.exp(scores - top), axis=-1, keepdims=True)
    log_total = top + jnp.log(total)
    probs = jnp.exp(scores - log_total)
    probs_low = probs.astype(BF)
    attended = jnp.einsum("hqk,khd->qhd", probs_low, v, preferred_element_type=F32)
    attended = attended.astype(BF).reshape(n_dp, rows, part)
    att = [attended[0]] + [ahead(attended[j], -j) for j in range(1, n_dp)]
    att_full = jnp.concatenate(att, axis=1)
    proj_rel = jnp.concatenate(
        [
            lax.dynamic_slice_in_dim(proj_full, ((me_d + j) % n_dp) * part, part, 0)
            for j in range(n_dp)
        ]
    )
    inputs = tokens[0].astype(F32)
    mixed = inputs + mm(att_full, proj_rel) + shift_proj
    unit2, rstd2 = normalise(mixed)
    normed2 = (unit2 * gain2 + shift2).astype(BF)
    logits = mm(normed2, router_full)
    p = jax.nn.softmax(logits, axis=-1)
    gate = jnp.sum(p * expert_hot, axis=-1)
    sent = mm(table, normed2, 0, 0).astype(BF)

    slots_in = to_experts(sent, n_ex)
    slots = jnp.concatenate([slots_in] + [ahead(slots_in, j) for j in range(1, n_dp)])
    slot_p = jax.nn.softmax(mm(slots, router_full), axis=-1)
    slot_gate = lax.dynamic_slice_in_dim(slot_p, me_e, 1, 1)
    d_rows = (slot_gate * grads_all.astype(F32)).astype(BF)
    up, down = up_weight[0], down_weight[0]
    pre = mm(slots, up) + up_bias[0].astype(F32)
    act, act_back = jax.vjp(lambda u: jax.nn.gelu(u, approximate=True), pre)
    act_low = act.astype(BF)
    result = mm(act_low, down)
    spread = lax.dynamic_update_slice_in_dim(
        jnp.zeros((width,), F32), down_bias[0].astype(F32), me_d * part, 0
    )
    result = (result + spread).astype(BF).reshape(n_dp, -1, width)
    d_pre = act_back(mm(d_rows, down, 1, 1))[0]
    d_pre_low = d_pre.astype(BF)
    d_slots = mm(d_pre_low, up, 1, 1).astype(BF).reshape(n_dp, -1, width)
    both = jnp.concatenate([result, d_slots], axis=1)
    line = both[0].astype(F32)
    for j in range(1, n_dp):
        line = line + ahead(both[j], -j).astype(F32)
    line = line.astype(BF)
    slot_rows = n_ex * capacity
    back = jnp.concatenate(
        [line[:slot_rows].reshape(n_ex, capacity, width), line[slot_rows:].reshape(n_ex, capacity, width)], axis=1
    )
    back = lax.all_to_all(back, "expert", split_axis=0, concat_axis=0, tiled=True)
    returned = back[:, :capacity].reshape(slot_rows, width)
    d_sent = back[:, capacity:].reshape(slot_rows, width)
    grad_up = mm(slots, d_pre_low, 0, 0)
    grad_down = mm(act_low, d_rows, 0, 0)
    grad_up_bias = jnp.sum(d_pre, axis=0)
    all_down_bias = jnp.sum(d_rows.astype(F32), axis=0)
    grad_down_bias = lax.dynamic_slice_in_dim(all_down_bias, me_d * part, part)

    combined = mm(table, returned)
    outputs = (mixed + gate[:, None] * combined).astype(BF)
    d_gate = jnp.sum(upstream * combined, axis=-1)
    d_logits = p * (d_gate[:, None] * expert_hot - (d_gate * gate)[:, None])
    grad_router = mm(normed2, d_logits.astype(BF), 0, 0)
    d_normed2 = mm(table, d_sent) + mm(d_logits.astype(BF), router_full, 1, 1)
    grad_gain2 = jnp.sum(d_normed2 * unit2, axis=0)
    grad_shift2 = jnp.sum(d_normed2, axis=0)
    d_mixed = upstream + norm_back(d_normed2, gain2, unit2, rstd2)
    grad_shift_proj = jnp.sum(d_mixed, axis=0)
    d_mixed_low = d_mixed.astype(BF)
    grad_proj = mm(att_full, d_mixed_low, 0, 0)
    d_att_own = mm(d_mixed_low, proj_rel, 1, 1).astype(BF)
    d_att = [d_att_own[:, :part]] + [
        ahead(d_att_own[:, j * part : (j + 1) * part], j) for j in range(1, n_dp)
    ]
    d_heads = jnp.concatenate(d_att).reshape(length, heads, head_dim)
    proj_pay = owned_sum(grad_proj.reshape(n_dp, n_ex, own, width), me_d, me_e)
    proj_low = proj_pay.astype(BF)
    owned_proj = proj_pay[0]
    for j in range(1, n_dp):
        owned_proj = owned_proj + ahead(proj_low[j], j).astype(F32)

    d_value = jnp.einsum("hqk,qhd->khd", probs_low, d_heads, preferred_element_type=F32)
    d_probs = jnp.einsum("qhd,khd->hqk", d_heads, v, preferred_element_type=F32)
    delta = jnp.sum(d_probs * probs, axis=-1, keepdims=True)
    d_scores = (probs * (d_probs - delta)).astype(BF)
    d_query = jnp.einsum("hqk,khd->qhd", d_scores, k, preferred_element_type=F32) * scale
    d_key = jnp.einsum("hqk,qhd->khd", d_scores, q, preferred_element_type=F32) * scale
    d_packed = jnp.concatenate(
        [t.reshape(length, part) for t in (d_query, d_key, d_value)], axis=1
    ).astype(BF)
    d_normed = mm(d_packed, qkv_own, 1, 1)
    d_blocks = d_normed.astype(BF).reshape(n_dp, rows, width)
    d_own = d_normed[:rows]
    for j in range(1, n_dp):
        d_own = d_own + ahead(d_blocks[j], -j).astype(F32)
    grad_qkv = mm(normed1, d_packed, 0, 0)
    grad_gain1 = jnp.sum(d_normed * unit1, axis=0)
    grad_shift1 = jnp.sum(d_normed, axis=0)
    sums = jnp.sum(d_packed.astype(F32), axis=0)
    place = lambda s: lax.dynamic_update_slice_in_dim(jnp.zeros((width,), F32), s, me_d * part, 0)
    extra = jnp.stack(
        [
            grad_gain1,
            grad_gain2,
            grad_shift1,
            place(sums[:part]),
            place(sums[2 * part :]),
            grad_shift_proj,
            grad_shift2,
        ],
        axis=1,
    )
    extra = jnp.concatenate([grad_router, extra, jnp.zeros((width, 128 - experts - 7), F32)], axis=1)
    pay = jnp.concatenate([grad_qkv, extra], axis=1).reshape(n_dp, n_ex, own, 3 * part + 128)
    pay = owned_sum(pay, me_d, me_e)
    low = pay.astype(BF)
    got = [pick(pay, me_d)]
    for j in range(1, n_dp):
        got.append(ahead(pick(low, (me_d + j) % n_dp), j).astype(F32))
    owned_small = got[0][:, 3 * part :]
    for j in range(1, n_dp):
        owned_small = owned_small + got[j][:, 3 * part :]
    cols = rotated([g[:, : 3 * part] for g in got], me_d)
    owned_qkv = jnp.transpose(cols.reshape(n_dp, own, 3, part), (1, 2, 0, 3)).reshape(own, 3 * width)
    owned_router = owned_small[:, :experts]
    owned_vec = owned_small[:, experts : experts + 7].T
    grad_tokens = d_mixed + norm_back(d_own, gain1, unit1[:rows], rstd1[:rows])
    return (
        outputs[None],
        grad_tokens[None],
        owned_qkv,
        owned_proj,
        owned_router,
        owned_vec[:2],
        owned_vec[2:],
        grad_up[None],
        grad_up_bias[None],
        grad_down[None],
        grad_down_bias[None],
    )


def solution(mesh):
    line = P(("dp", "expert"), None)
    across = P(None, ("dp", "expert"))
    act = P("expert", "dp", None)
    return jax.shard_map(
        shards,
        mesh=mesh,
        in_specs=(
            act,
            line,
            line,
            line,
            across,
            across,
            P("expert", None, "dp"),
            P("expert", "dp"),
            act,
            P("expert", "dp"),
            act,
            act,
            P("expert", None),
            P("expert", None),
            act,
        ),
        out_specs=(
            act,
            act,
            line,
            line,
            line,
            across,
            across,
            P("expert", None, "dp"),
            P("expert", "dp"),
            act,
            P("expert", "dp"),
        ),
        check_vma=False,
    )
```

time: 1670 us -> 374 us (0.22)
  waiting for transfers between devices: 1350 us -> 85.1 us
  blocking collectives: 158 us -> 0 us
  starting transfers between devices: 11.6 us -> 112 us
  local copies, waits for them, and re-layouts: 27.1 us -> 96.7 us
  matrix products: 77.5 us -> 44 us
    reduce_scatter x4 -> x0, waiting for transfers between devices: 583 us -> none  [the longest x1 158 us: shards(): lax.psum_scatter(grad_qkv, ('dp', 'expert'), scatter_dimension=0, tiled=T...]
    unnamed x21 -> x0, waiting for transfers between devices: 441 us -> none
    all_gather x5 -> x0, waiting for transfers between devices: 310 us -> none  [the longest x1 143 us: shards(): lax.all_gather(down_weight, 'dp', axis=1, tiled=True)]
    all_gather x5 -> x0, blocking collectives: 147 us -> none  [the longest x1 43.2 us: shards(): lax.all_gather(norm_gains, ('dp', 'expert'), axis=1, tiled=True)]
    ppermute x0 -> x55, starting transfers between devices: none -> 99.9 us  [the longest x33 85.3 us: ahead(): return lax.ppermute(x, 'dp', [(i, (i + step) % n) for i in range(n)])]
    ppermute x0 -> x55, waiting for transfers between devices: none -> 78.5 us  [the longest x33 58 us: ahead(): return lax.ppermute(x, 'dp', [(i, (i + step) % n) for i in range(n)])]
    dot_general x29, matrix products: 75.1 us -> 44 us  [the longest x23 35.6 us: mm(): lax.dot_general(a, b, (((ca,), (cb,)), ((), ())), preferred_element_type=...]
    unnamed x78 -> x203, local copies, waits for them, and re-layouts: 21 us -> 42.9 us
  transfers between devices with their start and end apart: 18 -> 58, of which waited for: 16 -> 21; matrix products, arithmetic and copies ran while one was open for 5% -> 38% of each run, Pallas kernels for 0% -> 0%
where the time goes in v1:
time: 374 us; the launch traced here: 368 us
  starting transfers between devices  112 us (30%)
  local copies, waits for them, and re-layouts  96.7 us (26%)
  waiting for transfers between devices  85.1 us (23%)
  matrix products  44 us (12%)
  other arithmetic  27.8 us (7%)
    ppermute x33, starting transfers between devices, ahead(): return lax.ppermute(x, 'dp', [(i, (i + step) % n) for i in range(n)])  85.3 us
    ppermute x33, waiting for transfers between devices, ahead(): return lax.ppermute(x, 'dp', [(i, (i + step) % n) for i in range(n)])  58 us
    unnamed x203, local copies, waits for them, and re-layouts  42.9 us
    dot_general x23, matrix products, mm(): lax.dot_general(a, b, (((ca,), (cb,)), ((), ())), preferred_element_type=...  35.6 us
    ppermute x22, waiting for transfers between devices, flip(): return lax.ppermute(x, 'expert', [(i, i ^ bits) for i in range(n)])  20.5 us
    concatenate x18, local copies, waits for them, and re-layouts, shards(): jnp.concatenate([grad_qkv, extra], axis=1)  16.2 us
    ppermute x22, starting transfers between devices, flip(): return lax.ppermute(x, 'expert', [(i, i ^ bits) for i in range(n)])  14.6 us
    all_to_all x2, starting transfers between devices, to_experts(): lax.all_to_all(blocks, 'expert', split_axis=0, concat_axis=0, tiled=True)  8.31 us
  transfers between devices with their start and end apart: 58, of which 21 were waited for; matrix products, arithmetic and copies ran while one was open for 38% of the time, Pallas kernels for 0%

profile of v1, /device:TPU:0, one launch (start us, length us, event | category | flops | bytes accessed | tf_op | source)
XLA Modules:
  0.0 368.4 jit_solution(17046494820258534874)
XLA Ops:
  4.1 5.1 %collective-permute-start.3 = (bf16[32,1152]{1,0:T(8,128)(2,1)S(1)}, bf16[32,1152]{1,0:T(8,128)(2,1)S(1)}, u32[]{:S(2)}, u32[]{:S(2)}) collective-permute-start(bf16[32,1152]{1,0:T(8,128)(2,1)S(1)} %concatenate.75), channel_id=1, source_target_pairs={{0,24},{8,0},{16,8},{24,16},{1,25},{9,1},{17,9},{25,17},{2,26},{10... | collective-permute-start | bytes 221192 | tf_op jit(solution)/shard_map/ppermute | solution.py:20
  12.3 2.8 collective-permute-start.13
  19.6 4.2 %all-to-all-start.1 = ((bf16[8,18,1024]{2,1,0:T(8,128)(2,1)}), bf16[8,18,1024]{2,1,0:T(8,128)(2,1)}, u32[]{:S(2)}, u32[]{:S(2)}) async-start(bf16[8,18,1024]{2,1,0:T(8,128)(2,1)} %reshape.333), calls=%async_computation.1 | async-start | bytes 786432 | tf_op jit(solution)/shard_map/all_to_all | solution.py:92
  27.9 3.8 %collective-permute-start.2 = (bf16[128,1024]{1,0:T(8,128)(2,1)S(1)}, bf16[128,1024]{1,0:T(8,128)(2,1)S(1)}, u32[]{:S(2)}, u32[]{:S(2)}) collective-permute-start(bf16[128,1024]{1,0:T(8,128)(2,1)S(1)} %bitcast.353), channel_id=1, source_target_pairs={{0,24},{8,0},{16,8},{24,16},{1,25},{9,1},{17,9},{25,17},{2,26},{10... | collective-permute-start | bytes 786440 | tf_op jit(solution)/shard_map/ppermute | solution.py:20
  60.8 3.8 %collective-permute-done.19 = bf16[4,32,768]{2,1,0:T(8,128)(2,1)S(1)} collective-permute-done((bf16[4,32,768]{2,1,0:T(8,128)(2,1)S(1)}, bf16[4,32,768]{2,1,0:T(8,128)(2,1)S(1)}, u32[]{:S(2)}, u32[]{:S(2)}) %collective-permute-start.19) | collective-permute-done | bytes 196640 | tf_op jit(solution)/shard_map/ppermute | solution.py:25
  65.1 3.9 %collective-permute-done.7 = bf16[4,32,1152]{2,1,0:T(8,128)(2,1)} collective-permute-done((bf16[4,32,1152]{2,1,0:T(8,128)(2,1)S(1)}, bf16[4,32,1152]{2,1,0:T(8,128)(2,1)}, u32[]{:S(2)}, u32[]{:S(2)}) %collective-permute-start.7) | collective-permute-done | bytes 294944 | tf_op jit(solution)/shard_map/ppermute | solution.py:25
  70.7 5.9 %collective-permute-done.9 = bf16[4,32,1152]{2,1,0:T(8,128)(2,1)} collective-permute-done((bf16[4,32,1152]{2,1,0:T(8,128)(2,1)S(1)}, bf16[4,32,1152]{2,1,0:T(8,128)(2,1)}, u32[]{:S(2)}, u32[]{:S(2)}) %collective-permute-start.9) | collective-permute-done | bytes 294944 | tf_op jit(solution)/shard_map/ppermute | solution.py:25
  80.7 3.3 gather_fusion.1
  95.4 4.0 %gather_fusion = bf16[8,4,32,1152]{3,2,1,0:T(8,128)(2,1)} fusion(bf16[8,4,32,1152]{3,2,1,0:T(8,128)(2,1)} %bitcast_dynamic-update-slice_fusion, s32[1024]{0:T(1024)} %pad_clamp_fusion), kind=kCustom, calls=%fused_computation | custom fusion | bytes 4718624 | tf_op jit(solution)/shard_map/jit(_take)/gather | solution.py:40
  113.7 3.4 collective-permute-start.25
  120.2 3.3 collective-permute-done.24
  127.4 4.1 %all-to-all-start = ((bf16[8,18,1024]{2,1,0:T(8,128)(2,1)}), bf16[8,18,1024]{2,1,0:T(8,128)(2,1)}, u32[]{:S(2)}, u32[]{:S(2)}) async-start(bf16[8,18,1024]{2,1,0:T(8,128)(2,1)} %reshape.330), calls=%async_computation | async-start | bytes 786432 | tf_op jit(solution)/shard_map/all_to_all | solution.py:92
  133.7 3.0 collective-permute-start.31
  147.0 10.4 %collective-permute-done.26 = bf16[144,1024]{1,0:T(8,128)(2,1)S(1)} collective-permute-done((bf16[144,1024]{1,0:T(8,128)(2,1)}, bf16[144,1024]{1,0:T(8,128)(2,1)S(1)}, u32[]{:S(2)}, u32[]{:S(2)}) %collective-permute-start.26) | collective-permute-done | bytes 294944 | tf_op jit(solution)/shard_map/ppermute | solution.py:20
  157.4 19.2 %collective-permute-start.29 = (bf16[144,1024]{1,0:T(8,128)(2,1)}, bf16[144,1024]{1,0:T(8,128)(2,1)S(1)}, u32[]{:S(2)}, u32[]{:S(2)}) collective-permute-start(bf16[144,1024]{1,0:T(8,128)(2,1)} %reshape.334), channel_id=1, source_target_pairs={{0,8},{8,16},{16,24},{24,0},{1,9},{9,17},{17,25},{25,1},{2,10},{10... | collective-permute-start | bytes 884744 | tf_op jit(solution)/shard_map/ppermute | solution.py:20
  176.6 6.4 %collective-permute-done.27 = bf16[144,1024]{1,0:T(8,128)(2,1)S(1)} collective-permute-done((bf16[144,1024]{1,0:T(8,128)(2,1)}, bf16[144,1024]{1,0:T(8,128)(2,1)S(1)}, u32[]{:S(2)}, u32[]{:S(2)}) %collective-permute-start.27) | collective-permute-done | bytes 294944 | tf_op jit(solution)/shard_map/ppermute | solution.py:20
  187.8 4.6 %fusion.127 = (f32[1024]{0:T(1024)}, bf16[576,1024]{1,0:T(8,128)(2,1)S(1)}) fusion(f32[576,1024]{1,0:T(8,128)S(1)} %fusion.17, f32[1024]{0:T(1024)S(1)} %bitcast.379, bf16[1,1024,1024]{2,1,0:T(8,128)(2,1)S(1)} %copy-done, bf16[144,1024]{1,0:T(8,128)(2,1)} %collective-permute-done.31, bf16[144,1024]{1,0:T(8,128)(2,1)} %collective-permute-done.30, ...), kind=kOutput, calls=%fused_computation.320 | convolution fusion | flops 1226832896 | bytes 6826240 | tf_op jit(solution)/shard_map/dot_general | solution.py:15
  193.9 6.3 %collective-permute-start.34 = (bf16[288,1024]{1,0:T(8,128)(2,1)S(1)}, bf16[288,1024]{1,0:T(8,128)(2,1)S(1)}, u32[]{:S(2)}, u32[]{:S(2)}) collective-permute-start(bf16[288,1024]{1,0:T(8,128)(2,1)S(1)} %get-tuple-element.66), channel_id=1, source_target_pairs={{0,8},{8,16},{16,24},{24,0},{1,9},{9,17},{17,25},{25,1},{2,10},{10... | collective-permute-start | bytes 1769480 | tf_op jit(solution)/shard_map/ppermute | solution.py:20
  204.7 3.8 %convolution_bitcast_fusion.1 = f32[1,1024,1024]{2,1,0:T(8,128)} fusion(bf16[576,1024]{1,0:T(8,128)(2,1)S(1)} %constant_dynamic-update-slice_fusion.16, bf16[576,1024]{1,0:T(8,128)(2,1)S(1)} %get-tuple-element.132), kind=kOutput, calls=%fused_computation.33 | convolution fusion | flops 1207959552 | bytes 6553600 | tf_op jit(solution)/shard_map/dot_general | solution.py:15
  208.5 5.5 %collective-permute-done.34 = bf16[288,1024]{1,0:T(8,128)(2,1)S(1)} collective-permute-done((bf16[288,1024]{1,0:T(8,128)(2,1)S(1)}, bf16[288,1024]{1,0:T(8,128)(2,1)S(1)}, u32[]{:S(2)}, u32[]{:S(2)}) %collective-permute-start.34) | collective-permute-done | bytes 589856 | tf_op jit(solution)/shard_map/ppermute | solution.py:20
  214.0 22.5 %collective-permute-done.33 = bf16[288,1024]{1,0:T(8,128)(2,1)S(1)} collective-permute-done((bf16[288,1024]{1,0:T(8,128)(2,1)S(1)}, bf16[288,1024]{1,0:T(8,128)(2,1)S(1)}, u32[]{:S(2)}, u32[]{:S(2)}) %collective-permute-start.33) | collective-permute-done | bytes 589856 | tf_op jit(solution)/shard_map/ppermute | solution.py:20
  239.6 4.1 %all-to-all-start.2 = ((bf16[8,36,1024]{2,1,0:T(8,128)(2,1)}), bf16[8,36,1024]{2,1,0:T(8,128)(2,1)S(1)}, u32[]{:S(2)}, u32[]{:S(2)}) async-start(bf16[8,36,1024]{2,1,0:T(8,128)(2,1)} %pad_maximum_fusion.5), calls=%async_computation.2 | async-start | bytes 1310720 | tf_op jit(solution)/shard_map/all_to_all | solution.py:246
  243.7 6.1 %convolution_bitcast_fusion = f32[1,1024,1024]{2,1,0:T(8,128)} fusion(f32[576,1024]{1,0:T(8,128)} %copy-done.79, f32[1024]{0:T(1024)S(1)} %bitcast.380, bf16[144,1024]{1,0:T(8,128)(2,1)} %collective-permute-done.31, bf16[144,1024]{1,0:T(8,128)(2,1)} %collective-permute-done.30, bf16[144,1024]{1,0:T(8,128)(2,1)S(1)} %copy-done.45, ...), kind=kOutput, calls=%fused_computation.32 | convolution fusion | flops 1219756032 | bytes 7739648 | tf_op jit(solution)/shard_map/dot_general | solution.py:15
  249.8 5.0 %all-to-all-done.2 = bf16[8,36,1024]{2,1,0:T(8,128)(2,1)S(1)} async-done(((bf16[8,36,1024]{2,1,0:T(8,128)(2,1)}), bf16[8,36,1024]{2,1,0:T(8,128)(2,1)S(1)}, u32[]{:S(2)}, u32[]{:S(2)}) %all-to-all-start.2) | async-done | bytes 589856 | tf_op jit(solution)/shard_map/all_to_all | solution.py:246
  261.6 15.7 %collective-permute-start.37 = (bf16[128,256]{1,0:T(8,128)(2,1)}, bf16[128,256]{1,0:T(8,128)(2,1)}, u32[]{:S(2)}, u32[]{:S(2)}) collective-permute-start(bf16[128,256]{1,0:T(8,128)(2,1)} %get-tuple-element.97), channel_id=1, source_target_pairs={{0,24},{8,0},{16,8},{24,16},{1,25},{9,1},{17,9},{25,17},{2,26},{10... | collective-permute-start | bytes 196616 | tf_op jit(solution)/shard_map/ppermute | solution.py:20
  286.8 3.5 convolution_convert_fusion.2
  295.7 3.7 fusion.109
  300.3 3.1 collective-permute-start.40
  315.7 6.7 %concatenate.98 = f32[4,8,32,896]{3,2,0,1:T(8,128)} concatenate(f32[4,8,32,768]{3,2,0,1:T(8,128)} %copy.110, f32[4,8,32,8]{3,2,0,1:T(8,128)S(1)} %copy.111, f32[4,8,32,1]{3,2,0,1:T(8,128)S(1)} %copy.112, f32[4,8,32,1]{3,2,0,1:T(8,128)S(1)} %copy-done.15, f32[4,8,32,1]{3,2,0,1:T(8,128)} %copy.114, f32[4,8,32,1]{3,2,0,1:T(8,128)} %copy.115, f32[4,8,32,1]{3,2,0,1:T(8,128)} %copy.116, ...), dimensions={3} | concatenate | bytes 7340032 | tf_op jit(solution)/shard_map/concatenate | solution.py:310
  339.1 4.4 %collective-permute-done.43 = bf16[4,32,896]{2,1,0:T(8,128)(2,1)S(1)} collective-permute-done((bf16[4,32,896]{2,1,0:T(8,128)(2,1)S(1)}, bf16[4,32,896]{2,1,0:T(8,128)(2,1)S(1)}, u32[]{:S(2)}, u32[]{:S(2)}) %collective-permute-start.43) | collective-permute-done | bytes 229408 | tf_op jit(solution)/shard_map/ppermute | solution.py:25
  343.8 3.6 collective-permute-start.45
  352.6 3.0 collective-permute-done.47
  (458 shorter events, 177.6 us)
Async XLA Ops:
  4.1 36.7 %collective-permute-start.3 = (bf16[32,1152]{1,0:T(8,128)(2,1)S(1)}, bf16[32,1152]{1,0:T(8,128)(2,1)S(1)}, u32[]{:S(2)}, u32[]{:S(2)}) collective-permute-start(bf16[32,1152]{1,0:T(8,128)(2,1)S(1)} %concatenate.75), channel_id=1, source_target_pairs={{0,24},{8,0},{16,8},{24,16},{1,25},{9,1},{17,9},{25,17},{2,26},{10... | collective-permute-start | bytes 221192 | tf_op jit(solution)/shard_map/ppermute | solution.py:20
  9.2 32.5 %collective-permute-start.4 = (bf16[32,1152]{1,0:T(8,128)(2,1)S(1)}, bf16[32,1152]{1,0:T(8,128)(2,1)}, u32[]{:S(2)}, u32[]{:S(2)}) collective-permute-start(bf16[32,1152]{1,0:T(8,128)(2,1)S(1)} %concatenate.75), channel_id=1, source_target_pairs={{0,16},{8,24},{16,0},{24,8},{1,17},{9,25},{17,1},{25,9},{2,18},{10... | collective-permute-start | bytes 221192 | tf_op jit(solution)/shard_map/ppermute | solution.py:20
  9.2 34.1 %collective-permute-start.5 = (bf16[32,1152]{1,0:T(8,128)(2,1)S(1)}, bf16[32,1152]{1,0:T(8,128)(2,1)}, u32[]{:S(2)}, u32[]{:S(2)}) collective-permute-start(bf16[32,1152]{1,0:T(8,128)(2,1)S(1)} %concatenate.75), channel_id=1, source_target_pairs={{0,8},{8,16},{16,24},{24,0},{1,9},{9,17},{17,25},{25,1},{2,10},{10... | collective-permute-start | bytes 221192 | tf_op jit(solution)/shard_map/ppermute | solution.py:20
  12.3 14.8 %collective-permute-start.13 = (bf16[32,768]{1,0:T(8,128)(2,1)}, bf16[32,768]{1,0:T(8,128)(2,1)S(1)}, u32[]{:S(2)}, u32[]{:S(2)}) collective-permute-start(bf16[32,768]{1,0:T(8,128)(2,1)} %get-tuple-element.110), channel_id=1, source_target_pairs={{0,24},{8,0},{16,8},{24,16},{1,25},{9,1},{17,9},{25,17},{2,26},{10... | collective-permute-start | bytes 147464 | tf_op jit(solution)/shard_map/ppermute | solution.py:20
  19.6 107.9 %all-to-all-start.1 = ((bf16[8,18,1024]{2,1,0:T(8,128)(2,1)}), bf16[8,18,1024]{2,1,0:T(8,128)(2,1)}, u32[]{:S(2)}, u32[]{:S(2)}) async-start(bf16[8,18,1024]{2,1,0:T(8,128)(2,1)} %reshape.333), calls=%async_computation.1 | async-start | bytes 786432 | tf_op jit(solution)/shard_map/all_to_all | solution.py:92
  27.9 27.7 %collective-permute-start.2 = (bf16[128,1024]{1,0:T(8,128)(2,1)S(1)}, bf16[128,1024]{1,0:T(8,128)(2,1)S(1)}, u32[]{:S(2)}, u32[]{:S(2)}) collective-permute-start(bf16[128,1024]{1,0:T(8,128)(2,1)S(1)} %bitcast.353), channel_id=1, source_target_pairs={{0,24},{8,0},{16,8},{24,16},{1,25},{9,1},{17,9},{25,17},{2,26},{10... | collective-permute-start | bytes 786440 | tf_op jit(solution)/shard_map/ppermute | solution.py:20
  33.7 22.0 %collective-permute-start.1 = (bf16[128,1024]{1,0:T(8,128)(2,1)S(1)}, bf16[128,1024]{1,0:T(8,128)(2,1)S(1)}, u32[]{:S(2)}, u32[]{:S(2)}) collective-permute-start(bf16[128,1024]{1,0:T(8,128)(2,1)S(1)} %bitcast.354), channel_id=1, source_target_pairs={{0,16},{8,24},{16,0},{24,8},{1,17},{9,25},{17,1},{25,9},{2,18},{10... | collective-permute-start | bytes 786440 | tf_op jit(solution)/shard_map/ppermute | solution.py:20
  40.8 16.8 %collective-permute-start = (bf16[128,1024]{1,0:T(8,128)(2,1)S(1)}, bf16[128,1024]{1,0:T(8,128)(2,1)S(1)}, u32[]{:S(2)}, u32[]{:S(2)}) collective-permute-start(bf16[128,1024]{1,0:T(8,128)(2,1)S(1)} %bitcast.355), channel_id=1, source_target_pairs={{0,8},{8,16},{16,24},{24,0},{1,9},{9,17},{17,25},{25,1},{2,10},{10... | collective-permute-start | bytes 786440 | tf_op jit(solution)/shard_map/ppermute | solution.py:20
  57.6 19.0 %collective-permute-start.9 = (bf16[4,32,1152]{2,1,0:T(8,128)(2,1)S(1)}, bf16[4,32,1152]{2,1,0:T(8,128)(2,1)}, u32[]{:S(2)}, u32[]{:S(2)}) collective-permute-start(bf16[4,32,1152]{2,1,0:T(8,128)(2,1)S(1)} %get-tuple-element.58), channel_id=1, source_target_pairs={{0,4},{1,5},{2,6},{3,7},{4,0},{5,1},{6,2},{7,3},{8,12},{9,13},{10,... | collective-permute-start | bytes 884744 | tf_op jit(solution)/shard_map/ppermute | solution.py:25
  59.8 16.9 %collective-permute-start.11 = (bf16[4,32,1152]{2,1,0:T(8,128)(2,1)S(1)}, bf16[4,32,1152]{2,1,0:T(8,128)(2,1)}, u32[]{:S(2)}, u32[]{:S(2)}) collective-permute-start(bf16[4,32,1152]{2,1,0:T(8,128)(2,1)S(1)} %get-tuple-element.58), channel_id=1, source_target_pairs={{0,6},{1,7},{2,4},{3,5},{4,2},{5,3},{6,0},{7,1},{8,14},{9,15},{10,... | collective-permute-start | bytes 884744 | tf_op jit(solution)/shard_map/ppermute | solution.py:25
  64.6 14.0 %collective-permute-start.20 = (bf16[4,32,768]{2,1,0:T(8,128)(2,1)S(1)}, bf16[4,32,768]{2,1,0:T(8,128)(2,1)S(1)}, u32[]{:S(2)}, u32[]{:S(2)}) collective-permute-start(bf16[4,32,768]{2,1,0:T(8,128)(2,1)S(1)} %collective-permute-done.19), channel_id=1, source_target_pairs={{0,1},{1,0},{2,3},{3,2},{4,5},{5,4},{6,7},{7,6},{8,9},{9,8},{10,11... | collective-permute-start | bytes 589832 | tf_op jit(solution)/shard_map/ppermute | solution.py:25
  76.7 13.7 %collective-permute-start.10 = (bf16[4,32,1152]{2,1,0:T(8,128)(2,1)}, bf16[4,32,1152]{2,1,0:T(8,128)(2,1)}, u32[]{:S(2)}, u32[]{:S(2)}) collective-permute-start(bf16[4,32,1152]{2,1,0:T(8,128)(2,1)} %collective-permute-done.9), channel_id=1, source_target_pairs={{0,1},{1,0},{2,3},{3,2},{4,5},{5,4},{6,7},{7,6},{8,9},{9,8},{10,11... | collective-permute-start | bytes 884744 | tf_op jit(solution)/shard_map/ppermute | solution.py:25
  77.2 16.5 %collective-permute-start.12 = (bf16[4,32,1152]{2,1,0:T(8,128)(2,1)}, bf16[4,32,1152]{2,1,0:T(8,128)(2,1)}, u32[]{:S(2)}, u32[]{:S(2)}) collective-permute-start(bf16[4,32,1152]{2,1,0:T(8,128)(2,1)} %collective-permute-done.11), channel_id=1, source_target_pairs={{0,1},{1,0},{2,3},{3,2},{4,5},{5,4},{6,7},{7,6},{8,9},{9,8},{10,11... | collective-permute-start | bytes 884744 | tf_op jit(solution)/shard_map/ppermute | solution.py:25
  133.7 54.1 %collective-permute-start.31 = (bf16[144,1024]{1,0:T(8,128)(2,1)}, bf16[144,1024]{1,0:T(8,128)(2,1)}, u32[]{:S(2)}, u32[]{:S(2)}) collective-permute-start(bf16[144,1024]{1,0:T(8,128)(2,1)} %reshape.334), channel_id=1, source_target_pairs={{0,24},{8,0},{16,8},{24,16},{1,25},{9,1},{17,9},{25,17},{2,26},{10... | collective-permute-start | bytes 884744 | tf_op jit(solution)/shard_map/ppermute | solution.py:20
  136.7 51.1 %collective-permute-start.30 = (bf16[144,1024]{1,0:T(8,128)(2,1)}, bf16[144,1024]{1,0:T(8,128)(2,1)}, u32[]{:S(2)}, u32[]{:S(2)}) collective-permute-start(bf16[144,1024]{1,0:T(8,128)(2,1)} %reshape.334), channel_id=1, source_target_pairs={{0,16},{8,24},{16,0},{24,8},{1,17},{9,25},{17,1},{25,9},{2,18},{10... | collective-permute-start | bytes 884744 | tf_op jit(solution)/shard_map/ppermute | solution.py:20
  141.7 15.7 %collective-permute-start.26 = (bf16[144,1024]{1,0:T(8,128)(2,1)}, bf16[144,1024]{1,0:T(8,128)(2,1)S(1)}, u32[]{:S(2)}, u32[]{:S(2)}) collective-permute-start(bf16[144,1024]{1,0:T(8,128)(2,1)} %reshape.331), channel_id=1, source_target_pairs={{0,8},{8,16},{16,24},{24,0},{1,9},{9,17},{17,25},{25,1},{2,10},{10... | collective-permute-start | bytes 884744 | tf_op jit(solution)/shard_map/ppermute | solution.py:20
  143.5 39.6 %collective-permute-start.27 = (bf16[144,1024]{1,0:T(8,128)(2,1)}, bf16[144,1024]{1,0:T(8,128)(2,1)S(1)}, u32[]{:S(2)}, u32[]{:S(2)}) collective-permute-start(bf16[144,1024]{1,0:T(8,128)(2,1)} %reshape.331), channel_id=1, source_target_pairs={{0,16},{8,24},{16,0},{24,8},{1,17},{9,25},{17,1},{25,9},{2,18},{10... | collective-permute-start | bytes 884744 | tf_op jit(solution)/shard_map/ppermute | solution.py:20
  145.2 37.9 %collective-permute-start.28 = (bf16[144,1024]{1,0:T(8,128)(2,1)}, bf16[144,1024]{1,0:T(8,128)(2,1)S(1)}, u32[]{:S(2)}, u32[]{:S(2)}) collective-permute-start(bf16[144,1024]{1,0:T(8,128)(2,1)} %reshape.331), channel_id=1, source_target_pairs={{0,24},{8,0},{16,8},{24,16},{1,25},{9,1},{17,9},{25,17},{2,26},{10... | collective-permute-start | bytes 884744 | tf_op jit(solution)/shard_map/ppermute | solution.py:20
  157.4 30.3 %collective-permute-start.29 = (bf16[144,1024]{1,0:T(8,128)(2,1)}, bf16[144,1024]{1,0:T(8,128)(2,1)S(1)}, u32[]{:S(2)}, u32[]{:S(2)}) collective-permute-start(bf16[144,1024]{1,0:T(8,128)(2,1)} %reshape.334), channel_id=1, source_target_pairs={{0,8},{8,16},{16,24},{24,0},{1,9},{9,17},{17,25},{25,1},{2,10},{10... | collective-permute-start | bytes 884744 | tf_op jit(solution)/shard_map/ppermute | solution.py:20
  193.9 20.1 %collective-permute-start.34 = (bf16[288,1024]{1,0:T(8,128)(2,1)S(1)}, bf16[288,1024]{1,0:T(8,128)(2,1)S(1)}, u32[]{:S(2)}, u32[]{:S(2)}) collective-permute-start(bf16[288,1024]{1,0:T(8,128)(2,1)S(1)} %get-tuple-element.66), channel_id=1, source_target_pairs={{0,8},{8,16},{16,24},{24,0},{1,9},{9,17},{17,25},{25,1},{2,10},{10... | collective-permute-start | bytes 1769480 | tf_op jit(solution)/shard_map/ppermute | solution.py:20
  200.3 36.3 %collective-permute-start.33 = (bf16[288,1024]{1,0:T(8,128)(2,1)S(1)}, bf16[288,1024]{1,0:T(8,128)(2,1)S(1)}, u32[]{:S(2)}, u32[]{:S(2)}) collective-permute-start(bf16[288,1024]{1,0:T(8,128)(2,1)S(1)} %get-tuple-element.67), channel_id=1, source_target_pairs={{0,16},{8,24},{16,0},{24,8},{1,17},{9,25},{17,1},{25,9},{2,18},{10... | collective-permute-start | bytes 1769480 | tf_op jit(solution)/shard_map/ppermute | solution.py:20
  200.3 37.6 %collective-permute-start.32 = (bf16[288,1024]{1,0:T(8,128)(2,1)S(1)}, bf16[288,1024]{1,0:T(8,128)(2,1)S(1)}, u32[]{:S(2)}, u32[]{:S(2)}) collective-permute-start(bf16[288,1024]{1,0:T(8,128)(2,1)S(1)} %get-tuple-element.65), channel_id=1, source_target_pairs={{0,24},{8,0},{16,8},{24,16},{1,25},{9,1},{17,9},{25,17},{2,26},{10... | collective-permute-start | bytes 1769480 | tf_op jit(solution)/shard_map/ppermute | solution.py:20
  239.6 15.2 %all-to-all-start.2 = ((bf16[8,36,1024]{2,1,0:T(8,128)(2,1)}), bf16[8,36,1024]{2,1,0:T(8,128)(2,1)S(1)}, u32[]{:S(2)}, u32[]{:S(2)}) async-start(bf16[8,36,1024]{2,1,0:T(8,128)(2,1)} %pad_maximum_fusion.5), calls=%async_computation.2 | async-start | bytes 1310720 | tf_op jit(solution)/shard_map/all_to_all | solution.py:246
  261.6 24.1 %collective-permute-start.37 = (bf16[128,256]{1,0:T(8,128)(2,1)}, bf16[128,256]{1,0:T(8,128)(2,1)}, u32[]{:S(2)}, u32[]{:S(2)}) collective-permute-start(bf16[128,256]{1,0:T(8,128)(2,1)} %get-tuple-element.97), channel_id=1, source_target_pairs={{0,24},{8,0},{16,8},{24,16},{1,25},{9,1},{17,9},{25,17},{2,26},{10... | collective-permute-start | bytes 196616 | tf_op jit(solution)/shard_map/ppermute | solution.py:20
  285.6 47.0 %collective-permute-start.48 = (bf16[4,4,32,1024]{3,2,1,0:T(8,128)(2,1)}, bf16[4,4,32,1024]{3,2,1,0:T(8,128)(2,1)}, u32[]{:S(2)}, u32[]{:S(2)}) collective-permute-start(bf16[4,4,32,1024]{3,2,1,0:T(8,128)(2,1)} %pad_maximum_fusion.2), channel_id=1, source_target_pairs={{0,1},{1,0},{2,3},{3,2},{4,5},{5,4},{6,7},{7,6},{8,9},{9,8},{10,11... | collective-permute-start | bytes 3145736 | tf_op jit(solution)/shard_map/ppermute | solution.py:25
  300.3 24.7 %collective-permute-start.40 = (bf16[128,1024]{1,0:T(8,128)(2,1)}, bf16[128,1024]{1,0:T(8,128)(2,1)}, u32[]{:S(2)}, u32[]{:S(2)}) collective-permute-start(bf16[128,1024]{1,0:T(8,128)(2,1)} %get-tuple-element.83), channel_id=1, source_target_pairs={{0,8},{8,16},{16,24},{24,0},{1,9},{9,17},{17,25},{25,1},{2,10},{10... | collective-permute-start | bytes 786440 | tf_op jit(solution)/shard_map/ppermute | solution.py:20
  303.4 21.6 %collective-permute-start.39 = (bf16[128,1024]{1,0:T(8,128)(2,1)}, bf16[128,1024]{1,0:T(8,128)(2,1)}, u32[]{:S(2)}, u32[]{:S(2)}) collective-permute-start(bf16[128,1024]{1,0:T(8,128)(2,1)} %get-tuple-element.84), channel_id=1, source_target_pairs={{0,16},{8,24},{16,0},{24,8},{1,17},{9,25},{17,1},{25,9},{2,18},{10... | collective-permute-start | bytes 786440 | tf_op jit(solution)/shard_map/ppermute | solution.py:20
  304.3 20.7 %collective-permute-start.38 = (bf16[128,1024]{1,0:T(8,128)(2,1)}, bf16[128,1024]{1,0:T(8,128)(2,1)}, u32[]{:S(2)}, u32[]{:S(2)}) collective-permute-start(bf16[128,1024]{1,0:T(8,128)(2,1)} %get-tuple-element.82), channel_id=1, source_target_pairs={{0,24},{8,0},{16,8},{24,16},{1,25},{9,1},{17,9},{25,17},{2,26},{10... | collective-permute-start | bytes 786440 | tf_op jit(solution)/shard_map/ppermute | solution.py:20
  329.8 13.8 %collective-permute-start.43 = (bf16[4,32,896]{2,1,0:T(8,128)(2,1)S(1)}, bf16[4,32,896]{2,1,0:T(8,128)(2,1)S(1)}, u32[]{:S(2)}, u32[]{:S(2)}) collective-permute-start(bf16[4,32,896]{2,1,0:T(8,128)(2,1)S(1)} %get-tuple-element.64), channel_id=1, source_target_pairs={{0,4},{1,5},{2,6},{3,7},{4,0},{5,1},{6,2},{7,3},{8,12},{9,13},{10,... | collective-permute-start | bytes 688136 | tf_op jit(solution)/shard_map/ppermute | solution.py:25
  334.1 22.3 %collective-permute-start.51 = (bf16[4,32,1024]{2,1,0:T(8,128)(2,1)S(1)}, bf16[4,32,1024]{2,1,0:T(8,128)(2,1)S(1)}, u32[]{:S(2)}, u32[]{:S(2)}) collective-permute-start(bf16[4,32,1024]{2,1,0:T(8,128)(2,1)S(1)} %get-tuple-element.60), channel_id=1, source_target_pairs={{0,6},{1,7},{2,4},{3,5},{4,2},{5,3},{6,0},{7,1},{8,14},{9,15},{10,... | collective-permute-start | bytes 786440 | tf_op jit(solution)/shard_map/ppermute | solution.py:25
  334.7 21.7 %collective-permute-start.50 = (bf16[4,32,1024]{2,1,0:T(8,128)(2,1)S(1)}, bf16[4,32,1024]{2,1,0:T(8,128)(2,1)S(1)}, u32[]{:S(2)}, u32[]{:S(2)}) collective-permute-start(bf16[4,32,1024]{2,1,0:T(8,128)(2,1)S(1)} %get-tuple-element.61), channel_id=1, source_target_pairs={{0,4},{1,5},{2,6},{3,7},{4,0},{5,1},{6,2},{7,3},{8,12},{9,13},{10,... | collective-permute-start | bytes 786440 | tf_op jit(solution)/shard_map/ppermute | solution.py:25
  338.5 17.9 %collective-permute-start.49 = (bf16[4,32,1024]{2,1,0:T(8,128)(2,1)S(1)}, bf16[4,32,1024]{2,1,0:T(8,128)(2,1)S(1)}, u32[]{:S(2)}, u32[]{:S(2)}) collective-permute-start(bf16[4,32,1024]{2,1,0:T(8,128)(2,1)S(1)} %get-tuple-element.59), channel_id=1, source_target_pairs={{0,2},{1,3},{2,0},{3,1},{4,6},{5,7},{6,4},{7,5},{8,10},{9,11},{10,... | collective-permute-start | bytes 786440 | tf_op jit(solution)/shard_map/ppermute | solution.py:25
  (107 other events, 1074.4 us)

commit v2 on v1

v2 whole, which is shorter than its diff:
```python
import functools

import jax
import jax.numpy as jnp
from jax import lax
from jax.experimental import pallas as pl
from jax.experimental.pallas import tpu as pltpu
from jax.sharding import PartitionSpec as P

H = 16
NSEG = 7
EPS = 1e-05
NEG = -1e30
BF = jnp.bfloat16
F32 = jnp.float32
I32 = jnp.int32


def mm(a, b, ca=1, cb=0):
    return lax.dot_general(a, b, (((ca,), (cb,)), ((), ())), preferred_element_type=F32)


def call(kernel, outs, me, *args, scratch=(), **static):
    smem = pl.BlockSpec(memory_space=pltpu.SMEM)
    vmem = pl.BlockSpec(memory_space=pltpu.VMEM)
    return pl.pallas_call(
        functools.partial(kernel, **static),
        out_shape=[jax.ShapeDtypeStruct(s, d) for s, d in outs],
        in_specs=[smem] + [vmem] * len(args),
        out_specs=[vmem] * len(outs),
        scratch_shapes=list(scratch),
        name=kernel.__name__,
    )(me, *args)


def ahead(x, step):
    n = lax.axis_size("dp")
    return lax.ppermute(x, "dp", [(i, (i + step) % n) for i in range(n)])


def flip(x, bits):
    n = lax.axis_size("expert")
    return lax.ppermute(x, "expert", [(i, i ^ bits) for i in range(n)])


def swap(x, axis):
    return lax.all_to_all(x, axis, split_axis=0, concat_axis=0, tiled=True)


def along(blocks, sign=1):
    return [blocks[0]] + [ahead(blocks[j], sign * j) for j in range(1, len(blocks))]


def gather_experts(x):
    n = lax.axis_size("expert")
    mine = [x] + [flip(x, 2 * k) for k in range(1, n // 2)]
    out = []
    for block in mine:
        out += [block, flip(block, 1)]
    return out


def normalise(values):
    mean = jnp.mean(values, axis=-1, keepdims=True)
    centred = values - mean
    scale = lax.rsqrt(jnp.mean(centred * centred, axis=-1, keepdims=True) + EPS)
    return centred * scale, scale


def norm_back(upstream, gain, unit, scale):
    e = upstream * gain
    return scale * (
        e - jnp.mean(e, axis=-1, keepdims=True) - unit * jnp.mean(e * unit, axis=-1, keepdims=True)
    )


def lanes(shape, dim):
    return lax.broadcasted_iota(I32, shape, dim)


def softmax_of(logits, experts):
    logits = jnp.where(lanes(logits.shape, 1) < experts, logits, NEG)
    top = jnp.max(logits, axis=-1, keepdims=True)
    weight = jnp.exp(logits - top)
    return weight / jnp.sum(weight, axis=-1, keepdims=True)


def weights_kernel(me, qkv, router, gains, biases, columns, turned, small, *, n_dp):
    own, width = qkv.shape[0], qkv.shape[1] // 3
    part = width // n_dp
    experts = router.shape[1]
    turned[...] = jnp.zeros_like(turned)
    turned[experts : experts + 2, :own] = gains[...].astype(F32)
    turned[experts + 2 : experts + 7, :own] = biases[...].astype(F32)
    small[...] = turned[...].T[:own]
    small[:, :experts] = router[...].astype(F32)
    few = small[...].astype(BF)
    for d in range(n_dp):
        for i in range(3):
            columns[d, :, i * part : (i + 1) * part] = qkv[
                :, i * width + d * part : i * width + (d + 1) * part
            ]
        columns[d, :, 3 * part :] = few


def slots_kernel(
    me, parents, route, order, cotangent, seg, grads, tableT, rank_out, bias, *, pad, capacity, experts
):
    tok = route.shape[0]
    r = jnp.broadcast_to(route[...].astype(F32), (tok, tok))
    rt = r.T
    o = jnp.broadcast_to(order[...].astype(F32), (tok, tok))
    ot = o.T
    same = r == rt
    rank = jnp.sum(jnp.where(same & (o < ot), 1.0, 0.0), axis=1, keepdims=True)
    rank_row = jnp.sum(jnp.where(same & (ot < o), 1.0, 0.0), axis=0, keepdims=True)
    rank_out[...] = rank.astype(I32)
    key = jnp.where(rank_row < capacity, rt[0:1] * pad + rank_row, -1.0).astype(I32)
    table = jnp.where(lanes((experts * pad, tok), 0) == key, 1.0, 0.0).astype(BF)
    tableT[...] = table
    grads[...] = mm(table, cotangent[...]).astype(BF)
    length = seg.shape[1]
    masks = [jnp.int32(1)]
    for s in range(1, NSEG):
        up = jnp.int32(0)
        for a in range(s):
            up = jnp.where(parents[0, s] == a, masks[a], up)
        masks.append(up | (1 << s))
    block = 128
    keys = seg[...]
    for i in range(length // block):
        col = jnp.broadcast_to(seg[:, i * block : (i + 1) * block].astype(F32), (block, block)).T
        col = jnp.broadcast_to(col[:, 0:1], (block, length)).astype(I32)
        mine = jnp.zeros((block, length), I32)
        for s in range(NSEG):
            mine = jnp.where(col == s, masks[s], mine)
        ok = jnp.zeros((block, length), I32)
        for s in range(NSEG):
            ok = jnp.where(keys == s, mine & (1 << s), ok)
        seen = lanes((block, length), 1) <= lanes((block, length), 0) + i * block
        bias[i * block : (i + 1) * block] = jnp.where(seen & (ok > 0), 0.0, NEG)


def pack_kernel(me, rows, out, *, pad, capacity):
    n_out, n_in = out.shape[0], rows.shape[0]
    r, c = lanes((n_out, n_in), 0), lanes((n_out, n_in), 1)
    pick = jnp.zeros((n_out, n_in), jnp.bool_)
    for e in range(n_in // pad):
        inside = (r >= e * capacity) & (r < (e + 1) * capacity)
        pick = pick | (inside & (c - e * pad == r - e * capacity))
    out[...] = mm(jnp.where(pick, 1.0, 0.0).astype(BF), rows[...]).astype(BF)


def assemble_kernel(me, *refs):
    out = refs[-1]
    for k, block in enumerate(refs[:-1]):
        e = me[1] ^ k
        for d in range(block.shape[0]):
            out[d, e] = block[d]


def attend_kernel(me, qkv, bias, *refs, n_dp, head_dim, experts):
    tokens, (normed, unit, packed, probs, attended, vectors) = refs[:n_dp], refs[n_dp:]
    rows, width = tokens[0].shape
    part = width // n_dp
    small = qkv[:, 3 * part :].astype(F32).T
    vectors[...] = small[experts : experts + 8]
    gain, shift = vectors[0:1], vectors[2:3]
    parts = [jnp.zeros((1, part), F32)] * 2
    for d in range(n_dp):
        for i in range(2):
            here = vectors[3 + i : 4 + i, d * part : (d + 1) * part]
            parts[i] = parts[i] + jnp.where(me[0] == d, here, 0.0)
    for j in range(n_dp):
        base = pl.multiple_of(((me[0] + n_dp - j) % n_dp) * rows, rows)
        centred, _ = normalise(tokens[j][...].astype(F32))
        unit[pl.ds(base, rows)] = centred
        normed[pl.ds(base, rows)] = (centred * gain + shift).astype(BF)
    raw = mm(normed[...], qkv[:, : 3 * part])
    packed[:, :part] = (raw[:, :part] + parts[0]).astype(BF)
    packed[:, part : 2 * part] = raw[:, part : 2 * part].astype(BF)
    packed[:, 2 * part :] = (raw[:, 2 * part :] + parts[1]).astype(BF)
    scale = head_dim ** (-0.5)
    length = rows * n_dp
    for h in range(part // head_dim):
        q = packed[:, h * head_dim : (h + 1) * head_dim]
        k = packed[:, part + h * head_dim : part + (h + 1) * head_dim]
        v = packed[:, 2 * part + h * head_dim : 2 * part + (h + 1) * head_dim]
        for i in range(n_dp):
            lo, hi = i * rows, (i + 1) * rows
            s = mm(q[lo:hi], k[:hi], 1, 1) * scale + bias[lo:hi, :hi]
            top = jnp.max(s, axis=-1, keepdims=True)
            p = jnp.exp(s - top)
            p = (p * (1.0 / jnp.sum(p, axis=-1, keepdims=True))).astype(BF)
            probs[h, lo:hi, :hi] = p
            if hi < length:
                probs[h, lo:hi, hi:] = jnp.zeros((rows, length - hi), BF)
            attended[i, :, h * head_dim : (h + 1) * head_dim] = mm(p, v[:hi]).astype(BF)


def mix_kernel(me, tokens, attended, proj, qkv, vectors, tableT, mixed, normed, p, sent, *, experts):
    n_dp, rows, part = attended.shape
    total = tokens[...].astype(F32) + vectors[5:6]
    for d in range(n_dp):
        total = total + mm(attended[d], proj[d * part : (d + 1) * part])
    mixed[...] = total
    unit, _ = normalise(total)
    low = (unit * vectors[1:2] + vectors[6:7]).astype(BF)
    normed[...] = low
    p[...] = softmax_of(mm(low, qkv[:, 3 * part :]), experts)
    sent[...] = mm(tableT[...], low).astype(BF)


def expert_kernel(me, qkv, up, down, up_bias, down_bias, *refs, n_dp, experts, part):
    ins, both = refs[: 2 * n_dp], refs[2 * n_dp : 3 * n_dp]
    act_out, d_pre_out, slots, d_rows, g_up_bias, g_down_bias, acc_r, acc_s = refs[3 * n_dp :]
    f = pl.program_id(0)
    last = pl.num_programs(0) - 1
    each, width = ins[0].shape

    @pl.when(f == 0)
    def _():
        sums = jnp.zeros((1, width), F32)
        for j in range(n_dp):
            rows = ins[j][...]
            slots[j * each : (j + 1) * each] = rows
            p = softmax_of(mm(rows, qkv[:, 3 * part :]), experts)
            gate = jnp.sum(jnp.where(lanes(p.shape, 1) == me[1], p, 0.0), axis=-1, keepdims=True)
            d = (gate * ins[n_dp + j][...].astype(F32)).astype(BF)
            d_rows[j * each : (j + 1) * each] = d
            sums = sums + jnp.sum(d.astype(F32), axis=0, keepdims=True)
        own = jnp.zeros((1, part), F32)
        for d in range(n_dp):
            own = own + jnp.where(me[0] == d, sums[:, d * part : (d + 1) * part], 0.0)
        g_down_bias[...] = own
        acc_r[...] = jnp.zeros_like(acc_r)
        acc_s[...] = jnp.zeros_like(acc_s)
        for d in range(n_dp):
            acc_r[:, d * part : (d + 1) * part] = jnp.broadcast_to(
                jnp.where(me[0] == d, down_bias[...].astype(F32), 0.0), (n_dp * each, part)
            )

    u = mm(slots[...], up[...]) + up_bias[...].astype(F32)
    c, a = 0.7978845608028654, 0.044715
    t = jnp.tanh(c * (u + a * (u * u * u)))
    act = (0.5 * u * (1.0 + t)).astype(BF)
    slope = 0.5 * (1.0 + t) + 0.5 * u * (1.0 - t * t) * (c * (1.0 + 3.0 * a * (u * u)))
    d_pre = mm(d_rows[...], down[...], 1, 1) * slope
    g_up_bias[...] = jnp.sum(d_pre, axis=0, keepdims=True)
    low = d_pre.astype(BF)
    act_out[...] = act
    d_pre_out[...] = low
    acc_r[...] += mm(act, down[...])
    acc_s[...] += mm(low, up[...], 1, 1)

    @pl.when(f == last)
    def _():
        for j in range(n_dp):
            both[j][:each] = acc_r[j * each : (j + 1) * each].astype(BF)
            both[j][each:] = acc_s[j * each : (j + 1) * each].astype(BF)


def experts_call(me, qkv, up, down, up_bias, down_bias, slots, grads, experts, part):
    n_dp = len(slots)
    each, width = slots[0].shape
    ff = up.shape[1]
    chunk = min(ff, 256)
    total = n_dp * each
    whole = pl.BlockSpec(memory_space=pltpu.VMEM)
    return pl.pallas_call(
        functools.partial(expert_kernel, n_dp=n_dp, experts=experts, part=part),
        grid=(ff // chunk,),
        out_shape=[jax.ShapeDtypeStruct((2 * each, width), BF)] * n_dp
        + [
            jax.ShapeDtypeStruct((total, ff), BF),
            jax.ShapeDtypeStruct((total, ff), BF),
            jax.ShapeDtypeStruct((total, width), BF),
            jax.ShapeDtypeStruct((total, width), BF),
            jax.ShapeDtypeStruct((1, ff), F32),
            jax.ShapeDtypeStruct((1, part), F32),
        ],
        in_specs=[
            pl.BlockSpec(memory_space=pltpu.SMEM),
            whole,
            pl.BlockSpec((width, chunk), lambda f: (0, f)),
            pl.BlockSpec((chunk, width), lambda f: (f, 0)),
            pl.BlockSpec((1, chunk), lambda f: (0, f)),
            whole,
        ]
        + [whole] * (2 * n_dp),
        out_specs=[whole] * n_dp
        + [
            pl.BlockSpec((total, chunk), lambda f: (0, f)),
            pl.BlockSpec((total, chunk), lambda f: (0, f)),
            whole,
            whole,
            pl.BlockSpec((1, chunk), lambda f: (0, f)),
            whole,
        ],
        scratch_shapes=[pltpu.VMEM((total, width), F32), pltpu.VMEM((total, width), F32)],
        name="expert_kernel",
    )(me, qkv, up, down, up_bias, down_bias, *slots, *grads)


def sum_of(refs):
    total = refs[0][...].astype(F32)
    for ref in refs[1:]:
        total = total + ref[...].astype(F32)
    return total


def line_sum_kernel(me, *refs, pad, capacity):
    out = refs[-1]
    two, width = refs[0].shape
    total = sum_of(refs[:-1])
    n_out = out.shape[0]
    r, c = lanes((n_out, two), 0), lanes((n_out, two), 1)
    pick = jnp.zeros((n_out, two), jnp.bool_)
    for e in range(n_out // (2 * pad)):
        for w in range(2):
            row, col = e * 2 * pad + w * pad, w * (two // 2) + e * capacity
            inside = (r >= row) & (r < row + capacity)
            pick = pick | (inside & (r - row == c - col))
    out[...] = mm(jnp.where(pick, 1.0, 0.0).astype(BF), total.astype(BF)).astype(BF)


def combine_kernel(
    me, back, route, rank, mixed, p, cotangent, qkv, vectors, proj,
    outputs, d_mixed, d_low_out, d_att, d_logits_out, sums, *, pad, capacity, experts, part,
):
    tok, width = mixed.shape
    n_back = back.shape[0]
    r, k = route[...], rank[...]
    key = jnp.where(k < capacity, r * (2 * pad) + k, -4 * pad * experts)
    slot = lanes((tok, n_back), 1)
    combined = mm(jnp.where(slot == key, 1.0, 0.0).astype(BF), back[...])
    d_slot = mm(jnp.where(slot == key + pad, 1.0, 0.0).astype(BF), back[...])
    hot = jnp.where(lanes(p.shape, 1) == r, 1.0, 0.0)
    gate = jnp.sum(p[...] * hot, axis=-1, keepdims=True)
    g = cotangent[...].astype(F32)
    outputs[...] = (mixed[...] + gate * combined).astype(BF)
    d_gate = jnp.sum(g * combined, axis=-1, keepdims=True)
    d_logits = (p[...] * (d_gate * hot - d_gate * gate)).astype(BF)
    d_logits_out[...] = d_logits
    d_normed = d_slot + mm(d_logits, qkv[:, 3 * part :], 1, 1)
    unit, scale = normalise(mixed[...])
    sums[0:1] = jnp.sum(d_normed * unit, axis=0, keepdims=True)
    sums[1:2] = jnp.sum(d_normed, axis=0, keepdims=True)
    d = g + norm_back(d_normed, vectors[1:2], unit, scale)
    sums[2:3] = jnp.sum(d, axis=0, keepdims=True)
    d_mixed[...] = d
    low = d.astype(BF)
    d_low_out[...] = low
    for i in range(d_att.shape[0]):
        d_att[i] = mm(low, proj[i * part : (i + 1) * part], 1, 1).astype(BF)


def share(me, whole, near, keep):
    half, n_dp, own, _ = near.shape
    for q in range(half):
        for d in range(n_dp):
            row = d * 2 * half * own
            other = pl.multiple_of(row + (me[1] ^ (2 * q + 1)) * own, own)
            same = pl.multiple_of(row + (me[1] ^ (2 * q)) * own, own)
            near[q, d] = whole[pl.ds(other, own)].astype(BF)
            keep[q, d] = whole[pl.ds(same, own)]


def proj_grad_kernel(me, attended, d_low, near, keep, whole):
    n_dp, rows, part = attended.shape
    for d in range(n_dp):
        whole[d * part : (d + 1) * part] = mm(attended[d], d_low[...], 0, 0)
    share(me, whole, near, keep)


def core_sum_kernel(me, keep, came, first, *rest):
    first[...] = keep[0] + came[0].astype(F32)
    for q, out in enumerate(rest):
        out[...] = (keep[q + 1] + came[q + 1].astype(F32)).astype(BF)


def chip_sum_kernel(me, *refs):
    out, half = refs[-1], (len(refs) - 1) // 2
    wide = refs[0].shape[2]
    out[:, :, :wide] = sum_of(refs[:half]).astype(BF)
    out[:, :, wide:] = sum_of(refs[half:-1]).astype(BF)


def core_sum(me, near, keep):
    half = near.shape[0]
    shape = near.shape[1:]
    return call(core_sum_kernel, [(shape, F32)] + [(shape, BF)] * (half - 1), me, keep, flip(near, 1))


def to_chips(parts):
    return [parts[0]] + [flip(part, 2 * (q + 1)) for q, part in enumerate(parts[1:])]


def attend_back_kernel(me, d_att, probs, packed, qkv, d_packed, d_normed, d_scores, *, head_dim):
    n_dp, rows, part = d_att.shape
    length = n_dp * rows
    scale = head_dim ** (-0.5)
    for h in range(part // head_dim):
        a, b = h * head_dim, (h + 1) * head_dim
        q, k, v = packed[:, a:b], packed[:, part + a : part + b], packed[:, 2 * part + a : 2 * part + b]
        g = jnp.concatenate([d_att[i, :, a:b] for i in range(n_dp)], axis=0)
        for i in range(n_dp):
            lo, hi = i * rows, (i + 1) * rows
            dp = mm(g[lo:hi], v[:hi], 1, 1)
            p = probs[h, lo:hi, :hi].astype(F32)
            delta = jnp.sum(p * dp, axis=-1, keepdims=True)
            ds = (p * (dp - delta)).astype(BF)
            d_scores[lo:hi, :hi] = ds
            if hi < length:
                d_scores[lo:hi, hi:] = jnp.zeros((rows, length - hi), BF)
            d_packed[lo:hi, a:b] = (mm(ds, k[:hi]) * scale).astype(BF)
        d_packed[:, part + a : part + b] = (mm(d_scores[...], q, 0, 0) * scale).astype(BF)
        d_packed[:, 2 * part + a : 2 * part + b] = mm(probs[h], g, 0, 0).astype(BF)
    for i in range(n_dp):
        d_normed[i] = mm(d_packed[i * rows : (i + 1) * rows], qkv[:, : 3 * part], 1, 1).astype(BF)


def qkv_grad_kernel(
    me, normed, unit, d_packed, d_normed, token_normed, d_logits, sums, near, keep, whole, turned, *, experts
):
    n_dp, rows, width = d_normed.shape
    part = width // n_dp
    whole[:, : 3 * part] = mm(normed[...], d_packed[...], 0, 0)
    gain = jnp.zeros((1, width), F32)
    shift = jnp.zeros((1, width), F32)
    for i in range(n_dp):
        d = d_normed[i].astype(F32)
        gain = gain + jnp.sum(d * unit[i * rows : (i + 1) * rows], axis=0, keepdims=True)
        shift = shift + jnp.sum(d, axis=0, keepdims=True)
    columns = jnp.sum(d_packed[...].astype(F32), axis=0, keepdims=True)
    turned[...] = jnp.zeros_like(turned)
    e = experts
    turned[e : e + 1] = gain
    turned[e + 1 : e + 2] = sums[0:1]
    turned[e + 2 : e + 3] = shift
    for d in range(n_dp):
        here = me[0] == d
        turned[e + 3 : e + 4, d * part : (d + 1) * part] = jnp.where(here, columns[:, :part], 0.0)
        turned[e + 4 : e + 5, d * part : (d + 1) * part] = jnp.where(here, columns[:, 2 * part :], 0.0)
    turned[e + 5 : e + 6] = sums[2:3]
    turned[e + 6 : e + 7] = sums[1:2]
    whole[:, 3 * part :] = turned[...].T + mm(token_normed[...], d_logits[...], 0, 0)
    share(me, whole, near, keep)


def weights_end_kernel(me, came, qkv, proj, router, gains, biases, wide):
    n_dp, own, _ = came.shape
    width = proj.shape[1]
    part = width // n_dp
    experts = router.shape[1]
    edge = 3 * part
    total = jnp.zeros((own, 128), F32)
    rows = jnp.zeros((own, width), F32)
    for d in range(n_dp):
        for i in range(3):
            qkv[:, i * width + d * part : i * width + (d + 1) * part] = came[
                d, :, i * part : (i + 1) * part
            ].astype(F32)
        total = total + came[d, :, edge : edge + 128].astype(F32)
        rows = rows + came[d, :, edge + 128 :].astype(F32)
    proj[...] = rows
    router[...] = total[:, :experts]
    wide[...] = jnp.zeros_like(wide)
    wide[:own] = total
    flat = wide[...].T
    gains[...] = flat[experts : experts + 2, :own]
    biases[...] = flat[experts + 2 : experts + 7, :own]


def tokens_end_kernel(me, came, tokens, vectors, d_mixed, out):
    total = came[0].astype(F32)
    for d in range(1, came.shape[0]):
        total = total + came[d].astype(F32)
    unit, scale = normalise(tokens[...].astype(F32))
    out[...] = d_mixed[...] + norm_back(total, vectors[0:1], unit, scale)


def shards(
    tokens,
    qkv_weight,
    proj_weight,
    router_weight,
    norm_gains,
    biases,
    up_weight,
    up_bias,
    down_weight,
    down_bias,
    routes,
    slot_order,
    segments,
    parents,
    cotangent,
):
    n_dp, n_ex = lax.axis_size("dp"), lax.axis_size("expert")
    me = jnp.stack([lax.axis_index("dp"), lax.axis_index("expert")]).astype(I32)
    rows, width = tokens.shape[1], tokens.shape[2]
    part = width // n_dp
    head_dim = width // H
    own = qkv_weight.shape[0]
    experts = router_weight.shape[1]
    capacity = (9 * rows + 8 * experts - 1) // (8 * experts)
    pad = -(-capacity // 8) * 8
    length = n_dp * rows
    each = n_ex * capacity
    cols = 3 * part + 128
    x = tokens[0]

    token_blocks = along([x] * n_dp)
    columns = call(
        weights_kernel,
        [((n_dp, own, cols), BF)],
        me, qkv_weight, router_weight, norm_gains, biases,
        scratch=[pltpu.VMEM((128, 128), F32), pltpu.VMEM((own, 128), F32)],
        n_dp=n_dp,
    )[0]
    middle = n_dp // 2
    stacked, token_blocks[middle] = lax.optimization_barrier((swap(columns, "dp"), token_blocks[middle]))
    qkv_blocks = gather_experts(stacked)
    smem = pl.BlockSpec(memory_space=pltpu.SMEM)
    vmem = pl.BlockSpec(memory_space=pltpu.VMEM)
    grads_out, tableT, rank, bias = pl.pallas_call(
        functools.partial(slots_kernel, pad=pad, capacity=capacity, experts=experts),
        out_shape=[
            jax.ShapeDtypeStruct((n_ex * pad, width), BF),
            jax.ShapeDtypeStruct((n_ex * pad, rows), BF),
            jax.ShapeDtypeStruct((rows, 1), I32),
            jax.ShapeDtypeStruct((length, length), F32),
        ],
        in_specs=[smem, smem] + [vmem] * 4,
        out_specs=[vmem] * 4,
        name="slots_kernel",
    )(me, parents, routes[0], slot_order[0], cotangent[0], segments)

    def dispatch(rows_out):
        came = swap(rows_out.reshape(n_ex, pad, width), "expert").reshape(n_ex * pad, width)
        mine = call(pack_kernel, [((each, width), BF)], me, came, pad=pad, capacity=capacity)[0]
        return mine

    grads_in = dispatch(grads_out)
    proj_blocks = gather_experts(swap(jnp.broadcast_to(proj_weight, (n_dp, own, width)), "dp"))
    grads_in, bias = lax.optimization_barrier((grads_in, bias))
    grads = along([grads_in] * n_dp)
    qkv = call(assemble_kernel, [((n_dp, n_ex, own, cols), BF)], me, *qkv_blocks)[0].reshape(width, cols)
    normed1, unit1, packed, probs, att_out, vectors = call(
        attend_kernel,
        [
            ((length, width), BF),
            ((length, width), F32),
            ((length, 3 * part), BF),
            ((part // head_dim, length, length), BF),
            ((n_dp, rows, part), BF),
            ((8, width), F32),
        ],
        me, qkv, bias, *token_blocks,
        n_dp=n_dp, head_dim=head_dim, experts=experts,
    )
    early = [j for j in range(1, n_dp) if j != n_dp // 2]
    att_out, *came = lax.optimization_barrier((att_out, *[grads[j] for j in early]))
    for j, block in zip(early, came):
        grads[j] = block
    attended = swap(att_out, "dp")
    proj = call(assemble_kernel, [((n_dp, n_ex, own, width), BF)], me, *proj_blocks)[0].reshape(width, width)
    mixed, normed2, p, sent = call(
        mix_kernel,
        [((rows, width), F32), ((rows, width), BF), ((rows, 128), F32), ((n_ex * pad, width), BF)],
        me, x, attended, proj, qkv, vectors, tableT,
        experts=experts,
    )
    mine, grads = lax.optimization_barrier((dispatch(sent), grads))
    slots = along([mine] * n_dp)
    *both, act, d_pre, slot_rows, d_rows, grad_up_bias, grad_down_bias = experts_call(
        me, qkv, up_weight[0], down_weight[0], up_bias, down_bias, slots, grads, experts, part
    )
    came = along(both, -1)
    grad_up = mm(slot_rows, d_pre, 0, 0)
    grad_down = mm(act, d_rows, 0, 0)
    grad_up, grad_down, *came = lax.optimization_barrier((grad_up, grad_down, *came))
    summed = call(line_sum_kernel, [((n_ex * 2 * pad, width), BF)], me, *came, pad=pad, capacity=capacity)[0]
    back = swap(summed.reshape(n_ex, 2 * pad, width), "expert").reshape(n_ex * 2 * pad, width)
    outputs, d_mixed, d_low, d_att, d_logits, sums = call(
        combine_kernel,
        [
            ((rows, width), BF),
            ((rows, width), F32),
            ((rows, width), BF),
            ((n_dp, rows, part), BF),
            ((rows, 128), BF),
            ((8, width), F32),
        ],
        me, back, routes[0], rank, mixed, p, cotangent[0], qkv, vectors, proj,
        pad=pad, capacity=capacity, experts=experts, part=part,
    )
    d_heads = swap(d_att, "dp")
    half = n_ex // 2
    near, keep = call(
        proj_grad_kernel,
        [((half, n_dp, own, width), BF), ((half, n_dp, own, width), F32)],
        me, attended, d_low,
        scratch=[pltpu.VMEM((width, width), F32)],
    )
    d_heads, *parts = lax.optimization_barrier((d_heads, *core_sum(me, near, keep)))
    proj_chips = to_chips(parts)
    d_packed, d_normed = call(
        attend_back_kernel,
        [((length, 3 * part), BF), ((n_dp, rows, width), BF)],
        me, d_heads, probs, packed, qkv,
        scratch=[pltpu.VMEM((length, length), BF)],
        head_dim=head_dim,
    )
    d_own = swap(d_normed, "dp")
    near, keep = call(
        qkv_grad_kernel,
        [((half, n_dp, own, cols), BF), ((half, n_dp, own, cols), F32)],
        me, normed1, unit1, d_packed, d_normed, normed2, d_logits, sums,
        scratch=[pltpu.VMEM((width, cols), F32), pltpu.VMEM((128, width), F32)],
        experts=experts,
    )
    near, keep, *proj_chips = lax.optimization_barrier((near, keep, *proj_chips))
    qkv_chips = to_chips(core_sum(me, near, keep))
    d_own, *qkv_chips = lax.optimization_barrier((d_own, *qkv_chips))
    summed = call(
        chip_sum_kernel, [((n_dp, own, cols + width), BF)], me, *qkv_chips, *proj_chips
    )[0]
    owned_qkv, owned_proj, owned_router, owned_gains, owned_biases = call(
        weights_end_kernel,
        [
            ((own, 3 * width), F32),
            ((own, width), F32),
            ((own, experts), F32),
            ((2, own), F32),
            ((5, own), F32),
        ],
        me, swap(summed, "dp"),
        scratch=[pltpu.VMEM((128, 128), F32)],
    )
    grad_tokens = call(tokens_end_kernel, [((rows, width), F32)], me, d_own, x, vectors, d_mixed)[0]
    return (
        outputs[None],
        grad_tokens[None],
        owned_qkv,
        owned_proj,
        owned_router,
        owned_gains,
        owned_biases,
        grad_up[None],
        grad_up_bias,
        grad_down[None],
        grad_down_bias,
    )


def solution(mesh):
    line = P(("dp", "expert"), None)
    across = P(None, ("dp", "expert"))
    act = P("expert", "dp", None)
    return jax.shard_map(
        shards,
        mesh=mesh,
        in_specs=(
            act,
            line,
            line,
            line,
            across,
            across,
            P("expert", None, "dp"),
            P("expert", "dp"),
            act,
            P("expert", "dp"),
            act,
            act,
            P("expert", None),
            P("expert", None),
            act,
        ),
        out_specs=(
            act,
            act,
            line,
            line,
            line,
            across,
            across,
            P("expert", None, "dp"),
            P("expert", "dp"),
            act,
            P("expert", "dp"),
        ),
        check_vma=False,
    )
```

time: 374 us -> 329 us (0.88); the launches traced: 368 us -> 328 us
  Pallas kernels: 0 us -> 84.2 us
  local copies, waits for them, and re-layouts: 96.7 us -> 14.1 us
  waiting for transfers between devices: 85.1 us -> 127 us
  starting transfers between devices: 112 us -> 74.3 us
  matrix products: 44 us -> 9.48 us
  other arithmetic: 27.8 us -> 0.58 us
  blocking collectives: 0 us -> 16.7 us
    pallas_call x0 -> x19, Pallas kernels: none -> 84.2 us  [the longest x17 67.3 us: call(): pl.pallas_call(functools.partial(kernel, **static), out_shape=[jax.ShapeD...]
    ppermute x33 -> x12, starting transfers between devices: 85.3 us -> 23.6 us  [ahead(): return lax.ppermute(x, 'dp', [(i, (i + step) % n) for i in range(n)])]
    unnamed x203 -> x96, local copies, waits for them, and re-layouts: 42.9 us -> 11.9 us
    dot_general x23 -> x2, matrix products: 35.6 us -> 9.48 us  [mm(): lax.dot_general(a, b, (((ca,), (cb,)), ((), ())), preferred_element_type=...]
    ppermute x33 -> x12, waiting for transfers between devices: 58 us -> 81.4 us  [ahead(): return lax.ppermute(x, 'dp', [(i, (i + step) % n) for i in range(n)])]
    all_to_all x3 -> x8, starting transfers between devices: 12.4 us -> 34.6 us  [swap(): return lax.all_to_all(x, axis, split_axis=0, concat_axis=0, tiled=True)]
    all_to_all x3 -> x8, waiting for transfers between devices: 6.6 us -> 27.3 us  [swap(): return lax.all_to_all(x, axis, split_axis=0, concat_axis=0, tiled=True)]
    concatenate x24 -> x0, local copies, waits for them, and re-layouts: 19.4 us -> none  [the longest x18 16.2 us: shards(): jnp.concatenate([grad_qkv, extra], axis=1)]
  transfers between devices with their start and end apart: 58 -> 42, of which waited for: 21 -> 20; matrix products, arithmetic and copies ran while one was open for 38% -> 4% of each run, Pallas kernels for 0% -> 12%
where the time goes in v2:
time: 329 us; the launch traced here: 328 us
  waiting for transfers between devices  127 us (39%)
  Pallas kernels  84.2 us (26%)
  starting transfers between devices  74.3 us (23%)
  blocking collectives  16.7 us (5%)
  local copies, waits for them, and re-layouts  14.1 us (4%)
  matrix products  9.48 us (3%)
    ppermute x12, waiting for transfers between devices, ahead(): return lax.ppermute(x, 'dp', [(i, (i + step) % n) for i in range(n)])  81.4 us
    pallas_call x17, Pallas kernels, call(): pl.pallas_call(functools.partial(kernel, **static), out_shape=[jax.ShapeD...  67.3 us
    all_to_all x8, starting transfers between devices, swap(): return lax.all_to_all(x, axis, split_axis=0, concat_axis=0, tiled=True)  34.6 us
    all_to_all x8, waiting for transfers between devices, swap(): return lax.all_to_all(x, axis, split_axis=0, concat_axis=0, tiled=True)  27.3 us
    ppermute x12, starting transfers between devices, ahead(): return lax.ppermute(x, 'dp', [(i, (i + step) % n) for i in range(n)])  23.6 us
    ppermute x22, waiting for transfers between devices, flip(): return lax.ppermute(x, 'expert', [(i, i ^ bits) for i in range(n)])  18.4 us
    all_to_all x1, blocking collectives, swap(): return lax.all_to_all(x, axis, split_axis=0, concat_axis=0, tiled=True)  16.7 us
    ppermute x22, starting transfers between devices, flip(): return lax.ppermute(x, 'expert', [(i, i ^ bits) for i in range(n)])  16.2 us
  transfers between devices with their start and end apart: 42, of which 20 were waited for; matrix products, arithmetic and copies ran while one was open for 4% of the time, Pallas kernels for 12%

profile of v2, /device:TPU:0, one launch (start us, length us, event | category | flops | bytes accessed | tf_op | source)
XLA Modules:
  0.0 327.6 jit_solution(6810165753109317229)
XLA Ops:
  4.4 6.3 %all-to-all-start = ((bf16[4,32,896]{2,1,0:T(8,128)(2,1)}), bf16[4,32,896]{2,1,0:T(8,128)(2,1)S(1)}, u32[]{:S(2)}, u32[]{:S(2)}) async-start(bf16[4,32,896]{2,1,0:T(8,128)(2,1)} %weights_kernel.1), calls=%async_computation | async-start | bytes 458752 | tf_op jit(solution)/shard_map/all_to_all | solution.py:47
  15.0 3.9 %all-to-all-done.refs_0_ = bf16[4,32,896]{2,1,0:T(8,128)(2,1)S(1)} async-done(((bf16[4,32,896]{2,1,0:T(8,128)(2,1)}), bf16[4,32,896]{2,1,0:T(8,128)(2,1)S(1)}, u32[]{:S(2)}, u32[]{:S(2)}) %all-to-all-start) | async-done | bytes 229408 | tf_op jit(solution)/shard_map/all_to_all | solution.py:47
  18.9 3.7 %all-to-all-start.1 = ((bf16[8,24,1024]{2,1,0:T(8,128)(2,1)}), bf16[8,24,1024]{2,1,0:T(8,128)(2,1)S(1)}, u32[]{:S(2)}, u32[]{:S(2)}) async-start(bf16[8,24,1024]{2,1,0:T(8,128)(2,1)} %bitcast.46), calls=%async_computation.1 | async-start | bytes 786432 | tf_op jit(solution)/shard_map/all_to_all | solution.py:47
  25.4 12.3 %collective-permute-done.refs_2_ = bf16[128,1024]{1,0:T(8,128)(2,1)S(1)} collective-permute-done((bf16[128,1024]{1,0:T(8,128)(2,1)S(1)}, bf16[128,1024]{1,0:T(8,128)(2,1)S(1)}, u32[]{:S(2)}, u32[]{:S(2)}) %collective-permute-start) | collective-permute-done | bytes 262176 | tf_op jit(solution)/shard_map/ppermute | solution.py:38
  41.2 4.2 %collective-permute-start.8 = (bf16[128,1024]{1,0:T(8,128)(2,1)S(1)}, bf16[128,1024]{1,0:T(8,128)(2,1)S(1)}, u32[]{:S(2)}, u32[]{:S(2)}) collective-permute-start(bf16[128,1024]{1,0:T(8,128)(2,1)S(1)} %bitcast.38), channel_id=1, source_target_pairs={{0,8},{8,16},{16,24},{24,0},{1,9},{9,17},{17,25},{25,1},{2,10},{10... | collective-permute-start | bytes 786440 | tf_op jit(solution)/shard_map/ppermute | solution.py:38
  46.2 4.6 %all-to-all-start.3 = ((bf16[4,32,1024]{2,1,0:T(8,128)(2,1)}), bf16[4,32,1024]{2,1,0:T(8,128)(2,1)S(1)}, u32[]{:S(2)}, u32[]{:S(2)}) async-start(bf16[4,32,1024]{2,1,0:T(8,128)(2,1)} %broadcast_in_dim.15), calls=%async_computation.3 | async-start | bytes 524288 | tf_op jit(solution)/shard_map/all_to_all | solution.py:47
  54.0 6.6 %collective-permute-start.11 = (bf16[144,1024]{1,0:T(8,128)(2,1)}, bf16[144,1024]{1,0:T(8,128)(2,1)S(1)}, u32[]{:S(2)}, u32[]{:S(2)}) collective-permute-start(bf16[144,1024]{1,0:T(8,128)(2,1)} %pack_kernel.2.refs_4_), channel_id=1, source_target_pairs={{0,24},{8,0},{16,8},{24,16},{1,25},{9,1},{17,9},{25,17},{2,26},{10... | collective-permute-start | bytes 884744 | tf_op jit(solution)/shard_map/ppermute | solution.py:38
  67.8 10.8 %attend_kernel.1 = (bf16[512,1024]{1,0:T(8,128)(2,1)}, f32[512,1024]{1,0:T(8,128)}, bf16[512,768]{1,0:T(8,128)(2,1)}, bf16[4,512,512]{2,1,0:T(8,128)(2,1)}, bf16...) custom-call(s32[2]{0:T(128)} %pad_add_fusion.me, bf16[1024,896]{1,0:T(8,128)(2,1)} %bitcast.24, ...), custom_call_target="tpu_custom_call" | custom-call | tf_op jit(solution)/shard_map/attend_kernel/pallas_call | solution.py:26
  78.7 4.5 %all-to-all-start.2 = ((bf16[4,128,256]{2,1,0:T(8,128)(2,1)}), bf16[4,128,256]{2,1,0:T(8,128)(2,1)S(1)}, u32[]{:S(2)}, u32[]{:S(2)}) async-start(bf16[4,128,256]{2,1,0:T(8,128)(2,1)} %get-tuple-element.101), calls=%async_computation.2 | async-start | bytes 524288 | tf_op jit(solution)/shard_map/all_to_all | solution.py:47
  91.9 4.0 %mix_kernel.1 = (f32[128,1024]{1,0:T(8,128)}, bf16[128,1024]{1,0:T(8,128)(2,1)}, f32[128,128]{1,0:T(8,128)}, bf16[192,1024]{1,0:T(8,128)(2,1)}) custom-call(s32[2]{0:T(128)} %pad_add_fusion.me, bf16[128,1024]{1,0:T(8,128)(2,1)} %bitcast.34, bf16[4,128,256]{2,1,0:T(8,128)(2,1)} %copy-done.1, bf16[1024,1024]{1,0:T(8,128)(2,1)} %bitcast.29, ...), custom_call_target="tpu_custom_call" | custom-call | tf_op jit(solution)/shard_map/mix_kernel/pallas_call | solution.py:26
  96.0 3.5 %all-to-all-start.4 = ((bf16[8,24,1024]{2,1,0:T(8,128)(2,1)}), bf16[8,24,1024]{2,1,0:T(8,128)(2,1)S(1)}, u32[]{:S(2)}, u32[]{:S(2)}) async-start(bf16[8,24,1024]{2,1,0:T(8,128)(2,1)} %bitcast.47), calls=%async_computation.4 | async-start | bytes 786432 | tf_op jit(solution)/shard_map/all_to_all | solution.py:47
  101.1 6.6 %all-to-all-done.4 = bf16[8,24,1024]{2,1,0:T(8,128)(2,1)S(1)} async-done(((bf16[8,24,1024]{2,1,0:T(8,128)(2,1)}), bf16[8,24,1024]{2,1,0:T(8,128)(2,1)S(1)}, u32[]{:S(2)}, u32[]{:S(2)}) %all-to-all-start.4) | async-done | bytes 393248 | tf_op jit(solution)/shard_map/all_to_all | solution.py:47
  110.4 5.6 %collective-permute-done.19.refs_6_ = bf16[144,1024]{1,0:T(8,128)(2,1)S(1)} collective-permute-done((bf16[144,1024]{1,0:T(8,128)(2,1)S(1)}, bf16[144,1024]{1,0:T(8,128)(2,1)S(1)}, u32[]{:S(2)}, u32[]{:S(2)}) %collective-permute-start.19) | collective-permute-done | bytes 294944 | tf_op jit(solution)/shard_map/ppermute | solution.py:38
  119.0 7.7 %collective-permute-done.22.refs_3_ = bf16[144,1024]{1,0:T(8,128)(2,1)S(1)} collective-permute-done((bf16[144,1024]{1,0:T(8,128)(2,1)}, bf16[144,1024]{1,0:T(8,128)(2,1)S(1)}, u32[]{:S(2)}, u32[]{:S(2)}) %collective-permute-start.22) | collective-permute-done | bytes 294944 | tf_op jit(solution)/shard_map/ppermute | solution.py:38
  126.7 16.4 %collective-permute-done.21.refs_2_ = bf16[144,1024]{1,0:T(8,128)(2,1)S(1)} collective-permute-done((bf16[144,1024]{1,0:T(8,128)(2,1)}, bf16[144,1024]{1,0:T(8,128)(2,1)S(1)}, u32[]{:S(2)}, u32[]{:S(2)}) %collective-permute-start.21) | collective-permute-done | bytes 294944 | tf_op jit(solution)/shard_map/ppermute | solution.py:38
  144.0 14.0 %expert_kernel.1 = (bf16[288,1024]{1,0:T(8,128)(2,1)}, bf16[288,1024]{1,0:T(8,128)(2,1)}, bf16[288,1024]{1,0:T(8,128)(2,1)}, bf16[288,1024]{1,0:T(8,128)(2,1)}, ...) custom-call(s32[2]{0:T(128)} %pad_add_fusion.me, ...), custom_call_target="tpu_custom_call" | custom-call | tf_op jit(solution)/shard_map/expert_kernel/pallas_call | solution.py:270
  163.4 5.6 %fusion = f32[1024,1024]{1,0:T(8,128)} fusion(bf16[576,1024]{1,0:T(8,128)(2,1)} %get-tuple-element.112, bf16[576,1024]{1,0:T(8,128)(2,1)} %get-tuple-element.113), kind=kOutput, calls=%fused_computation.1 | convolution fusion | flops 1207959552 | bytes 6553600 | tf_op jit(solution)/shard_map/dot_general | solution.py:20
  169.0 3.9 %fusion.1 = f32[1024,1024]{1,0:T(8,128)} fusion(bf16[576,1024]{1,0:T(8,128)(2,1)S(1)} %copy-done.42, bf16[576,1024]{1,0:T(8,128)(2,1)S(1)} %copy-done.43), kind=kOutput, calls=%fused_computation.2 | convolution fusion | flops 1207959552 | bytes 6553600 | tf_op jit(solution)/shard_map/dot_general | solution.py:20
  172.9 39.3 %collective-permute-done.24.refs_2_ = bf16[288,1024]{1,0:T(8,128)(2,1)S(1)} collective-permute-done((bf16[288,1024]{1,0:T(8,128)(2,1)}, bf16[288,1024]{1,0:T(8,128)(2,1)S(1)}, u32[]{:S(2)}, u32[]{:S(2)}) %collective-permute-start.24) | collective-permute-done | bytes 589856 | tf_op jit(solution)/shard_map/ppermute | solution.py:38
  216.3 16.7 %all_to_all.45 = bf16[8,48,1024]{2,1,0:T(8,128)(2,1)} all-to-all(bf16[8,48,1024]{2,1,0:T(8,128)(2,1)} %bitcast.32), channel_id=1, replica_groups=mesh['dp'=4,'expert'=8] {'expert'}, dimensions={0} | all-to-all | bytes 1572864 | tf_op jit(solution)/shard_map/all_to_all | solution.py:47
  233.1 5.1 %combine_kernel.1 = (bf16[128,1024]{1,0:T(8,128)(2,1)}, f32[128,1024]{1,0:T(8,128)}, bf16[128,1024]{1,0:T(8,128)(2,1)}, bf16[4,128,256]{2,1,0:T(8,128)(2,1)}, bf...) custom-call(s32[2]{0:T(128)} %pad_add_fusion.me, bf16[384,1024]{1,0:T(8,128)(2,1)} %bitcast.31, s32[128,1]{1,0:T(8,128)} %copy.27.route, ...), custom_call_target="tpu_custom_call" | custom-call | tf_op jit(solution)/shard_map/combine_kernel/pallas_call | solution.py:26
  238.2 3.5 %proj_grad_kernel.1 = (bf16[4,4,32,1024]{3,2,1,0:T(8,128)(2,1)}, f32[4,4,32,1024]{3,2,1,0:T(8,128)}) custom-call(s32[2]{0:T(128)} %pad_add_fusion.me, bf16[4,128,256]{2,1,0:T(8,128)(2,1)} %copy-done.1, bf16[128,1024]{1,0:T(8,128)(2,1)} %get-tuple-element.129.d_low), custom_call_target="tpu_custom_call" | custom-call | tf_op jit(solution)/shard_map/proj_grad_kernel/pallas_call | solution.py:26
  241.7 3.6 %all-to-all-start.6 = ((bf16[4,128,256]{2,1,0:T(8,128)(2,1)}), bf16[4,128,256]{2,1,0:T(8,128)(2,1)S(1)}, u32[]{:S(2)}, u32[]{:S(2)}) async-start(bf16[4,128,256]{2,1,0:T(8,128)(2,1)} %get-tuple-element.128), calls=%async_computation.6 | async-start | bytes 524288 | tf_op jit(solution)/shard_map/all_to_all | solution.py:47
  249.3 5.6 %all-to-all-done.6.d_att = bf16[4,128,256]{2,1,0:T(8,128)(2,1)S(1)} async-done(((bf16[4,128,256]{2,1,0:T(8,128)(2,1)}), bf16[4,128,256]{2,1,0:T(8,128)(2,1)S(1)}, u32[]{:S(2)}, u32[]{:S(2)}) %all-to-all-start.6) | async-done | bytes 262176 | tf_op jit(solution)/shard_map/all_to_all | solution.py:47
  255.7 10.2 %attend_back_kernel.1 = (bf16[512,768]{1,0:T(8,128)(2,1)}, bf16[4,128,1024]{2,1,0:T(8,128)(2,1)}) custom-call(s32[2]{0:T(128)} %pad_add_fusion.me, bf16[4,128,256]{2,1,0:T(8,128)(2,1)} %copy-done.8, bf16[4,512,512]{2,1,0:T(8,128)(2,1)} %get-tuple-element.137.probs, bf16[512,768]{1,0:T(8,128)(2,1)} %get-tuple-element.138.packed, bf16[1024,896]{1,0:T(8,128)(2,1)} %bitcast.28), custom_call_target="tpu_custom_call" | custom-call | tf_op jit(solution)/shard_map/attend_back_kernel/pallas_call | solution.py:26
  265.8 3.7 %all-to-all-start.7 = ((bf16[4,128,1024]{2,1,0:T(8,128)(2,1)}), bf16[4,128,1024]{2,1,0:T(8,128)(2,1)S(1)}, u32[]{:S(2)}, u32[]{:S(2)}) async-start(bf16[4,128,1024]{2,1,0:T(8,128)(2,1)} %get-tuple-element.139.d_normed), calls=%async_computation.7 | async-start | bytes 2097152 | tf_op jit(solution)/shard_map/all_to_all | solution.py:47
  273.1 5.7 %qkv_grad_kernel.1 = (bf16[4,4,32,896]{3,2,1,0:T(8,128)(2,1)}, f32[4,4,32,896]{3,2,1,0:T(8,128)}) custom-call(s32[2]{0:T(128)} %pad_add_fusion.me, bf16[512,1024]{1,0:T(8,128)(2,1)} %get-tuple-element.140.normed, f32[512,1024]{1,0:T(8,128)} %get-tuple-element.141.unit, bf16[512,768]{1,0:T(8,128)(2,1)} %get-tuple-element.142.d_packed, ...), custom_call_target="tpu_custom_call" | custom-call | tf_op jit(solution)/shard_map/qkv_grad_kernel/pallas_call | solution.py:26
  278.8 3.6 %collective-permute-done.28.refs_6_ = bf16[4,32,1024]{2,1,0:T(8,128)(2,1)S(1)} collective-permute-done((bf16[4,32,1024]{2,1,0:T(8,128)(2,1)S(1)}, bf16[4,32,1024]{2,1,0:T(8,128)(2,1)S(1)}, u32[]{:S(2)}, u32[]{:S(2)}) %collective-permute-start.28) | collective-permute-done | bytes 262176 | tf_op jit(solution)/shard_map/ppermute | solution.py:43
  292.3 5.2 %collective-permute-done.31.refs_1_ = bf16[4,32,896]{2,1,0:T(8,128)(2,1)S(1)} collective-permute-done((bf16[4,32,896]{2,1,0:T(8,128)(2,1)}, bf16[4,32,896]{2,1,0:T(8,128)(2,1)S(1)}, u32[]{:S(2)}, u32[]{:S(2)}) %collective-permute-start.31) | collective-permute-done | bytes 229408 | tf_op jit(solution)/shard_map/ppermute | solution.py:43
  297.5 5.3 %collective-permute-done.32.refs_2_ = bf16[4,32,896]{2,1,0:T(8,128)(2,1)S(1)} collective-permute-done((bf16[4,32,896]{2,1,0:T(8,128)(2,1)}, bf16[4,32,896]{2,1,0:T(8,128)(2,1)S(1)}, u32[]{:S(2)}, u32[]{:S(2)}) %collective-permute-start.32) | collective-permute-done | bytes 229408 | tf_op jit(solution)/shard_map/ppermute | solution.py:43
  306.3 4.7 %all-to-all-start.8 = ((bf16[4,32,1920]{2,1,0:T(8,128)(2,1)}), bf16[4,32,1920]{2,1,0:T(8,128)(2,1)S(1)}, u32[]{:S(2)}, u32[]{:S(2)}) async-start(bf16[4,32,1920]{2,1,0:T(8,128)(2,1)} %chip_sum_kernel.1), calls=%async_computation.8 | async-start | bytes 983040 | tf_op jit(solution)/shard_map/all_to_all | solution.py:47
  313.8 9.8 %all-to-all-done.8.came = bf16[4,32,1920]{2,1,0:T(8,128)(2,1)S(1)} async-done(((bf16[4,32,1920]{2,1,0:T(8,128)(2,1)}), bf16[4,32,1920]{2,1,0:T(8,128)(2,1)S(1)}, u32[]{:S(2)}, u32[]{:S(2)}) %all-to-all-start.8) | async-done | bytes 491552 | tf_op jit(solution)/shard_map/all_to_all | solution.py:47
  (173 shorter events, 80.5 us)
Async XLA Ops:
  4.4 14.5 %all-to-all-start = ((bf16[4,32,896]{2,1,0:T(8,128)(2,1)}), bf16[4,32,896]{2,1,0:T(8,128)(2,1)S(1)}, u32[]{:S(2)}, u32[]{:S(2)}) async-start(bf16[4,32,896]{2,1,0:T(8,128)(2,1)} %weights_kernel.1), calls=%async_computation | async-start | bytes 458752 | tf_op jit(solution)/shard_map/all_to_all | solution.py:47
  18.9 26.5 %all-to-all-start.1 = ((bf16[8,24,1024]{2,1,0:T(8,128)(2,1)}), bf16[8,24,1024]{2,1,0:T(8,128)(2,1)S(1)}, u32[]{:S(2)}, u32[]{:S(2)}) async-start(bf16[8,24,1024]{2,1,0:T(8,128)(2,1)} %bitcast.46), calls=%async_computation.1 | async-start | bytes 786432 | tf_op jit(solution)/shard_map/all_to_all | solution.py:47
  22.7 15.0 %collective-permute-start = (bf16[128,1024]{1,0:T(8,128)(2,1)S(1)}, bf16[128,1024]{1,0:T(8,128)(2,1)S(1)}, u32[]{:S(2)}, u32[]{:S(2)}) collective-permute-start(bf16[128,1024]{1,0:T(8,128)(2,1)S(1)} %bitcast.36), channel_id=1, source_target_pairs={{0,16},{8,24},{16,0},{24,8},{1,17},{9,25},{17,1},{25,9},{2,18},{10... | collective-permute-start | bytes 786440 | tf_op jit(solution)/shard_map/ppermute | solution.py:38
  22.7 28.1 %collective-permute-start.9 = (bf16[128,1024]{1,0:T(8,128)(2,1)S(1)}, bf16[128,1024]{1,0:T(8,128)(2,1)S(1)}, u32[]{:S(2)}, u32[]{:S(2)}) collective-permute-start(bf16[128,1024]{1,0:T(8,128)(2,1)S(1)} %bitcast.37), channel_id=1, source_target_pairs={{0,24},{8,0},{16,8},{24,16},{1,25},{9,1},{17,9},{25,17},{2,26},{10... | collective-permute-start | bytes 786440 | tf_op jit(solution)/shard_map/ppermute | solution.py:38
  37.7 13.2 %collective-permute-start.6 = (bf16[4,32,896]{2,1,0:T(8,128)(2,1)S(1)}, bf16[4,32,896]{2,1,0:T(8,128)(2,1)S(1)}, u32[]{:S(2)}, u32[]{:S(2)}) collective-permute-start(bf16[4,32,896]{2,1,0:T(8,128)(2,1)S(1)} %all-to-all-done.refs_0_), channel_id=1, source_target_pairs={{0,6},{1,7},{2,4},{3,5},{4,2},{5,3},{6,0},{7,1},{8,14},{9,15},{10,... | collective-permute-start | bytes 688136 | tf_op jit(solution)/shard_map/ppermute | solution.py:43
  40.3 11.1 %collective-permute-start.4 = (bf16[4,32,896]{2,1,0:T(8,128)(2,1)S(1)}, bf16[4,32,896]{2,1,0:T(8,128)(2,1)S(1)}, u32[]{:S(2)}, u32[]{:S(2)}) collective-permute-start(bf16[4,32,896]{2,1,0:T(8,128)(2,1)S(1)} %all-to-all-done.refs_0_), channel_id=1, source_target_pairs={{0,4},{1,5},{2,6},{3,7},{4,0},{5,1},{6,2},{7,3},{8,12},{9,13},{10,... | collective-permute-start | bytes 688136 | tf_op jit(solution)/shard_map/ppermute | solution.py:43
  40.9 10.6 %collective-permute-start.2 = (bf16[4,32,896]{2,1,0:T(8,128)(2,1)S(1)}, bf16[4,32,896]{2,1,0:T(8,128)(2,1)S(1)}, u32[]{:S(2)}, u32[]{:S(2)}) collective-permute-start(bf16[4,32,896]{2,1,0:T(8,128)(2,1)S(1)} %all-to-all-done.refs_0_), channel_id=1, source_target_pairs={{0,2},{1,3},{2,0},{3,1},{4,6},{5,7},{6,4},{7,5},{8,10},{9,11},{10,... | collective-permute-start | bytes 688136 | tf_op jit(solution)/shard_map/ppermute | solution.py:43
  41.2 12.8 %collective-permute-start.8 = (bf16[128,1024]{1,0:T(8,128)(2,1)S(1)}, bf16[128,1024]{1,0:T(8,128)(2,1)S(1)}, u32[]{:S(2)}, u32[]{:S(2)}) collective-permute-start(bf16[128,1024]{1,0:T(8,128)(2,1)S(1)} %bitcast.38), channel_id=1, source_target_pairs={{0,8},{8,16},{16,24},{24,0},{1,9},{9,17},{17,25},{25,1},{2,10},{10... | collective-permute-start | bytes 786440 | tf_op jit(solution)/shard_map/ppermute | solution.py:38
  46.2 14.4 %all-to-all-start.3 = ((bf16[4,32,1024]{2,1,0:T(8,128)(2,1)}), bf16[4,32,1024]{2,1,0:T(8,128)(2,1)S(1)}, u32[]{:S(2)}, u32[]{:S(2)}) async-start(bf16[4,32,1024]{2,1,0:T(8,128)(2,1)} %broadcast_in_dim.15), calls=%async_computation.3 | async-start | bytes 524288 | tf_op jit(solution)/shard_map/all_to_all | solution.py:47
  51.4 11.6 %collective-permute-start.5 = (bf16[4,32,896]{2,1,0:T(8,128)(2,1)S(1)}, bf16[4,32,896]{2,1,0:T(8,128)(2,1)}, u32[]{:S(2)}, u32[]{:S(2)}) collective-permute-start(bf16[4,32,896]{2,1,0:T(8,128)(2,1)S(1)} %collective-permute-done.4.refs_4_), channel_id=1, source_target_pairs={{0,1},{1,0},{2,3},{3,2},{4,5},{5,4},{6,7},{7,6},{8,9},{9,8},{10,11... | collective-permute-start | bytes 688136 | tf_op jit(solution)/shard_map/ppermute | solution.py:43
  51.5 12.9 %collective-permute-start.3 = (bf16[4,32,896]{2,1,0:T(8,128)(2,1)S(1)}, bf16[4,32,896]{2,1,0:T(8,128)(2,1)}, u32[]{:S(2)}, u32[]{:S(2)}) collective-permute-start(bf16[4,32,896]{2,1,0:T(8,128)(2,1)S(1)} %collective-permute-done.2.refs_2_), channel_id=1, source_target_pairs={{0,1},{1,0},{2,3},{3,2},{4,5},{5,4},{6,7},{7,6},{8,9},{9,8},{10,11... | collective-permute-start | bytes 688136 | tf_op jit(solution)/shard_map/ppermute | solution.py:43
  54.0 24.6 %collective-permute-start.11 = (bf16[144,1024]{1,0:T(8,128)(2,1)}, bf16[144,1024]{1,0:T(8,128)(2,1)S(1)}, u32[]{:S(2)}, u32[]{:S(2)}) collective-permute-start(bf16[144,1024]{1,0:T(8,128)(2,1)} %pack_kernel.2.refs_4_), channel_id=1, source_target_pairs={{0,24},{8,0},{16,8},{24,16},{1,25},{9,1},{17,9},{25,17},{2,26},{10... | collective-permute-start | bytes 884744 | tf_op jit(solution)/shard_map/ppermute | solution.py:38
  60.6 18.1 %collective-permute-start.10 = (bf16[144,1024]{1,0:T(8,128)(2,1)}, bf16[144,1024]{1,0:T(8,128)(2,1)S(1)}, u32[]{:S(2)}, u32[]{:S(2)}) collective-permute-start(bf16[144,1024]{1,0:T(8,128)(2,1)} %pack_kernel.2.refs_4_), channel_id=1, source_target_pairs={{0,8},{8,16},{16,24},{24,0},{1,9},{9,17},{17,25},{25,1},{2,10},{10... | collective-permute-start | bytes 884744 | tf_op jit(solution)/shard_map/ppermute | solution.py:38
  61.3 21.9 %collective-permute-start.17 = (bf16[4,32,1024]{2,1,0:T(8,128)(2,1)S(1)}, bf16[4,32,1024]{2,1,0:T(8,128)(2,1)S(1)}, u32[]{:S(2)}, u32[]{:S(2)}) collective-permute-start(bf16[4,32,1024]{2,1,0:T(8,128)(2,1)S(1)} %all-to-all-done.3.refs_0_), channel_id=1, source_target_pairs={{0,6},{1,7},{2,4},{3,5},{4,2},{5,3},{6,0},{7,1},{8,14},{9,15},{10,... | collective-permute-start | bytes 786440 | tf_op jit(solution)/shard_map/ppermute | solution.py:43
  63.0 20.7 %collective-permute-start.15 = (bf16[4,32,1024]{2,1,0:T(8,128)(2,1)S(1)}, bf16[4,32,1024]{2,1,0:T(8,128)(2,1)S(1)}, u32[]{:S(2)}, u32[]{:S(2)}) collective-permute-start(bf16[4,32,1024]{2,1,0:T(8,128)(2,1)S(1)} %all-to-all-done.3.refs_0_), channel_id=1, source_target_pairs={{0,4},{1,5},{2,6},{3,7},{4,0},{5,1},{6,2},{7,3},{8,12},{9,13},{10,... | collective-permute-start | bytes 786440 | tf_op jit(solution)/shard_map/ppermute | solution.py:43
  64.4 19.4 %collective-permute-start.13 = (bf16[4,32,1024]{2,1,0:T(8,128)(2,1)S(1)}, bf16[4,32,1024]{2,1,0:T(8,128)(2,1)S(1)}, u32[]{:S(2)}, u32[]{:S(2)}) collective-permute-start(bf16[4,32,1024]{2,1,0:T(8,128)(2,1)S(1)} %all-to-all-done.3.refs_0_), channel_id=1, source_target_pairs={{0,2},{1,3},{2,0},{3,1},{4,6},{5,7},{6,4},{7,5},{8,10},{9,11},{10,... | collective-permute-start | bytes 786440 | tf_op jit(solution)/shard_map/ppermute | solution.py:43
  78.7 12.5 %all-to-all-start.2 = ((bf16[4,128,256]{2,1,0:T(8,128)(2,1)}), bf16[4,128,256]{2,1,0:T(8,128)(2,1)S(1)}, u32[]{:S(2)}, u32[]{:S(2)}) async-start(bf16[4,128,256]{2,1,0:T(8,128)(2,1)} %get-tuple-element.101), calls=%async_computation.2 | async-start | bytes 524288 | tf_op jit(solution)/shard_map/all_to_all | solution.py:47
  96.0 11.7 %all-to-all-start.4 = ((bf16[8,24,1024]{2,1,0:T(8,128)(2,1)}), bf16[8,24,1024]{2,1,0:T(8,128)(2,1)S(1)}, u32[]{:S(2)}, u32[]{:S(2)}) async-start(bf16[8,24,1024]{2,1,0:T(8,128)(2,1)} %bitcast.47), calls=%async_computation.4 | async-start | bytes 786432 | tf_op jit(solution)/shard_map/all_to_all | solution.py:47
  99.4 16.5 %collective-permute-start.19 = (bf16[144,1024]{1,0:T(8,128)(2,1)S(1)}, bf16[144,1024]{1,0:T(8,128)(2,1)S(1)}, u32[]{:S(2)}, u32[]{:S(2)}) collective-permute-start(bf16[144,1024]{1,0:T(8,128)(2,1)S(1)} %copy-done.6), channel_id=1, source_target_pairs={{0,16},{8,24},{16,0},{24,8},{1,17},{9,25},{17,1},{25,9},{2,18},{10... | collective-permute-start | bytes 884744 | tf_op jit(solution)/shard_map/ppermute | solution.py:38
  116.0 10.8 %collective-permute-start.22 = (bf16[144,1024]{1,0:T(8,128)(2,1)}, bf16[144,1024]{1,0:T(8,128)(2,1)S(1)}, u32[]{:S(2)}, u32[]{:S(2)}) collective-permute-start(bf16[144,1024]{1,0:T(8,128)(2,1)} %pack_kernel.3.refs_0_), channel_id=1, source_target_pairs={{0,24},{8,0},{16,8},{24,16},{1,25},{9,1},{17,9},{25,17},{2,26},{10... | collective-permute-start | bytes 884744 | tf_op jit(solution)/shard_map/ppermute | solution.py:38
  118.4 24.7 %collective-permute-start.21 = (bf16[144,1024]{1,0:T(8,128)(2,1)}, bf16[144,1024]{1,0:T(8,128)(2,1)S(1)}, u32[]{:S(2)}, u32[]{:S(2)}) collective-permute-start(bf16[144,1024]{1,0:T(8,128)(2,1)} %pack_kernel.3.refs_0_), channel_id=1, source_target_pairs={{0,16},{8,24},{16,0},{24,8},{1,17},{9,25},{17,1},{25,9},{2,18},{10... | collective-permute-start | bytes 884744 | tf_op jit(solution)/shard_map/ppermute | solution.py:38
  118.4 24.7 %collective-permute-start.20 = (bf16[144,1024]{1,0:T(8,128)(2,1)}, bf16[144,1024]{1,0:T(8,128)(2,1)S(1)}, u32[]{:S(2)}, u32[]{:S(2)}) collective-permute-start(bf16[144,1024]{1,0:T(8,128)(2,1)} %pack_kernel.3.refs_0_), channel_id=1, source_target_pairs={{0,8},{8,16},{16,24},{24,0},{1,9},{9,17},{17,25},{25,1},{2,10},{10... | collective-permute-start | bytes 884744 | tf_op jit(solution)/shard_map/ppermute | solution.py:38
  158.0 14.9 %collective-permute-start.23 = (bf16[288,1024]{1,0:T(8,128)(2,1)}, bf16[288,1024]{1,0:T(8,128)(2,1)S(1)}, u32[]{:S(2)}, u32[]{:S(2)}) collective-permute-start(bf16[288,1024]{1,0:T(8,128)(2,1)} %get-tuple-element.117), channel_id=1, source_target_pairs={{0,24},{8,0},{16,8},{24,16},{1,25},{9,1},{17,9},{25,17},{2,26},{10... | collective-permute-start | bytes 1769480 | tf_op jit(solution)/shard_map/ppermute | solution.py:38
  158.0 54.1 %collective-permute-start.24 = (bf16[288,1024]{1,0:T(8,128)(2,1)}, bf16[288,1024]{1,0:T(8,128)(2,1)S(1)}, u32[]{:S(2)}, u32[]{:S(2)}) collective-permute-start(bf16[288,1024]{1,0:T(8,128)(2,1)} %get-tuple-element.118), channel_id=1, source_target_pairs={{0,16},{8,24},{16,0},{24,8},{1,17},{9,25},{17,1},{25,9},{2,18},{10... | collective-permute-start | bytes 1769480 | tf_op jit(solution)/shard_map/ppermute | solution.py:38
  161.4 50.7 %collective-permute-start.25 = (bf16[288,1024]{1,0:T(8,128)(2,1)}, bf16[288,1024]{1,0:T(8,128)(2,1)S(1)}, u32[]{:S(2)}, u32[]{:S(2)}) collective-permute-start(bf16[288,1024]{1,0:T(8,128)(2,1)} %get-tuple-element.119), channel_id=1, source_target_pairs={{0,8},{8,16},{16,24},{24,0},{1,9},{9,17},{17,25},{25,1},{2,10},{10... | collective-permute-start | bytes 1769480 | tf_op jit(solution)/shard_map/ppermute | solution.py:38
  241.7 13.2 %all-to-all-start.6 = ((bf16[4,128,256]{2,1,0:T(8,128)(2,1)}), bf16[4,128,256]{2,1,0:T(8,128)(2,1)S(1)}, u32[]{:S(2)}, u32[]{:S(2)}) async-start(bf16[4,128,256]{2,1,0:T(8,128)(2,1)} %get-tuple-element.128), calls=%async_computation.6 | async-start | bytes 524288 | tf_op jit(solution)/shard_map/all_to_all | solution.py:47
  265.8 37.0 %all-to-all-start.7 = ((bf16[4,128,1024]{2,1,0:T(8,128)(2,1)}), bf16[4,128,1024]{2,1,0:T(8,128)(2,1)S(1)}, u32[]{:S(2)}, u32[]{:S(2)}) async-start(bf16[4,128,1024]{2,1,0:T(8,128)(2,1)} %get-tuple-element.139.d_normed), calls=%async_computation.7 | async-start | bytes 2097152 | tf_op jit(solution)/shard_map/all_to_all | solution.py:47
  270.1 12.3 %collective-permute-start.28 = (bf16[4,32,1024]{2,1,0:T(8,128)(2,1)S(1)}, bf16[4,32,1024]{2,1,0:T(8,128)(2,1)S(1)}, u32[]{:S(2)}, u32[]{:S(2)}) collective-permute-start(bf16[4,32,1024]{2,1,0:T(8,128)(2,1)S(1)} %copy-done.45), channel_id=1, source_target_pairs={{0,4},{1,5},{2,6},{3,7},{4,0},{5,1},{6,2},{7,3},{8,12},{9,13},{10,... | collective-permute-start | bytes 786440 | tf_op jit(solution)/shard_map/ppermute | solution.py:43
  270.7 11.7 %collective-permute-start.29 = (bf16[4,32,1024]{2,1,0:T(8,128)(2,1)S(1)}, bf16[4,32,1024]{2,1,0:T(8,128)(2,1)S(1)}, u32[]{:S(2)}, u32[]{:S(2)}) collective-permute-start(bf16[4,32,1024]{2,1,0:T(8,128)(2,1)S(1)} %copy-done.44), channel_id=1, source_target_pairs={{0,6},{1,7},{2,4},{3,5},{4,2},{5,3},{6,0},{7,1},{8,14},{9,15},{10,... | collective-permute-start | bytes 786440 | tf_op jit(solution)/shard_map/ppermute | solution.py:43
  290.3 12.5 %collective-permute-start.32 = (bf16[4,32,896]{2,1,0:T(8,128)(2,1)}, bf16[4,32,896]{2,1,0:T(8,128)(2,1)S(1)}, u32[]{:S(2)}, u32[]{:S(2)}) collective-permute-start(bf16[4,32,896]{2,1,0:T(8,128)(2,1)} %get-tuple-element.156), channel_id=1, source_target_pairs={{0,4},{1,5},{2,6},{3,7},{4,0},{5,1},{6,2},{7,3},{8,12},{9,13},{10,... | collective-permute-start | bytes 688136 | tf_op jit(solution)/shard_map/ppermute | solution.py:43
  290.9 11.9 %collective-permute-start.33 = (bf16[4,32,896]{2,1,0:T(8,128)(2,1)}, bf16[4,32,896]{2,1,0:T(8,128)(2,1)S(1)}, u32[]{:S(2)}, u32[]{:S(2)}) collective-permute-start(bf16[4,32,896]{2,1,0:T(8,128)(2,1)} %get-tuple-element.157), channel_id=1, source_target_pairs={{0,6},{1,7},{2,4},{3,5},{4,2},{5,3},{6,0},{7,1},{8,14},{9,15},{10,... | collective-permute-start | bytes 688136 | tf_op jit(solution)/shard_map/ppermute | solution.py:43
  306.3 17.3 %all-to-all-start.8 = ((bf16[4,32,1920]{2,1,0:T(8,128)(2,1)}), bf16[4,32,1920]{2,1,0:T(8,128)(2,1)S(1)}, u32[]{:S(2)}, u32[]{:S(2)}) async-start(bf16[4,32,1920]{2,1,0:T(8,128)(2,1)} %chip_sum_kernel.1), calls=%async_computation.8 | async-start | bytes 983040 | tf_op jit(solution)/shard_map/all_to_all | solution.py:47
  (57 other events, 523.3 us)

commit v3 on v2

--- a/solution.py
+++ b/solution.py
@@ -20,17 +20,23 @@
     return lax.dot_general(a, b, (((ca,), (cb,)), ((), ())), preferred_element_type=F32)
 
 
-def call(kernel, outs, me, *args, scratch=(), **static):
-    smem = pl.BlockSpec(memory_space=pltpu.SMEM)
+def placed(kernel):
+    def body(*refs):
+        kernel((lax.axis_index("dp"), lax.axis_index("expert")), *refs)
+
+    return body
+
+
+def call(kernel, outs, *args, scratch=(), **static):
     vmem = pl.BlockSpec(memory_space=pltpu.VMEM)
     return pl.pallas_call(
-        functools.partial(kernel, **static),
+        placed(functools.partial(kernel, **static)),
         out_shape=[jax.ShapeDtypeStruct(s, d) for s, d in outs],
-        in_specs=[smem] + [vmem] * len(args),
+        in_specs=[vmem] * len(args),
         out_specs=[vmem] * len(outs),
         scratch_shapes=list(scratch),
         name=kernel.__name__,
-    )(me, *args)
+    )(*args)
 
 
 def ahead(x, step):
@@ -49,6 +55,31 @@
 
 def along(blocks, sign=1):
     return [blocks[0]] + [ahead(blocks[j], sign * j) for j in range(1, len(blocks))]
+
+
+def spread(x):
+    n = lax.axis_size("dp")
+    if n != 4:
+        return [x] + [ahead(x, j) for j in range(1, n)]
+    far = lax.ppermute(x, "dp", [(0, 2), (1, 3), (2, 0), (3, 1)])
+    up = lax.ppermute(x, "dp", [(0, 1), (1, 2), (2, 3)])
+    down = lax.ppermute(x, "dp", [(1, 0), (2, 1), (3, 2)])
+    end = lax.ppermute(far, "dp", [(1, 0), (2, 3)])
+    return [x, up, down, far, end]
+
+
+def place(me, blocks, put):
+    d, n = me[0], len(blocks)
+    if n != 5:
+        for j, block in enumerate(blocks):
+            put(block, (d + n - j) % n)
+        return
+    own, up, down, far, end = blocks
+    put(own, d)
+    pl.when(d > 0)(lambda: put(up, d - 1))
+    pl.when(d < 3)(lambda: put(down, d + 1))
+    put(far, d ^ 2)
+    pl.when((d == 0) | (d == 3))(lambda: put(end, d ^ 3))
 
 
 def gather_experts(x):
@@ -85,30 +116,30 @@
     return weight / jnp.sum(weight, axis=-1, keepdims=True)
 
 
-def weights_kernel(me, qkv, router, gains, biases, columns, turned, small, *, n_dp):
+def weights_kernel(me, qkv, router, gains, biases, out, turned, *, n_dp):
     own, width = qkv.shape[0], qkv.shape[1] // 3
     part = width // n_dp
-    experts = router.shape[1]
+    experts = router.shape[0]
     turned[...] = jnp.zeros_like(turned)
+    turned[:experts, :own] = router[...].astype(F32)
     turned[experts : experts + 2, :own] = gains[...].astype(F32)
     turned[experts + 2 : experts + 7, :own] = biases[...].astype(F32)
-    small[...] = turned[...].T[:own]
-    small[:, :experts] = router[...].astype(F32)
-    few = small[...].astype(BF)
+    small = turned[...].T[:own].astype(BF)
     for d in range(n_dp):
         for i in range(3):
-            columns[d, :, i * part : (i + 1) * part] = qkv[
+            out[d, :, i * part : (i + 1) * part] = qkv[
                 :, i * width + d * part : i * width + (d + 1) * part
             ]
-        columns[d, :, 3 * part :] = few
+        out[d, :, 3 * part :] = small
 
 
 def slots_kernel(
-    me, parents, route, order, cotangent, seg, grads, tableT, rank_out, bias, *, pad, capacity, experts
+    me, parents, route, order, cotangent, seg, grads, tableT, route_out, rank_out, bias, *, pad, capacity, experts
 ):
-    tok = route.shape[0]
-    r = jnp.broadcast_to(route[...].astype(F32), (tok, tok))
-    rt = r.T
+    tok = route.shape[1]
+    rt = jnp.broadcast_to(route[...].astype(F32), (tok, tok))
+    r = rt.T
+    route_out[...] = r[:, 0:1].astype(I32)
     o = jnp.broadcast_to(order[...].astype(F32), (tok, tok))
     ot = o.T
     same = r == rt
@@ -160,7 +191,7 @@
 
 
 def attend_kernel(me, qkv, bias, *refs, n_dp, head_dim, experts):
-    tokens, (normed, unit, packed, probs, attended, vectors) = refs[:n_dp], refs[n_dp:]
+    tokens, (normed, unit, packed, probs, attended, vectors) = refs[:-6], refs[-6:]
     rows, width = tokens[0].shape
     part = width // n_dp
     small = qkv[:, 3 * part :].astype(F32).T
@@ -171,11 +202,14 @@
         for i in range(2):
             here = vectors[3 + i : 4 + i, d * part : (d + 1) * part]
             parts[i] = parts[i] + jnp.where(me[0] == d, here, 0.0)
-    for j in range(n_dp):
-        base = pl.multiple_of(((me[0] + n_dp - j) % n_dp) * rows, rows)
-        centred, _ = normalise(tokens[j][...].astype(F32))
+
+    def put(block, d):
+        base = pl.multiple_of(d * rows, rows)
+        centred, _ = normalise(block[...].astype(F32))
         unit[pl.ds(base, rows)] = centred
         normed[pl.ds(base, rows)] = (centred * gain + shift).astype(BF)
+
+    place(me, tokens, put)
     raw = mm(normed[...], qkv[:, : 3 * part])
     packed[:, :part] = (raw[:, :part] + parts[0]).astype(BF)
     packed[:, part : 2 * part] = raw[:, part : 2 * part].astype(BF)
@@ -211,33 +245,23 @@
     sent[...] = mm(tableT[...], low).astype(BF)
 
 
-def expert_kernel(me, qkv, up, down, up_bias, down_bias, *refs, n_dp, experts, part):
-    ins, both = refs[: 2 * n_dp], refs[2 * n_dp : 3 * n_dp]
-    act_out, d_pre_out, slots, d_rows, g_up_bias, g_down_bias, acc_r, acc_s = refs[3 * n_dp :]
+def expert_kernel(
+    me, qkv, up, down, up_bias, down_bias, slots, grads,
+    both, act_out, d_pre_out, d_rows, g_up_bias, acc_r, acc_s, *, n_dp, experts,
+):
     f = pl.program_id(0)
-    last = pl.num_programs(0) - 1
-    each, width = ins[0].shape
+    each, width = slots.shape
+    part = width // n_dp
 
     @pl.when(f == 0)
     def _():
-        sums = jnp.zeros((1, width), F32)
-        for j in range(n_dp):
-            rows = ins[j][...]
-            slots[j * each : (j + 1) * each] = rows
-            p = softmax_of(mm(rows, qkv[:, 3 * part :]), experts)
-            gate = jnp.sum(jnp.where(lanes(p.shape, 1) == me[1], p, 0.0), axis=-1, keepdims=True)
-            d = (gate * ins[n_dp + j][...].astype(F32)).astype(BF)
-            d_rows[j * each : (j + 1) * each] = d
-            sums = sums + jnp.sum(d.astype(F32), axis=0, keepdims=True)
-        own = jnp.zeros((1, part), F32)
-        for d in range(n_dp):
-            own = own + jnp.where(me[0] == d, sums[:, d * part : (d + 1) * part], 0.0)
-        g_down_bias[...] = own
-        acc_r[...] = jnp.zeros_like(acc_r)
+        p = softmax_of(mm(slots[...], qkv[:, 3 * part :]), experts)
+        gate = jnp.sum(jnp.where(lanes(p.shape, 1) == me[1], p, 0.0), axis=-1, keepdims=True)
+        d_rows[...] = (gate * grads[...].astype(F32)).astype(BF)
         acc_s[...] = jnp.zeros_like(acc_s)
         for d in range(n_dp):
             acc_r[:, d * part : (d + 1) * part] = jnp.broadcast_to(
-                jnp.where(me[0] == d, down_bias[...].astype(F32), 0.0), (n_dp * each, part)
+                jnp.where(me[0] == d, down_bias[...].astype(F32), 0.0), (each, part)
             )
 
     u = mm(slots[...], up[...]) + up_bias[...].astype(F32)
@@ -253,53 +277,87 @@
     acc_r[...] += mm(act, down[...])
     acc_s[...] += mm(low, up[...], 1, 1)
 
-    @pl.when(f == last)
+    @pl.when(f == pl.num_programs(0) - 1)
     def _():
-        for j in range(n_dp):
-            both[j][:each] = acc_r[j * each : (j + 1) * each].astype(BF)
-            both[j][each:] = acc_s[j * each : (j + 1) * each].astype(BF)
-
-
-def experts_call(me, qkv, up, down, up_bias, down_bias, slots, grads, experts, part):
+        both[:each] = acc_r[...].astype(BF)
+        both[each:] = acc_s[...].astype(BF)
+
+
+def expert_call(qkv, up, down, up_bias, down_bias, slots, grads, n_dp, experts):
+    each, width = slots.shape
+    ff = up.shape[1]
+    chunk = min(ff, 256)
+    whole = pl.BlockSpec(memory_space=pltpu.VMEM)
+    across = pl.BlockSpec((each, chunk), lambda f: (0, f))
+    row = pl.BlockSpec((1, chunk), lambda f: (0, f))
+    return pl.pallas_call(
+        placed(functools.partial(expert_kernel, n_dp=n_dp, experts=experts)),
+        grid=(ff // chunk,),
+        out_shape=[
+            jax.ShapeDtypeStruct((2 * each, width), BF),
+            jax.ShapeDtypeStruct((each, ff), BF),
+            jax.ShapeDtypeStruct((each, ff), BF),
+            jax.ShapeDtypeStruct((each, width), BF),
+            jax.ShapeDtypeStruct((1, ff), F32),
+        ],
+        in_specs=[
+            whole,
+            pl.BlockSpec((width, chunk), lambda f: (0, f)),
+            pl.BlockSpec((chunk, width), lambda f: (f, 0)),
+            row,
+            whole,
+            whole,
+            whole,
+        ],
+        out_specs=[whole, across, across, whole, row],
+        scratch_shapes=[pltpu.VMEM((each, width), F32), pltpu.VMEM((each, width), F32)],
+        name="expert_kernel",
+    )(qkv, up, down, up_bias, down_bias, slots, grads)
+
+
+def expert_grad_kernel(me, *refs, n_dp):
+    slots, act, d_pre, d_rows, up_bias = (refs[i * n_dp : (i + 1) * n_dp] for i in range(5))
+    grad_up, grad_down, g_up_bias, g_down_bias = refs[5 * n_dp :]
+    grad_up[...] = sum(mm(a[...], b[...], 0, 0) for a, b in zip(slots, d_pre))
+    grad_down[...] = sum(mm(a[...], b[...], 0, 0) for a, b in zip(act, d_rows))
+
+    @pl.when(pl.program_id(0) == 0)
+    def _():
+        g_up_bias[...] = sum_of(up_bias)
+        sums = sum(jnp.sum(r[...].astype(F32), axis=0, keepdims=True) for r in d_rows)
+        part = g_down_bias.shape[1]
+        own = jnp.zeros((1, part), F32)
+        for d in range(n_dp):
+            own = own + jnp.where(me[0] == d, sums[:, d * part : (d + 1) * part], 0.0)
+        g_down_bias[...] = own
+
+
+def expert_grads(slots, act, d_pre, d_rows, up_bias, part):
     n_dp = len(slots)
     each, width = slots[0].shape
-    ff = up.shape[1]
-    chunk = min(ff, 256)
-    total = n_dp * each
+    ff = act[0].shape[1]
+    steps = 4
     whole = pl.BlockSpec(memory_space=pltpu.VMEM)
     return pl.pallas_call(
-        functools.partial(expert_kernel, n_dp=n_dp, experts=experts, part=part),
-        grid=(ff // chunk,),
-        out_shape=[jax.ShapeDtypeStruct((2 * each, width), BF)] * n_dp
-        + [
-            jax.ShapeDtypeStruct((total, ff), BF),
-            jax.ShapeDtypeStruct((total, ff), BF),
-            jax.ShapeDtypeStruct((total, width), BF),
-            jax.ShapeDtypeStruct((total, width), BF),
+        placed(functools.partial(expert_grad_kernel, n_dp=n_dp)),
+        grid=(steps,),
+        out_shape=[
+            jax.ShapeDtypeStruct((width, ff), F32),
+            jax.ShapeDtypeStruct((ff, width), F32),
             jax.ShapeDtypeStruct((1, ff), F32),
             jax.ShapeDtypeStruct((1, part), F32),
         ],
-        in_specs=[
-            pl.BlockSpec(memory_space=pltpu.SMEM),
-            whole,
-            pl.BlockSpec((width, chunk), lambda f: (0, f)),
-            pl.BlockSpec((chunk, width), lambda f: (f, 0)),
-            pl.BlockSpec((1, chunk), lambda f: (0, f)),
-            whole,
-        ]
-        + [whole] * (2 * n_dp),
-        out_specs=[whole] * n_dp
-        + [
-            pl.BlockSpec((total, chunk), lambda f: (0, f)),
-            pl.BlockSpec((total, chunk), lambda f: (0, f)),
+        in_specs=[pl.BlockSpec((each, width // steps), lambda f: (0, f))] * n_dp
+        + [pl.BlockSpec((each, ff // steps), lambda f: (0, f))] * n_dp
+        + [whole] * (3 * n_dp),
+        out_specs=[
+            pl.BlockSpec((width // steps, ff), lambda f: (f, 0)),
+            pl.BlockSpec((ff // steps, width), lambda f: (f, 0)),
             whole,
             whole,
-            pl.BlockSpec((1, chunk), lambda f: (0, f)),
-            whole,
         ],
-        scratch_shapes=[pltpu.VMEM((total, width), F32), pltpu.VMEM((total, width), F32)],
-        name="expert_kernel",
-    )(me, qkv, up, down, up_bias, down_bias, *slots, *grads)
+        name="expert_grad_kernel",
+    )(*slots, *act, *d_pre, *d_rows, *up_bias)
 
 
 def sum_of(refs):
@@ -386,10 +444,10 @@
     out[:, :, wide:] = sum_of(refs[half:-1]).astype(BF)
 
 
-def core_sum(me, near, keep):
+def core_sum(near, keep):
     half = near.shape[0]
     shape = near.shape[1:]
-    return call(core_sum_kernel, [(shape, F32)] + [(shape, BF)] * (half - 1), me, keep, flip(near, 1))
+    return call(core_sum_kernel, [(shape, F32)] + [(shape, BF)] * (half - 1), keep, flip(near, 1))
 
 
 def to_chips(parts):
@@ -452,7 +510,7 @@
     n_dp, own, _ = came.shape
     width = proj.shape[1]
     part = width // n_dp
-    experts = router.shape[1]
+    experts = router.shape[0]
     edge = 3 * part
     total = jnp.zeros((own, 128), F32)
     rows = jnp.zeros((own, width), F32)
@@ -464,10 +522,10 @@
         total = total + came[d, :, edge : edge + 128].astype(F32)
         rows = rows + came[d, :, edge + 128 :].astype(F32)
     proj[...] = rows
-    router[...] = total[:, :experts]
     wide[...] = jnp.zeros_like(wide)
     wide[:own] = total
     flat = wide[...].T
+    router[...] = flat[:experts, :own]
     gains[...] = flat[experts : experts + 2, :own]
     biases[...] = flat[experts + 2 : experts + 7, :own]
 
@@ -498,7 +556,6 @@
     cotangent,
 ):
     n_dp, n_ex = lax.axis_size("dp"), lax.axis_size("expert")
-    me = jnp.stack([lax.axis_index("dp"), lax.axis_index("expert")]).astype(I32)
     rows, width = tokens.shape[1], tokens.shape[2]
     part = width // n_dp
     head_dim = width // H
@@ -511,42 +568,41 @@
     cols = 3 * part + 128
     x = tokens[0]
 
-    token_blocks = along([x] * n_dp)
+    token_blocks = spread(x)
     columns = call(
         weights_kernel,
         [((n_dp, own, cols), BF)],
-        me, qkv_weight, router_weight, norm_gains, biases,
-        scratch=[pltpu.VMEM((128, 128), F32), pltpu.VMEM((own, 128), F32)],
+        qkv_weight, router_weight.T, norm_gains, biases,
+        scratch=[pltpu.VMEM((128, 128), F32)],
         n_dp=n_dp,
     )[0]
-    middle = n_dp // 2
-    stacked, token_blocks[middle] = lax.optimization_barrier((swap(columns, "dp"), token_blocks[middle]))
-    qkv_blocks = gather_experts(stacked)
+    qkv_blocks = gather_experts(swap(columns, "dp"))
     smem = pl.BlockSpec(memory_space=pltpu.SMEM)
     vmem = pl.BlockSpec(memory_space=pltpu.VMEM)
-    grads_out, tableT, rank, bias = pl.pallas_call(
-        functools.partial(slots_kernel, pad=pad, capacity=capacity, experts=experts),
+    grads_out, tableT, route, rank, bias = pl.pallas_call(
+        placed(functools.partial(slots_kernel, pad=pad, capacity=capacity, experts=experts)),
         out_shape=[
             jax.ShapeDtypeStruct((n_ex * pad, width), BF),
             jax.ShapeDtypeStruct((n_ex * pad, rows), BF),
             jax.ShapeDtypeStruct((rows, 1), I32),
+            jax.ShapeDtypeStruct((rows, 1), I32),
             jax.ShapeDtypeStruct((length, length), F32),
         ],
-        in_specs=[smem, smem] + [vmem] * 4,
-        out_specs=[vmem] * 4,
+        in_specs=[smem] + [vmem] * 4,
+        out_specs=[vmem] * 5,
         name="slots_kernel",
-    )(me, parents, routes[0], slot_order[0], cotangent[0], segments)
+    )(parents, routes.reshape(1, rows), slot_order[0], cotangent[0], segments)
 
     def dispatch(rows_out):
         came = swap(rows_out.reshape(n_ex, pad, width), "expert").reshape(n_ex * pad, width)
-        mine = call(pack_kernel, [((each, width), BF)], me, came, pad=pad, capacity=capacity)[0]
+        mine = call(pack_kernel, [((each, width), BF)], came, pad=pad, capacity=capacity)[0]
         return mine
 
     grads_in = dispatch(grads_out)
     proj_blocks = gather_experts(swap(jnp.broadcast_to(proj_weight, (n_dp, own, width)), "dp"))
     grads_in, bias = lax.optimization_barrier((grads_in, bias))
     grads = along([grads_in] * n_dp)
-    qkv = call(assemble_kernel, [((n_dp, n_ex, own, cols), BF)], me, *qkv_blocks)[0].reshape(width, cols)
+    qkv = call(assemble_kernel, [((n_dp, n_ex, own, cols), BF)], *qkv_blocks)[0].reshape(width, cols)
     normed1, unit1, packed, probs, att_out, vectors = call(
         attend_kernel,
         [
@@ -557,7 +613,7 @@
             ((n_dp, rows, part), BF),
             ((8, width), F32),
         ],
-        me, qkv, bias, *token_blocks,
+        qkv, bias, *token_blocks,
         n_dp=n_dp, head_dim=head_dim, experts=experts,
     )
     early = [j for j in range(1, n_dp) if j != n_dp // 2]
@@ -565,23 +621,32 @@
     for j, block in zip(early, came):
         grads[j] = block
     attended = swap(att_out, "dp")
-    proj = call(assemble_kernel, [((n_dp, n_ex, own, width), BF)], me, *proj_blocks)[0].reshape(width, width)
+    proj = call(assemble_kernel, [((n_dp, n_ex, own, width), BF)], *proj_blocks)[0].reshape(width, width)
     mixed, normed2, p, sent = call(
         mix_kernel,
         [((rows, width), F32), ((rows, width), BF), ((rows, 128), F32), ((n_ex * pad, width), BF)],
-        me, x, attended, proj, qkv, vectors, tableT,
+        x, attended, proj, qkv, vectors, tableT,
         experts=experts,
     )
     mine, grads = lax.optimization_barrier((dispatch(sent), grads))
     slots = along([mine] * n_dp)
-    *both, act, d_pre, slot_rows, d_rows, grad_up_bias, grad_down_bias = experts_call(
-        me, qkv, up_weight[0], down_weight[0], up_bias, down_bias, slots, grads, experts, part
-    )
-    came = along(both, -1)
-    grad_up = mm(slot_rows, d_pre, 0, 0)
-    grad_down = mm(act, d_rows, 0, 0)
+    order = [0] + early + [n_dp // 2]
+    done = {}
+    came = [None] * n_dp
+    for i, j in enumerate(order):
+        if i > 0:
+            last = order[i - 1]
+            slots[j], *done[last] = lax.optimization_barrier((slots[j], *done[last]))
+        done[j] = expert_call(
+            qkv, up_weight[0], down_weight[0], up_bias, down_bias, slots[j], grads[j], n_dp, experts
+        )
+        came[j] = ahead(done[j][0], -j) if j else done[j][0]
+    act, d_pre, d_rows, g_up_bias = ([done[j][i] for j in range(n_dp)] for i in range(1, 5))
+    grad_up, grad_down, grad_up_bias, grad_down_bias = expert_grads(
+        slots, act, d_pre, d_rows, g_up_bias, part
+    )
     grad_up, grad_down, *came = lax.optimization_barrier((grad_up, grad_down, *came))
-    summed = call(line_sum_kernel, [((n_ex * 2 * pad, width), BF)], me, *came, pad=pad, capacity=capacity)[0]
+    summed = call(line_sum_kernel, [((n_ex * 2 * pad, width), BF)], *came, pad=pad, capacity=capacity)[0]
     back = swap(summed.reshape(n_ex, 2 * pad, width), "expert").reshape(n_ex * 2 * pad, width)
     outputs, d_mixed, d_low, d_att, d_logits, sums = call(
         combine_kernel,
@@ -593,7 +658,7 @@
             ((rows, 128), BF),
             ((8, width), F32),
         ],
-        me, back, routes[0], rank, mixed, p, cotangent[0], qkv, vectors, proj,
+        back, route, rank, mixed, p, cotangent[0], qkv, vectors, proj,
         pad=pad, capacity=capacity, experts=experts, part=part,
     )
     d_heads = swap(d_att, "dp")
@@ -601,51 +666,52 @@
     near, keep = call(
         proj_grad_kernel,
         [((half, n_dp, own, width), BF), ((half, n_dp, own, width), F32)],
-        me, attended, d_low,
+        attended, d_low,
         scratch=[pltpu.VMEM((width, width), F32)],
     )
-    d_heads, *parts = lax.optimization_barrier((d_heads, *core_sum(me, near, keep)))
+    d_heads, *parts = lax.optimization_barrier((d_heads, *core_sum(near, keep)))
     proj_chips = to_chips(parts)
     d_packed, d_normed = call(
         attend_back_kernel,
         [((length, 3 * part), BF), ((n_dp, rows, width), BF)],
-        me, d_heads, probs, packed, qkv,
+        d_heads, probs, packed, qkv,
         scratch=[pltpu.VMEM((length, length), BF)],
         head_dim=head_dim,
     )
-    d_own = swap(d_normed, "dp")
+    d_packed, *proj_chips = lax.optimization_barrier((d_packed, *proj_chips))
     near, keep = call(
         qkv_grad_kernel,
         [((half, n_dp, own, cols), BF), ((half, n_dp, own, cols), F32)],
-        me, normed1, unit1, d_packed, d_normed, normed2, d_logits, sums,
+        normed1, unit1, d_packed, d_normed, normed2, d_logits, sums,
         scratch=[pltpu.VMEM((width, cols), F32), pltpu.VMEM((128, width), F32)],
         experts=experts,
     )
-    near, keep, *proj_chips = lax.optimization_barrier((near, keep, *proj_chips))
-    qkv_chips = to_chips(core_sum(me, near, keep))
+    near, d_normed = lax.optimization_barrier((near, d_normed))
+    d_own = swap(d_normed, "dp")
+    qkv_chips = to_chips(core_sum(near, keep))
     d_own, *qkv_chips = lax.optimization_barrier((d_own, *qkv_chips))
     summed = call(
-        chip_sum_kernel, [((n_dp, own, cols + width), BF)], me, *qkv_chips, *proj_chips
+        chip_sum_kernel, [((n_dp, own, cols + width), BF)], *qkv_chips, *proj_chips
     )[0]
     owned_qkv, owned_proj, owned_router, owned_gains, owned_biases = call(
         weights_end_kernel,
         [
             ((own, 3 * width), F32),
             ((own, width), F32),
-            ((own, experts), F32),
+            ((experts, own), F32),
             ((2, own), F32),
             ((5, own), F32),
         ],
-        me, swap(summed, "dp"),
+        swap(summed, "dp"),
         scratch=[pltpu.VMEM((128, 128), F32)],
     )
-    grad_tokens = call(tokens_end_kernel, [((rows, width), F32)], me, d_own, x, vectors, d_mixed)[0]
+    grad_tokens = call(tokens_end_kernel, [((rows, width), F32)], d_own, x, vectors, d_mixed)[0]
     return (
         outputs[None],
         grad_tokens[None],
         owned_qkv,
         owned_proj,
-        owned_router,
+        owned_router.T,
         owned_gains,
         owned_biases,
         grad_up[None],

time: 329 us -> 304 us (0.924)
  waiting for transfers between devices: 127 us -> 86.3 us
  Pallas kernels: 84.2 us -> 110 us
  matrix products: 9.48 us -> 0 us
  local copies, waits for them, and re-layouts: 14.1 us -> 9.91 us
  starting transfers between devices: 74.3 us -> 78 us
    ppermute x12 -> x9, waiting for transfers between devices: 81.4 us -> 31.6 us  [ahead(): return lax.ppermute(x, 'dp', [(i, (i + step) % n) for i in range(n)])]
    pallas_call x19 -> x23, Pallas kernels: 84.2 us -> 110 us  [the longest x17 67.8 us: call(): pl.pallas_call(placed(functools.partial(kernel, **static)), out_shape=[ja...]
    dot_general x2 -> x0, matrix products: 9.48 us -> none  [mm(): lax.dot_general(a, b, (((ca,), (cb,)), ((), ())), preferred_element_type=...]
    ppermute x0 -> x4, starting transfers between devices: none -> 7.14 us  [the longest x1 4.57 us: spread(): up = lax.ppermute(x, 'dp', [(0, 1), (1, 2), (2, 3)])]
    all_to_all x8, waiting for transfers between devices: 27.3 us -> 34.3 us  [swap(): return lax.all_to_all(x, axis, split_axis=0, concat_axis=0, tiled=True)]
    ppermute x0 -> x4, waiting for transfers between devices: none -> 6.71 us  [the longest x1 5.9 us: spread(): far = lax.ppermute(x, 'dp', [(0, 2), (1, 3), (2, 0), (3, 1)])]
    ppermute x22, waiting for transfers between devices: 18.4 us -> 13.7 us  [flip(): return lax.ppermute(x, 'expert', [(i, i ^ bits) for i in range(n)])]
    ppermute x12 -> x9, starting transfers between devices: 23.6 us -> 19.1 us  [ahead(): return lax.ppermute(x, 'dp', [(i, (i + step) % n) for i in range(n)])]
  transfers between devices with their start and end apart: 42 -> 43, of which waited for: 20 -> 19; matrix products, arithmetic and copies ran while one was open for 4% -> 1% of each run, Pallas kernels for 12% -> 27%
where the time goes in v3:
time: 304 us; the launch traced here: 302 us
  Pallas kernels  110 us (36%)
  waiting for transfers between devices  86.3 us (28%)
  starting transfers between devices  78 us (26%)
  blocking collectives  16.8 us (6%)
  local copies, waits for them, and re-layouts  9.91 us (3%)
    pallas_call x17, Pallas kernels, call(): pl.pallas_call(placed(functools.partial(kernel, **static)), out_shape=[ja...  67.8 us
    all_to_all x8, waiting for transfers between devices, swap(): return lax.all_to_all(x, axis, split_axis=0, concat_axis=0, tiled=True)  34.3 us
    all_to_all x8, starting transfers between devices, swap(): return lax.all_to_all(x, axis, split_axis=0, concat_axis=0, tiled=True)  33.8 us
    ppermute x9, waiting for transfers between devices, ahead(): return lax.ppermute(x, 'dp', [(i, (i + step) % n) for i in range(n)])  31.6 us
    pallas_call x4, Pallas kernels, expert_call(): pl.pallas_call(placed(functools.partial(expert_kernel, n_dp=n_dp, experts...  29.8 us
    ppermute x9, starting transfers between devices, ahead(): return lax.ppermute(x, 'dp', [(i, (i + step) % n) for i in range(n)])  19.1 us
    ppermute x22, starting transfers between devices, flip(): return lax.ppermute(x, 'expert', [(i, i ^ bits) for i in range(n)])  18 us
    all_to_all x1, blocking collectives, swap(): return lax.all_to_all(x, axis, split_axis=0, concat_axis=0, tiled=True)  16.8 us
  transfers between devices with their start and end apart: 43, of which 19 were waited for; matrix products, arithmetic and copies ran while one was open for 1% of the time, Pallas kernels for 27%

profile of v3, /device:TPU:0, one launch (start us, length us, event | category | flops | bytes accessed | tf_op | source)
XLA Modules:
  0.0 301.9 jit_solution(12417577086374077277)
XLA Ops:
  2.4 6.3 %all-to-all-start = ((bf16[4,32,896]{2,1,0:T(8,128)(2,1)}), bf16[4,32,896]{2,1,0:T(8,128)(2,1)S(1)}, u32[]{:S(2)}, u32[]{:S(2)}) async-start(bf16[4,32,896]{2,1,0:T(8,128)(2,1)} %weights_kernel.1), calls=%async_computation | async-start | bytes 458752 | tf_op jit(solution)/shard_map/all_to_all | solution.py:53
  11.5 5.3 %all-to-all-done.refs_0_ = bf16[4,32,896]{2,1,0:T(8,128)(2,1)S(1)} async-done(((bf16[4,32,896]{2,1,0:T(8,128)(2,1)}), bf16[4,32,896]{2,1,0:T(8,128)(2,1)S(1)}, u32[]{:S(2)}, u32[]{:S(2)}) %all-to-all-start) | async-done | bytes 229408 | tf_op jit(solution)/shard_map/all_to_all | solution.py:53
  16.9 3.7 %all-to-all-start.1 = ((bf16[8,24,1024]{2,1,0:T(8,128)(2,1)}), bf16[8,24,1024]{2,1,0:T(8,128)(2,1)S(1)}, u32[]{:S(2)}, u32[]{:S(2)}) async-start(bf16[8,24,1024]{2,1,0:T(8,128)(2,1)} %bitcast.51), calls=%async_computation.1 | async-start | bytes 786432 | tf_op jit(solution)/shard_map/all_to_all | solution.py:53
  21.9 4.6 %collective-permute-start.7 = (bf16[128,1024]{1,0:T(8,128)(2,1)}, bf16[128,1024]{1,0:T(8,128)(2,1)S(1)}, u32[]{:S(2)}, u32[]{:S(2)}) collective-permute-start(bf16[128,1024]{1,0:T(8,128)(2,1)} %bitcast.42), channel_id=1, source_target_pairs={{0,8},{8,16},{16,24},{1,9},{9,17},{17,25},{2,10},{10,18},{18,26},{... | collective-permute-start | bytes 786440 | tf_op jit(solution)/shard_map/ppermute | solution.py:65
  30.0 5.9 %collective-permute-done.9.refs_5_ = bf16[128,1024]{1,0:T(8,128)(2,1)S(1)} collective-permute-done((bf16[128,1024]{1,0:T(8,128)(2,1)}, bf16[128,1024]{1,0:T(8,128)(2,1)S(1)}, u32[]{:S(2)}, u32[]{:S(2)}) %collective-permute-start.9) | collective-permute-done | bytes 262176 | tf_op jit(solution)/shard_map/ppermute | solution.py:64
  40.6 5.7 %all-to-all-start.3 = ((bf16[4,32,1024]{2,1,0:T(8,128)(2,1)}), bf16[4,32,1024]{2,1,0:T(8,128)(2,1)S(1)}, u32[]{:S(2)}, u32[]{:S(2)}) async-start(bf16[4,32,1024]{2,1,0:T(8,128)(2,1)} %broadcast_in_dim.15), calls=%async_computation.3 | async-start | bytes 524288 | tf_op jit(solution)/shard_map/all_to_all | solution.py:53
  62.9 11.0 %attend_kernel.1 = (bf16[512,1024]{1,0:T(8,128)(2,1)}, f32[512,1024]{1,0:T(8,128)}, bf16[512,768]{1,0:T(8,128)(2,1)}, bf16[4,512,512]{2,1,0:T(8,128)(2,1)}, bf16...) custom-call(bf16[1024,896]{1,0:T(8,128)(2,1)} %bitcast.20, f32[512,512]{1,0:T(8,128)} %get-tuple-element.125.refs_1_, ...), custom_call_target="tpu_custom_call" | custom-call | tf_op jit(solution)/shard_map/attend_kernel/pallas_call | solution.py:32
  74.0 3.4 %all-to-all-start.2 = ((bf16[4,128,256]{2,1,0:T(8,128)(2,1)}), bf16[4,128,256]{2,1,0:T(8,128)(2,1)S(1)}, u32[]{:S(2)}, u32[]{:S(2)}) async-start(bf16[4,128,256]{2,1,0:T(8,128)(2,1)} %get-tuple-element.128), calls=%async_computation.2 | async-start | bytes 524288 | tf_op jit(solution)/shard_map/all_to_all | solution.py:53
  84.8 4.0 %mix_kernel.1 = (f32[128,1024]{1,0:T(8,128)}, bf16[128,1024]{1,0:T(8,128)(2,1)}, f32[128,128]{1,0:T(8,128)}, bf16[192,1024]{1,0:T(8,128)(2,1)}) custom-call(bf16[128,1024]{1,0:T(8,128)(2,1)} %bitcast.44, bf16[4,128,256]{2,1,0:T(8,128)(2,1)} %copy-done.1, bf16[1024,1024]{1,0:T(8,128)(2,1)} %bitcast.36, bf16[1024,896]{1,0:T(8,128)(2,1)} %bitcast.21, ...), custom_call_target="tpu_custom_call" | custom-call | tf_op jit(solution)/shard_map/mix_kernel/pallas_call | solution.py:32
  88.9 3.8 %all-to-all-start.4 = ((bf16[8,24,1024]{2,1,0:T(8,128)(2,1)}), bf16[8,24,1024]{2,1,0:T(8,128)(2,1)S(1)}, u32[]{:S(2)}, u32[]{:S(2)}) async-start(bf16[8,24,1024]{2,1,0:T(8,128)(2,1)} %bitcast.52), calls=%async_computation.4 | async-start | bytes 786432 | tf_op jit(solution)/shard_map/all_to_all | solution.py:53
  95.6 5.5 %all-to-all-done.4 = bf16[8,24,1024]{2,1,0:T(8,128)(2,1)S(1)} async-done(((bf16[8,24,1024]{2,1,0:T(8,128)(2,1)}), bf16[8,24,1024]{2,1,0:T(8,128)(2,1)S(1)}, u32[]{:S(2)}, u32[]{:S(2)}) %all-to-all-start.4) | async-done | bytes 393248 | tf_op jit(solution)/shard_map/all_to_all | solution.py:53
  103.7 5.8 %collective-permute-done.20.refs_6_ = bf16[144,1024]{1,0:T(8,128)(2,1)S(1)} collective-permute-done((bf16[144,1024]{1,0:T(8,128)(2,1)S(1)}, bf16[144,1024]{1,0:T(8,128)(2,1)S(1)}, u32[]{:S(2)}, u32[]{:S(2)}) %collective-permute-start.20) | collective-permute-done | bytes 294944 | tf_op jit(solution)/shard_map/ppermute | solution.py:44
  113.6 7.4 %expert_kernel.4 = (bf16[288,1024]{1,0:T(8,128)(2,1)}, bf16[144,1024]{1,0:T(8,128)(2,1)}, bf16[144,1024]{1,0:T(8,128)(2,1)}, bf16[144,1024]{1,0:T(8,128)(2,1)}, f32[1,1024]{1,0:T(1,128)}) custom-call(bf16[1024,896]{1,0:T(8,128)(2,1)} %bitcast.22, bf16[1024,1024]{1,0:T(8,128)(2,1)} %bitcast.28, bf16[1024,1024]{1,0:T(8,128)(2,1)} %bitcast.32, ...), custom_call_target="tpu_custom_call" | custom-call | tf_op jit(solution)/shard_map/expert_kernel/pallas_call | solution.py:293
  122.1 7.4 %expert_kernel.5 = (bf16[288,1024]{1,0:T(8,128)(2,1)}, bf16[144,1024]{1,0:T(8,128)(2,1)}, bf16[144,1024]{1,0:T(8,128)(2,1)}, bf16[144,1024]{1,0:T(8,128)(2,1)}, f32[1,1024]{1,0:T(1,128)}) custom-call(bf16[1024,896]{1,0:T(8,128)(2,1)} %bitcast.23, bf16[1024,1024]{1,0:T(8,128)(2,1)} %bitcast.29, bf16[1024,1024]{1,0:T(8,128)(2,1)} %bitcast.33, ...), custom_call_target="tpu_custom_call" | custom-call | tf_op jit(solution)/shard_map/expert_kernel/pallas_call | solution.py:293
  129.6 8.5 %collective-permute-start.24 = (bf16[288,1024]{1,0:T(8,128)(2,1)}, bf16[288,1024]{1,0:T(8,128)(2,1)S(1)}, u32[]{:S(2)}, u32[]{:S(2)}) collective-permute-start(bf16[288,1024]{1,0:T(8,128)(2,1)} %get-tuple-element.143), channel_id=1, source_target_pairs={{0,24},{8,0},{16,8},{24,16},{1,25},{9,1},{17,9},{25,17},{2,26},{10... | collective-permute-start | bytes 1769480 | tf_op jit(solution)/shard_map/ppermute | solution.py:44
  138.8 7.4 %expert_kernel.6 = (bf16[288,1024]{1,0:T(8,128)(2,1)}, bf16[144,1024]{1,0:T(8,128)(2,1)}, bf16[144,1024]{1,0:T(8,128)(2,1)}, bf16[144,1024]{1,0:T(8,128)(2,1)}, f32[1,1024]{1,0:T(1,128)}) custom-call(bf16[1024,896]{1,0:T(8,128)(2,1)} %bitcast.24, bf16[1024,1024]{1,0:T(8,128)(2,1)} %bitcast.30, bf16[1024,1024]{1,0:T(8,128)(2,1)} %bitcast.34, ...), custom_call_target="tpu_custom_call" | custom-call | tf_op jit(solution)/shard_map/expert_kernel/pallas_call | solution.py:293
  147.0 7.5 %expert_kernel.7 = (bf16[288,1024]{1,0:T(8,128)(2,1)}, bf16[144,1024]{1,0:T(8,128)(2,1)}, bf16[144,1024]{1,0:T(8,128)(2,1)}, bf16[144,1024]{1,0:T(8,128)(2,1)}, f32[1,1024]{1,0:T(1,128)}) custom-call(bf16[1024,896]{1,0:T(8,128)(2,1)} %bitcast.25, bf16[1024,1024]{1,0:T(8,128)(2,1)} %bitcast.31, bf16[1024,1024]{1,0:T(8,128)(2,1)} %bitcast.35, ...), custom_call_target="tpu_custom_call" | custom-call | tf_op jit(solution)/shard_map/expert_kernel/pallas_call | solution.py:293
  155.2 9.4 %expert_grad_kernel.1 = (f32[1024,1024]{1,0:T(8,128)}, f32[1024,1024]{1,0:T(8,128)}, f32[1,1024]{1,0:T(1,128)}, f32[1,256]{1,0:T(1,128)}) custom-call(bf16[144,1024]{1,0:T(8,128)(2,1)} %pack_kernel.3.refs_5_.refs_0_, bf16[144,1024]{1,0:T(8,128)(2,1)} %copy-done.5, bf16[144,1024]{1,0:T(8,128)(2,1)} %copy-done.7, bf16[144,1024]{1,0:T(8,128)(2,1)} %copy-done.6, ...), custom_call_target="tpu_custom_call" | custom-call | tf_op jit(solution)/shard_map/expert_grad_kernel/pallas_call | solution.py:341
  164.9 25.2 %collective-permute-done.25.refs_2_ = bf16[288,1024]{1,0:T(8,128)(2,1)S(1)} collective-permute-done((bf16[288,1024]{1,0:T(8,128)(2,1)}, bf16[288,1024]{1,0:T(8,128)(2,1)S(1)}, u32[]{:S(2)}, u32[]{:S(2)}) %collective-permute-start.25) | collective-permute-done | bytes 589856 | tf_op jit(solution)/shard_map/ppermute | solution.py:44
  194.1 16.8 %all_to_all.45 = bf16[8,48,1024]{2,1,0:T(8,128)(2,1)} all-to-all(bf16[8,48,1024]{2,1,0:T(8,128)(2,1)} %bitcast.38), channel_id=1, replica_groups=mesh['dp'=4,'expert'=8] {'expert'}, dimensions={0} | all-to-all | bytes 1572864 | tf_op jit(solution)/shard_map/all_to_all | solution.py:53
  210.8 5.1 %combine_kernel.1 = (bf16[128,1024]{1,0:T(8,128)(2,1)}, f32[128,1024]{1,0:T(8,128)}, bf16[128,1024]{1,0:T(8,128)(2,1)}, bf16[4,128,256]{2,1,0:T(8,128)(2,1)}, bf...) custom-call(bf16[384,1024]{1,0:T(8,128)(2,1)} %bitcast.39, s32[128,1]{1,0:T(8,128)} %get-tuple-element.180.refs_1_, ...), custom_call_target="tpu_custom_call" | custom-call | tf_op jit(solution)/shard_map/combine_kernel/pallas_call | solution.py:32
  215.9 3.5 %proj_grad_kernel.1 = (bf16[4,4,32,1024]{3,2,1,0:T(8,128)(2,1)}, f32[4,4,32,1024]{3,2,1,0:T(8,128)}) custom-call(bf16[4,128,256]{2,1,0:T(8,128)(2,1)} %copy-done.1, bf16[128,1024]{1,0:T(8,128)(2,1)} %get-tuple-element.188.refs_1_), custom_call_target="tpu_custom_call" | custom-call | tf_op jit(solution)/shard_map/proj_grad_kernel/pallas_call | solution.py:32
  219.4 3.7 %all-to-all-start.6 = ((bf16[4,128,256]{2,1,0:T(8,128)(2,1)}), bf16[4,128,256]{2,1,0:T(8,128)(2,1)S(1)}, u32[]{:S(2)}, u32[]{:S(2)}) async-start(bf16[4,128,256]{2,1,0:T(8,128)(2,1)} %get-tuple-element.187), calls=%async_computation.6 | async-start | bytes 524288 | tf_op jit(solution)/shard_map/all_to_all | solution.py:53
  227.0 5.6 %all-to-all-done.6.refs_0_ = bf16[4,128,256]{2,1,0:T(8,128)(2,1)S(1)} async-done(((bf16[4,128,256]{2,1,0:T(8,128)(2,1)}), bf16[4,128,256]{2,1,0:T(8,128)(2,1)S(1)}, u32[]{:S(2)}, u32[]{:S(2)}) %all-to-all-start.6) | async-done | bytes 262176 | tf_op jit(solution)/shard_map/all_to_all | solution.py:53
  236.1 10.2 %attend_back_kernel.1 = (bf16[512,768]{1,0:T(8,128)(2,1)}, bf16[4,128,1024]{2,1,0:T(8,128)(2,1)}) custom-call(bf16[4,128,256]{2,1,0:T(8,128)(2,1)} %copy-done.11, bf16[4,512,512]{2,1,0:T(8,128)(2,1)} %get-tuple-element.196.refs_1_, bf16[512,768]{1,0:T(8,128)(2,1)} %get-tuple-element.197.refs_2_, bf16[1024,896]{1,0:T(8,128)(2,1)} %bitcast.27), custom_call_target="tpu_custom_call" | custom-call | tf_op jit(solution)/shard_map/attend_back_kernel/pallas_call | solution.py:32
  246.4 5.9 %qkv_grad_kernel.1 = (bf16[4,4,32,896]{3,2,1,0:T(8,128)(2,1)}, f32[4,4,32,896]{3,2,1,0:T(8,128)}) custom-call(bf16[512,1024]{1,0:T(8,128)(2,1)} %get-tuple-element.185.refs_0_, f32[512,1024]{1,0:T(8,128)} %get-tuple-element.186.refs_1_, bf16[512,768]{1,0:T(8,128)(2,1)} %get-tuple-element.203.refs_2_, bf16[4,128,1024]{2,1,0:T(8,128)(2,1)} %get-tuple-element.209.refs_3_, ...), custom_call_target="tpu_custom_call" | custom-call | tf_op jit(solution)/shard_map/qkv_grad_kernel/pallas_call | solution.py:32
  252.3 3.7 %all-to-all-start.7 = ((bf16[4,128,1024]{2,1,0:T(8,128)(2,1)}), bf16[4,128,1024]{2,1,0:T(8,128)(2,1)S(1)}, u32[]{:S(2)}, u32[]{:S(2)}) async-start(bf16[4,128,1024]{2,1,0:T(8,128)(2,1)} %get-tuple-element.209.refs_3_), calls=%async_computation.7 | async-start | bytes 2097152 | tf_op jit(solution)/shard_map/all_to_all | solution.py:53
  265.7 5.2 %collective-permute-done.32.refs_1_ = bf16[4,32,896]{2,1,0:T(8,128)(2,1)S(1)} collective-permute-done((bf16[4,32,896]{2,1,0:T(8,128)(2,1)}, bf16[4,32,896]{2,1,0:T(8,128)(2,1)S(1)}, u32[]{:S(2)}, u32[]{:S(2)}) %collective-permute-start.32) | collective-permute-done | bytes 229408 | tf_op jit(solution)/shard_map/ppermute | solution.py:49
  270.8 4.4 %collective-permute-done.33.refs_2_ = bf16[4,32,896]{2,1,0:T(8,128)(2,1)S(1)} collective-permute-done((bf16[4,32,896]{2,1,0:T(8,128)(2,1)}, bf16[4,32,896]{2,1,0:T(8,128)(2,1)S(1)}, u32[]{:S(2)}, u32[]{:S(2)}) %collective-permute-start.33) | collective-permute-done | bytes 229408 | tf_op jit(solution)/shard_map/ppermute | solution.py:49
  275.2 4.2 %all-to-all-done.7.refs_0_ = bf16[4,128,1024]{2,1,0:T(8,128)(2,1)S(1)} async-done(((bf16[4,128,1024]{2,1,0:T(8,128)(2,1)}), bf16[4,128,1024]{2,1,0:T(8,128)(2,1)S(1)}, u32[]{:S(2)}, u32[]{:S(2)}) %all-to-all-start.7) | async-done | bytes 1048608 | tf_op jit(solution)/shard_map/all_to_all | solution.py:53
  282.5 3.5 %all-to-all-start.8 = ((bf16[4,32,1920]{2,1,0:T(8,128)(2,1)}), bf16[4,32,1920]{2,1,0:T(8,128)(2,1)S(1)}, u32[]{:S(2)}, u32[]{:S(2)}) async-start(bf16[4,32,1920]{2,1,0:T(8,128)(2,1)} %chip_sum_kernel.1), calls=%async_computation.8 | async-start | bytes 983040 | tf_op jit(solution)/shard_map/all_to_all | solution.py:53
  288.7 10.5 %all-to-all-done.8.refs_0_ = bf16[4,32,1920]{2,1,0:T(8,128)(2,1)S(1)} async-done(((bf16[4,32,1920]{2,1,0:T(8,128)(2,1)}), bf16[4,32,1920]{2,1,0:T(8,128)(2,1)S(1)}, u32[]{:S(2)}, u32[]{:S(2)}) %all-to-all-start.8) | async-done | bytes 491552 | tf_op jit(solution)/shard_map/all_to_all | solution.py:53
  (163 shorter events, 80.8 us)
Async XLA Ops:
  2.4 14.5 %all-to-all-start = ((bf16[4,32,896]{2,1,0:T(8,128)(2,1)}), bf16[4,32,896]{2,1,0:T(8,128)(2,1)S(1)}, u32[]{:S(2)}, u32[]{:S(2)}) async-start(bf16[4,32,896]{2,1,0:T(8,128)(2,1)} %weights_kernel.1), calls=%async_computation | async-start | bytes 458752 | tf_op jit(solution)/shard_map/all_to_all | solution.py:53
  16.9 22.0 %all-to-all-start.1 = ((bf16[8,24,1024]{2,1,0:T(8,128)(2,1)}), bf16[8,24,1024]{2,1,0:T(8,128)(2,1)S(1)}, u32[]{:S(2)}, u32[]{:S(2)}) async-start(bf16[8,24,1024]{2,1,0:T(8,128)(2,1)} %bitcast.51), calls=%async_computation.1 | async-start | bytes 786432 | tf_op jit(solution)/shard_map/all_to_all | solution.py:53
  20.6 15.3 %collective-permute-start.9 = (bf16[128,1024]{1,0:T(8,128)(2,1)}, bf16[128,1024]{1,0:T(8,128)(2,1)S(1)}, u32[]{:S(2)}, u32[]{:S(2)}) collective-permute-start(bf16[128,1024]{1,0:T(8,128)(2,1)} %bitcast.40), channel_id=1, source_target_pairs={{0,16},{8,24},{16,0},{24,8},{1,17},{9,25},{17,1},{25,9},{2,18},{10... | collective-permute-start | bytes 786440 | tf_op jit(solution)/shard_map/ppermute | solution.py:64
  20.6 17.0 %collective-permute-start.8 = (bf16[128,1024]{1,0:T(8,128)(2,1)}, bf16[128,1024]{1,0:T(8,128)(2,1)S(1)}, u32[]{:S(2)}, u32[]{:S(2)}) collective-permute-start(bf16[128,1024]{1,0:T(8,128)(2,1)} %bitcast.41), channel_id=1, source_target_pairs={{8,0},{16,8},{24,16},{9,1},{17,9},{25,17},{10,2},{18,10},{26,18},{... | collective-permute-start | bytes 786440 | tf_op jit(solution)/shard_map/ppermute | solution.py:66
  21.9 24.4 %collective-permute-start.7 = (bf16[128,1024]{1,0:T(8,128)(2,1)}, bf16[128,1024]{1,0:T(8,128)(2,1)S(1)}, u32[]{:S(2)}, u32[]{:S(2)}) collective-permute-start(bf16[128,1024]{1,0:T(8,128)(2,1)} %bitcast.42), channel_id=1, source_target_pairs={{0,8},{8,16},{16,24},{1,9},{9,17},{17,25},{2,10},{10,18},{18,26},{... | collective-permute-start | bytes 786440 | tf_op jit(solution)/shard_map/ppermute | solution.py:65
  26.5 19.9 %collective-permute-start.5 = (bf16[4,32,896]{2,1,0:T(8,128)(2,1)S(1)}, bf16[4,32,896]{2,1,0:T(8,128)(2,1)S(1)}, u32[]{:S(2)}, u32[]{:S(2)}) collective-permute-start(bf16[4,32,896]{2,1,0:T(8,128)(2,1)S(1)} %all-to-all-done.refs_0_), channel_id=1, source_target_pairs={{0,6},{1,7},{2,4},{3,5},{4,2},{5,3},{6,0},{7,1},{8,14},{9,15},{10,... | collective-permute-start | bytes 688136 | tf_op jit(solution)/shard_map/ppermute | solution.py:49
  29.5 17.4 %collective-permute-start.3 = (bf16[4,32,896]{2,1,0:T(8,128)(2,1)S(1)}, bf16[4,32,896]{2,1,0:T(8,128)(2,1)S(1)}, u32[]{:S(2)}, u32[]{:S(2)}) collective-permute-start(bf16[4,32,896]{2,1,0:T(8,128)(2,1)S(1)} %all-to-all-done.refs_0_), channel_id=1, source_target_pairs={{0,4},{1,5},{2,6},{3,7},{4,0},{5,1},{6,2},{7,3},{8,12},{9,13},{10,... | collective-permute-start | bytes 688136 | tf_op jit(solution)/shard_map/ppermute | solution.py:49
  37.6 12.5 %collective-permute-start.10 = (bf16[128,1024]{1,0:T(8,128)(2,1)S(1)}, bf16[128,1024]{1,0:T(8,128)(2,1)S(1)}, u32[]{:S(2)}, u32[]{:S(2)}) collective-permute-start(bf16[128,1024]{1,0:T(8,128)(2,1)S(1)} %collective-permute-done.9.refs_5_), channel_id=1, source_target_pairs={{8,0},{16,24},{9,1},{17,25},{10,2},{18,26},{11,3},{19,27},{12,4},{... | collective-permute-start | bytes 786440 | tf_op jit(solution)/shard_map/ppermute | solution.py:67
  40.6 15.7 %all-to-all-start.3 = ((bf16[4,32,1024]{2,1,0:T(8,128)(2,1)}), bf16[4,32,1024]{2,1,0:T(8,128)(2,1)S(1)}, u32[]{:S(2)}, u32[]{:S(2)}) async-start(bf16[4,32,1024]{2,1,0:T(8,128)(2,1)} %broadcast_in_dim.15), calls=%async_computation.3 | async-start | bytes 524288 | tf_op jit(solution)/shard_map/all_to_all | solution.py:53
  46.9 12.0 %collective-permute-start.4 = (bf16[4,32,896]{2,1,0:T(8,128)(2,1)S(1)}, bf16[4,32,896]{2,1,0:T(8,128)(2,1)}, u32[]{:S(2)}, u32[]{:S(2)}) collective-permute-start(bf16[4,32,896]{2,1,0:T(8,128)(2,1)S(1)} %collective-permute-done.3.refs_4_), channel_id=1, source_target_pairs={{0,1},{1,0},{2,3},{3,2},{4,5},{5,4},{6,7},{7,6},{8,9},{9,8},{10,11... | collective-permute-start | bytes 688136 | tf_op jit(solution)/shard_map/ppermute | solution.py:49
  47.0 12.5 %collective-permute-start.2 = (bf16[4,32,896]{2,1,0:T(8,128)(2,1)S(1)}, bf16[4,32,896]{2,1,0:T(8,128)(2,1)}, u32[]{:S(2)}, u32[]{:S(2)}) collective-permute-start(bf16[4,32,896]{2,1,0:T(8,128)(2,1)S(1)} %collective-permute-done.1.refs_2_), channel_id=1, source_target_pairs={{0,1},{1,0},{2,3},{3,2},{4,5},{5,4},{6,7},{7,6},{8,9},{9,8},{10,11... | collective-permute-start | bytes 688136 | tf_op jit(solution)/shard_map/ppermute | solution.py:49
  50.1 23.8 %collective-permute-start.12 = (bf16[144,1024]{1,0:T(8,128)(2,1)}, bf16[144,1024]{1,0:T(8,128)(2,1)S(1)}, u32[]{:S(2)}, u32[]{:S(2)}) collective-permute-start(bf16[144,1024]{1,0:T(8,128)(2,1)} %pack_kernel.2.refs_6_), channel_id=1, source_target_pairs={{0,24},{8,0},{16,8},{24,16},{1,25},{9,1},{17,9},{25,17},{2,26},{10... | collective-permute-start | bytes 884744 | tf_op jit(solution)/shard_map/ppermute | solution.py:44
  53.1 20.8 %collective-permute-start.11 = (bf16[144,1024]{1,0:T(8,128)(2,1)}, bf16[144,1024]{1,0:T(8,128)(2,1)S(1)}, u32[]{:S(2)}, u32[]{:S(2)}) collective-permute-start(bf16[144,1024]{1,0:T(8,128)(2,1)} %pack_kernel.2.refs_6_), channel_id=1, source_target_pairs={{0,8},{8,16},{16,24},{24,0},{1,9},{9,17},{17,25},{25,1},{2,10},{10... | collective-permute-start | bytes 884744 | tf_op jit(solution)/shard_map/ppermute | solution.py:44
  56.3 21.2 %collective-permute-start.18 = (bf16[4,32,1024]{2,1,0:T(8,128)(2,1)S(1)}, bf16[4,32,1024]{2,1,0:T(8,128)(2,1)S(1)}, u32[]{:S(2)}, u32[]{:S(2)}) collective-permute-start(bf16[4,32,1024]{2,1,0:T(8,128)(2,1)S(1)} %all-to-all-done.3.refs_0_), channel_id=1, source_target_pairs={{0,6},{1,7},{2,4},{3,5},{4,2},{5,3},{6,0},{7,1},{8,14},{9,15},{10,... | collective-permute-start | bytes 786440 | tf_op jit(solution)/shard_map/ppermute | solution.py:49
  58.9 19.1 %collective-permute-start.16 = (bf16[4,32,1024]{2,1,0:T(8,128)(2,1)S(1)}, bf16[4,32,1024]{2,1,0:T(8,128)(2,1)S(1)}, u32[]{:S(2)}, u32[]{:S(2)}) collective-permute-start(bf16[4,32,1024]{2,1,0:T(8,128)(2,1)S(1)} %all-to-all-done.3.refs_0_), channel_id=1, source_target_pairs={{0,4},{1,5},{2,6},{3,7},{4,0},{5,1},{6,2},{7,3},{8,12},{9,13},{10,... | collective-permute-start | bytes 786440 | tf_op jit(solution)/shard_map/ppermute | solution.py:49
  59.5 18.6 %collective-permute-start.14 = (bf16[4,32,1024]{2,1,0:T(8,128)(2,1)S(1)}, bf16[4,32,1024]{2,1,0:T(8,128)(2,1)S(1)}, u32[]{:S(2)}, u32[]{:S(2)}) collective-permute-start(bf16[4,32,1024]{2,1,0:T(8,128)(2,1)S(1)} %all-to-all-done.3.refs_0_), channel_id=1, source_target_pairs={{0,2},{1,3},{2,0},{3,1},{4,6},{5,7},{6,4},{7,5},{8,10},{9,11},{10,... | collective-permute-start | bytes 786440 | tf_op jit(solution)/shard_map/ppermute | solution.py:49
  88.9 12.1 %all-to-all-start.4 = ((bf16[8,24,1024]{2,1,0:T(8,128)(2,1)}), bf16[8,24,1024]{2,1,0:T(8,128)(2,1)S(1)}, u32[]{:S(2)}, u32[]{:S(2)}) async-start(bf16[8,24,1024]{2,1,0:T(8,128)(2,1)} %bitcast.52), calls=%async_computation.4 | async-start | bytes 786432 | tf_op jit(solution)/shard_map/all_to_all | solution.py:53
  92.7 16.8 %collective-permute-start.20 = (bf16[144,1024]{1,0:T(8,128)(2,1)S(1)}, bf16[144,1024]{1,0:T(8,128)(2,1)S(1)}, u32[]{:S(2)}, u32[]{:S(2)}) collective-permute-start(bf16[144,1024]{1,0:T(8,128)(2,1)S(1)} %copy-done.8), channel_id=1, source_target_pairs={{0,16},{8,24},{16,0},{24,8},{1,17},{9,25},{17,1},{25,9},{2,18},{10... | collective-permute-start | bytes 884744 | tf_op jit(solution)/shard_map/ppermute | solution.py:44
  109.5 11.9 %collective-permute-start.21 = (bf16[144,1024]{1,0:T(8,128)(2,1)}, bf16[144,1024]{1,0:T(8,128)(2,1)S(1)}, u32[]{:S(2)}, u32[]{:S(2)}) collective-permute-start(bf16[144,1024]{1,0:T(8,128)(2,1)} %pack_kernel.3.refs_5_.refs_0_), channel_id=1, source_target_pairs={{0,8},{8,16},{16,24},{24,0},{1,9},{9,17},{17,25},{25,1},{2,10},{10... | collective-permute-start | bytes 884744 | tf_op jit(solution)/shard_map/ppermute | solution.py:44
  110.2 27.8 %collective-permute-start.23 = (bf16[144,1024]{1,0:T(8,128)(2,1)}, bf16[144,1024]{1,0:T(8,128)(2,1)S(1)}, u32[]{:S(2)}, u32[]{:S(2)}) collective-permute-start(bf16[144,1024]{1,0:T(8,128)(2,1)} %pack_kernel.3.refs_5_.refs_0_), channel_id=1, source_target_pairs={{0,24},{8,0},{16,8},{24,16},{1,25},{9,1},{17,9},{25,17},{2,26},{10... | collective-permute-start | bytes 884744 | tf_op jit(solution)/shard_map/ppermute | solution.py:44
  113.3 33.0 %collective-permute-start.22 = (bf16[144,1024]{1,0:T(8,128)(2,1)}, bf16[144,1024]{1,0:T(8,128)(2,1)S(1)}, u32[]{:S(2)}, u32[]{:S(2)}) collective-permute-start(bf16[144,1024]{1,0:T(8,128)(2,1)} %pack_kernel.3.refs_5_.refs_0_), channel_id=1, source_target_pairs={{0,16},{8,24},{16,0},{24,8},{1,17},{9,25},{17,1},{25,9},{2,18},{10... | collective-permute-start | bytes 884744 | tf_op jit(solution)/shard_map/ppermute | solution.py:44
  129.6 35.0 %collective-permute-start.24 = (bf16[288,1024]{1,0:T(8,128)(2,1)}, bf16[288,1024]{1,0:T(8,128)(2,1)S(1)}, u32[]{:S(2)}, u32[]{:S(2)}) collective-permute-start(bf16[288,1024]{1,0:T(8,128)(2,1)} %get-tuple-element.143), channel_id=1, source_target_pairs={{0,24},{8,0},{16,8},{24,16},{1,25},{9,1},{17,9},{25,17},{2,26},{10... | collective-permute-start | bytes 1769480 | tf_op jit(solution)/shard_map/ppermute | solution.py:44
  146.2 18.7 %collective-permute-start.26 = (bf16[288,1024]{1,0:T(8,128)(2,1)}, bf16[288,1024]{1,0:T(8,128)(2,1)S(1)}, u32[]{:S(2)}, u32[]{:S(2)}) collective-permute-start(bf16[288,1024]{1,0:T(8,128)(2,1)} %get-tuple-element.150), channel_id=1, source_target_pairs={{0,8},{8,16},{16,24},{24,0},{1,9},{9,17},{17,25},{25,1},{2,10},{10... | collective-permute-start | bytes 1769480 | tf_op jit(solution)/shard_map/ppermute | solution.py:44
  154.5 35.5 %collective-permute-start.25 = (bf16[288,1024]{1,0:T(8,128)(2,1)}, bf16[288,1024]{1,0:T(8,128)(2,1)S(1)}, u32[]{:S(2)}, u32[]{:S(2)}) collective-permute-start(bf16[288,1024]{1,0:T(8,128)(2,1)} %get-tuple-element.175), channel_id=1, source_target_pairs={{0,16},{8,24},{16,0},{24,8},{1,17},{9,25},{17,1},{25,9},{2,18},{10... | collective-permute-start | bytes 1769480 | tf_op jit(solution)/shard_map/ppermute | solution.py:44
  219.4 13.2 %all-to-all-start.6 = ((bf16[4,128,256]{2,1,0:T(8,128)(2,1)}), bf16[4,128,256]{2,1,0:T(8,128)(2,1)S(1)}, u32[]{:S(2)}, u32[]{:S(2)}) async-start(bf16[4,128,256]{2,1,0:T(8,128)(2,1)} %get-tuple-element.187), calls=%async_computation.6 | async-start | bytes 524288 | tf_op jit(solution)/shard_map/all_to_all | solution.py:53
  232.6 13.7 %collective-permute-start.28 = (bf16[4,32,1024]{2,1,0:T(8,128)(2,1)}, bf16[4,32,1024]{2,1,0:T(8,128)(2,1)S(1)}, u32[]{:S(2)}, u32[]{:S(2)}) collective-permute-start(bf16[4,32,1024]{2,1,0:T(8,128)(2,1)} %get-tuple-element.200), channel_id=1, source_target_pairs={{0,2},{1,3},{2,0},{3,1},{4,6},{5,7},{6,4},{7,5},{8,10},{9,11},{10,... | collective-permute-start | bytes 786440 | tf_op jit(solution)/shard_map/ppermute | solution.py:49
  233.2 13.1 %collective-permute-start.29 = (bf16[4,32,1024]{2,1,0:T(8,128)(2,1)}, bf16[4,32,1024]{2,1,0:T(8,128)(2,1)S(1)}, u32[]{:S(2)}, u32[]{:S(2)}) collective-permute-start(bf16[4,32,1024]{2,1,0:T(8,128)(2,1)} %get-tuple-element.201), channel_id=1, source_target_pairs={{0,4},{1,5},{2,6},{3,7},{4,0},{5,1},{6,2},{7,3},{8,12},{9,13},{10,... | collective-permute-start | bytes 786440 | tf_op jit(solution)/shard_map/ppermute | solution.py:49
  233.8 12.6 %collective-permute-start.30 = (bf16[4,32,1024]{2,1,0:T(8,128)(2,1)}, bf16[4,32,1024]{2,1,0:T(8,128)(2,1)S(1)}, u32[]{:S(2)}, u32[]{:S(2)}) collective-permute-start(bf16[4,32,1024]{2,1,0:T(8,128)(2,1)} %get-tuple-element.202), channel_id=1, source_target_pairs={{0,6},{1,7},{2,4},{3,5},{4,2},{5,3},{6,0},{7,1},{8,14},{9,15},{10,... | collective-permute-start | bytes 786440 | tf_op jit(solution)/shard_map/ppermute | solution.py:49
  252.3 27.2 %all-to-all-start.7 = ((bf16[4,128,1024]{2,1,0:T(8,128)(2,1)}), bf16[4,128,1024]{2,1,0:T(8,128)(2,1)S(1)}, u32[]{:S(2)}, u32[]{:S(2)}) async-start(bf16[4,128,1024]{2,1,0:T(8,128)(2,1)} %get-tuple-element.209.refs_3_), calls=%async_computation.7 | async-start | bytes 2097152 | tf_op jit(solution)/shard_map/all_to_all | solution.py:53
  262.7 12.5 %collective-permute-start.33 = (bf16[4,32,896]{2,1,0:T(8,128)(2,1)}, bf16[4,32,896]{2,1,0:T(8,128)(2,1)S(1)}, u32[]{:S(2)}, u32[]{:S(2)}) collective-permute-start(bf16[4,32,896]{2,1,0:T(8,128)(2,1)} %get-tuple-element.214), channel_id=1, source_target_pairs={{0,4},{1,5},{2,6},{3,7},{4,0},{5,1},{6,2},{7,3},{8,12},{9,13},{10,... | collective-permute-start | bytes 688136 | tf_op jit(solution)/shard_map/ppermute | solution.py:49
  263.3 11.9 %collective-permute-start.34 = (bf16[4,32,896]{2,1,0:T(8,128)(2,1)}, bf16[4,32,896]{2,1,0:T(8,128)(2,1)S(1)}, u32[]{:S(2)}, u32[]{:S(2)}) collective-permute-start(bf16[4,32,896]{2,1,0:T(8,128)(2,1)} %get-tuple-element.215), channel_id=1, source_target_pairs={{0,6},{1,7},{2,4},{3,5},{4,2},{5,3},{6,0},{7,1},{8,14},{9,15},{10,... | collective-permute-start | bytes 688136 | tf_op jit(solution)/shard_map/ppermute | solution.py:49
  282.5 16.7 %all-to-all-start.8 = ((bf16[4,32,1920]{2,1,0:T(8,128)(2,1)}), bf16[4,32,1920]{2,1,0:T(8,128)(2,1)S(1)}, u32[]{:S(2)}, u32[]{:S(2)}) async-start(bf16[4,32,1920]{2,1,0:T(8,128)(2,1)} %chip_sum_kernel.1), calls=%async_computation.8 | async-start | bytes 983040 | tf_op jit(solution)/shard_map/all_to_all | solution.py:53
  (53 other events, 407.9 us)

commit v4 on v3

v4 whole, which is shorter than its diff:
```python
import functools

import jax
import jax.numpy as jnp
import numpy as np
from jax import lax
from jax.experimental import pallas as pl
from jax.experimental.pallas import tpu as pltpu
from jax.sharding import PartitionSpec as P

H = 16
NSEG = 7
EPS = 1e-05
NEG = -1e30
BF = jnp.bfloat16
F32 = jnp.float32
I32 = jnp.int32


def mm(a, b, ca=1, cb=0):
    return lax.dot_general(a, b, (((ca,), (cb,)), ((), ())), preferred_element_type=F32)


def placed(kernel):
    def body(*refs):
        kernel((lax.axis_index("dp"), lax.axis_index("expert")), *refs)

    return body


PARAMS = pltpu.CompilerParams(vmem_limit_bytes=24 << 20)


def far(*arrays):
    return [pltpu.with_memory_space_constraint(x, pltpu.HBM) for x in arrays]


def call(kernel, outs, *args, scratch=(), **static):
    vmem = pl.BlockSpec(memory_space=pltpu.VMEM)
    return pl.pallas_call(
        placed(functools.partial(kernel, **static)),
        out_shape=[o if isinstance(o, pl.MemoryRef) else jax.ShapeDtypeStruct(*o) for o in outs],
        in_specs=[vmem] * len(args),
        out_specs=[vmem] * len(outs),
        scratch_shapes=list(scratch),
        compiler_params=PARAMS,
        name=kernel.__name__,
    )(*args)


def ahead(x, step):
    n = lax.axis_size("dp")
    return lax.ppermute(x, "dp", [(i, (i + step) % n) for i in range(n)])


def flip(x, bits):
    n = lax.axis_size("expert")
    return lax.ppermute(x, "expert", [(i, i ^ bits) for i in range(n)])


def swap(x, axis):
    return lax.all_to_all(x, axis, split_axis=0, concat_axis=0, tiled=True)


def along(blocks, sign=1):
    return [blocks[0]] + [ahead(blocks[j], sign * j) for j in range(1, len(blocks))]


def across(x, bits):
    n = lax.axis_size("dp")
    return lax.ppermute(x, "dp", [(i, i ^ bits) for i in range(n)])


def spread(x, hold=None):
    n = lax.axis_size("dp")
    out = [[x]] + [[across(x, k)] for k in range(1, n - 1)]
    if n != 4:
        return out + [[across(x, n - 1)]]
    own = lax.ppermute(x, "dp", [(1, 2), (2, 1)])
    if hold is not None:
        out[2] = [hold(out[2][0])]
    return out + [[own, lax.ppermute(out[2][0], "dp", [(1, 0), (2, 3)])]]


def added(refs):
    return refs[0][...] if len(refs) == 1 else refs[0][...] + refs[1][...]


def split(refs, counts):
    out, at = [], 0
    for count in counts:
        out.append(refs[at : at + count])
        at += count
    return out


def gather_experts(x):
    n = lax.axis_size("expert")
    mine = [x] + [flip(x, 2 * k) for k in range(1, n // 2)]
    out = []
    for block in mine:
        out += [block, flip(block, 1)]
    return out


def normalise(values):
    mean = jnp.mean(values, axis=-1, keepdims=True)
    centred = values - mean
    scale = lax.rsqrt(jnp.mean(centred * centred, axis=-1, keepdims=True) + EPS)
    return centred * scale, scale


def norm_back(upstream, gain, unit, scale):
    e = upstream * gain
    return scale * (
        e - jnp.mean(e, axis=-1, keepdims=True) - unit * jnp.mean(e * unit, axis=-1, keepdims=True)
    )


def lanes(shape, dim):
    return lax.broadcasted_iota(I32, shape, dim)


def softmax_of(logits, experts):
    logits = jnp.where(lanes(logits.shape, 1) < experts, logits, NEG)
    top = jnp.max(logits, axis=-1, keepdims=True)
    weight = jnp.exp(logits - top)
    return weight / jnp.sum(weight, axis=-1, keepdims=True)


def weights_kernel(me, qkv, router, gains, biases, out, turned, *, n_dp):
    own, width = qkv.shape[0], qkv.shape[1] // 3
    part = width // n_dp
    experts = router.shape[0]
    turned[...] = jnp.zeros_like(turned)
    turned[:experts, :own] = router[...].astype(F32)
    turned[experts : experts + 2, :own] = gains[...].astype(F32)
    turned[experts + 2 : experts + 7, :own] = biases[...].astype(F32)
    small = turned[...].T[:own].astype(BF)
    for d in range(n_dp):
        for i in range(3):
            out[d, :, i * part : (i + 1) * part] = qkv[
                :, i * width + d * part : i * width + (d + 1) * part
            ]
        out[d, :, 3 * part :] = small


def slots_kernel(
    me, parents, route, order, cotangent, seg, grads, tableT, route_out, rank_out, bias, *, pad, capacity, experts
):
    tok = route.shape[1]
    rt = jnp.broadcast_to(route[...].astype(F32), (tok, tok))
    r = rt.T
    route_out[...] = r[:, 0:1].astype(I32)
    o = jnp.broadcast_to(order[...].astype(F32), (tok, tok))
    ot = o.T
    same = r == rt
    rank = jnp.sum(jnp.where(same & (o < ot), 1.0, 0.0), axis=1, keepdims=True)
    rank_row = jnp.sum(jnp.where(same & (ot < o), 1.0, 0.0), axis=0, keepdims=True)
    rank_out[...] = rank.astype(I32)
    key = jnp.where(rank_row < capacity, rt[0:1] * pad + rank_row, -1.0).astype(I32)
    table = jnp.where(lanes((experts * pad, tok), 0) == key, 1.0, 0.0).astype(BF)
    tableT[...] = table
    grads[...] = mm(table, cotangent[...]).astype(BF)
    length = seg.shape[1]
    masks = [jnp.int32(1)]
    for s in range(1, NSEG):
        up = jnp.int32(0)
        for a in range(s):
            up = jnp.where(parents[0, s] == a, masks[a], up)
        masks.append(up | (1 << s))
    block = 128
    mine = jnp.zeros((1, length), I32)
    for s in range(NSEG):
        mine = jnp.where(seg[...] == s, masks[s], mine)
    for i in range(length // block):
        col = jnp.broadcast_to(seg[:, i * block : (i + 1) * block].astype(F32), (block, block)).T
        bit = jnp.left_shift(1, jnp.broadcast_to(col[:, 0:1], (block, length)).astype(I32))
        seen = lanes((block, length), 0) + i * block <= lanes((block, length), 1)
        bias[i * block : (i + 1) * block] = jnp.where(seen & ((mine & bit) != 0), 0.0, NEG).astype(BF)


def pack_kernel(me, pick, rows, out):
    out[...] = mm(pick[...], rows[...]).astype(BF)


def pack_picks(n_ex, pad, capacity):
    pick = np.zeros((n_ex * capacity, n_ex * pad), np.float32)
    for e in range(n_ex):
        for c in range(capacity):
            pick[e * capacity + c, e * pad + c] = 1
    return jnp.asarray(pick, BF)


def line_picks(n_ex, pair, capacity):
    pick = np.zeros((n_ex * pair, 2 * n_ex * capacity), np.float32)
    for e in range(n_ex):
        for w in range(2):
            for c in range(capacity):
                pick[e * pair + w * capacity + c, (w * n_ex + e) * capacity + c] = 1
    return jnp.asarray(pick, BF)


def assemble_kernel(me, *refs):
    out = refs[-1]
    for k, block in enumerate(refs[:-1]):
        e = me[1] ^ k
        for d in range(block.shape[0]):
            out[d, e] = block[d]


def assembled(me, blocks, whole):
    own = blocks[0].shape[1]
    n_ex = len(blocks)
    for k, block in enumerate(blocks):
        for d in range(block.shape[0]):
            row = pl.multiple_of((d * n_ex + (me[1] ^ k)) * own, own)
            whole[pl.ds(row, own)] = block[d]


def attend_kernel(me, bias, *refs, counts, n_ex, head_dim, experts):
    blocks, refs = refs[:n_ex], refs[n_ex:]
    tokens, (normed, packed, probs, attended, vectors, small, qkv) = split(refs, counts), refs[-7:]
    n_dp = len(counts)
    rows, width = tokens[0][0].shape
    part = width // n_dp
    assembled(me, blocks, qkv)
    few = qkv[:, 3 * part :]
    small[...] = few
    vectors[...] = few.astype(F32).T[experts : experts + 8]
    gain, shift = vectors[0:1], vectors[2:3]
    parts = [jnp.zeros((1, part), F32)] * 2
    for d in range(n_dp):
        for i in range(2):
            here = vectors[3 + i : 4 + i, d * part : (d + 1) * part]
            parts[i] = parts[i] + jnp.where(me[0] == d, here, 0.0)

    for k, blocks in enumerate(tokens):
        base = pl.multiple_of((me[0] ^ k) * rows, rows)
        unit, _ = normalise(added(blocks).astype(F32))
        normed[pl.ds(base, rows)] = (unit * gain + shift).astype(BF)

    raw = mm(normed[...], qkv[:, : 3 * part])
    packed[:, :part] = (raw[:, :part] + parts[0]).astype(BF)
    packed[:, part : 2 * part] = raw[:, part : 2 * part].astype(BF)
    packed[:, 2 * part :] = (raw[:, 2 * part :] + parts[1]).astype(BF)
    scale = head_dim ** (-0.5)
    for h in range(part // head_dim):
        q = packed[:, h * head_dim : (h + 1) * head_dim]
        k = packed[:, part + h * head_dim : part + (h + 1) * head_dim]
        vt = packed[:, 2 * part + h * head_dim : 2 * part + (h + 1) * head_dim].T
        for i in range(n_dp):
            lo, hi = i * rows, (i + 1) * rows
            s = mm(k[:hi], q[lo:hi], 1, 1) * scale + bias[:hi, lo:hi].astype(F32)
            p = jnp.exp(s - jnp.max(s, axis=0, keepdims=True))
            p = (p * (1.0 / jnp.sum(p, axis=0, keepdims=True))).astype(BF)
            probs[h, :hi, lo:hi] = p
            attended[i, :, h * head_dim : (h + 1) * head_dim] = mm(vt[:, :hi], p).T.astype(BF)


def mix_kernel(me, tokens, attended, proj, small, vectors, tableT, mixed, normed, p, sent, *, experts):
    n_dp, rows, part = attended.shape
    total = tokens[...].astype(F32) + vectors[5:6]
    for d in range(n_dp):
        total = total + mm(attended[d], proj[d * part : (d + 1) * part])
    mixed[...] = total
    unit, _ = normalise(total)
    low = (unit * vectors[1:2] + vectors[6:7]).astype(BF)
    normed[...] = low
    p[...] = softmax_of(mm(low, small[...]), experts)
    sent[...] = mm(tableT[...], low).astype(BF)


def expert_kernel(
    me, small, up, down, up_bias, down_bias, *refs, counts, n_dp, experts
):
    came, grads, (both, slots, act_out, d_pre_out, d_rows, g_up_bias, acc_r, acc_s) = split(refs, [*counts, 8])
    f = pl.program_id(0)
    each, width = slots.shape
    part = width // n_dp

    @pl.when(f == 0)
    def _():
        slots[...] = added(came)
        p = softmax_of(mm(slots[...], small[...]), experts)
        gate = jnp.sum(jnp.where(lanes(p.shape, 1) == me[1], p, 0.0), axis=-1, keepdims=True)
        d_rows[...] = (gate * added(grads).astype(F32)).astype(BF)
        acc_s[...] = jnp.zeros_like(acc_s)
        for d in range(n_dp):
            acc_r[:, d * part : (d + 1) * part] = jnp.broadcast_to(
                jnp.where(me[0] == d, down_bias[...].astype(F32), 0.0), (each, part)
            )

    u = mm(slots[...], up[...]) + up_bias[...].astype(F32)
    c, a = 0.7978845608028654, 0.044715
    t = jnp.tanh(c * (u + a * (u * u * u)))
    act = (0.5 * u * (1.0 + t)).astype(BF)
    slope = 0.5 * (1.0 + t) + 0.5 * u * (1.0 - t * t) * (c * (1.0 + 3.0 * a * (u * u)))
    d_pre = mm(d_rows[...], down[...], 1, 1) * slope
    g_up_bias[...] = jnp.sum(d_pre, axis=0, keepdims=True)
    low = d_pre.astype(BF)
    act_out[...] = act
    d_pre_out[...] = low
    acc_r[...] += mm(act, down[...])
    acc_s[...] += mm(low, up[...], 1, 1)

    @pl.when(f == pl.num_programs(0) - 1)
    def _():
        both[:each] = acc_r[...].astype(BF)
        both[each:] = acc_s[...].astype(BF)


def expert_call(small, up, down, up_bias, down_bias, slots, grads, n_dp, experts):
    each, width = slots[0].shape
    ff = up.shape[1]
    chunk = min(ff, 256)
    whole = pl.BlockSpec(memory_space=pltpu.VMEM)
    wide = pl.BlockSpec((each, chunk), lambda f: (0, f))
    row = pl.BlockSpec((1, chunk), lambda f: (0, f))
    return pl.pallas_call(
        placed(
            functools.partial(
                expert_kernel, counts=(len(slots), len(grads)), n_dp=n_dp, experts=experts
            )
        ),
        grid=(ff // chunk,),
        out_shape=[
            pltpu.HBM((2 * each, width), BF),
            jax.ShapeDtypeStruct((each, width), BF),
            jax.ShapeDtypeStruct((each, ff), BF),
            jax.ShapeDtypeStruct((each, ff), BF),
            jax.ShapeDtypeStruct((each, width), BF),
            jax.ShapeDtypeStruct((1, ff), F32),
        ],
        in_specs=[
            whole,
            pl.BlockSpec((width, chunk), lambda f: (0, f)),
            pl.BlockSpec((chunk, width), lambda f: (f, 0)),
            row,
            whole,
        ]
        + [whole] * (len(slots) + len(grads)),
        out_specs=[whole, whole, wide, wide, whole, row],
        scratch_shapes=[pltpu.VMEM((each, width), F32), pltpu.VMEM((each, width), F32)],
        compiler_params=PARAMS,
        name="expert_kernel",
    )(small, up, down, up_bias, down_bias, *slots, *grads)


def expert_grad_kernel(me, *refs, n_dp):
    slots, act, d_pre, d_rows, up_bias = (refs[i * n_dp : (i + 1) * n_dp] for i in range(5))
    grad_up, grad_down, g_up_bias, g_down_bias = refs[5 * n_dp :]
    grad_up[...] = sum(mm(a[...], b[...], 0, 0) for a, b in zip(slots, d_pre))
    grad_down[...] = sum(mm(a[...], b[...], 0, 0) for a, b in zip(act, d_rows))

    @pl.when(pl.program_id(0) == 0)
    def _():
        g_up_bias[...] = sum_of(up_bias)
        sums = sum(jnp.sum(r[...].astype(F32), axis=0, keepdims=True) for r in d_rows)
        part = g_down_bias.shape[1]
        own = jnp.zeros((1, part), F32)
        for d in range(n_dp):
            own = own + jnp.where(me[0] == d, sums[:, d * part : (d + 1) * part], 0.0)
        g_down_bias[...] = own


def expert_grads(slots, act, d_pre, d_rows, up_bias, part):
    n_dp = len(slots)
    each, width = slots[0].shape
    ff = act[0].shape[1]
    steps = 4
    whole = pl.BlockSpec(memory_space=pltpu.VMEM)
    return pl.pallas_call(
        placed(functools.partial(expert_grad_kernel, n_dp=n_dp)),
        grid=(steps,),
        out_shape=[
            pltpu.HBM((width, ff), F32),
            pltpu.HBM((ff, width), F32),
            jax.ShapeDtypeStruct((1, ff), F32),
            jax.ShapeDtypeStruct((1, part), F32),
        ],
        in_specs=[pl.BlockSpec((each, width // steps), lambda f: (0, f))] * n_dp
        + [pl.BlockSpec((each, ff // steps), lambda f: (0, f))] * n_dp
        + [whole] * (3 * n_dp),
        out_specs=[
            pl.BlockSpec((width // steps, ff), lambda f: (f, 0)),
            pl.BlockSpec((ff // steps, width), lambda f: (f, 0)),
            whole,
            whole,
        ],
        compiler_params=PARAMS,
        name="expert_grad_kernel",
    )(*slots, *act, *d_pre, *d_rows, *up_bias)


def sum_of(refs):
    total = refs[0][...].astype(F32)
    for ref in refs[1:]:
        total = total + ref[...].astype(F32)
    return total


def line_sum_kernel(me, pick, *refs):
    refs[-1][...] = mm(pick[...], sum_of(refs[:-1]).astype(BF)).astype(BF)


def combine_kernel(
    me, back, route, rank, mixed, p, cotangent, small, vectors, proj,
    outputs, d_mixed, d_low_out, d_att, d_logits_out, sums, *, pair, capacity, experts, part,
):
    tok, width = mixed.shape
    n_back = back.shape[0]
    r, k = route[...], rank[...]
    key = jnp.where(k < capacity, r * pair + k, -2 * pair * experts)
    slot = lanes((tok, n_back), 1)
    combined = mm(jnp.where(slot == key, 1.0, 0.0).astype(BF), back[...])
    d_slot = mm(jnp.where(slot == key + capacity, 1.0, 0.0).astype(BF), back[...])
    hot = jnp.where(lanes(p.shape, 1) == r, 1.0, 0.0)
    gate = jnp.sum(p[...] * hot, axis=-1, keepdims=True)
    g = cotangent[...].astype(F32)
    outputs[...] = (mixed[...] + gate * combined).astype(BF)
    d_gate = jnp.sum(g * combined, axis=-1, keepdims=True)
    d_logits = (p[...] * (d_gate * hot - d_gate * gate)).astype(BF)
    d_logits_out[...] = d_logits
    d_normed = d_slot + mm(d_logits, small[...], 1, 1)
    unit, scale = normalise(mixed[...])
    sums[0:1] = jnp.sum(d_normed * unit, axis=0, keepdims=True)
    sums[1:2] = jnp.sum(d_normed, axis=0, keepdims=True)
    d = g + norm_back(d_normed, vectors[1:2], unit, scale)
    sums[2:3] = jnp.sum(d, axis=0, keepdims=True)
    d_mixed[...] = d
    low = d.astype(BF)
    d_low_out[...] = low
    for i in range(d_att.shape[0]):
        d_att[i] = mm(low, proj[i * part : (i + 1) * part], 1, 1).astype(BF)


def share(me, whole, near, keep):
    half, n_dp, own, _ = near.shape
    for q in range(half):
        for d in range(n_dp):
            row = d * 2 * half * own
            other = pl.multiple_of(row + (me[1] ^ (2 * q + 1)) * own, own)
            same = pl.multiple_of(row + (me[1] ^ (2 * q)) * own, own)
            near[q, d] = whole[pl.ds(other, own)].astype(BF)
            keep[q, d] = whole[pl.ds(same, own)].astype(BF)


def proj_grad_kernel(me, attended, d_low, near, keep, whole):
    n_dp, rows, part = attended.shape
    for d in range(n_dp):
        whole[d * part : (d + 1) * part] = mm(attended[d], d_low[...], 0, 0)
    share(me, whole, near, keep)


def core_sum_kernel(me, keep, came, first, *rest):
    for q, out in enumerate([first, *rest]):
        out[...] = (keep[q].astype(F32) + came[q].astype(F32)).astype(BF)


def chip_sum_kernel(me, *refs, n_dp):
    outs, total = refs[-1 - n_dp : -1], refs[-1]
    parts = refs[: -1 - n_dp]
    half = len(parts) // 2
    wide = parts[0].shape[2]
    total[:, :, :wide] = sum_of(parts[:half]).astype(BF)
    total[:, :, wide:] = sum_of(parts[half:]).astype(BF)
    for j in range(n_dp):
        outs[j][...] = total[(me[0] + j) % n_dp]


def core_sum(near, keep):
    half = near.shape[0]
    shape = near.shape[1:]
    return call(core_sum_kernel, [(shape, BF)] + [pltpu.HBM(shape, BF)] * (half - 1), keep, flip(near, 1))


def to_chips(parts):
    return [parts[0]] + [flip(part, 2 * (q + 1)) for q, part in enumerate(parts[1:])]


def attend_back_kernel(me, d_att, probs, packed, *refs, head_dim):
    blocks, (d_packed, d_normed, d_scores, qkv) = refs[:-4], refs[-4:]
    n_dp, rows, part = d_att.shape
    scale = head_dim ** (-0.5)
    assembled(me, blocks, qkv)
    for h in range(part // head_dim):
        a, b = h * head_dim, (h + 1) * head_dim
        q, k, v = packed[:, a:b], packed[:, part + a : part + b], packed[:, 2 * part + a : 2 * part + b]
        kt = k.T
        g = jnp.concatenate([d_att[i, :, a:b] for i in range(n_dp)], axis=0)
        for i in range(n_dp):
            lo, hi = i * rows, (i + 1) * rows
            dp = mm(v[:hi], g[lo:hi], 1, 1)
            p = probs[h, :hi, lo:hi].astype(F32)
            delta = jnp.sum(p * dp, axis=0, keepdims=True)
            ds = (p * (dp - delta)).astype(BF)
            d_scores[:hi, lo:hi] = ds
            d_packed[lo:hi, a:b] = (mm(kt[:, :hi], ds).T * scale).astype(BF)
        for i in range(n_dp):
            lo, hi = i * rows, (i + 1) * rows
            d_packed[lo:hi, part + a : part + b] = (mm(d_scores[lo:hi, lo:], q[lo:]) * scale).astype(BF)
            d_packed[lo:hi, 2 * part + a : 2 * part + b] = mm(probs[h, lo:hi, lo:], g[lo:]).astype(BF)
    for i in range(n_dp):
        d_normed[i] = mm(d_packed[i * rows : (i + 1) * rows], qkv[:, : 3 * part], 1, 1).astype(BF)


def qkv_grad_kernel(
    me, normed, vectors, d_packed, d_normed, token_normed, d_logits, sums, near, keep, whole, turned, *, experts
):
    n_dp, rows, width = d_normed.shape
    part = width // n_dp
    whole[:, : 3 * part] = mm(normed[...], d_packed[...], 0, 0)
    gain = jnp.zeros((1, width), F32)
    shift = jnp.zeros((1, width), F32)
    for i in range(n_dp):
        d = d_normed[i].astype(F32)
        gain = gain + jnp.sum(d * normed[i * rows : (i + 1) * rows].astype(F32), axis=0, keepdims=True)
        shift = shift + jnp.sum(d, axis=0, keepdims=True)
    gain = (gain - vectors[2:3] * shift) / vectors[0:1]
    columns = jnp.sum(d_packed[...].astype(F32), axis=0, keepdims=True)
    turned[...] = jnp.zeros_like(turned)
    e = experts
    turned[e : e + 1] = gain
    turned[e + 1 : e + 2] = sums[0:1]
    turned[e + 2 : e + 3] = shift
    for d in range(n_dp):
        here = me[0] == d
        turned[e + 3 : e + 4, d * part : (d + 1) * part] = jnp.where(here, columns[:, :part], 0.0)
        turned[e + 4 : e + 5, d * part : (d + 1) * part] = jnp.where(here, columns[:, 2 * part :], 0.0)
    turned[e + 5 : e + 6] = sums[2:3]
    turned[e + 6 : e + 7] = sums[1:2]
    whole[:, 3 * part :] = turned[...].T + mm(token_normed[...], d_logits[...], 0, 0)
    share(me, whole, near, keep)


def weights_end_kernel(me, *refs):
    (qkv, proj, router, gains, biases, wide, came), blocks = refs[-7:], refs[:-7]
    n_dp, own, _ = came.shape
    for j in range(n_dp):
        came[(me[0] + n_dp - j) % n_dp] = blocks[j][...]
    width = proj.shape[1]
    part = width // n_dp
    experts = router.shape[0]
    edge = 3 * part
    total = jnp.zeros((own, 128), F32)
    rows = jnp.zeros((own, width), F32)
    for d in range(n_dp):
        for i in range(3):
            qkv[:, i * width + d * part : i * width + (d + 1) * part] = came[
                d, :, i * part : (i + 1) * part
            ].astype(F32)
        total = total + came[d, :, edge : edge + 128].astype(F32)
        rows = rows + came[d, :, edge + 128 :].astype(F32)
    proj[...] = rows
    wide[...] = jnp.zeros_like(wide)
    wide[:own] = total
    flat = wide[...].T
    router[...] = flat[:experts, :own]
    gains[...] = flat[experts : experts + 2, :own]
    biases[...] = flat[experts + 2 : experts + 7, :own]


def tokens_end_kernel(me, came, tokens, vectors, d_mixed, out):
    total = came[0].astype(F32)
    for d in range(1, came.shape[0]):
        total = total + came[d].astype(F32)
    unit, scale = normalise(tokens[...].astype(F32))
    out[...] = d_mixed[...] + norm_back(total, vectors[0:1], unit, scale)


def shards(
    tokens,
    qkv_weight,
    proj_weight,
    router_weight,
    norm_gains,
    biases,
    up_weight,
    up_bias,
    down_weight,
    down_bias,
    routes,
    slot_order,
    segments,
    parents,
    cotangent,
):
    n_dp, n_ex = lax.axis_size("dp"), lax.axis_size("expert")
    rows, width = tokens.shape[1], tokens.shape[2]
    part = width // n_dp
    head_dim = width // H
    own = qkv_weight.shape[0]
    experts = router_weight.shape[1]
    capacity = (9 * rows + 8 * experts - 1) // (8 * experts)
    pad = -(-capacity // 8) * 8
    pair = -(-capacity // 4) * 8
    length = n_dp * rows
    each = n_ex * capacity
    cols = 3 * part + 128
    x = tokens[0]

    token_blocks = spread(x)
    columns = call(
        weights_kernel,
        [pltpu.HBM((n_dp, own, cols), BF)],
        *far(qkv_weight, router_weight.T, norm_gains, biases),
        scratch=[pltpu.VMEM((128, 128), F32)],
        n_dp=n_dp,
    )[0]
    qkv_blocks = gather_experts(swap(columns, "dp"))
    smem = pl.BlockSpec(memory_space=pltpu.SMEM)
    vmem = pl.BlockSpec(memory_space=pltpu.VMEM)
    grads_out, tableT, route, rank, bias = pl.pallas_call(
        placed(functools.partial(slots_kernel, pad=pad, capacity=capacity, experts=experts)),
        out_shape=[
            pltpu.HBM((n_ex * pad, width), BF),
            pltpu.HBM((n_ex * pad, rows), BF),
            pltpu.HBM((rows, 1), I32),
            pltpu.HBM((rows, 1), I32),
            jax.ShapeDtypeStruct((length, length), BF),
        ],
        in_specs=[smem] + [vmem] * 4,
        out_specs=[vmem] * 5,
        compiler_params=PARAMS,
        name="slots_kernel",
    )(parents, *far(routes.reshape(1, rows), slot_order[0], cotangent[0], segments))

    def dispatch(rows_out):
        came = swap(rows_out.reshape(n_ex, pad, width), "expert").reshape(n_ex * pad, width)
        mine = call(pack_kernel, [pltpu.HBM((each, width), BF)], *far(pack_picks(n_ex, pad, capacity)), came)[0]
        return mine

    grads_in = dispatch(grads_out)
    proj_blocks = gather_experts(swap(jnp.broadcast_to(proj_weight, (n_dp, own, width)), "dp"))
    grads_in, bias = lax.optimization_barrier((grads_in, bias))
    grads = spread(grads_in)
    normed1, packed, probs, att_out, vectors, small = call(
        attend_kernel,
        [
            pltpu.HBM((length, width), BF),
            pltpu.HBM((length, 3 * part), BF),
            pltpu.HBM((part // head_dim, length, length), BF),
            pltpu.HBM((n_dp, rows, part), BF),
            ((8, width), F32),
            ((width, 128), BF),
        ],
        bias, *far(*qkv_blocks, *sum(token_blocks, [])),
        scratch=[pltpu.VMEM((width, cols), BF)],
        counts=[len(b) for b in token_blocks], n_ex=n_ex, head_dim=head_dim, experts=experts,
    )
    early = list(range(1, n_dp - 1))
    att_out, *came = lax.optimization_barrier((att_out, *[grads[k][0] for k in early]))
    for k, block in zip(early, came):
        grads[k] = [block]
    attended = swap(att_out, "dp")
    proj = call(assemble_kernel, [((n_dp, n_ex, own, width), BF)], *proj_blocks)[0].reshape(width, width)
    mixed, normed2, p, sent = call(
        mix_kernel,
        [pltpu.HBM((rows, width), F32), pltpu.HBM((rows, width), BF), pltpu.HBM((rows, 128), F32), pltpu.HBM((n_ex * pad, width), BF)],
        *far(x), attended, proj, small, vectors, *far(tableT),
        experts=experts,
    )
    mine = dispatch(sent)
    grads = lax.optimization_barrier(grads)
    def expert(slots, k):
        return expert_call(
            small, up_weight[0], down_weight[0], up_bias, down_bias, slots, grads[k], n_dp, experts
        )

    done = {0: expert([mine], 0)}

    def after_own(block):
        block, done[0] = lax.optimization_barrier((block, done[0]))
        return block

    slots = spread(mine, after_own)
    came = [done[0][0]] + [None] * (n_dp - 1)
    last = 0
    for k in [2, 1, 3] if n_dp == 4 else range(1, n_dp):
        slots[k], done[last] = lax.optimization_barrier((slots[k], done[last]))
        done[k] = expert(slots[k], k)
        came[k] = across(done[k][0], k)
        last = k
    came[0] = done[0][0]
    all_slots, act, d_pre, d_rows, g_up_bias = ([done[k][i] for k in range(n_dp)] for i in range(1, 6))
    grad_up, grad_down, grad_up_bias, grad_down_bias = expert_grads(
        all_slots, act, d_pre, d_rows, g_up_bias, part
    )
    grad_up, grad_down, *came = lax.optimization_barrier((grad_up, grad_down, *came))
    summed = call(line_sum_kernel, [pltpu.HBM((n_ex * pair, width), BF)], *far(line_picks(n_ex, pair, capacity)), *came)[0]
    back = swap(summed.reshape(n_ex, pair, width), "expert").reshape(n_ex * pair, width)
    outputs, d_mixed, d_low, d_att, d_logits, sums = call(
        combine_kernel,
        [
            pltpu.HBM((rows, width), BF),
            pltpu.HBM((rows, width), F32),
            ((rows, width), BF),
            pltpu.HBM((n_dp, rows, part), BF),
            pltpu.HBM((rows, 128), BF),
            pltpu.HBM((8, width), F32),
        ],
        back, *far(route, rank, mixed, p, cotangent[0]), small, vectors, proj,
        pair=pair, capacity=capacity, experts=experts, part=part,
    )
    d_heads = swap(d_att, "dp")
    half = n_ex // 2
    near, keep = call(
        proj_grad_kernel,
        [pltpu.HBM((half, n_dp, own, width), BF), ((half, n_dp, own, width), BF)],
        *far(attended), d_low,
        scratch=[pltpu.VMEM((width, width), F32)],
    )
    d_heads, *parts = lax.optimization_barrier((d_heads, *core_sum(near, keep)))
    proj_chips = to_chips(parts)
    d_packed, d_normed = call(
        attend_back_kernel,
        [((length, 3 * part), BF), pltpu.HBM((n_dp, rows, width), BF)],
        d_heads, *far(probs, packed, *qkv_blocks),
        scratch=[pltpu.VMEM((length, length), BF), pltpu.VMEM((width, cols), BF)],
        head_dim=head_dim,
    )
    d_packed, *proj_chips = lax.optimization_barrier((d_packed, *proj_chips))
    near, keep = call(
        qkv_grad_kernel,
        [pltpu.HBM((half, n_dp, own, cols), BF), ((half, n_dp, own, cols), BF)],
        *far(normed1), vectors, d_packed, *far(d_normed, normed2, d_logits, sums),
        scratch=[pltpu.VMEM((width, cols), F32), pltpu.VMEM((128, width), F32)],
        experts=experts,
    )
    near, d_normed = lax.optimization_barrier((near, d_normed))
    d_own = swap(d_normed, "dp")
    qkv_chips = to_chips(core_sum(near, keep))
    summed = call(
        chip_sum_kernel, [pltpu.HBM((own, cols + width), BF)] * n_dp, *qkv_chips, *proj_chips,
        scratch=[pltpu.VMEM((n_dp, own, cols + width), BF)], n_dp=n_dp,
    )
    d_own, *summed = lax.optimization_barrier((d_own, *summed))
    owned_qkv, owned_proj, owned_router, owned_gains, owned_biases = call(
        weights_end_kernel,
        [
            pltpu.HBM((own, 3 * width), F32),
            pltpu.HBM((own, width), F32),
            pltpu.HBM((experts, own), F32),
            pltpu.HBM((2, own), F32),
            pltpu.HBM((5, own), F32),
        ],
        *along(summed),
        scratch=[pltpu.VMEM((128, 128), F32), pltpu.VMEM((n_dp, own, cols + width), BF)],
    )
    grad_tokens = call(tokens_end_kernel, [pltpu.HBM((rows, width), F32)], d_own, *far(x), vectors, *far(d_mixed))[0]
    return (
        outputs[None],
        grad_tokens[None],
        owned_qkv,
        owned_proj,
        owned_router.T,
        owned_gains,
        owned_biases,
        grad_up[None],
        grad_up_bias,
        grad_down[None],
        grad_down_bias,
    )


def solution(mesh):
    line = P(("dp", "expert"), None)
    across = P(None, ("dp", "expert"))
    act = P("expert", "dp", None)
    return jax.shard_map(
        shards,
        mesh=mesh,
        in_specs=(
            act,
            line,
            line,
            line,
            across,
            across,
            P("expert", None, "dp"),
            P("expert", "dp"),
            act,
            P("expert", "dp"),
            act,
            act,
            P("expert", None),
            P("expert", None),
            act,
        ),
        out_specs=(
            act,
            act,
            line,
            line,
            line,
            across,
            across,
            P("expert", None, "dp"),
            P("expert", "dp"),
            act,
            P("expert", "dp"),
        ),
        check_vma=False,
    )
```

time: 304 us -> 272 us (0.89)
  Pallas kernels: 110 us -> 76.1 us
  waiting for transfers between devices: 86.3 us -> 95.4 us
    ppermute x4 -> x15, waiting for transfers between devices: 6.71 us -> 43.7 us  [the longest x9 40.6 us: across(): return lax.ppermute(x, 'dp', [(i, i ^ bits) for i in range(n)])]
    pallas_call x21 -> x20, Pallas kernels: 97.6 us -> 66.7 us  [the longest x16 46.2 us: call(): pl.pallas_call(placed(functools.partial(kernel, **static)), out_shape=[o...]
    ppermute x9 -> x3, waiting for transfers between devices: 31.6 us -> 5.53 us  [ahead(): return lax.ppermute(x, 'dp', [(i, (i + step) % n) for i in range(n)])]
    ppermute x9 -> x3, starting transfers between devices: 19.1 us -> 3.83 us  [ahead(): return lax.ppermute(x, 'dp', [(i, (i + step) % n) for i in range(n)])]
    ppermute x4 -> x15, starting transfers between devices: 7.14 us -> 19.3 us  [the longest x9 12.4 us: across(): return lax.ppermute(x, 'dp', [(i, i ^ bits) for i in range(n)])]
    all_to_all x8 -> x7, waiting for transfers between devices: 34.3 us -> 31.3 us  [swap(): return lax.all_to_all(x, axis, split_axis=0, concat_axis=0, tiled=True)]
    all_to_all x8 -> x7, starting transfers between devices: 33.8 us -> 36.4 us  [swap(): return lax.all_to_all(x, axis, split_axis=0, concat_axis=0, tiled=True)]
    unnamed x84 -> x54, local copies, waits for them, and re-layouts: 8.28 us -> 6.94 us
  transfers between devices with their start and end apart: 43 -> 47, of which waited for: 19 -> 21; matrix products, arithmetic and copies ran while one was open for 1% -> 1% of each run, Pallas kernels for 27% -> 21%
where the time goes in v4:
time: 272 us; the launch traced here: 271 us
  waiting for transfers between devices  95.4 us (35%)
  Pallas kernels  76.1 us (28%)
  starting transfers between devices  75.3 us (28%)
  blocking collectives  14.9 us (5%)
  local copies, waits for them, and re-layouts  8.51 us (3%)
    pallas_call x16, Pallas kernels, call(): pl.pallas_call(placed(functools.partial(kernel, **static)), out_shape=[o...  46.2 us
    ppermute x9, waiting for transfers between devices, across(): return lax.ppermute(x, 'dp', [(i, i ^ bits) for i in range(n)])  40.6 us
    all_to_all x7, starting transfers between devices, swap(): return lax.all_to_all(x, axis, split_axis=0, concat_axis=0, tiled=True)  36.4 us
    all_to_all x7, waiting for transfers between devices, swap(): return lax.all_to_all(x, axis, split_axis=0, concat_axis=0, tiled=True)  31.3 us
    pallas_call x4, Pallas kernels, expert_call(): pl.pallas_call(placed(functools.partial(expert_kernel, counts=(len(slots)...  20.4 us
    ppermute x22, starting transfers between devices, flip(): return lax.ppermute(x, 'expert', [(i, i ^ bits) for i in range(n)])  15.9 us
    all_to_all x1, blocking collectives, swap(): return lax.all_to_all(x, axis, split_axis=0, concat_axis=0, tiled=True)  14.9 us
    ppermute x22, waiting for transfers between devices, flip(): return lax.ppermute(x, 'expert', [(i, i ^ bits) for i in range(n)])  14.8 us
  transfers between devices with their start and end apart: 47, of which 21 were waited for; matrix products, arithmetic and copies ran while one was open for 1% of the time, Pallas kernels for 21%

profile of v4, /device:TPU:0, one launch (start us, length us, event | category | flops | bytes accessed | tf_op | source)
XLA Modules:
  0.0 271.1 jit_solution(7763990309420210533)
XLA Ops:
  2.4 6.3 %all-to-all-start.1 = ((bf16[4,32,896]{2,1,0:T(8,128)(2,1)}), bf16[4,32,896]{2,1,0:T(8,128)(2,1)S(1)}, u32[]{:S(2)}, u32[]{:S(2)}) async-start(bf16[4,32,896]{2,1,0:T(8,128)(2,1)} %weights_kernel.1), calls=%async_computation.1 | async-start | bytes 458752 | tf_op jit(solution)/shard_map/all_to_all | solution.py:62
  11.5 5.4 %all-to-all-done.1.refs_1_.refs_3_ = bf16[4,32,896]{2,1,0:T(8,128)(2,1)S(1)} async-done(((bf16[4,32,896]{2,1,0:T(8,128)(2,1)}), bf16[4,32,896]{2,1,0:T(8,128)(2,1)S(1)}, u32[]{:S(2)}, u32[]{:S(2)}) %all-to-all-start.1) | async-done | bytes 229408 | tf_op jit(solution)/shard_map/all_to_all | solution.py:62
  16.9 3.7 %all-to-all-start = ((bf16[8,24,1024]{2,1,0:T(8,128)(2,1)}), bf16[8,24,1024]{2,1,0:T(8,128)(2,1)S(1)}, u32[]{:S(2)}, u32[]{:S(2)}) async-start(bf16[8,24,1024]{2,1,0:T(8,128)(2,1)} %bitcast.42), calls=%async_computation | async-start | bytes 786432 | tf_op jit(solution)/shard_map/all_to_all | solution.py:62
  21.3 3.1 %collective-permute-start.8 = (bf16[128,1024]{1,0:T(8,128)(2,1)}, bf16[128,1024]{1,0:T(8,128)(2,1)S(1)}, u32[]{:S(2)}, u32[]{:S(2)}) collective-permute-start(bf16[128,1024]{1,0:T(8,128)(2,1)} %bitcast.34), channel_id=1, source_target_pairs={{0,16},{8,24},{16,0},{24,8},{1,17},{9,25},{17,1},{25,9},{2,18},{10... | collective-permute-start | bytes 786440 | tf_op jit(solution)/shard_map/ppermute | solution.py:71
  24.4 2.9 %collective-permute-start.5 = (bf16[4,32,896]{2,1,0:T(8,128)(2,1)S(1)}, bf16[4,32,896]{2,1,0:T(8,128)(2,1)S(1)}, u32[]{:S(2)}, u32[]{:S(2)}) collective-permute-start(bf16[4,32,896]{2,1,0:T(8,128)(2,1)S(1)} %all-to-all-done.1.refs_1_.refs_3_), channel_id=1, source_target_pairs={{0,6},{1,7},{2,4},{3,5},{4,2},{5,3},{6,0},{7,1},{8,14},{9,15},{10,... | collective-permute-start | bytes 688136 | tf_op jit(solution)/shard_map/ppermute | solution.py:58
  28.0 14.5 %collective-permute-done.8.refs_11_ = bf16[128,1024]{1,0:T(8,128)(2,1)S(1)} collective-permute-done((bf16[128,1024]{1,0:T(8,128)(2,1)}, bf16[128,1024]{1,0:T(8,128)(2,1)S(1)}, u32[]{:S(2)}, u32[]{:S(2)}) %collective-permute-start.8) | collective-permute-done | bytes 262176 | tf_op jit(solution)/shard_map/ppermute | solution.py:71
  45.3 3.9 %all-to-all-start.3 = ((bf16[4,32,1024]{2,1,0:T(8,128)(2,1)}), bf16[4,32,1024]{2,1,0:T(8,128)(2,1)S(1)}, u32[]{:S(2)}, u32[]{:S(2)}) async-start(bf16[4,32,1024]{2,1,0:T(8,128)(2,1)} %broadcast_in_dim.15), calls=%async_computation.3 | async-start | bytes 524288 | tf_op jit(solution)/shard_map/all_to_all | solution.py:62
  61.8 9.2 %attend_kernel.1 = (bf16[512,1024]{1,0:T(8,128)(2,1)}, bf16[512,768]{1,0:T(8,128)(2,1)}, bf16[4,512,512]{2,1,0:T(8,128)(2,1)}, bf16[4,128,256]{2,1,0:T(8,128)(2,...) custom-call(bf16[512,512]{1,0:T(8,128)(2,1)S(1)} %get-tuple-element.139.refs_0_, ...), custom_call_target="tpu_custom_call" | custom-call | tf_op jit(solution)/shard_map/attend_kernel/pallas_call | solution.py:40
  71.0 3.4 %all-to-all-start.2 = ((bf16[4,128,256]{2,1,0:T(8,128)(2,1)}), bf16[4,128,256]{2,1,0:T(8,128)(2,1)S(1)}, u32[]{:S(2)}, u32[]{:S(2)}) async-start(bf16[4,128,256]{2,1,0:T(8,128)(2,1)} %get-tuple-element.142), calls=%async_computation.2 | async-start | bytes 524288 | tf_op jit(solution)/shard_map/all_to_all | solution.py:62
  78.6 4.8 %all-to-all-done.2.refs_1_.refs_0_ = bf16[4,128,256]{2,1,0:T(8,128)(2,1)S(1)} async-done(((bf16[4,128,256]{2,1,0:T(8,128)(2,1)}), bf16[4,128,256]{2,1,0:T(8,128)(2,1)S(1)}, u32[]{:S(2)}, u32[]{:S(2)}) %all-to-all-start.2) | async-done | bytes 262176 | tf_op jit(solution)/shard_map/all_to_all | solution.py:62
  87.9 3.8 %all-to-all-start.4 = ((bf16[8,24,1024]{2,1,0:T(8,128)(2,1)}), bf16[8,24,1024]{2,1,0:T(8,128)(2,1)S(1)}, u32[]{:S(2)}, u32[]{:S(2)}) async-start(bf16[8,24,1024]{2,1,0:T(8,128)(2,1)} %bitcast.43), calls=%async_computation.4 | async-start | bytes 786432 | tf_op jit(solution)/shard_map/all_to_all | solution.py:62
  94.4 5.7 %all-to-all-done.4 = bf16[8,24,1024]{2,1,0:T(8,128)(2,1)S(1)} async-done(((bf16[8,24,1024]{2,1,0:T(8,128)(2,1)}), bf16[8,24,1024]{2,1,0:T(8,128)(2,1)S(1)}, u32[]{:S(2)}, u32[]{:S(2)}) %all-to-all-start.4) | async-done | bytes 393248 | tf_op jit(solution)/shard_map/all_to_all | solution.py:62
  101.9 2.9 %collective-permute-done.22.refs_8_ = bf16[144,1024]{1,0:T(8,128)(2,1)} collective-permute-done((bf16[144,1024]{1,0:T(8,128)(2,1)}, bf16[144,1024]{1,0:T(8,128)(2,1)}, u32[]{:S(2)}, u32[]{:S(2)}) %collective-permute-start.22) | collective-permute-done | bytes 294944 | tf_op jit(solution)/shard_map/ppermute | solution.py:82
  108.1 4.8 %expert_kernel.4 = (bf16[288,1024]{1,0:T(8,128)(2,1)}, bf16[144,1024]{1,0:T(8,128)(2,1)S(1)}, bf16[144,1024]{1,0:T(8,128)(2,1)S(1)}, bf16[144,1024]{1,0:T(8,128)...) custom-call(bf16[1024,128]{1,0:T(8,128)(2,1)S(1)} %get-tuple-element.143.refs_3_.refs_0_.refs_6_, ...), custom_call_target="tpu_custom_call" | custom-call | tf_op jit(solution)/shard_map/expert_kernel/pallas_call | solution.py:320
  112.9 3.2 %collective-permute-done.20.refs_5_ = bf16[144,1024]{1,0:T(8,128)(2,1)S(1)} collective-permute-done((bf16[144,1024]{1,0:T(8,128)(2,1)}, bf16[144,1024]{1,0:T(8,128)(2,1)S(1)}, u32[]{:S(2)}, u32[]{:S(2)}) %collective-permute-start.20) | collective-permute-done | bytes 294944 | tf_op jit(solution)/shard_map/ppermute | solution.py:71
  117.7 4.9 %expert_kernel.5 = (bf16[288,1024]{1,0:T(8,128)(2,1)}, bf16[144,1024]{1,0:T(8,128)(2,1)S(1)}, bf16[144,1024]{1,0:T(8,128)(2,1)S(1)}, bf16[144,1024]{1,0:T(8,128)...) custom-call(bf16[1024,128]{1,0:T(8,128)(2,1)S(1)} %get-tuple-element.143.refs_3_.refs_0_.refs_6_, ...), custom_call_target="tpu_custom_call" | custom-call | tf_op jit(solution)/shard_map/expert_kernel/pallas_call | solution.py:320
  125.4 4.9 %expert_kernel.6 = (bf16[288,1024]{1,0:T(8,128)(2,1)}, bf16[144,1024]{1,0:T(8,128)(2,1)S(1)}, bf16[144,1024]{1,0:T(8,128)(2,1)S(1)}, bf16[144,1024]{1,0:T(8,128)...) custom-call(bf16[1024,128]{1,0:T(8,128)(2,1)S(1)} %get-tuple-element.143.refs_3_.refs_0_.refs_6_, ...), custom_call_target="tpu_custom_call" | custom-call | tf_op jit(solution)/shard_map/expert_kernel/pallas_call | solution.py:320
  130.3 5.9 %expert_kernel.7 = (bf16[288,1024]{1,0:T(8,128)(2,1)}, bf16[144,1024]{1,0:T(8,128)(2,1)S(1)}, bf16[144,1024]{1,0:T(8,128)(2,1)S(1)}, bf16[144,1024]{1,0:T(8,128)...) custom-call(bf16[1024,128]{1,0:T(8,128)(2,1)S(1)} %get-tuple-element.143.refs_3_.refs_0_.refs_6_, ...), custom_call_target="tpu_custom_call" | custom-call | tf_op jit(solution)/shard_map/expert_kernel/pallas_call | solution.py:320
  138.4 7.3 %expert_grad_kernel.1 = (f32[1024,1024]{1,0:T(8,128)}, f32[1024,1024]{1,0:T(8,128)}, f32[1,1024]{1,0:T(1,128)}, f32[1,256]{1,0:T(1,128)}) custom-call(bf16[144,1024]{1,0:T(8,128)(2,1)S(1)} %get-tuple-element.156.refs_0_, bf16[144,1024]{1,0:T(8,128)(2,1)S(1)} %get-tuple-element.174.refs_1_, bf16[144,1024]{1,0:T(8,128)(2,1)S(1)} %get-tuple-element.175.refs_2_, ...), custom_call_target="tpu_custom_call" | custom-call | tf_op jit(solution)/shard_map/expert_grad_kernel/pallas_call | solution.py:373
  145.7 7.5 %collective-permute-done.27.refs_3_ = bf16[288,1024]{1,0:T(8,128)(2,1)S(1)} collective-permute-done((bf16[288,1024]{1,0:T(8,128)(2,1)}, bf16[288,1024]{1,0:T(8,128)(2,1)S(1)}, u32[]{:S(2)}, u32[]{:S(2)}) %collective-permute-start.27) | collective-permute-done | bytes 589856 | tf_op jit(solution)/shard_map/ppermute | solution.py:71
  153.1 15.4 %collective-permute-done.26.refs_2_ = bf16[288,1024]{1,0:T(8,128)(2,1)S(1)} collective-permute-done((bf16[288,1024]{1,0:T(8,128)(2,1)}, bf16[288,1024]{1,0:T(8,128)(2,1)S(1)}, u32[]{:S(2)}, u32[]{:S(2)}) %collective-permute-start.26) | collective-permute-done | bytes 589856 | tf_op jit(solution)/shard_map/ppermute | solution.py:71
  171.1 14.9 %all_to_all.40 = bf16[8,40,1024]{2,1,0:T(8,128)(2,1)S(1)} all-to-all(bf16[8,40,1024]{2,1,0:T(8,128)(2,1)} %bitcast.32), channel_id=1, replica_groups=mesh['dp'=4,'expert'=8] {'expert'}, dimensions={0} | all-to-all | bytes 1310720 | tf_op jit(solution)/shard_map/all_to_all | solution.py:62
  186.0 3.6 %combine_kernel.1 = (bf16[128,1024]{1,0:T(8,128)(2,1)}, f32[128,1024]{1,0:T(8,128)}, bf16[128,1024]{1,0:T(8,128)(2,1)S(1)}, bf16[4,128,256]{2,1,0:T(8,128)(2,1)}...) custom-call(bf16[320,1024]{1,0:T(8,128)(2,1)S(1)} %bitcast.29, s32[128,1]{1,0:T(8,128)} %get-tuple-element.205.refs_1_, ...), custom_call_target="tpu_custom_call" | custom-call | tf_op jit(solution)/shard_map/combine_kernel/pallas_call | solution.py:40
  192.5 10.9 %all-to-all-start.6 = ((bf16[4,128,256]{2,1,0:T(8,128)(2,1)}), bf16[4,128,256]{2,1,0:T(8,128)(2,1)S(1)}, u32[]{:S(2)}, u32[]{:S(2)}) async-start(bf16[4,128,256]{2,1,0:T(8,128)(2,1)} %get-tuple-element.211), calls=%async_computation.6 | async-start | bytes 524288 | tf_op jit(solution)/shard_map/all_to_all | solution.py:62
  204.4 8.5 %all-to-all-done.6.refs_0_ = bf16[4,128,256]{2,1,0:T(8,128)(2,1)S(1)} async-done(((bf16[4,128,256]{2,1,0:T(8,128)(2,1)}), bf16[4,128,256]{2,1,0:T(8,128)(2,1)S(1)}, u32[]{:S(2)}, u32[]{:S(2)}) %all-to-all-start.6) | async-done | bytes 262176 | tf_op jit(solution)/shard_map/all_to_all | solution.py:62
  216.4 9.2 %attend_back_kernel.1 = (bf16[512,768]{1,0:T(8,128)(2,1)S(1)}, bf16[4,128,1024]{2,1,0:T(8,128)(2,1)}) custom-call(bf16[4,128,256]{2,1,0:T(8,128)(2,1)S(1)} %all-to-all-done.6.refs_0_, bf16[4,512,512]{2,1,0:T(8,128)(2,1)} %get-tuple-element.220.refs_1_, bf16[512,768]{1,0:T(8,128)(2,1)} %get-tuple-element.221.refs_2_, bf16[4,32,896]{2,1,0:T(8,128)(2,1)} %copy-done.17, ...), custom_call_target="tpu_custom_call" | custom-call | tf_op jit(solution)/shard_map/attend_back_kernel/pallas_call | solution.py:40
  225.7 4.0 %qkv_grad_kernel.1 = (bf16[4,4,32,896]{3,2,1,0:T(8,128)(2,1)}, bf16[4,4,32,896]{3,2,1,0:T(8,128)(2,1)S(1)}) custom-call(bf16[512,1024]{1,0:T(8,128)(2,1)} %get-tuple-element.210.refs_0_, f32[8,1024]{1,0:T(8,128)S(1)} %get-tuple-element.144.refs_4_.refs_7_.refs_1_.refs_2_, bf16[512,768]{1,0:T(8,128)(2,1)S(1)} %get-tuple-element.227.refs_2_, ...), custom_call_target="tpu_custom_call" | custom-call | tf_op jit(solution)/shard_map/qkv_grad_kernel/pallas_call | solution.py:40
  229.7 4.3 %all-to-all-start.7 = ((bf16[4,128,1024]{2,1,0:T(8,128)(2,1)}), bf16[4,128,1024]{2,1,0:T(8,128)(2,1)S(1)}, u32[]{:S(2)}, u32[]{:S(2)}) async-start(bf16[4,128,1024]{2,1,0:T(8,128)(2,1)} %get-tuple-element.233.refs_3_), calls=%async_computation.7 | async-start | bytes 2097152 | tf_op jit(solution)/shard_map/all_to_all | solution.py:62
  241.1 5.2 %collective-permute-done.34.refs_1_ = bf16[4,32,896]{2,1,0:T(8,128)(2,1)S(1)} collective-permute-done((bf16[4,32,896]{2,1,0:T(8,128)(2,1)}, bf16[4,32,896]{2,1,0:T(8,128)(2,1)S(1)}, u32[]{:S(2)}, u32[]{:S(2)}) %collective-permute-start.34) | collective-permute-done | bytes 229408 | tf_op jit(solution)/shard_map/ppermute | solution.py:58
  246.2 5.3 %collective-permute-done.35.refs_2_ = bf16[4,32,896]{2,1,0:T(8,128)(2,1)S(1)} collective-permute-done((bf16[4,32,896]{2,1,0:T(8,128)(2,1)}, bf16[4,32,896]{2,1,0:T(8,128)(2,1)S(1)}, u32[]{:S(2)}, u32[]{:S(2)}) %collective-permute-start.35) | collective-permute-done | bytes 229408 | tf_op jit(solution)/shard_map/ppermute | solution.py:58
  252.7 5.7 %all-to-all-done.7.refs_0_ = bf16[4,128,1024]{2,1,0:T(8,128)(2,1)S(1)} async-done(((bf16[4,128,1024]{2,1,0:T(8,128)(2,1)}), bf16[4,128,1024]{2,1,0:T(8,128)(2,1)S(1)}, u32[]{:S(2)}, u32[]{:S(2)}) %all-to-all-start.7) | async-done | bytes 1048608 | tf_op jit(solution)/shard_map/all_to_all | solution.py:62
  266.8 3.4 %collective-permute-done.38.refs_2_ = bf16[32,1920]{1,0:T(8,128)(2,1)S(1)} collective-permute-done((bf16[32,1920]{1,0:T(8,128)(2,1)}, bf16[32,1920]{1,0:T(8,128)(2,1)S(1)}, u32[]{:S(2)}, u32[]{:S(2)}) %collective-permute-start.38) | collective-permute-done | bytes 122912 | tf_op jit(solution)/shard_map/ppermute | solution.py:53
  (140 shorter events, 71.7 us)
Async XLA Ops:
  2.4 14.5 %all-to-all-start.1 = ((bf16[4,32,896]{2,1,0:T(8,128)(2,1)}), bf16[4,32,896]{2,1,0:T(8,128)(2,1)S(1)}, u32[]{:S(2)}, u32[]{:S(2)}) async-start(bf16[4,32,896]{2,1,0:T(8,128)(2,1)} %weights_kernel.1), calls=%async_computation.1 | async-start | bytes 458752 | tf_op jit(solution)/shard_map/all_to_all | solution.py:62
  16.9 26.8 %all-to-all-start = ((bf16[8,24,1024]{2,1,0:T(8,128)(2,1)}), bf16[8,24,1024]{2,1,0:T(8,128)(2,1)S(1)}, u32[]{:S(2)}, u32[]{:S(2)}) async-start(bf16[8,24,1024]{2,1,0:T(8,128)(2,1)} %bitcast.42), calls=%async_computation | async-start | bytes 786432 | tf_op jit(solution)/shard_map/all_to_all | solution.py:62
  21.3 21.1 %collective-permute-start.8 = (bf16[128,1024]{1,0:T(8,128)(2,1)}, bf16[128,1024]{1,0:T(8,128)(2,1)S(1)}, u32[]{:S(2)}, u32[]{:S(2)}) collective-permute-start(bf16[128,1024]{1,0:T(8,128)(2,1)} %bitcast.34), channel_id=1, source_target_pairs={{0,16},{8,24},{16,0},{24,8},{1,17},{9,25},{17,1},{25,9},{2,18},{10... | collective-permute-start | bytes 786440 | tf_op jit(solution)/shard_map/ppermute | solution.py:71
  24.4 24.8 %collective-permute-start.7 = (bf16[128,1024]{1,0:T(8,128)(2,1)}, bf16[128,1024]{1,0:T(8,128)(2,1)S(1)}, u32[]{:S(2)}, u32[]{:S(2)}) collective-permute-start(bf16[128,1024]{1,0:T(8,128)(2,1)} %bitcast.35), channel_id=1, source_target_pairs={{0,8},{8,0},{16,24},{24,16},{1,9},{9,1},{17,25},{25,17},{2,10},{10... | collective-permute-start | bytes 786440 | tf_op jit(solution)/shard_map/ppermute | solution.py:71
  24.4 25.6 %collective-permute-start.5 = (bf16[4,32,896]{2,1,0:T(8,128)(2,1)S(1)}, bf16[4,32,896]{2,1,0:T(8,128)(2,1)S(1)}, u32[]{:S(2)}, u32[]{:S(2)}) collective-permute-start(bf16[4,32,896]{2,1,0:T(8,128)(2,1)S(1)} %all-to-all-done.1.refs_1_.refs_3_), channel_id=1, source_target_pairs={{0,6},{1,7},{2,4},{3,5},{4,2},{5,3},{6,0},{7,1},{8,14},{9,15},{10,... | collective-permute-start | bytes 688136 | tf_op jit(solution)/shard_map/ppermute | solution.py:58
  27.3 22.6 %collective-permute-start.3 = (bf16[4,32,896]{2,1,0:T(8,128)(2,1)S(1)}, bf16[4,32,896]{2,1,0:T(8,128)(2,1)S(1)}, u32[]{:S(2)}, u32[]{:S(2)}) collective-permute-start(bf16[4,32,896]{2,1,0:T(8,128)(2,1)S(1)} %all-to-all-done.1.refs_1_.refs_3_), channel_id=1, source_target_pairs={{0,4},{1,5},{2,6},{3,7},{4,0},{5,1},{6,2},{7,3},{8,12},{9,13},{10,... | collective-permute-start | bytes 688136 | tf_op jit(solution)/shard_map/ppermute | solution.py:58
  27.9 22.6 %collective-permute-start.1 = (bf16[4,32,896]{2,1,0:T(8,128)(2,1)S(1)}, bf16[4,32,896]{2,1,0:T(8,128)(2,1)S(1)}, u32[]{:S(2)}, u32[]{:S(2)}) collective-permute-start(bf16[4,32,896]{2,1,0:T(8,128)(2,1)S(1)} %all-to-all-done.1.refs_1_.refs_3_), channel_id=1, source_target_pairs={{0,2},{1,3},{2,0},{3,1},{4,6},{5,7},{6,4},{7,5},{8,10},{9,11},{10,... | collective-permute-start | bytes 688136 | tf_op jit(solution)/shard_map/ppermute | solution.py:58
  45.3 12.8 %all-to-all-start.3 = ((bf16[4,32,1024]{2,1,0:T(8,128)(2,1)}), bf16[4,32,1024]{2,1,0:T(8,128)(2,1)S(1)}, u32[]{:S(2)}, u32[]{:S(2)}) async-start(bf16[4,32,1024]{2,1,0:T(8,128)(2,1)} %broadcast_in_dim.15), calls=%async_computation.3 | async-start | bytes 524288 | tf_op jit(solution)/shard_map/all_to_all | solution.py:62
  52.6 18.4 %collective-permute-start.12 = (bf16[144,1024]{1,0:T(8,128)(2,1)}, bf16[144,1024]{1,0:T(8,128)(2,1)S(1)}, u32[]{:S(2)}, u32[]{:S(2)}) collective-permute-start(bf16[144,1024]{1,0:T(8,128)(2,1)} %pack_kernel.2.refs_6_), channel_id=1, source_target_pairs={{0,16},{8,24},{16,0},{24,8},{1,17},{9,25},{17,1},{25,9},{2,18},{10... | collective-permute-start | bytes 884744 | tf_op jit(solution)/shard_map/ppermute | solution.py:71
  55.3 15.7 %collective-permute-start.11 = (bf16[144,1024]{1,0:T(8,128)(2,1)}, bf16[144,1024]{1,0:T(8,128)(2,1)S(1)}, u32[]{:S(2)}, u32[]{:S(2)}) collective-permute-start(bf16[144,1024]{1,0:T(8,128)(2,1)} %pack_kernel.2.refs_6_), channel_id=1, source_target_pairs={{0,8},{8,0},{16,24},{24,16},{1,9},{9,1},{17,25},{25,17},{2,10},{10... | collective-permute-start | bytes 884744 | tf_op jit(solution)/shard_map/ppermute | solution.py:71
  58.1 16.4 %collective-permute-start.18 = (bf16[4,32,1024]{2,1,0:T(8,128)(2,1)S(1)}, bf16[4,32,1024]{2,1,0:T(8,128)(2,1)S(1)}, u32[]{:S(2)}, u32[]{:S(2)}) collective-permute-start(bf16[4,32,1024]{2,1,0:T(8,128)(2,1)S(1)} %all-to-all-done.3.refs_0_), channel_id=1, source_target_pairs={{0,6},{1,7},{2,4},{3,5},{4,2},{5,3},{6,0},{7,1},{8,14},{9,15},{10,... | collective-permute-start | bytes 786440 | tf_op jit(solution)/shard_map/ppermute | solution.py:58
  60.4 14.6 %collective-permute-start.16 = (bf16[4,32,1024]{2,1,0:T(8,128)(2,1)S(1)}, bf16[4,32,1024]{2,1,0:T(8,128)(2,1)S(1)}, u32[]{:S(2)}, u32[]{:S(2)}) collective-permute-start(bf16[4,32,1024]{2,1,0:T(8,128)(2,1)S(1)} %all-to-all-done.3.refs_0_), channel_id=1, source_target_pairs={{0,4},{1,5},{2,6},{3,7},{4,0},{5,1},{6,2},{7,3},{8,12},{9,13},{10,... | collective-permute-start | bytes 786440 | tf_op jit(solution)/shard_map/ppermute | solution.py:58
  61.0 14.1 %collective-permute-start.14 = (bf16[4,32,1024]{2,1,0:T(8,128)(2,1)S(1)}, bf16[4,32,1024]{2,1,0:T(8,128)(2,1)S(1)}, u32[]{:S(2)}, u32[]{:S(2)}) collective-permute-start(bf16[4,32,1024]{2,1,0:T(8,128)(2,1)S(1)} %all-to-all-done.3.refs_0_), channel_id=1, source_target_pairs={{0,2},{1,3},{2,0},{3,1},{4,6},{5,7},{6,4},{7,5},{8,10},{9,11},{10,... | collective-permute-start | bytes 786440 | tf_op jit(solution)/shard_map/ppermute | solution.py:58
  71.0 12.4 %all-to-all-start.2 = ((bf16[4,128,256]{2,1,0:T(8,128)(2,1)}), bf16[4,128,256]{2,1,0:T(8,128)(2,1)S(1)}, u32[]{:S(2)}, u32[]{:S(2)}) async-start(bf16[4,128,256]{2,1,0:T(8,128)(2,1)} %get-tuple-element.142), calls=%async_computation.2 | async-start | bytes 524288 | tf_op jit(solution)/shard_map/all_to_all | solution.py:62
  87.9 12.1 %all-to-all-start.4 = ((bf16[8,24,1024]{2,1,0:T(8,128)(2,1)}), bf16[8,24,1024]{2,1,0:T(8,128)(2,1)S(1)}, u32[]{:S(2)}, u32[]{:S(2)}) async-start(bf16[8,24,1024]{2,1,0:T(8,128)(2,1)} %bitcast.43), calls=%async_computation.4 | async-start | bytes 786432 | tf_op jit(solution)/shard_map/all_to_all | solution.py:62
  93.1 11.7 %collective-permute-start.22 = (bf16[144,1024]{1,0:T(8,128)(2,1)}, bf16[144,1024]{1,0:T(8,128)(2,1)}, u32[]{:S(2)}, u32[]{:S(2)}) collective-permute-start(bf16[144,1024]{1,0:T(8,128)(2,1)} %copy-done.11), channel_id=1, source_target_pairs={{8,0},{16,24},{9,1},{17,25},{10,2},{18,26},{11,3},{19,27},{12,4},{... | collective-permute-start | bytes 884744 | tf_op jit(solution)/shard_map/ppermute | solution.py:82
  101.9 14.2 %collective-permute-start.20 = (bf16[144,1024]{1,0:T(8,128)(2,1)}, bf16[144,1024]{1,0:T(8,128)(2,1)S(1)}, u32[]{:S(2)}, u32[]{:S(2)}) collective-permute-start(bf16[144,1024]{1,0:T(8,128)(2,1)} %pack_kernel.3.refs_5_), channel_id=1, source_target_pairs={{0,16},{8,24},{16,0},{24,8},{1,17},{9,25},{17,1},{25,9},{2,18},{10... | collective-permute-start | bytes 884744 | tf_op jit(solution)/shard_map/ppermute | solution.py:71
  104.8 20.6 %collective-permute-start.25 = (bf16[144,1024]{1,0:T(8,128)(2,1)}, bf16[144,1024]{1,0:T(8,128)(2,1)S(1)}, u32[]{:S(2)}, u32[]{:S(2)}) collective-permute-start(bf16[144,1024]{1,0:T(8,128)(2,1)} %pack_kernel.3.refs_5_), channel_id=1, source_target_pairs={{0,8},{8,0},{16,24},{24,16},{1,9},{9,1},{17,25},{25,17},{2,10},{10... | collective-permute-start | bytes 884744 | tf_op jit(solution)/shard_map/ppermute | solution.py:71
  104.8 25.5 %collective-permute-start.23 = (bf16[144,1024]{1,0:T(8,128)(2,1)}, bf16[144,1024]{1,0:T(8,128)(2,1)S(1)}, u32[]{:S(2)}, u32[]{:S(2)}) collective-permute-start(bf16[144,1024]{1,0:T(8,128)(2,1)} %pack_kernel.3.refs_5_), channel_id=1, source_target_pairs={{8,16},{16,8},{9,17},{17,9},{10,18},{18,10},{11,19},{19,11},{12,20... | collective-permute-start | bytes 884744 | tf_op jit(solution)/shard_map/ppermute | solution.py:79
  116.1 14.2 %collective-permute-start.24 = (bf16[144,1024]{1,0:T(8,128)(2,1)S(1)}, bf16[144,1024]{1,0:T(8,128)(2,1)S(1)}, u32[]{:S(2)}, u32[]{:S(2)}) collective-permute-start(bf16[144,1024]{1,0:T(8,128)(2,1)S(1)} %collective-permute-done.20.refs_5_), channel_id=1, source_target_pairs={{8,0},{16,24},{9,1},{17,25},{10,2},{18,26},{11,3},{19,27},{12,4},{... | collective-permute-start | bytes 884744 | tf_op jit(solution)/shard_map/ppermute | solution.py:82
  122.6 30.6 %collective-permute-start.27 = (bf16[288,1024]{1,0:T(8,128)(2,1)}, bf16[288,1024]{1,0:T(8,128)(2,1)S(1)}, u32[]{:S(2)}, u32[]{:S(2)}) collective-permute-start(bf16[288,1024]{1,0:T(8,128)(2,1)} %get-tuple-element.160), channel_id=1, source_target_pairs={{0,16},{8,24},{16,0},{24,8},{1,17},{9,25},{17,1},{25,9},{2,18},{10... | collective-permute-start | bytes 1769480 | tf_op jit(solution)/shard_map/ppermute | solution.py:71
  130.3 38.2 %collective-permute-start.26 = (bf16[288,1024]{1,0:T(8,128)(2,1)}, bf16[288,1024]{1,0:T(8,128)(2,1)S(1)}, u32[]{:S(2)}, u32[]{:S(2)}) collective-permute-start(bf16[288,1024]{1,0:T(8,128)(2,1)} %get-tuple-element.168), channel_id=1, source_target_pairs={{0,8},{8,0},{16,24},{24,16},{1,9},{9,1},{17,25},{25,17},{2,10},{10... | collective-permute-start | bytes 1769480 | tf_op jit(solution)/shard_map/ppermute | solution.py:71
  136.2 32.3 %collective-permute-start.28 = (bf16[288,1024]{1,0:T(8,128)(2,1)}, bf16[288,1024]{1,0:T(8,128)(2,1)S(1)}, u32[]{:S(2)}, u32[]{:S(2)}) collective-permute-start(bf16[288,1024]{1,0:T(8,128)(2,1)} %get-tuple-element.200), channel_id=1, source_target_pairs={{0,24},{8,16},{16,8},{24,0},{1,25},{9,17},{17,9},{25,1},{2,26},{10... | collective-permute-start | bytes 1769480 | tf_op jit(solution)/shard_map/ppermute | solution.py:71
  192.5 10.9 %collective-permute-start.29 = (bf16[4,4,32,1024]{3,2,1,0:T(8,128)(2,1)}, bf16[4,4,32,1024]{3,2,1,0:T(8,128)(2,1)S(1)}, u32[]{:S(2)}, u32[]{:S(2)}) collective-permute-start(bf16[4,4,32,1024]{3,2,1,0:T(8,128)(2,1)} %get-tuple-element.214), channel_id=1, source_target_pairs={{0,1},{1,0},{2,3},{3,2},{4,5},{5,4},{6,7},{7,6},{8,9},{9,8},{10,11... | collective-permute-start | bytes 3145736 | tf_op jit(solution)/shard_map/ppermute | solution.py:58
  192.5 20.5 %all-to-all-start.6 = ((bf16[4,128,256]{2,1,0:T(8,128)(2,1)}), bf16[4,128,256]{2,1,0:T(8,128)(2,1)S(1)}, u32[]{:S(2)}, u32[]{:S(2)}) async-start(bf16[4,128,256]{2,1,0:T(8,128)(2,1)} %get-tuple-element.211), calls=%async_computation.6 | async-start | bytes 524288 | tf_op jit(solution)/shard_map/all_to_all | solution.py:62
  213.0 12.7 %collective-permute-start.30 = (bf16[4,32,1024]{2,1,0:T(8,128)(2,1)}, bf16[4,32,1024]{2,1,0:T(8,128)(2,1)S(1)}, u32[]{:S(2)}, u32[]{:S(2)}) collective-permute-start(bf16[4,32,1024]{2,1,0:T(8,128)(2,1)} %get-tuple-element.224), channel_id=1, source_target_pairs={{0,2},{1,3},{2,0},{3,1},{4,6},{5,7},{6,4},{7,5},{8,10},{9,11},{10,... | collective-permute-start | bytes 786440 | tf_op jit(solution)/shard_map/ppermute | solution.py:58
  213.5 12.1 %collective-permute-start.31 = (bf16[4,32,1024]{2,1,0:T(8,128)(2,1)}, bf16[4,32,1024]{2,1,0:T(8,128)(2,1)S(1)}, u32[]{:S(2)}, u32[]{:S(2)}) collective-permute-start(bf16[4,32,1024]{2,1,0:T(8,128)(2,1)} %get-tuple-element.225), channel_id=1, source_target_pairs={{0,4},{1,5},{2,6},{3,7},{4,0},{5,1},{6,2},{7,3},{8,12},{9,13},{10,... | collective-permute-start | bytes 786440 | tf_op jit(solution)/shard_map/ppermute | solution.py:58
  214.1 11.6 %collective-permute-start.32 = (bf16[4,32,1024]{2,1,0:T(8,128)(2,1)}, bf16[4,32,1024]{2,1,0:T(8,128)(2,1)S(1)}, u32[]{:S(2)}, u32[]{:S(2)}) collective-permute-start(bf16[4,32,1024]{2,1,0:T(8,128)(2,1)} %get-tuple-element.226), channel_id=1, source_target_pairs={{0,6},{1,7},{2,4},{3,5},{4,2},{5,3},{6,0},{7,1},{8,14},{9,15},{10,... | collective-permute-start | bytes 786440 | tf_op jit(solution)/shard_map/ppermute | solution.py:58
  229.7 28.7 %all-to-all-start.7 = ((bf16[4,128,1024]{2,1,0:T(8,128)(2,1)}), bf16[4,128,1024]{2,1,0:T(8,128)(2,1)S(1)}, u32[]{:S(2)}, u32[]{:S(2)}) async-start(bf16[4,128,1024]{2,1,0:T(8,128)(2,1)} %get-tuple-element.233.refs_3_), calls=%async_computation.7 | async-start | bytes 2097152 | tf_op jit(solution)/shard_map/all_to_all | solution.py:62
  239.0 12.5 %collective-permute-start.35 = (bf16[4,32,896]{2,1,0:T(8,128)(2,1)}, bf16[4,32,896]{2,1,0:T(8,128)(2,1)S(1)}, u32[]{:S(2)}, u32[]{:S(2)}) collective-permute-start(bf16[4,32,896]{2,1,0:T(8,128)(2,1)} %get-tuple-element.238), channel_id=1, source_target_pairs={{0,4},{1,5},{2,6},{3,7},{4,0},{5,1},{6,2},{7,3},{8,12},{9,13},{10,... | collective-permute-start | bytes 688136 | tf_op jit(solution)/shard_map/ppermute | solution.py:58
  239.6 11.9 %collective-permute-start.36 = (bf16[4,32,896]{2,1,0:T(8,128)(2,1)}, bf16[4,32,896]{2,1,0:T(8,128)(2,1)S(1)}, u32[]{:S(2)}, u32[]{:S(2)}) collective-permute-start(bf16[4,32,896]{2,1,0:T(8,128)(2,1)} %get-tuple-element.239), channel_id=1, source_target_pairs={{0,6},{1,7},{2,4},{3,5},{4,2},{5,3},{6,0},{7,1},{8,14},{9,15},{10,... | collective-permute-start | bytes 688136 | tf_op jit(solution)/shard_map/ppermute | solution.py:58
  258.5 11.8 %collective-permute-start.38 = (bf16[32,1920]{1,0:T(8,128)(2,1)}, bf16[32,1920]{1,0:T(8,128)(2,1)S(1)}, u32[]{:S(2)}, u32[]{:S(2)}) collective-permute-start(bf16[32,1920]{1,0:T(8,128)(2,1)} %get-tuple-element.252), channel_id=1, source_target_pairs={{0,16},{8,24},{16,0},{24,8},{1,17},{9,25},{17,1},{25,9},{2,18},{10... | collective-permute-start | bytes 368648 | tf_op jit(solution)/shard_map/ppermute | solution.py:53
  (42 other events, 420.3 us)

commit v5 on v4

--- a/solution.py
+++ b/solution.py
@@ -249,13 +249,15 @@
         q = packed[:, h * head_dim : (h + 1) * head_dim]
         k = packed[:, part + h * head_dim : part + (h + 1) * head_dim]
         vt = packed[:, 2 * part + h * head_dim : 2 * part + (h + 1) * head_dim].T
-        for i in range(n_dp):
-            lo, hi = i * rows, (i + 1) * rows
+        for i in range(0, n_dp, 2):
+            lo, hi = i * rows, (i + 2) * rows
             s = mm(k[:hi], q[lo:hi], 1, 1) * scale + bias[:hi, lo:hi].astype(F32)
             p = jnp.exp(s - jnp.max(s, axis=0, keepdims=True))
             p = (p * (1.0 / jnp.sum(p, axis=0, keepdims=True))).astype(BF)
             probs[h, :hi, lo:hi] = p
-            attended[i, :, h * head_dim : (h + 1) * head_dim] = mm(vt[:, :hi], p).T.astype(BF)
+            out = mm(vt[:, :hi], p).T.astype(BF)
+            attended[i, :, h * head_dim : (h + 1) * head_dim] = out[:rows]
+            attended[i + 1, :, h * head_dim : (h + 1) * head_dim] = out[rows:]
 
 
 def mix_kernel(me, tokens, attended, proj, small, vectors, tableT, mixed, normed, p, sent, *, experts):
@@ -489,16 +491,16 @@
         q, k, v = packed[:, a:b], packed[:, part + a : part + b], packed[:, 2 * part + a : 2 * part + b]
         kt = k.T
         g = jnp.concatenate([d_att[i, :, a:b] for i in range(n_dp)], axis=0)
-        for i in range(n_dp):
-            lo, hi = i * rows, (i + 1) * rows
+        for i in range(0, n_dp, 2):
+            lo, hi = i * rows, (i + 2) * rows
             dp = mm(v[:hi], g[lo:hi], 1, 1)
             p = probs[h, :hi, lo:hi].astype(F32)
             delta = jnp.sum(p * dp, axis=0, keepdims=True)
             ds = (p * (dp - delta)).astype(BF)
             d_scores[:hi, lo:hi] = ds
             d_packed[lo:hi, a:b] = (mm(kt[:, :hi], ds).T * scale).astype(BF)
-        for i in range(n_dp):
-            lo, hi = i * rows, (i + 1) * rows
+        for i in range(0, n_dp, 2):
+            lo, hi = i * rows, (i + 2) * rows
             d_packed[lo:hi, part + a : part + b] = (mm(d_scores[lo:hi, lo:], q[lo:]) * scale).astype(BF)
             d_packed[lo:hi, 2 * part + a : 2 * part + b] = mm(probs[h, lo:hi, lo:], g[lo:]).astype(BF)
     for i in range(n_dp):
@@ -735,7 +737,8 @@
         chip_sum_kernel, [pltpu.HBM((own, cols + width), BF)] * n_dp, *qkv_chips, *proj_chips,
         scratch=[pltpu.VMEM((n_dp, own, cols + width), BF)], n_dp=n_dp,
     )
-    d_own, *summed = lax.optimization_barrier((d_own, *summed))
+    summed = along(summed)
+    d_own, summed[1] = lax.optimization_barrier((d_own, summed[1]))
     owned_qkv, owned_proj, owned_router, owned_gains, owned_biases = call(
         weights_end_kernel,
         [
@@ -745,7 +748,7 @@
             pltpu.HBM((2, own), F32),
             pltpu.HBM((5, own), F32),
         ],
-        *along(summed),
+        *summed,
         scratch=[pltpu.VMEM((128, 128), F32), pltpu.VMEM((n_dp, own, cols + width), BF)],
     )
     grad_tokens = call(tokens_end_kernel, [pltpu.HBM((rows, width), F32)], d_own, *far(x), vectors, *far(d_mixed))[0]

time: 272 us -> 270 us (level)
  waiting for transfers between devices: 95.4 us -> 92 us
    ppermute x3, waiting for transfers between devices: 5.53 us -> 2.51 us  [ahead(): return lax.ppermute(x, 'dp', [(i, (i + step) % n) for i in range(n)])]
  transfers between devices with their start and end apart: 47 -> 47, of which waited for: 21 -> 23; matrix products, arithmetic and copies ran while one was open for 1% -> 1% of each run, Pallas kernels for 21% -> 21%
where the time goes in v5:
time: 270 us; the launch traced here: 268 us
  waiting for transfers between devices  92 us (34%)
  starting transfers between devices  77.7 us (29%)
  Pallas kernels  74.4 us (28%)
  blocking collectives  14.9 us (6%)
  local copies, waits for them, and re-layouts  8.51 us (3%)
    pallas_call x16, Pallas kernels, call(): pl.pallas_call(placed(functools.partial(kernel, **static)), out_shape=[o...  44.5 us
    ppermute x9, waiting for transfers between devices, across(): return lax.ppermute(x, 'dp', [(i, i ^ bits) for i in range(n)])  41.2 us
    all_to_all x7, starting transfers between devices, swap(): return lax.all_to_all(x, axis, split_axis=0, concat_axis=0, tiled=True)  36.8 us
    all_to_all x7, waiting for transfers between devices, swap(): return lax.all_to_all(x, axis, split_axis=0, concat_axis=0, tiled=True)  29.8 us
    pallas_call x4, Pallas kernels, expert_call(): pl.pallas_call(placed(functools.partial(expert_kernel, counts=(len(slots)...  20.4 us
    ppermute x22, starting transfers between devices, flip(): return lax.ppermute(x, 'expert', [(i, i ^ bits) for i in range(n)])  15.8 us
    ppermute x22, waiting for transfers between devices, flip(): return lax.ppermute(x, 'expert', [(i, i ^ bits) for i in range(n)])  15.4 us
    all_to_all x1, blocking collectives, swap(): return lax.all_to_all(x, axis, split_axis=0, concat_axis=0, tiled=True)  14.9 us
  transfers between devices with their start and end apart: 47, of which 23 were waited for; matrix products, arithmetic and copies ran while one was open for 1% of the time, Pallas kernels for 21%

profile of v5, /device:TPU:0, one launch (start us, length us, event | category | flops | bytes accessed | tf_op | source)
XLA Modules:
  0.0 268.3 jit_solution(12485510422884244835)
XLA Ops:
  2.4 6.3 %all-to-all-start.1 = ((bf16[4,32,896]{2,1,0:T(8,128)(2,1)}), bf16[4,32,896]{2,1,0:T(8,128)(2,1)S(1)}, u32[]{:S(2)}, u32[]{:S(2)}) async-start(bf16[4,32,896]{2,1,0:T(8,128)(2,1)} %weights_kernel.1), calls=%async_computation.1 | async-start | bytes 458752 | tf_op jit(solution)/shard_map/all_to_all | solution.py:62
  11.5 5.4 %all-to-all-done.1.refs_1_.refs_3_ = bf16[4,32,896]{2,1,0:T(8,128)(2,1)S(1)} async-done(((bf16[4,32,896]{2,1,0:T(8,128)(2,1)}), bf16[4,32,896]{2,1,0:T(8,128)(2,1)S(1)}, u32[]{:S(2)}, u32[]{:S(2)}) %all-to-all-start.1) | async-done | bytes 229408 | tf_op jit(solution)/shard_map/all_to_all | solution.py:62
  16.9 3.7 %all-to-all-start = ((bf16[8,24,1024]{2,1,0:T(8,128)(2,1)}), bf16[8,24,1024]{2,1,0:T(8,128)(2,1)S(1)}, u32[]{:S(2)}, u32[]{:S(2)}) async-start(bf16[8,24,1024]{2,1,0:T(8,128)(2,1)} %bitcast.42), calls=%async_computation | async-start | bytes 786432 | tf_op jit(solution)/shard_map/all_to_all | solution.py:62
  21.3 3.1 %collective-permute-start.8 = (bf16[128,1024]{1,0:T(8,128)(2,1)}, bf16[128,1024]{1,0:T(8,128)(2,1)S(1)}, u32[]{:S(2)}, u32[]{:S(2)}) collective-permute-start(bf16[128,1024]{1,0:T(8,128)(2,1)} %bitcast.34), channel_id=1, source_target_pairs={{0,16},{8,24},{16,0},{24,8},{1,17},{9,25},{17,1},{25,9},{2,18},{10... | collective-permute-start | bytes 786440 | tf_op jit(solution)/shard_map/ppermute | solution.py:71
  24.4 2.9 %collective-permute-start.5 = (bf16[4,32,896]{2,1,0:T(8,128)(2,1)S(1)}, bf16[4,32,896]{2,1,0:T(8,128)(2,1)S(1)}, u32[]{:S(2)}, u32[]{:S(2)}) collective-permute-start(bf16[4,32,896]{2,1,0:T(8,128)(2,1)S(1)} %all-to-all-done.1.refs_1_.refs_3_), channel_id=1, source_target_pairs={{0,6},{1,7},{2,4},{3,5},{4,2},{5,3},{6,0},{7,1},{8,14},{9,15},{10,... | collective-permute-start | bytes 688136 | tf_op jit(solution)/shard_map/ppermute | solution.py:58
  28.0 14.5 %collective-permute-done.8.refs_11_ = bf16[128,1024]{1,0:T(8,128)(2,1)S(1)} collective-permute-done((bf16[128,1024]{1,0:T(8,128)(2,1)}, bf16[128,1024]{1,0:T(8,128)(2,1)S(1)}, u32[]{:S(2)}, u32[]{:S(2)}) %collective-permute-start.8) | collective-permute-done | bytes 262176 | tf_op jit(solution)/shard_map/ppermute | solution.py:71
  45.3 3.9 %all-to-all-start.3 = ((bf16[4,32,1024]{2,1,0:T(8,128)(2,1)}), bf16[4,32,1024]{2,1,0:T(8,128)(2,1)S(1)}, u32[]{:S(2)}, u32[]{:S(2)}) async-start(bf16[4,32,1024]{2,1,0:T(8,128)(2,1)} %broadcast_in_dim.15), calls=%async_computation.3 | async-start | bytes 524288 | tf_op jit(solution)/shard_map/all_to_all | solution.py:62
  61.8 8.1 %attend_kernel.1 = (bf16[512,1024]{1,0:T(8,128)(2,1)}, bf16[512,768]{1,0:T(8,128)(2,1)}, bf16[4,512,512]{2,1,0:T(8,128)(2,1)}, bf16[4,128,256]{2,1,0:T(8,128)(2,...) custom-call(bf16[512,512]{1,0:T(8,128)(2,1)S(1)} %get-tuple-element.136.refs_0_, ...), custom_call_target="tpu_custom_call" | custom-call | tf_op jit(solution)/shard_map/attend_kernel/pallas_call | solution.py:40
  70.5 3.7 %all-to-all-start.2 = ((bf16[4,128,256]{2,1,0:T(8,128)(2,1)}), bf16[4,128,256]{2,1,0:T(8,128)(2,1)S(1)}, u32[]{:S(2)}, u32[]{:S(2)}) async-start(bf16[4,128,256]{2,1,0:T(8,128)(2,1)} %get-tuple-element.139), calls=%async_computation.2 | async-start | bytes 524288 | tf_op jit(solution)/shard_map/all_to_all | solution.py:62
  78.4 5.0 %all-to-all-done.2.refs_1_.refs_0_ = bf16[4,128,256]{2,1,0:T(8,128)(2,1)S(1)} async-done(((bf16[4,128,256]{2,1,0:T(8,128)(2,1)}), bf16[4,128,256]{2,1,0:T(8,128)(2,1)S(1)}, u32[]{:S(2)}, u32[]{:S(2)}) %all-to-all-start.2) | async-done | bytes 262176 | tf_op jit(solution)/shard_map/all_to_all | solution.py:62
  87.9 3.8 %all-to-all-start.4 = ((bf16[8,24,1024]{2,1,0:T(8,128)(2,1)}), bf16[8,24,1024]{2,1,0:T(8,128)(2,1)S(1)}, u32[]{:S(2)}, u32[]{:S(2)}) async-start(bf16[8,24,1024]{2,1,0:T(8,128)(2,1)} %bitcast.43), calls=%async_computation.4 | async-start | bytes 786432 | tf_op jit(solution)/shard_map/all_to_all | solution.py:62
  94.4 5.7 %all-to-all-done.4 = bf16[8,24,1024]{2,1,0:T(8,128)(2,1)S(1)} async-done(((bf16[8,24,1024]{2,1,0:T(8,128)(2,1)}), bf16[8,24,1024]{2,1,0:T(8,128)(2,1)S(1)}, u32[]{:S(2)}, u32[]{:S(2)}) %all-to-all-start.4) | async-done | bytes 393248 | tf_op jit(solution)/shard_map/all_to_all | solution.py:62
  101.9 2.9 %collective-permute-done.22.refs_8_ = bf16[144,1024]{1,0:T(8,128)(2,1)} collective-permute-done((bf16[144,1024]{1,0:T(8,128)(2,1)}, bf16[144,1024]{1,0:T(8,128)(2,1)}, u32[]{:S(2)}, u32[]{:S(2)}) %collective-permute-start.22) | collective-permute-done | bytes 294944 | tf_op jit(solution)/shard_map/ppermute | solution.py:82
  108.1 4.8 %expert_kernel.4 = (bf16[288,1024]{1,0:T(8,128)(2,1)}, bf16[144,1024]{1,0:T(8,128)(2,1)S(1)}, bf16[144,1024]{1,0:T(8,128)(2,1)S(1)}, bf16[144,1024]{1,0:T(8,128)...) custom-call(bf16[1024,128]{1,0:T(8,128)(2,1)S(1)} %get-tuple-element.140.refs_3_.refs_0_.refs_6_, ...), custom_call_target="tpu_custom_call" | custom-call | tf_op jit(solution)/shard_map/expert_kernel/pallas_call | solution.py:322
  112.9 3.2 %collective-permute-done.20.refs_5_ = bf16[144,1024]{1,0:T(8,128)(2,1)S(1)} collective-permute-done((bf16[144,1024]{1,0:T(8,128)(2,1)}, bf16[144,1024]{1,0:T(8,128)(2,1)S(1)}, u32[]{:S(2)}, u32[]{:S(2)}) %collective-permute-start.20) | collective-permute-done | bytes 294944 | tf_op jit(solution)/shard_map/ppermute | solution.py:71
  117.7 4.9 %expert_kernel.5 = (bf16[288,1024]{1,0:T(8,128)(2,1)}, bf16[144,1024]{1,0:T(8,128)(2,1)S(1)}, bf16[144,1024]{1,0:T(8,128)(2,1)S(1)}, bf16[144,1024]{1,0:T(8,128)...) custom-call(bf16[1024,128]{1,0:T(8,128)(2,1)S(1)} %get-tuple-element.140.refs_3_.refs_0_.refs_6_, ...), custom_call_target="tpu_custom_call" | custom-call | tf_op jit(solution)/shard_map/expert_kernel/pallas_call | solution.py:322
  125.4 4.9 %expert_kernel.6 = (bf16[288,1024]{1,0:T(8,128)(2,1)}, bf16[144,1024]{1,0:T(8,128)(2,1)S(1)}, bf16[144,1024]{1,0:T(8,128)(2,1)S(1)}, bf16[144,1024]{1,0:T(8,128)...) custom-call(bf16[1024,128]{1,0:T(8,128)(2,1)S(1)} %get-tuple-element.140.refs_3_.refs_0_.refs_6_, ...), custom_call_target="tpu_custom_call" | custom-call | tf_op jit(solution)/shard_map/expert_kernel/pallas_call | solution.py:322
  130.3 5.9 %expert_kernel.7 = (bf16[288,1024]{1,0:T(8,128)(2,1)}, bf16[144,1024]{1,0:T(8,128)(2,1)S(1)}, bf16[144,1024]{1,0:T(8,128)(2,1)S(1)}, bf16[144,1024]{1,0:T(8,128)...) custom-call(bf16[1024,128]{1,0:T(8,128)(2,1)S(1)} %get-tuple-element.140.refs_3_.refs_0_.refs_6_, ...), custom_call_target="tpu_custom_call" | custom-call | tf_op jit(solution)/shard_map/expert_kernel/pallas_call | solution.py:322
  138.4 7.3 %expert_grad_kernel.1 = (f32[1024,1024]{1,0:T(8,128)}, f32[1024,1024]{1,0:T(8,128)}, f32[1,1024]{1,0:T(1,128)}, f32[1,256]{1,0:T(1,128)}) custom-call(bf16[144,1024]{1,0:T(8,128)(2,1)S(1)} %get-tuple-element.153.refs_0_, bf16[144,1024]{1,0:T(8,128)(2,1)S(1)} %get-tuple-element.171.refs_1_, bf16[144,1024]{1,0:T(8,128)(2,1)S(1)} %get-tuple-element.172.refs_2_, ...), custom_call_target="tpu_custom_call" | custom-call | tf_op jit(solution)/shard_map/expert_grad_kernel/pallas_call | solution.py:375
  145.7 7.5 %collective-permute-done.27.refs_3_ = bf16[288,1024]{1,0:T(8,128)(2,1)S(1)} collective-permute-done((bf16[288,1024]{1,0:T(8,128)(2,1)}, bf16[288,1024]{1,0:T(8,128)(2,1)S(1)}, u32[]{:S(2)}, u32[]{:S(2)}) %collective-permute-start.27) | collective-permute-done | bytes 589856 | tf_op jit(solution)/shard_map/ppermute | solution.py:71
  153.1 15.4 %collective-permute-done.26.refs_2_ = bf16[288,1024]{1,0:T(8,128)(2,1)S(1)} collective-permute-done((bf16[288,1024]{1,0:T(8,128)(2,1)}, bf16[288,1024]{1,0:T(8,128)(2,1)S(1)}, u32[]{:S(2)}, u32[]{:S(2)}) %collective-permute-start.26) | collective-permute-done | bytes 589856 | tf_op jit(solution)/shard_map/ppermute | solution.py:71
  171.1 14.9 %all_to_all.40 = bf16[8,40,1024]{2,1,0:T(8,128)(2,1)S(1)} all-to-all(bf16[8,40,1024]{2,1,0:T(8,128)(2,1)} %bitcast.32), channel_id=1, replica_groups=mesh['dp'=4,'expert'=8] {'expert'}, dimensions={0} | all-to-all | bytes 1310720 | tf_op jit(solution)/shard_map/all_to_all | solution.py:62
  186.0 3.6 %combine_kernel.1 = (bf16[128,1024]{1,0:T(8,128)(2,1)}, f32[128,1024]{1,0:T(8,128)}, bf16[128,1024]{1,0:T(8,128)(2,1)S(1)}, bf16[4,128,256]{2,1,0:T(8,128)(2,1)}...) custom-call(bf16[320,1024]{1,0:T(8,128)(2,1)S(1)} %bitcast.29, s32[128,1]{1,0:T(8,128)} %get-tuple-element.202.refs_1_, ...), custom_call_target="tpu_custom_call" | custom-call | tf_op jit(solution)/shard_map/combine_kernel/pallas_call | solution.py:40
  189.6 2.9 %proj_grad_kernel.1 = (bf16[4,4,32,1024]{3,2,1,0:T(8,128)(2,1)}, bf16[4,4,32,1024]{3,2,1,0:T(8,128)(2,1)S(1)}) custom-call(bf16[4,128,256]{2,1,0:T(8,128)(2,1)} %copy-done.5, bf16[128,1024]{1,0:T(8,128)(2,1)S(1)} %get-tuple-element.209.refs_1_), custom_call_target="tpu_custom_call" | custom-call | tf_op jit(solution)/shard_map/proj_grad_kernel/pallas_call | solution.py:40
  192.5 10.9 %all-to-all-start.6 = ((bf16[4,128,256]{2,1,0:T(8,128)(2,1)}), bf16[4,128,256]{2,1,0:T(8,128)(2,1)S(1)}, u32[]{:S(2)}, u32[]{:S(2)}) async-start(bf16[4,128,256]{2,1,0:T(8,128)(2,1)} %get-tuple-element.208), calls=%async_computation.6 | async-start | bytes 524288 | tf_op jit(solution)/shard_map/all_to_all | solution.py:62
  204.4 8.5 %all-to-all-done.6.refs_0_ = bf16[4,128,256]{2,1,0:T(8,128)(2,1)S(1)} async-done(((bf16[4,128,256]{2,1,0:T(8,128)(2,1)}), bf16[4,128,256]{2,1,0:T(8,128)(2,1)S(1)}, u32[]{:S(2)}, u32[]{:S(2)}) %all-to-all-start.6) | async-done | bytes 262176 | tf_op jit(solution)/shard_map/all_to_all | solution.py:62
  216.4 8.5 %attend_back_kernel.1 = (bf16[512,768]{1,0:T(8,128)(2,1)S(1)}, bf16[4,128,1024]{2,1,0:T(8,128)(2,1)}) custom-call(bf16[4,128,256]{2,1,0:T(8,128)(2,1)S(1)} %all-to-all-done.6.refs_0_, bf16[4,512,512]{2,1,0:T(8,128)(2,1)} %get-tuple-element.217.refs_1_, bf16[512,768]{1,0:T(8,128)(2,1)} %get-tuple-element.218.refs_2_, bf16[4,32,896]{2,1,0:T(8,128)(2,1)} %copy-done.17, ...), custom_call_target="tpu_custom_call" | custom-call | tf_op jit(solution)/shard_map/attend_back_kernel/pallas_call | solution.py:40
  225.5 4.0 %qkv_grad_kernel.1 = (bf16[4,4,32,896]{3,2,1,0:T(8,128)(2,1)}, bf16[4,4,32,896]{3,2,1,0:T(8,128)(2,1)S(1)}) custom-call(bf16[512,1024]{1,0:T(8,128)(2,1)} %get-tuple-element.207.refs_0_, f32[8,1024]{1,0:T(8,128)S(1)} %get-tuple-element.141.refs_4_.refs_7_.refs_1_.refs_2_, bf16[512,768]{1,0:T(8,128)(2,1)S(1)} %get-tuple-element.224.refs_2_, ...), custom_call_target="tpu_custom_call" | custom-call | tf_op jit(solution)/shard_map/qkv_grad_kernel/pallas_call | solution.py:40
  229.5 4.4 %all-to-all-start.7 = ((bf16[4,128,1024]{2,1,0:T(8,128)(2,1)}), bf16[4,128,1024]{2,1,0:T(8,128)(2,1)S(1)}, u32[]{:S(2)}, u32[]{:S(2)}) async-start(bf16[4,128,1024]{2,1,0:T(8,128)(2,1)} %get-tuple-element.230.refs_3_), calls=%async_computation.7 | async-start | bytes 2097152 | tf_op jit(solution)/shard_map/all_to_all | solution.py:62
  241.1 5.2 %collective-permute-done.34.refs_1_ = bf16[4,32,896]{2,1,0:T(8,128)(2,1)S(1)} collective-permute-done((bf16[4,32,896]{2,1,0:T(8,128)(2,1)}, bf16[4,32,896]{2,1,0:T(8,128)(2,1)S(1)}, u32[]{:S(2)}, u32[]{:S(2)}) %collective-permute-start.34) | collective-permute-done | bytes 229408 | tf_op jit(solution)/shard_map/ppermute | solution.py:58
  246.2 5.3 %collective-permute-done.35.refs_2_ = bf16[4,32,896]{2,1,0:T(8,128)(2,1)S(1)} collective-permute-done((bf16[4,32,896]{2,1,0:T(8,128)(2,1)}, bf16[4,32,896]{2,1,0:T(8,128)(2,1)S(1)}, u32[]{:S(2)}, u32[]{:S(2)}) %collective-permute-start.35) | collective-permute-done | bytes 229408 | tf_op jit(solution)/shard_map/ppermute | solution.py:58
  260.9 3.9 %all-to-all-done.7.refs_0_ = bf16[4,128,1024]{2,1,0:T(8,128)(2,1)S(1)} async-done(((bf16[4,128,1024]{2,1,0:T(8,128)(2,1)}), bf16[4,128,1024]{2,1,0:T(8,128)(2,1)S(1)}, u32[]{:S(2)}, u32[]{:S(2)}) %all-to-all-start.7) | async-done | bytes 1048608 | tf_op jit(solution)/shard_map/all_to_all | solution.py:62
  (140 shorter events, 72.4 us)
Async XLA Ops:
  2.4 14.5 %all-to-all-start.1 = ((bf16[4,32,896]{2,1,0:T(8,128)(2,1)}), bf16[4,32,896]{2,1,0:T(8,128)(2,1)S(1)}, u32[]{:S(2)}, u32[]{:S(2)}) async-start(bf16[4,32,896]{2,1,0:T(8,128)(2,1)} %weights_kernel.1), calls=%async_computation.1 | async-start | bytes 458752 | tf_op jit(solution)/shard_map/all_to_all | solution.py:62
  16.9 26.8 %all-to-all-start = ((bf16[8,24,1024]{2,1,0:T(8,128)(2,1)}), bf16[8,24,1024]{2,1,0:T(8,128)(2,1)S(1)}, u32[]{:S(2)}, u32[]{:S(2)}) async-start(bf16[8,24,1024]{2,1,0:T(8,128)(2,1)} %bitcast.42), calls=%async_computation | async-start | bytes 786432 | tf_op jit(solution)/shard_map/all_to_all | solution.py:62
  21.3 21.1 %collective-permute-start.8 = (bf16[128,1024]{1,0:T(8,128)(2,1)}, bf16[128,1024]{1,0:T(8,128)(2,1)S(1)}, u32[]{:S(2)}, u32[]{:S(2)}) collective-permute-start(bf16[128,1024]{1,0:T(8,128)(2,1)} %bitcast.34), channel_id=1, source_target_pairs={{0,16},{8,24},{16,0},{24,8},{1,17},{9,25},{17,1},{25,9},{2,18},{10... | collective-permute-start | bytes 786440 | tf_op jit(solution)/shard_map/ppermute | solution.py:71
  24.4 24.8 %collective-permute-start.7 = (bf16[128,1024]{1,0:T(8,128)(2,1)}, bf16[128,1024]{1,0:T(8,128)(2,1)S(1)}, u32[]{:S(2)}, u32[]{:S(2)}) collective-permute-start(bf16[128,1024]{1,0:T(8,128)(2,1)} %bitcast.35), channel_id=1, source_target_pairs={{0,8},{8,0},{16,24},{24,16},{1,9},{9,1},{17,25},{25,17},{2,10},{10... | collective-permute-start | bytes 786440 | tf_op jit(solution)/shard_map/ppermute | solution.py:71
  24.4 25.6 %collective-permute-start.5 = (bf16[4,32,896]{2,1,0:T(8,128)(2,1)S(1)}, bf16[4,32,896]{2,1,0:T(8,128)(2,1)S(1)}, u32[]{:S(2)}, u32[]{:S(2)}) collective-permute-start(bf16[4,32,896]{2,1,0:T(8,128)(2,1)S(1)} %all-to-all-done.1.refs_1_.refs_3_), channel_id=1, source_target_pairs={{0,6},{1,7},{2,4},{3,5},{4,2},{5,3},{6,0},{7,1},{8,14},{9,15},{10,... | collective-permute-start | bytes 688136 | tf_op jit(solution)/shard_map/ppermute | solution.py:58
  27.3 22.6 %collective-permute-start.3 = (bf16[4,32,896]{2,1,0:T(8,128)(2,1)S(1)}, bf16[4,32,896]{2,1,0:T(8,128)(2,1)S(1)}, u32[]{:S(2)}, u32[]{:S(2)}) collective-permute-start(bf16[4,32,896]{2,1,0:T(8,128)(2,1)S(1)} %all-to-all-done.1.refs_1_.refs_3_), channel_id=1, source_target_pairs={{0,4},{1,5},{2,6},{3,7},{4,0},{5,1},{6,2},{7,3},{8,12},{9,13},{10,... | collective-permute-start | bytes 688136 | tf_op jit(solution)/shard_map/ppermute | solution.py:58
  27.9 22.6 %collective-permute-start.1 = (bf16[4,32,896]{2,1,0:T(8,128)(2,1)S(1)}, bf16[4,32,896]{2,1,0:T(8,128)(2,1)S(1)}, u32[]{:S(2)}, u32[]{:S(2)}) collective-permute-start(bf16[4,32,896]{2,1,0:T(8,128)(2,1)S(1)} %all-to-all-done.1.refs_1_.refs_3_), channel_id=1, source_target_pairs={{0,2},{1,3},{2,0},{3,1},{4,6},{5,7},{6,4},{7,5},{8,10},{9,11},{10,... | collective-permute-start | bytes 688136 | tf_op jit(solution)/shard_map/ppermute | solution.py:58
  45.3 12.8 %all-to-all-start.3 = ((bf16[4,32,1024]{2,1,0:T(8,128)(2,1)}), bf16[4,32,1024]{2,1,0:T(8,128)(2,1)S(1)}, u32[]{:S(2)}, u32[]{:S(2)}) async-start(bf16[4,32,1024]{2,1,0:T(8,128)(2,1)} %broadcast_in_dim.15), calls=%async_computation.3 | async-start | bytes 524288 | tf_op jit(solution)/shard_map/all_to_all | solution.py:62
  52.6 17.9 %collective-permute-start.12 = (bf16[144,1024]{1,0:T(8,128)(2,1)}, bf16[144,1024]{1,0:T(8,128)(2,1)S(1)}, u32[]{:S(2)}, u32[]{:S(2)}) collective-permute-start(bf16[144,1024]{1,0:T(8,128)(2,1)} %pack_kernel.2.refs_6_), channel_id=1, source_target_pairs={{0,16},{8,24},{16,0},{24,8},{1,17},{9,25},{17,1},{25,9},{2,18},{10... | collective-permute-start | bytes 884744 | tf_op jit(solution)/shard_map/ppermute | solution.py:71
  55.3 15.2 %collective-permute-start.11 = (bf16[144,1024]{1,0:T(8,128)(2,1)}, bf16[144,1024]{1,0:T(8,128)(2,1)S(1)}, u32[]{:S(2)}, u32[]{:S(2)}) collective-permute-start(bf16[144,1024]{1,0:T(8,128)(2,1)} %pack_kernel.2.refs_6_), channel_id=1, source_target_pairs={{0,8},{8,0},{16,24},{24,16},{1,9},{9,1},{17,25},{25,17},{2,10},{10... | collective-permute-start | bytes 884744 | tf_op jit(solution)/shard_map/ppermute | solution.py:71
  58.1 16.2 %collective-permute-start.18 = (bf16[4,32,1024]{2,1,0:T(8,128)(2,1)S(1)}, bf16[4,32,1024]{2,1,0:T(8,128)(2,1)S(1)}, u32[]{:S(2)}, u32[]{:S(2)}) collective-permute-start(bf16[4,32,1024]{2,1,0:T(8,128)(2,1)S(1)} %all-to-all-done.3.refs_0_), channel_id=1, source_target_pairs={{0,6},{1,7},{2,4},{3,5},{4,2},{5,3},{6,0},{7,1},{8,14},{9,15},{10,... | collective-permute-start | bytes 786440 | tf_op jit(solution)/shard_map/ppermute | solution.py:58
  60.4 14.4 %collective-permute-start.16 = (bf16[4,32,1024]{2,1,0:T(8,128)(2,1)S(1)}, bf16[4,32,1024]{2,1,0:T(8,128)(2,1)S(1)}, u32[]{:S(2)}, u32[]{:S(2)}) collective-permute-start(bf16[4,32,1024]{2,1,0:T(8,128)(2,1)S(1)} %all-to-all-done.3.refs_0_), channel_id=1, source_target_pairs={{0,4},{1,5},{2,6},{3,7},{4,0},{5,1},{6,2},{7,3},{8,12},{9,13},{10,... | collective-permute-start | bytes 786440 | tf_op jit(solution)/shard_map/ppermute | solution.py:58
  61.0 13.9 %collective-permute-start.14 = (bf16[4,32,1024]{2,1,0:T(8,128)(2,1)S(1)}, bf16[4,32,1024]{2,1,0:T(8,128)(2,1)S(1)}, u32[]{:S(2)}, u32[]{:S(2)}) collective-permute-start(bf16[4,32,1024]{2,1,0:T(8,128)(2,1)S(1)} %all-to-all-done.3.refs_0_), channel_id=1, source_target_pairs={{0,2},{1,3},{2,0},{3,1},{4,6},{5,7},{6,4},{7,5},{8,10},{9,11},{10,... | collective-permute-start | bytes 786440 | tf_op jit(solution)/shard_map/ppermute | solution.py:58
  70.5 12.9 %all-to-all-start.2 = ((bf16[4,128,256]{2,1,0:T(8,128)(2,1)}), bf16[4,128,256]{2,1,0:T(8,128)(2,1)S(1)}, u32[]{:S(2)}, u32[]{:S(2)}) async-start(bf16[4,128,256]{2,1,0:T(8,128)(2,1)} %get-tuple-element.139), calls=%async_computation.2 | async-start | bytes 524288 | tf_op jit(solution)/shard_map/all_to_all | solution.py:62
  87.9 12.1 %all-to-all-start.4 = ((bf16[8,24,1024]{2,1,0:T(8,128)(2,1)}), bf16[8,24,1024]{2,1,0:T(8,128)(2,1)S(1)}, u32[]{:S(2)}, u32[]{:S(2)}) async-start(bf16[8,24,1024]{2,1,0:T(8,128)(2,1)} %bitcast.43), calls=%async_computation.4 | async-start | bytes 786432 | tf_op jit(solution)/shard_map/all_to_all | solution.py:62
  93.1 11.7 %collective-permute-start.22 = (bf16[144,1024]{1,0:T(8,128)(2,1)}, bf16[144,1024]{1,0:T(8,128)(2,1)}, u32[]{:S(2)}, u32[]{:S(2)}) collective-permute-start(bf16[144,1024]{1,0:T(8,128)(2,1)} %copy-done.11), channel_id=1, source_target_pairs={{8,0},{16,24},{9,1},{17,25},{10,2},{18,26},{11,3},{19,27},{12,4},{... | collective-permute-start | bytes 884744 | tf_op jit(solution)/shard_map/ppermute | solution.py:82
  101.9 14.2 %collective-permute-start.20 = (bf16[144,1024]{1,0:T(8,128)(2,1)}, bf16[144,1024]{1,0:T(8,128)(2,1)S(1)}, u32[]{:S(2)}, u32[]{:S(2)}) collective-permute-start(bf16[144,1024]{1,0:T(8,128)(2,1)} %pack_kernel.3.refs_5_), channel_id=1, source_target_pairs={{0,16},{8,24},{16,0},{24,8},{1,17},{9,25},{17,1},{25,9},{2,18},{10... | collective-permute-start | bytes 884744 | tf_op jit(solution)/shard_map/ppermute | solution.py:71
  104.8 20.6 %collective-permute-start.25 = (bf16[144,1024]{1,0:T(8,128)(2,1)}, bf16[144,1024]{1,0:T(8,128)(2,1)S(1)}, u32[]{:S(2)}, u32[]{:S(2)}) collective-permute-start(bf16[144,1024]{1,0:T(8,128)(2,1)} %pack_kernel.3.refs_5_), channel_id=1, source_target_pairs={{0,8},{8,0},{16,24},{24,16},{1,9},{9,1},{17,25},{25,17},{2,10},{10... | collective-permute-start | bytes 884744 | tf_op jit(solution)/shard_map/ppermute | solution.py:71
  104.8 25.5 %collective-permute-start.23 = (bf16[144,1024]{1,0:T(8,128)(2,1)}, bf16[144,1024]{1,0:T(8,128)(2,1)S(1)}, u32[]{:S(2)}, u32[]{:S(2)}) collective-permute-start(bf16[144,1024]{1,0:T(8,128)(2,1)} %pack_kernel.3.refs_5_), channel_id=1, source_target_pairs={{8,16},{16,8},{9,17},{17,9},{10,18},{18,10},{11,19},{19,11},{12,20... | collective-permute-start | bytes 884744 | tf_op jit(solution)/shard_map/ppermute | solution.py:79
  116.1 14.2 %collective-permute-start.24 = (bf16[144,1024]{1,0:T(8,128)(2,1)S(1)}, bf16[144,1024]{1,0:T(8,128)(2,1)S(1)}, u32[]{:S(2)}, u32[]{:S(2)}) collective-permute-start(bf16[144,1024]{1,0:T(8,128)(2,1)S(1)} %collective-permute-done.20.refs_5_), channel_id=1, source_target_pairs={{8,0},{16,24},{9,1},{17,25},{10,2},{18,26},{11,3},{19,27},{12,4},{... | collective-permute-start | bytes 884744 | tf_op jit(solution)/shard_map/ppermute | solution.py:82
  122.6 30.6 %collective-permute-start.27 = (bf16[288,1024]{1,0:T(8,128)(2,1)}, bf16[288,1024]{1,0:T(8,128)(2,1)S(1)}, u32[]{:S(2)}, u32[]{:S(2)}) collective-permute-start(bf16[288,1024]{1,0:T(8,128)(2,1)} %get-tuple-element.157), channel_id=1, source_target_pairs={{0,16},{8,24},{16,0},{24,8},{1,17},{9,25},{17,1},{25,9},{2,18},{10... | collective-permute-start | bytes 1769480 | tf_op jit(solution)/shard_map/ppermute | solution.py:71
  130.3 38.2 %collective-permute-start.26 = (bf16[288,1024]{1,0:T(8,128)(2,1)}, bf16[288,1024]{1,0:T(8,128)(2,1)S(1)}, u32[]{:S(2)}, u32[]{:S(2)}) collective-permute-start(bf16[288,1024]{1,0:T(8,128)(2,1)} %get-tuple-element.165), channel_id=1, source_target_pairs={{0,8},{8,0},{16,24},{24,16},{1,9},{9,1},{17,25},{25,17},{2,10},{10... | collective-permute-start | bytes 1769480 | tf_op jit(solution)/shard_map/ppermute | solution.py:71
  136.2 32.3 %collective-permute-start.28 = (bf16[288,1024]{1,0:T(8,128)(2,1)}, bf16[288,1024]{1,0:T(8,128)(2,1)S(1)}, u32[]{:S(2)}, u32[]{:S(2)}) collective-permute-start(bf16[288,1024]{1,0:T(8,128)(2,1)} %get-tuple-element.197), channel_id=1, source_target_pairs={{0,24},{8,16},{16,8},{24,0},{1,25},{9,17},{17,9},{25,1},{2,26},{10... | collective-permute-start | bytes 1769480 | tf_op jit(solution)/shard_map/ppermute | solution.py:71
  192.5 10.9 %collective-permute-start.29 = (bf16[4,4,32,1024]{3,2,1,0:T(8,128)(2,1)}, bf16[4,4,32,1024]{3,2,1,0:T(8,128)(2,1)S(1)}, u32[]{:S(2)}, u32[]{:S(2)}) collective-permute-start(bf16[4,4,32,1024]{3,2,1,0:T(8,128)(2,1)} %get-tuple-element.211), channel_id=1, source_target_pairs={{0,1},{1,0},{2,3},{3,2},{4,5},{5,4},{6,7},{7,6},{8,9},{9,8},{10,11... | collective-permute-start | bytes 3145736 | tf_op jit(solution)/shard_map/ppermute | solution.py:58
  192.5 20.5 %all-to-all-start.6 = ((bf16[4,128,256]{2,1,0:T(8,128)(2,1)}), bf16[4,128,256]{2,1,0:T(8,128)(2,1)S(1)}, u32[]{:S(2)}, u32[]{:S(2)}) async-start(bf16[4,128,256]{2,1,0:T(8,128)(2,1)} %get-tuple-element.208), calls=%async_computation.6 | async-start | bytes 524288 | tf_op jit(solution)/shard_map/all_to_all | solution.py:62
  213.0 11.9 %collective-permute-start.30 = (bf16[4,32,1024]{2,1,0:T(8,128)(2,1)}, bf16[4,32,1024]{2,1,0:T(8,128)(2,1)S(1)}, u32[]{:S(2)}, u32[]{:S(2)}) collective-permute-start(bf16[4,32,1024]{2,1,0:T(8,128)(2,1)} %get-tuple-element.221), channel_id=1, source_target_pairs={{0,2},{1,3},{2,0},{3,1},{4,6},{5,7},{6,4},{7,5},{8,10},{9,11},{10,... | collective-permute-start | bytes 786440 | tf_op jit(solution)/shard_map/ppermute | solution.py:58
  213.5 12.0 %collective-permute-start.31 = (bf16[4,32,1024]{2,1,0:T(8,128)(2,1)}, bf16[4,32,1024]{2,1,0:T(8,128)(2,1)S(1)}, u32[]{:S(2)}, u32[]{:S(2)}) collective-permute-start(bf16[4,32,1024]{2,1,0:T(8,128)(2,1)} %get-tuple-element.222), channel_id=1, source_target_pairs={{0,4},{1,5},{2,6},{3,7},{4,0},{5,1},{6,2},{7,3},{8,12},{9,13},{10,... | collective-permute-start | bytes 786440 | tf_op jit(solution)/shard_map/ppermute | solution.py:58
  214.1 11.4 %collective-permute-start.32 = (bf16[4,32,1024]{2,1,0:T(8,128)(2,1)}, bf16[4,32,1024]{2,1,0:T(8,128)(2,1)S(1)}, u32[]{:S(2)}, u32[]{:S(2)}) collective-permute-start(bf16[4,32,1024]{2,1,0:T(8,128)(2,1)} %get-tuple-element.223), channel_id=1, source_target_pairs={{0,6},{1,7},{2,4},{3,5},{4,2},{5,3},{6,0},{7,1},{8,14},{9,15},{10,... | collective-permute-start | bytes 786440 | tf_op jit(solution)/shard_map/ppermute | solution.py:58
  229.5 35.3 %all-to-all-start.7 = ((bf16[4,128,1024]{2,1,0:T(8,128)(2,1)}), bf16[4,128,1024]{2,1,0:T(8,128)(2,1)S(1)}, u32[]{:S(2)}, u32[]{:S(2)}) async-start(bf16[4,128,1024]{2,1,0:T(8,128)(2,1)} %get-tuple-element.230.refs_3_), calls=%async_computation.7 | async-start | bytes 2097152 | tf_op jit(solution)/shard_map/all_to_all | solution.py:62
  239.0 12.5 %collective-permute-start.35 = (bf16[4,32,896]{2,1,0:T(8,128)(2,1)}, bf16[4,32,896]{2,1,0:T(8,128)(2,1)S(1)}, u32[]{:S(2)}, u32[]{:S(2)}) collective-permute-start(bf16[4,32,896]{2,1,0:T(8,128)(2,1)} %get-tuple-element.235), channel_id=1, source_target_pairs={{0,4},{1,5},{2,6},{3,7},{4,0},{5,1},{6,2},{7,3},{8,12},{9,13},{10,... | collective-permute-start | bytes 688136 | tf_op jit(solution)/shard_map/ppermute | solution.py:58
  239.6 11.9 %collective-permute-start.36 = (bf16[4,32,896]{2,1,0:T(8,128)(2,1)}, bf16[4,32,896]{2,1,0:T(8,128)(2,1)S(1)}, u32[]{:S(2)}, u32[]{:S(2)}) collective-permute-start(bf16[4,32,896]{2,1,0:T(8,128)(2,1)} %get-tuple-element.236), channel_id=1, source_target_pairs={{0,6},{1,7},{2,4},{3,5},{4,2},{5,3},{6,0},{7,1},{8,14},{9,15},{10,... | collective-permute-start | bytes 688136 | tf_op jit(solution)/shard_map/ppermute | solution.py:58
  254.8 12.7 %collective-permute-start.38 = (bf16[32,1920]{1,0:T(8,128)(2,1)}, bf16[32,1920]{1,0:T(8,128)(2,1)S(1)}, u32[]{:S(2)}, u32[]{:S(2)}) collective-permute-start(bf16[32,1920]{1,0:T(8,128)(2,1)} %get-tuple-element.246), channel_id=1, source_target_pairs={{0,16},{8,24},{16,0},{24,8},{1,17},{9,25},{17,1},{25,9},{2,18},{10... | collective-permute-start | bytes 368648 | tf_op jit(solution)/shard_map/ppermute | solution.py:53
  (42 other events, 418.6 us)

commit v6 on v5

--- a/solution.py
+++ b/solution.py
@@ -128,7 +128,7 @@
     return weight / jnp.sum(weight, axis=-1, keepdims=True)
 
 
-def weights_kernel(me, qkv, router, gains, biases, out, turned, *, n_dp):
+def weights_kernel(me, qkv, proj, router, gains, biases, out, rows, turned, *, n_dp):
     own, width = qkv.shape[0], qkv.shape[1] // 3
     part = width // n_dp
     experts = router.shape[0]
@@ -143,6 +143,7 @@
                 :, i * width + d * part : i * width + (d + 1) * part
             ]
         out[d, :, 3 * part :] = small
+        rows[d] = proj[...]
 
 
 def slots_kernel(
@@ -603,13 +604,13 @@
     x = tokens[0]
 
     token_blocks = spread(x)
-    columns = call(
+    columns, proj_rows = call(
         weights_kernel,
-        [pltpu.HBM((n_dp, own, cols), BF)],
-        *far(qkv_weight, router_weight.T, norm_gains, biases),
+        [pltpu.HBM((n_dp, own, cols), BF), pltpu.HBM((n_dp, own, width), BF)],
+        *far(qkv_weight, proj_weight, router_weight.T, norm_gains, biases),
         scratch=[pltpu.VMEM((128, 128), F32)],
         n_dp=n_dp,
-    )[0]
+    )
     qkv_blocks = gather_experts(swap(columns, "dp"))
     smem = pl.BlockSpec(memory_space=pltpu.SMEM)
     vmem = pl.BlockSpec(memory_space=pltpu.VMEM)
@@ -634,7 +635,7 @@
         return mine
 
     grads_in = dispatch(grads_out)
-    proj_blocks = gather_experts(swap(jnp.broadcast_to(proj_weight, (n_dp, own, width)), "dp"))
+    proj_blocks = gather_experts(swap(proj_rows, "dp"))
     grads_in, bias = lax.optimization_barrier((grads_in, bias))
     grads = spread(grads_in)
     normed1, packed, probs, att_out, vectors, small = call(
@@ -656,11 +657,11 @@
     for k, block in zip(early, came):
         grads[k] = [block]
     attended = swap(att_out, "dp")
-    proj = call(assemble_kernel, [((n_dp, n_ex, own, width), BF)], *proj_blocks)[0].reshape(width, width)
+    proj = call(assemble_kernel, [pltpu.HBM((n_dp, n_ex, own, width), BF)], *proj_blocks)[0].reshape(width, width)
     mixed, normed2, p, sent = call(
         mix_kernel,
         [pltpu.HBM((rows, width), F32), pltpu.HBM((rows, width), BF), pltpu.HBM((rows, 128), F32), pltpu.HBM((n_ex * pad, width), BF)],
-        *far(x), attended, proj, small, vectors, *far(tableT),
+        *far(x), attended, *far(proj), small, vectors, *far(tableT),
         experts=experts,
     )
     mine = dispatch(sent)
@@ -702,7 +703,7 @@
             pltpu.HBM((rows, 128), BF),
             pltpu.HBM((8, width), F32),
         ],
-        back, *far(route, rank, mixed, p, cotangent[0]), small, vectors, proj,
+        back, *far(route, rank, mixed, p, cotangent[0]), small, vectors, *far(proj),
         pair=pair, capacity=capacity, experts=experts, part=part,
     )
     d_heads = swap(d_att, "dp")

time: 270 us -> 268 us (level)
  local copies, waits for them, and re-layouts: 8.51 us -> 3.91 us
  starting transfers between devices: 77.7 us -> 74.4 us
  waiting for transfers between devices: 92 us -> 95.3 us
    ppermute x3, waiting for transfers between devices: 3.11 us -> 7.43 us  [spread(): return out + [[own, lax.ppermute(out[2][0], 'dp', [(1, 0), (2, 3)])]]]
    ppermute x9, starting transfers between devices: 12.4 us -> 8.94 us  [across(): return lax.ppermute(x, 'dp', [(i, i ^ bits) for i in range(n)])]
    unnamed x54 -> x48, local copies, waits for them, and re-layouts: 6.93 us -> 3.91 us
  transfers between devices with their start and end apart: 47 -> 47, of which waited for: 23 -> 24; matrix products, arithmetic and copies ran while one was open for 1% -> 0% of each run, Pallas kernels for 21% -> 21%
where the time goes in v6:
time: 268 us; the launch traced here: 266 us
  waiting for transfers between devices  95.3 us (36%)
  Pallas kernels  76.9 us (29%)
  starting transfers between devices  74.4 us (28%)
  blocking collectives  14.9 us (6%)
  local copies, waits for them, and re-layouts  3.91 us (1%)
    pallas_call x16, Pallas kernels, call(): pl.pallas_call(placed(functools.partial(kernel, **static)), out_shape=[o...  47.1 us
    ppermute x9, waiting for transfers between devices, across(): return lax.ppermute(x, 'dp', [(i, i ^ bits) for i in range(n)])  40.8 us
    all_to_all x7, starting transfers between devices, swap(): return lax.all_to_all(x, axis, split_axis=0, concat_axis=0, tiled=True)  37 us
    all_to_all x7, waiting for transfers between devices, swap(): return lax.all_to_all(x, axis, split_axis=0, concat_axis=0, tiled=True)  29.1 us
    pallas_call x4, Pallas kernels, expert_call(): pl.pallas_call(placed(functools.partial(expert_kernel, counts=(len(slots)...  20.4 us
    ppermute x22, starting transfers between devices, flip(): return lax.ppermute(x, 'expert', [(i, i ^ bits) for i in range(n)])  15.8 us
    ppermute x22, waiting for transfers between devices, flip(): return lax.ppermute(x, 'expert', [(i, i ^ bits) for i in range(n)])  15.4 us
    all_to_all x1, blocking collectives, swap(): return lax.all_to_all(x, axis, split_axis=0, concat_axis=0, tiled=True)  14.9 us
  transfers between devices with their start and end apart: 47, of which 24 were waited for; matrix products, arithmetic and copies ran while one was open for 0% of the time, Pallas kernels for 21%

profile of v6, /device:TPU:0, one launch (start us, length us, event | category | flops | bytes accessed | tf_op | source)
XLA Modules:
  0.0 266.3 jit_solution(553083501876553829)
XLA Ops:
  2.4 6.3 %all-to-all-start.1 = ((bf16[4,32,896]{2,1,0:T(8,128)(2,1)}), bf16[4,32,896]{2,1,0:T(8,128)(2,1)S(1)}, u32[]{:S(2)}, u32[]{:S(2)}) async-start(bf16[4,32,896]{2,1,0:T(8,128)(2,1)} %get-tuple-element.139), calls=%async_computation.1 | async-start | bytes 458752 | tf_op jit(solution)/shard_map/all_to_all | solution.py:62
  11.6 5.4 %all-to-all-done.1.refs_1_.refs_3_ = bf16[4,32,896]{2,1,0:T(8,128)(2,1)S(1)} async-done(((bf16[4,32,896]{2,1,0:T(8,128)(2,1)}), bf16[4,32,896]{2,1,0:T(8,128)(2,1)S(1)}, u32[]{:S(2)}, u32[]{:S(2)}) %all-to-all-start.1) | async-done | bytes 229408 | tf_op jit(solution)/shard_map/all_to_all | solution.py:62
  17.0 3.7 %all-to-all-start = ((bf16[8,24,1024]{2,1,0:T(8,128)(2,1)}), bf16[8,24,1024]{2,1,0:T(8,128)(2,1)S(1)}, u32[]{:S(2)}, u32[]{:S(2)}) async-start(bf16[8,24,1024]{2,1,0:T(8,128)(2,1)} %bitcast.42), calls=%async_computation | async-start | bytes 786432 | tf_op jit(solution)/shard_map/all_to_all | solution.py:62
  21.4 3.1 %collective-permute-start.8 = (bf16[128,1024]{1,0:T(8,128)(2,1)}, bf16[128,1024]{1,0:T(8,128)(2,1)S(1)}, u32[]{:S(2)}, u32[]{:S(2)}) collective-permute-start(bf16[128,1024]{1,0:T(8,128)(2,1)} %bitcast.34), channel_id=1, source_target_pairs={{0,16},{8,24},{16,0},{24,8},{1,17},{9,25},{17,1},{25,9},{2,18},{10... | collective-permute-start | bytes 786440 | tf_op jit(solution)/shard_map/ppermute | solution.py:71
  24.5 2.9 %collective-permute-start.5 = (bf16[4,32,896]{2,1,0:T(8,128)(2,1)S(1)}, bf16[4,32,896]{2,1,0:T(8,128)(2,1)S(1)}, u32[]{:S(2)}, u32[]{:S(2)}) collective-permute-start(bf16[4,32,896]{2,1,0:T(8,128)(2,1)S(1)} %all-to-all-done.1.refs_1_.refs_3_), channel_id=1, source_target_pairs={{0,6},{1,7},{2,4},{3,5},{4,2},{5,3},{6,0},{7,1},{8,14},{9,15},{10,... | collective-permute-start | bytes 688136 | tf_op jit(solution)/shard_map/ppermute | solution.py:58
  28.0 14.5 %collective-permute-done.8.refs_11_ = bf16[128,1024]{1,0:T(8,128)(2,1)S(1)} collective-permute-done((bf16[128,1024]{1,0:T(8,128)(2,1)}, bf16[128,1024]{1,0:T(8,128)(2,1)S(1)}, u32[]{:S(2)}, u32[]{:S(2)}) %collective-permute-start.8) | collective-permute-done | bytes 262176 | tf_op jit(solution)/shard_map/ppermute | solution.py:71
  43.8 3.9 %all-to-all-start.3 = ((bf16[4,32,1024]{2,1,0:T(8,128)(2,1)}), bf16[4,32,1024]{2,1,0:T(8,128)(2,1)S(1)}, u32[]{:S(2)}, u32[]{:S(2)}) async-start(bf16[4,32,1024]{2,1,0:T(8,128)(2,1)} %get-tuple-element.143), calls=%async_computation.3 | async-start | bytes 524288 | tf_op jit(solution)/shard_map/all_to_all | solution.py:62
  50.9 4.5 %collective-permute-done.10.refs_13_ = bf16[128,1024]{1,0:T(8,128)(2,1)S(1)} collective-permute-done((bf16[128,1024]{1,0:T(8,128)(2,1)S(1)}, bf16[128,1024]{1,0:T(8,128)(2,1)S(1)}, u32[]{:S(2)}, u32[]{:S(2)}) %collective-permute-start.10) | collective-permute-done | bytes 262176 | tf_op jit(solution)/shard_map/ppermute | solution.py:82
  60.8 8.2 %attend_kernel.1 = (bf16[512,1024]{1,0:T(8,128)(2,1)}, bf16[512,768]{1,0:T(8,128)(2,1)}, bf16[4,512,512]{2,1,0:T(8,128)(2,1)}, bf16[4,128,256]{2,1,0:T(8,128)(2,...) custom-call(bf16[512,512]{1,0:T(8,128)(2,1)S(1)} %get-tuple-element.138.refs_0_, ...), custom_call_target="tpu_custom_call" | custom-call | tf_op jit(solution)/shard_map/attend_kernel/pallas_call | solution.py:40
  69.2 3.8 %all-to-all-start.2 = ((bf16[4,128,256]{2,1,0:T(8,128)(2,1)}), bf16[4,128,256]{2,1,0:T(8,128)(2,1)S(1)}, u32[]{:S(2)}, u32[]{:S(2)}) async-start(bf16[4,128,256]{2,1,0:T(8,128)(2,1)} %get-tuple-element.142), calls=%async_computation.2 | async-start | bytes 524288 | tf_op jit(solution)/shard_map/all_to_all | solution.py:62
  77.2 4.8 %all-to-all-done.2.refs_1_.refs_0_ = bf16[4,128,256]{2,1,0:T(8,128)(2,1)S(1)} async-done(((bf16[4,128,256]{2,1,0:T(8,128)(2,1)}), bf16[4,128,256]{2,1,0:T(8,128)(2,1)S(1)}, u32[]{:S(2)}, u32[]{:S(2)}) %all-to-all-start.2) | async-done | bytes 262176 | tf_op jit(solution)/shard_map/all_to_all | solution.py:62
  81.9 3.5 %mix_kernel.1 = (f32[128,1024]{1,0:T(8,128)}, bf16[128,1024]{1,0:T(8,128)(2,1)}, f32[128,128]{1,0:T(8,128)}, bf16[192,1024]{1,0:T(8,128)(2,1)}) custom-call(bf16[128,1024]{1,0:T(8,128)(2,1)} %bitcast.37, bf16[4,128,256]{2,1,0:T(8,128)(2,1)S(1)} %all-to-all-done.2.refs_1_.refs_0_, bf16[1024,1024]{1,0:T(8,128)(2,1)} %bitcast.30, ...), custom_call_target="tpu_custom_call" | custom-call | tf_op jit(solution)/shard_map/mix_kernel/pallas_call | solution.py:40
  85.4 3.9 %all-to-all-start.4 = ((bf16[8,24,1024]{2,1,0:T(8,128)(2,1)}), bf16[8,24,1024]{2,1,0:T(8,128)(2,1)S(1)}, u32[]{:S(2)}, u32[]{:S(2)}) async-start(bf16[8,24,1024]{2,1,0:T(8,128)(2,1)} %bitcast.43), calls=%async_computation.4 | async-start | bytes 786432 | tf_op jit(solution)/shard_map/all_to_all | solution.py:62
  91.9 5.7 %all-to-all-done.4 = bf16[8,24,1024]{2,1,0:T(8,128)(2,1)S(1)} async-done(((bf16[8,24,1024]{2,1,0:T(8,128)(2,1)}), bf16[8,24,1024]{2,1,0:T(8,128)(2,1)S(1)}, u32[]{:S(2)}, u32[]{:S(2)}) %all-to-all-start.4) | async-done | bytes 393248 | tf_op jit(solution)/shard_map/all_to_all | solution.py:62
  105.6 4.8 %expert_kernel.4 = (bf16[288,1024]{1,0:T(8,128)(2,1)}, bf16[144,1024]{1,0:T(8,128)(2,1)S(1)}, bf16[144,1024]{1,0:T(8,128)(2,1)S(1)}, bf16[144,1024]{1,0:T(8,128)...) custom-call(bf16[1024,128]{1,0:T(8,128)(2,1)S(1)} %get-tuple-element.144.refs_3_.refs_0_.refs_6_, ...), custom_call_target="tpu_custom_call" | custom-call | tf_op jit(solution)/shard_map/expert_kernel/pallas_call | solution.py:323
  110.4 3.2 %collective-permute-done.20.refs_5_ = bf16[144,1024]{1,0:T(8,128)(2,1)S(1)} collective-permute-done((bf16[144,1024]{1,0:T(8,128)(2,1)}, bf16[144,1024]{1,0:T(8,128)(2,1)S(1)}, u32[]{:S(2)}, u32[]{:S(2)}) %collective-permute-start.20) | collective-permute-done | bytes 294944 | tf_op jit(solution)/shard_map/ppermute | solution.py:71
  115.3 4.9 %expert_kernel.5 = (bf16[288,1024]{1,0:T(8,128)(2,1)}, bf16[144,1024]{1,0:T(8,128)(2,1)S(1)}, bf16[144,1024]{1,0:T(8,128)(2,1)S(1)}, bf16[144,1024]{1,0:T(8,128)...) custom-call(bf16[1024,128]{1,0:T(8,128)(2,1)S(1)} %get-tuple-element.144.refs_3_.refs_0_.refs_6_, ...), custom_call_target="tpu_custom_call" | custom-call | tf_op jit(solution)/shard_map/expert_kernel/pallas_call | solution.py:323
  123.0 4.9 %expert_kernel.6 = (bf16[288,1024]{1,0:T(8,128)(2,1)}, bf16[144,1024]{1,0:T(8,128)(2,1)S(1)}, bf16[144,1024]{1,0:T(8,128)(2,1)S(1)}, bf16[144,1024]{1,0:T(8,128)...) custom-call(bf16[1024,128]{1,0:T(8,128)(2,1)S(1)} %get-tuple-element.144.refs_3_.refs_0_.refs_6_, ...), custom_call_target="tpu_custom_call" | custom-call | tf_op jit(solution)/shard_map/expert_kernel/pallas_call | solution.py:323
  127.9 5.9 %expert_kernel.7 = (bf16[288,1024]{1,0:T(8,128)(2,1)}, bf16[144,1024]{1,0:T(8,128)(2,1)S(1)}, bf16[144,1024]{1,0:T(8,128)(2,1)S(1)}, bf16[144,1024]{1,0:T(8,128)...) custom-call(bf16[1024,128]{1,0:T(8,128)(2,1)S(1)} %get-tuple-element.144.refs_3_.refs_0_.refs_6_, ...), custom_call_target="tpu_custom_call" | custom-call | tf_op jit(solution)/shard_map/expert_kernel/pallas_call | solution.py:323
  135.9 7.3 %expert_grad_kernel.1 = (f32[1024,1024]{1,0:T(8,128)}, f32[1024,1024]{1,0:T(8,128)}, f32[1,1024]{1,0:T(1,128)}, f32[1,256]{1,0:T(1,128)}) custom-call(bf16[144,1024]{1,0:T(8,128)(2,1)S(1)} %get-tuple-element.157.refs_0_, bf16[144,1024]{1,0:T(8,128)(2,1)S(1)} %get-tuple-element.175.refs_1_, bf16[144,1024]{1,0:T(8,128)(2,1)S(1)} %get-tuple-element.176.refs_2_, ...), custom_call_target="tpu_custom_call" | custom-call | tf_op jit(solution)/shard_map/expert_grad_kernel/pallas_call | solution.py:376
  143.2 7.5 %collective-permute-done.27.refs_3_ = bf16[288,1024]{1,0:T(8,128)(2,1)S(1)} collective-permute-done((bf16[288,1024]{1,0:T(8,128)(2,1)}, bf16[288,1024]{1,0:T(8,128)(2,1)S(1)}, u32[]{:S(2)}, u32[]{:S(2)}) %collective-permute-start.27) | collective-permute-done | bytes 589856 | tf_op jit(solution)/shard_map/ppermute | solution.py:71
  150.7 15.4 %collective-permute-done.26.refs_2_ = bf16[288,1024]{1,0:T(8,128)(2,1)S(1)} collective-permute-done((bf16[288,1024]{1,0:T(8,128)(2,1)}, bf16[288,1024]{1,0:T(8,128)(2,1)S(1)}, u32[]{:S(2)}, u32[]{:S(2)}) %collective-permute-start.26) | collective-permute-done | bytes 589856 | tf_op jit(solution)/shard_map/ppermute | solution.py:71
  168.5 14.9 %all_to_all.40 = bf16[8,40,1024]{2,1,0:T(8,128)(2,1)S(1)} all-to-all(bf16[8,40,1024]{2,1,0:T(8,128)(2,1)} %bitcast.32), channel_id=1, replica_groups=mesh['dp'=4,'expert'=8] {'expert'}, dimensions={0} | all-to-all | bytes 1310720 | tf_op jit(solution)/shard_map/all_to_all | solution.py:62
  183.4 4.4 %combine_kernel.1 = (bf16[128,1024]{1,0:T(8,128)(2,1)}, f32[128,1024]{1,0:T(8,128)}, bf16[128,1024]{1,0:T(8,128)(2,1)S(1)}, bf16[4,128,256]{2,1,0:T(8,128)(2,1)}...) custom-call(bf16[320,1024]{1,0:T(8,128)(2,1)S(1)} %bitcast.27, s32[128,1]{1,0:T(8,128)} %get-tuple-element.206.refs_1_, ...), custom_call_target="tpu_custom_call" | custom-call | tf_op jit(solution)/shard_map/combine_kernel/pallas_call | solution.py:40
  190.6 10.9 %all-to-all-start.6 = ((bf16[4,128,256]{2,1,0:T(8,128)(2,1)}), bf16[4,128,256]{2,1,0:T(8,128)(2,1)S(1)}, u32[]{:S(2)}, u32[]{:S(2)}) async-start(bf16[4,128,256]{2,1,0:T(8,128)(2,1)} %get-tuple-element.212), calls=%async_computation.6 | async-start | bytes 524288 | tf_op jit(solution)/shard_map/all_to_all | solution.py:62
  202.5 8.5 %all-to-all-done.6.refs_0_ = bf16[4,128,256]{2,1,0:T(8,128)(2,1)S(1)} async-done(((bf16[4,128,256]{2,1,0:T(8,128)(2,1)}), bf16[4,128,256]{2,1,0:T(8,128)(2,1)S(1)}, u32[]{:S(2)}, u32[]{:S(2)}) %all-to-all-start.6) | async-done | bytes 262176 | tf_op jit(solution)/shard_map/all_to_all | solution.py:62
  214.5 8.4 %attend_back_kernel.1 = (bf16[512,768]{1,0:T(8,128)(2,1)S(1)}, bf16[4,128,1024]{2,1,0:T(8,128)(2,1)}) custom-call(bf16[4,128,256]{2,1,0:T(8,128)(2,1)S(1)} %all-to-all-done.6.refs_0_, bf16[4,512,512]{2,1,0:T(8,128)(2,1)} %get-tuple-element.221.refs_1_, bf16[512,768]{1,0:T(8,128)(2,1)} %get-tuple-element.222.refs_2_, bf16[4,32,896]{2,1,0:T(8,128)(2,1)} %copy-done.14, ...), custom_call_target="tpu_custom_call" | custom-call | tf_op jit(solution)/shard_map/attend_back_kernel/pallas_call | solution.py:40
  223.6 4.0 %qkv_grad_kernel.1 = (bf16[4,4,32,896]{3,2,1,0:T(8,128)(2,1)}, bf16[4,4,32,896]{3,2,1,0:T(8,128)(2,1)S(1)}) custom-call(bf16[512,1024]{1,0:T(8,128)(2,1)} %get-tuple-element.211.refs_0_, f32[8,1024]{1,0:T(8,128)S(1)} %get-tuple-element.145.refs_4_.refs_7_.refs_1_.refs_2_, bf16[512,768]{1,0:T(8,128)(2,1)S(1)} %get-tuple-element.228.refs_2_, ...), custom_call_target="tpu_custom_call" | custom-call | tf_op jit(solution)/shard_map/qkv_grad_kernel/pallas_call | solution.py:40
  227.6 4.4 %all-to-all-start.7 = ((bf16[4,128,1024]{2,1,0:T(8,128)(2,1)}), bf16[4,128,1024]{2,1,0:T(8,128)(2,1)S(1)}, u32[]{:S(2)}, u32[]{:S(2)}) async-start(bf16[4,128,1024]{2,1,0:T(8,128)(2,1)} %get-tuple-element.234.refs_3_), calls=%async_computation.7 | async-start | bytes 2097152 | tf_op jit(solution)/shard_map/all_to_all | solution.py:62
  239.1 5.2 %collective-permute-done.34.refs_1_ = bf16[4,32,896]{2,1,0:T(8,128)(2,1)S(1)} collective-permute-done((bf16[4,32,896]{2,1,0:T(8,128)(2,1)}, bf16[4,32,896]{2,1,0:T(8,128)(2,1)S(1)}, u32[]{:S(2)}, u32[]{:S(2)}) %collective-permute-start.34) | collective-permute-done | bytes 229408 | tf_op jit(solution)/shard_map/ppermute | solution.py:58
  244.3 5.3 %collective-permute-done.35.refs_2_ = bf16[4,32,896]{2,1,0:T(8,128)(2,1)S(1)} collective-permute-done((bf16[4,32,896]{2,1,0:T(8,128)(2,1)}, bf16[4,32,896]{2,1,0:T(8,128)(2,1)S(1)}, u32[]{:S(2)}, u32[]{:S(2)}) %collective-permute-start.35) | collective-permute-done | bytes 229408 | tf_op jit(solution)/shard_map/ppermute | solution.py:58
  258.9 3.9 %all-to-all-done.7.refs_0_ = bf16[4,128,1024]{2,1,0:T(8,128)(2,1)S(1)} async-done(((bf16[4,128,1024]{2,1,0:T(8,128)(2,1)}), bf16[4,128,1024]{2,1,0:T(8,128)(2,1)S(1)}, u32[]{:S(2)}, u32[]{:S(2)}) %all-to-all-start.7) | async-done | bytes 1048608 | tf_op jit(solution)/shard_map/all_to_all | solution.py:62
  (133 shorter events, 67.6 us)
Async XLA Ops:
  2.4 14.5 %all-to-all-start.1 = ((bf16[4,32,896]{2,1,0:T(8,128)(2,1)}), bf16[4,32,896]{2,1,0:T(8,128)(2,1)S(1)}, u32[]{:S(2)}, u32[]{:S(2)}) async-start(bf16[4,32,896]{2,1,0:T(8,128)(2,1)} %get-tuple-element.139), calls=%async_computation.1 | async-start | bytes 458752 | tf_op jit(solution)/shard_map/all_to_all | solution.py:62
  17.0 26.8 %all-to-all-start = ((bf16[8,24,1024]{2,1,0:T(8,128)(2,1)}), bf16[8,24,1024]{2,1,0:T(8,128)(2,1)S(1)}, u32[]{:S(2)}, u32[]{:S(2)}) async-start(bf16[8,24,1024]{2,1,0:T(8,128)(2,1)} %bitcast.42), calls=%async_computation | async-start | bytes 786432 | tf_op jit(solution)/shard_map/all_to_all | solution.py:62
  21.4 21.1 %collective-permute-start.8 = (bf16[128,1024]{1,0:T(8,128)(2,1)}, bf16[128,1024]{1,0:T(8,128)(2,1)S(1)}, u32[]{:S(2)}, u32[]{:S(2)}) collective-permute-start(bf16[128,1024]{1,0:T(8,128)(2,1)} %bitcast.34), channel_id=1, source_target_pairs={{0,16},{8,24},{16,0},{24,8},{1,17},{9,25},{17,1},{25,9},{2,18},{10... | collective-permute-start | bytes 786440 | tf_op jit(solution)/shard_map/ppermute | solution.py:71
  24.5 23.3 %collective-permute-start.7 = (bf16[128,1024]{1,0:T(8,128)(2,1)}, bf16[128,1024]{1,0:T(8,128)(2,1)S(1)}, u32[]{:S(2)}, u32[]{:S(2)}) collective-permute-start(bf16[128,1024]{1,0:T(8,128)(2,1)} %bitcast.35), channel_id=1, source_target_pairs={{0,8},{8,0},{16,24},{24,16},{1,9},{9,1},{17,25},{25,17},{2,10},{10... | collective-permute-start | bytes 786440 | tf_op jit(solution)/shard_map/ppermute | solution.py:71
  24.5 24.0 %collective-permute-start.5 = (bf16[4,32,896]{2,1,0:T(8,128)(2,1)S(1)}, bf16[4,32,896]{2,1,0:T(8,128)(2,1)S(1)}, u32[]{:S(2)}, u32[]{:S(2)}) collective-permute-start(bf16[4,32,896]{2,1,0:T(8,128)(2,1)S(1)} %all-to-all-done.1.refs_1_.refs_3_), channel_id=1, source_target_pairs={{0,6},{1,7},{2,4},{3,5},{4,2},{5,3},{6,0},{7,1},{8,14},{9,15},{10,... | collective-permute-start | bytes 688136 | tf_op jit(solution)/shard_map/ppermute | solution.py:58
  27.4 21.1 %collective-permute-start.3 = (bf16[4,32,896]{2,1,0:T(8,128)(2,1)S(1)}, bf16[4,32,896]{2,1,0:T(8,128)(2,1)S(1)}, u32[]{:S(2)}, u32[]{:S(2)}) collective-permute-start(bf16[4,32,896]{2,1,0:T(8,128)(2,1)S(1)} %all-to-all-done.1.refs_1_.refs_3_), channel_id=1, source_target_pairs={{0,4},{1,5},{2,6},{3,7},{4,0},{5,1},{6,2},{7,3},{8,12},{9,13},{10,... | collective-permute-start | bytes 688136 | tf_op jit(solution)/shard_map/ppermute | solution.py:58
  28.0 21.0 %collective-permute-start.1 = (bf16[4,32,896]{2,1,0:T(8,128)(2,1)S(1)}, bf16[4,32,896]{2,1,0:T(8,128)(2,1)S(1)}, u32[]{:S(2)}, u32[]{:S(2)}) collective-permute-start(bf16[4,32,896]{2,1,0:T(8,128)(2,1)S(1)} %all-to-all-done.1.refs_1_.refs_3_), channel_id=1, source_target_pairs={{0,2},{1,3},{2,0},{3,1},{4,6},{5,7},{6,4},{7,5},{8,10},{9,11},{10,... | collective-permute-start | bytes 688136 | tf_op jit(solution)/shard_map/ppermute | solution.py:58
  42.5 12.9 %collective-permute-start.10 = (bf16[128,1024]{1,0:T(8,128)(2,1)S(1)}, bf16[128,1024]{1,0:T(8,128)(2,1)S(1)}, u32[]{:S(2)}, u32[]{:S(2)}) collective-permute-start(bf16[128,1024]{1,0:T(8,128)(2,1)S(1)} %collective-permute-done.8.refs_11_), channel_id=1, source_target_pairs={{8,0},{16,24},{9,1},{17,25},{10,2},{18,26},{11,3},{19,27},{12,4},{... | collective-permute-start | bytes 786440 | tf_op jit(solution)/shard_map/ppermute | solution.py:82
  43.8 13.3 %all-to-all-start.3 = ((bf16[4,32,1024]{2,1,0:T(8,128)(2,1)}), bf16[4,32,1024]{2,1,0:T(8,128)(2,1)S(1)}, u32[]{:S(2)}, u32[]{:S(2)}) async-start(bf16[4,32,1024]{2,1,0:T(8,128)(2,1)} %get-tuple-element.143), calls=%async_computation.3 | async-start | bytes 524288 | tf_op jit(solution)/shard_map/all_to_all | solution.py:62
  55.4 13.6 %collective-permute-start.12 = (bf16[144,1024]{1,0:T(8,128)(2,1)}, bf16[144,1024]{1,0:T(8,128)(2,1)S(1)}, u32[]{:S(2)}, u32[]{:S(2)}) collective-permute-start(bf16[144,1024]{1,0:T(8,128)(2,1)} %pack_kernel.2.refs_6_), channel_id=1, source_target_pairs={{0,16},{8,24},{16,0},{24,8},{1,17},{9,25},{17,1},{25,9},{2,18},{10... | collective-permute-start | bytes 884744 | tf_op jit(solution)/shard_map/ppermute | solution.py:71
  55.5 13.7 %collective-permute-start.11 = (bf16[144,1024]{1,0:T(8,128)(2,1)}, bf16[144,1024]{1,0:T(8,128)(2,1)S(1)}, u32[]{:S(2)}, u32[]{:S(2)}) collective-permute-start(bf16[144,1024]{1,0:T(8,128)(2,1)} %pack_kernel.2.refs_6_), channel_id=1, source_target_pairs={{0,8},{8,0},{16,24},{24,16},{1,9},{9,1},{17,25},{25,17},{2,10},{10... | collective-permute-start | bytes 884744 | tf_op jit(solution)/shard_map/ppermute | solution.py:71
  57.1 15.9 %collective-permute-start.18 = (bf16[4,32,1024]{2,1,0:T(8,128)(2,1)S(1)}, bf16[4,32,1024]{2,1,0:T(8,128)(2,1)S(1)}, u32[]{:S(2)}, u32[]{:S(2)}) collective-permute-start(bf16[4,32,1024]{2,1,0:T(8,128)(2,1)S(1)} %all-to-all-done.3.refs_0_), channel_id=1, source_target_pairs={{0,6},{1,7},{2,4},{3,5},{4,2},{5,3},{6,0},{7,1},{8,14},{9,15},{10,... | collective-permute-start | bytes 786440 | tf_op jit(solution)/shard_map/ppermute | solution.py:58
  59.6 13.9 %collective-permute-start.16 = (bf16[4,32,1024]{2,1,0:T(8,128)(2,1)S(1)}, bf16[4,32,1024]{2,1,0:T(8,128)(2,1)S(1)}, u32[]{:S(2)}, u32[]{:S(2)}) collective-permute-start(bf16[4,32,1024]{2,1,0:T(8,128)(2,1)S(1)} %all-to-all-done.3.refs_0_), channel_id=1, source_target_pairs={{0,4},{1,5},{2,6},{3,7},{4,0},{5,1},{6,2},{7,3},{8,12},{9,13},{10,... | collective-permute-start | bytes 786440 | tf_op jit(solution)/shard_map/ppermute | solution.py:58
  60.2 13.4 %collective-permute-start.14 = (bf16[4,32,1024]{2,1,0:T(8,128)(2,1)S(1)}, bf16[4,32,1024]{2,1,0:T(8,128)(2,1)S(1)}, u32[]{:S(2)}, u32[]{:S(2)}) collective-permute-start(bf16[4,32,1024]{2,1,0:T(8,128)(2,1)S(1)} %all-to-all-done.3.refs_0_), channel_id=1, source_target_pairs={{0,2},{1,3},{2,0},{3,1},{4,6},{5,7},{6,4},{7,5},{8,10},{9,11},{10,... | collective-permute-start | bytes 786440 | tf_op jit(solution)/shard_map/ppermute | solution.py:58
  69.2 12.7 %all-to-all-start.2 = ((bf16[4,128,256]{2,1,0:T(8,128)(2,1)}), bf16[4,128,256]{2,1,0:T(8,128)(2,1)S(1)}, u32[]{:S(2)}, u32[]{:S(2)}) async-start(bf16[4,128,256]{2,1,0:T(8,128)(2,1)} %get-tuple-element.142), calls=%async_computation.2 | async-start | bytes 524288 | tf_op jit(solution)/shard_map/all_to_all | solution.py:62
  85.4 12.2 %all-to-all-start.4 = ((bf16[8,24,1024]{2,1,0:T(8,128)(2,1)}), bf16[8,24,1024]{2,1,0:T(8,128)(2,1)S(1)}, u32[]{:S(2)}, u32[]{:S(2)}) async-start(bf16[8,24,1024]{2,1,0:T(8,128)(2,1)} %bitcast.43), calls=%async_computation.4 | async-start | bytes 786432 | tf_op jit(solution)/shard_map/all_to_all | solution.py:62
  90.6 11.7 %collective-permute-start.22 = (bf16[144,1024]{1,0:T(8,128)(2,1)}, bf16[144,1024]{1,0:T(8,128)(2,1)}, u32[]{:S(2)}, u32[]{:S(2)}) collective-permute-start(bf16[144,1024]{1,0:T(8,128)(2,1)} %copy-done.8), channel_id=1, source_target_pairs={{8,0},{16,24},{9,1},{17,25},{10,2},{18,26},{11,3},{19,27},{12,4},{... | collective-permute-start | bytes 884744 | tf_op jit(solution)/shard_map/ppermute | solution.py:82
  99.4 14.2 %collective-permute-start.20 = (bf16[144,1024]{1,0:T(8,128)(2,1)}, bf16[144,1024]{1,0:T(8,128)(2,1)S(1)}, u32[]{:S(2)}, u32[]{:S(2)}) collective-permute-start(bf16[144,1024]{1,0:T(8,128)(2,1)} %pack_kernel.3.refs_5_), channel_id=1, source_target_pairs={{0,16},{8,24},{16,0},{24,8},{1,17},{9,25},{17,1},{25,9},{2,18},{10... | collective-permute-start | bytes 884744 | tf_op jit(solution)/shard_map/ppermute | solution.py:71
  102.3 20.6 %collective-permute-start.25 = (bf16[144,1024]{1,0:T(8,128)(2,1)}, bf16[144,1024]{1,0:T(8,128)(2,1)S(1)}, u32[]{:S(2)}, u32[]{:S(2)}) collective-permute-start(bf16[144,1024]{1,0:T(8,128)(2,1)} %pack_kernel.3.refs_5_), channel_id=1, source_target_pairs={{0,8},{8,0},{16,24},{24,16},{1,9},{9,1},{17,25},{25,17},{2,10},{10... | collective-permute-start | bytes 884744 | tf_op jit(solution)/shard_map/ppermute | solution.py:71
  102.3 25.5 %collective-permute-start.23 = (bf16[144,1024]{1,0:T(8,128)(2,1)}, bf16[144,1024]{1,0:T(8,128)(2,1)S(1)}, u32[]{:S(2)}, u32[]{:S(2)}) collective-permute-start(bf16[144,1024]{1,0:T(8,128)(2,1)} %pack_kernel.3.refs_5_), channel_id=1, source_target_pairs={{8,16},{16,8},{9,17},{17,9},{10,18},{18,10},{11,19},{19,11},{12,20... | collective-permute-start | bytes 884744 | tf_op jit(solution)/shard_map/ppermute | solution.py:79
  113.6 14.2 %collective-permute-start.24 = (bf16[144,1024]{1,0:T(8,128)(2,1)S(1)}, bf16[144,1024]{1,0:T(8,128)(2,1)S(1)}, u32[]{:S(2)}, u32[]{:S(2)}) collective-permute-start(bf16[144,1024]{1,0:T(8,128)(2,1)S(1)} %collective-permute-done.20.refs_5_), channel_id=1, source_target_pairs={{8,0},{16,24},{9,1},{17,25},{10,2},{18,26},{11,3},{19,27},{12,4},{... | collective-permute-start | bytes 884744 | tf_op jit(solution)/shard_map/ppermute | solution.py:82
  120.1 30.6 %collective-permute-start.27 = (bf16[288,1024]{1,0:T(8,128)(2,1)}, bf16[288,1024]{1,0:T(8,128)(2,1)S(1)}, u32[]{:S(2)}, u32[]{:S(2)}) collective-permute-start(bf16[288,1024]{1,0:T(8,128)(2,1)} %get-tuple-element.161), channel_id=1, source_target_pairs={{0,16},{8,24},{16,0},{24,8},{1,17},{9,25},{17,1},{25,9},{2,18},{10... | collective-permute-start | bytes 1769480 | tf_op jit(solution)/shard_map/ppermute | solution.py:71
  127.8 38.2 %collective-permute-start.26 = (bf16[288,1024]{1,0:T(8,128)(2,1)}, bf16[288,1024]{1,0:T(8,128)(2,1)S(1)}, u32[]{:S(2)}, u32[]{:S(2)}) collective-permute-start(bf16[288,1024]{1,0:T(8,128)(2,1)} %get-tuple-element.169), channel_id=1, source_target_pairs={{0,8},{8,0},{16,24},{24,16},{1,9},{9,1},{17,25},{25,17},{2,10},{10... | collective-permute-start | bytes 1769480 | tf_op jit(solution)/shard_map/ppermute | solution.py:71
  133.7 32.4 %collective-permute-start.28 = (bf16[288,1024]{1,0:T(8,128)(2,1)}, bf16[288,1024]{1,0:T(8,128)(2,1)S(1)}, u32[]{:S(2)}, u32[]{:S(2)}) collective-permute-start(bf16[288,1024]{1,0:T(8,128)(2,1)} %get-tuple-element.201), channel_id=1, source_target_pairs={{0,24},{8,16},{16,8},{24,0},{1,25},{9,17},{17,9},{25,1},{2,26},{10... | collective-permute-start | bytes 1769480 | tf_op jit(solution)/shard_map/ppermute | solution.py:71
  190.6 20.5 %all-to-all-start.6 = ((bf16[4,128,256]{2,1,0:T(8,128)(2,1)}), bf16[4,128,256]{2,1,0:T(8,128)(2,1)S(1)}, u32[]{:S(2)}, u32[]{:S(2)}) async-start(bf16[4,128,256]{2,1,0:T(8,128)(2,1)} %get-tuple-element.212), calls=%async_computation.6 | async-start | bytes 524288 | tf_op jit(solution)/shard_map/all_to_all | solution.py:62
  211.0 11.9 %collective-permute-start.30 = (bf16[4,32,1024]{2,1,0:T(8,128)(2,1)}, bf16[4,32,1024]{2,1,0:T(8,128)(2,1)S(1)}, u32[]{:S(2)}, u32[]{:S(2)}) collective-permute-start(bf16[4,32,1024]{2,1,0:T(8,128)(2,1)} %get-tuple-element.225), channel_id=1, source_target_pairs={{0,2},{1,3},{2,0},{3,1},{4,6},{5,7},{6,4},{7,5},{8,10},{9,11},{10,... | collective-permute-start | bytes 786440 | tf_op jit(solution)/shard_map/ppermute | solution.py:58
  211.6 12.0 %collective-permute-start.31 = (bf16[4,32,1024]{2,1,0:T(8,128)(2,1)}, bf16[4,32,1024]{2,1,0:T(8,128)(2,1)S(1)}, u32[]{:S(2)}, u32[]{:S(2)}) collective-permute-start(bf16[4,32,1024]{2,1,0:T(8,128)(2,1)} %get-tuple-element.226), channel_id=1, source_target_pairs={{0,4},{1,5},{2,6},{3,7},{4,0},{5,1},{6,2},{7,3},{8,12},{9,13},{10,... | collective-permute-start | bytes 786440 | tf_op jit(solution)/shard_map/ppermute | solution.py:58
  212.2 11.4 %collective-permute-start.32 = (bf16[4,32,1024]{2,1,0:T(8,128)(2,1)}, bf16[4,32,1024]{2,1,0:T(8,128)(2,1)S(1)}, u32[]{:S(2)}, u32[]{:S(2)}) collective-permute-start(bf16[4,32,1024]{2,1,0:T(8,128)(2,1)} %get-tuple-element.227), channel_id=1, source_target_pairs={{0,6},{1,7},{2,4},{3,5},{4,2},{5,3},{6,0},{7,1},{8,14},{9,15},{10,... | collective-permute-start | bytes 786440 | tf_op jit(solution)/shard_map/ppermute | solution.py:58
  227.6 35.2 %all-to-all-start.7 = ((bf16[4,128,1024]{2,1,0:T(8,128)(2,1)}), bf16[4,128,1024]{2,1,0:T(8,128)(2,1)S(1)}, u32[]{:S(2)}, u32[]{:S(2)}) async-start(bf16[4,128,1024]{2,1,0:T(8,128)(2,1)} %get-tuple-element.234.refs_3_), calls=%async_computation.7 | async-start | bytes 2097152 | tf_op jit(solution)/shard_map/all_to_all | solution.py:62
  237.1 12.5 %collective-permute-start.35 = (bf16[4,32,896]{2,1,0:T(8,128)(2,1)}, bf16[4,32,896]{2,1,0:T(8,128)(2,1)S(1)}, u32[]{:S(2)}, u32[]{:S(2)}) collective-permute-start(bf16[4,32,896]{2,1,0:T(8,128)(2,1)} %get-tuple-element.239), channel_id=1, source_target_pairs={{0,4},{1,5},{2,6},{3,7},{4,0},{5,1},{6,2},{7,3},{8,12},{9,13},{10,... | collective-permute-start | bytes 688136 | tf_op jit(solution)/shard_map/ppermute | solution.py:58
  237.6 11.9 %collective-permute-start.36 = (bf16[4,32,896]{2,1,0:T(8,128)(2,1)}, bf16[4,32,896]{2,1,0:T(8,128)(2,1)S(1)}, u32[]{:S(2)}, u32[]{:S(2)}) collective-permute-start(bf16[4,32,896]{2,1,0:T(8,128)(2,1)} %get-tuple-element.240), channel_id=1, source_target_pairs={{0,6},{1,7},{2,4},{3,5},{4,2},{5,3},{6,0},{7,1},{8,14},{9,15},{10,... | collective-permute-start | bytes 688136 | tf_op jit(solution)/shard_map/ppermute | solution.py:58
  252.8 12.6 %collective-permute-start.38 = (bf16[32,1920]{1,0:T(8,128)(2,1)}, bf16[32,1920]{1,0:T(8,128)(2,1)S(1)}, u32[]{:S(2)}, u32[]{:S(2)}) collective-permute-start(bf16[32,1920]{1,0:T(8,128)(2,1)} %get-tuple-element.250), channel_id=1, source_target_pairs={{0,16},{8,24},{16,0},{24,8},{1,17},{9,25},{17,1},{25,9},{2,18},{10... | collective-permute-start | bytes 368648 | tf_op jit(solution)/shard_map/ppermute | solution.py:53
  (39 other events, 390.4 us)

commit v7 on v6

--- a/solution.py
+++ b/solution.py
@@ -681,7 +681,8 @@
     came = [done[0][0]] + [None] * (n_dp - 1)
     last = 0
     for k in [2, 1, 3] if n_dp == 4 else range(1, n_dp):
-        slots[k], done[last] = lax.optimization_barrier((slots[k], done[last]))
+        if last != 1:
+            slots[k], done[last] = lax.optimization_barrier((slots[k], done[last]))
         done[k] = expert(slots[k], k)
         came[k] = across(done[k][0], k)
         last = k

time: 268 us -> 268 us (level)
  no operation moved by 1% of the time
where the time goes in v7:
time: 268 us; the launch traced here: 266 us
  waiting for transfers between devices  93.3 us (35%)
  Pallas kernels  77 us (29%)
  starting transfers between devices  76.3 us (28%)
  blocking collectives  14.9 us (6%)
  local copies, waits for them, and re-layouts  3.91 us (1%)
    pallas_call x16, Pallas kernels, call(): pl.pallas_call(placed(functools.partial(kernel, **static)), out_shape=[o...  47.1 us
    ppermute x9, waiting for transfers between devices, across(): return lax.ppermute(x, 'dp', [(i, i ^ bits) for i in range(n)])  38.9 us
    all_to_all x7, starting transfers between devices, swap(): return lax.all_to_all(x, axis, split_axis=0, concat_axis=0, tiled=True)  37 us
    all_to_all x7, waiting for transfers between devices, swap(): return lax.all_to_all(x, axis, split_axis=0, concat_axis=0, tiled=True)  29.1 us
    pallas_call x4, Pallas kernels, expert_call(): pl.pallas_call(placed(functools.partial(expert_kernel, counts=(len(slots)...  20.5 us
    ppermute x22, starting transfers between devices, flip(): return lax.ppermute(x, 'expert', [(i, i ^ bits) for i in range(n)])  15.8 us
    ppermute x22, waiting for transfers between devices, flip(): return lax.ppermute(x, 'expert', [(i, i ^ bits) for i in range(n)])  15.4 us
    all_to_all x1, blocking collectives, swap(): return lax.all_to_all(x, axis, split_axis=0, concat_axis=0, tiled=True)  14.9 us
  transfers between devices with their start and end apart: 47, of which 24 were waited for; matrix products, arithmetic and copies ran while one was open for 0% of the time, Pallas kernels for 21%

profile of v7, /device:TPU:0, one launch (start us, length us, event | category | flops | bytes accessed | tf_op | source)
XLA Modules:
  0.0 266.3 jit_solution(7604854922210971479)
XLA Ops:
  2.4 6.3 %all-to-all-start.1 = ((bf16[4,32,896]{2,1,0:T(8,128)(2,1)}), bf16[4,32,896]{2,1,0:T(8,128)(2,1)S(1)}, u32[]{:S(2)}, u32[]{:S(2)}) async-start(bf16[4,32,896]{2,1,0:T(8,128)(2,1)} %get-tuple-element.132), calls=%async_computation.1 | async-start | bytes 458752 | tf_op jit(solution)/shard_map/all_to_all | solution.py:62
  11.6 5.4 %all-to-all-done.1.refs_1_.refs_3_ = bf16[4,32,896]{2,1,0:T(8,128)(2,1)S(1)} async-done(((bf16[4,32,896]{2,1,0:T(8,128)(2,1)}), bf16[4,32,896]{2,1,0:T(8,128)(2,1)S(1)}, u32[]{:S(2)}, u32[]{:S(2)}) %all-to-all-start.1) | async-done | bytes 229408 | tf_op jit(solution)/shard_map/all_to_all | solution.py:62
  17.0 3.7 %all-to-all-start = ((bf16[8,24,1024]{2,1,0:T(8,128)(2,1)}), bf16[8,24,1024]{2,1,0:T(8,128)(2,1)S(1)}, u32[]{:S(2)}, u32[]{:S(2)}) async-start(bf16[8,24,1024]{2,1,0:T(8,128)(2,1)} %bitcast.42), calls=%async_computation | async-start | bytes 786432 | tf_op jit(solution)/shard_map/all_to_all | solution.py:62
  21.4 3.1 %collective-permute-start.8 = (bf16[128,1024]{1,0:T(8,128)(2,1)}, bf16[128,1024]{1,0:T(8,128)(2,1)S(1)}, u32[]{:S(2)}, u32[]{:S(2)}) collective-permute-start(bf16[128,1024]{1,0:T(8,128)(2,1)} %bitcast.34), channel_id=1, source_target_pairs={{0,16},{8,24},{16,0},{24,8},{1,17},{9,25},{17,1},{25,9},{2,18},{10... | collective-permute-start | bytes 786440 | tf_op jit(solution)/shard_map/ppermute | solution.py:71
  24.5 2.9 %collective-permute-start.5 = (bf16[4,32,896]{2,1,0:T(8,128)(2,1)S(1)}, bf16[4,32,896]{2,1,0:T(8,128)(2,1)S(1)}, u32[]{:S(2)}, u32[]{:S(2)}) collective-permute-start(bf16[4,32,896]{2,1,0:T(8,128)(2,1)S(1)} %all-to-all-done.1.refs_1_.refs_3_), channel_id=1, source_target_pairs={{0,6},{1,7},{2,4},{3,5},{4,2},{5,3},{6,0},{7,1},{8,14},{9,15},{10,... | collective-permute-start | bytes 688136 | tf_op jit(solution)/shard_map/ppermute | solution.py:58
  28.0 14.5 %collective-permute-done.8.refs_11_ = bf16[128,1024]{1,0:T(8,128)(2,1)S(1)} collective-permute-done((bf16[128,1024]{1,0:T(8,128)(2,1)}, bf16[128,1024]{1,0:T(8,128)(2,1)S(1)}, u32[]{:S(2)}, u32[]{:S(2)}) %collective-permute-start.8) | collective-permute-done | bytes 262176 | tf_op jit(solution)/shard_map/ppermute | solution.py:71
  43.8 3.9 %all-to-all-start.3 = ((bf16[4,32,1024]{2,1,0:T(8,128)(2,1)}), bf16[4,32,1024]{2,1,0:T(8,128)(2,1)S(1)}, u32[]{:S(2)}, u32[]{:S(2)}) async-start(bf16[4,32,1024]{2,1,0:T(8,128)(2,1)} %get-tuple-element.136), calls=%async_computation.3 | async-start | bytes 524288 | tf_op jit(solution)/shard_map/all_to_all | solution.py:62
  50.9 4.5 %collective-permute-done.10.refs_13_ = bf16[128,1024]{1,0:T(8,128)(2,1)S(1)} collective-permute-done((bf16[128,1024]{1,0:T(8,128)(2,1)S(1)}, bf16[128,1024]{1,0:T(8,128)(2,1)S(1)}, u32[]{:S(2)}, u32[]{:S(2)}) %collective-permute-start.10) | collective-permute-done | bytes 262176 | tf_op jit(solution)/shard_map/ppermute | solution.py:82
  60.8 8.2 %attend_kernel.1 = (bf16[512,1024]{1,0:T(8,128)(2,1)}, bf16[512,768]{1,0:T(8,128)(2,1)}, bf16[4,512,512]{2,1,0:T(8,128)(2,1)}, bf16[4,128,256]{2,1,0:T(8,128)(2,...) custom-call(bf16[512,512]{1,0:T(8,128)(2,1)S(1)} %get-tuple-element.131.refs_0_, ...), custom_call_target="tpu_custom_call" | custom-call | tf_op jit(solution)/shard_map/attend_kernel/pallas_call | solution.py:40
  69.2 3.8 %all-to-all-start.2 = ((bf16[4,128,256]{2,1,0:T(8,128)(2,1)}), bf16[4,128,256]{2,1,0:T(8,128)(2,1)S(1)}, u32[]{:S(2)}, u32[]{:S(2)}) async-start(bf16[4,128,256]{2,1,0:T(8,128)(2,1)} %get-tuple-element.135), calls=%async_computation.2 | async-start | bytes 524288 | tf_op jit(solution)/shard_map/all_to_all | solution.py:62
  77.2 4.8 %all-to-all-done.2.refs_1_.refs_0_ = bf16[4,128,256]{2,1,0:T(8,128)(2,1)S(1)} async-done(((bf16[4,128,256]{2,1,0:T(8,128)(2,1)}), bf16[4,128,256]{2,1,0:T(8,128)(2,1)S(1)}, u32[]{:S(2)}, u32[]{:S(2)}) %all-to-all-start.2) | async-done | bytes 262176 | tf_op jit(solution)/shard_map/all_to_all | solution.py:62
  81.9 3.5 %mix_kernel.1 = (f32[128,1024]{1,0:T(8,128)}, bf16[128,1024]{1,0:T(8,128)(2,1)}, f32[128,128]{1,0:T(8,128)}, bf16[192,1024]{1,0:T(8,128)(2,1)}) custom-call(bf16[128,1024]{1,0:T(8,128)(2,1)} %bitcast.37, bf16[4,128,256]{2,1,0:T(8,128)(2,1)S(1)} %all-to-all-done.2.refs_1_.refs_0_, bf16[1024,1024]{1,0:T(8,128)(2,1)} %bitcast.30, ...), custom_call_target="tpu_custom_call" | custom-call | tf_op jit(solution)/shard_map/mix_kernel/pallas_call | solution.py:40
  85.4 3.9 %all-to-all-start.4 = ((bf16[8,24,1024]{2,1,0:T(8,128)(2,1)}), bf16[8,24,1024]{2,1,0:T(8,128)(2,1)S(1)}, u32[]{:S(2)}, u32[]{:S(2)}) async-start(bf16[8,24,1024]{2,1,0:T(8,128)(2,1)} %bitcast.43), calls=%async_computation.4 | async-start | bytes 786432 | tf_op jit(solution)/shard_map/all_to_all | solution.py:62
  91.9 5.7 %all-to-all-done.4 = bf16[8,24,1024]{2,1,0:T(8,128)(2,1)S(1)} async-done(((bf16[8,24,1024]{2,1,0:T(8,128)(2,1)}), bf16[8,24,1024]{2,1,0:T(8,128)(2,1)S(1)}, u32[]{:S(2)}, u32[]{:S(2)}) %all-to-all-start.4) | async-done | bytes 393248 | tf_op jit(solution)/shard_map/all_to_all | solution.py:62
  99.4 2.9 %collective-permute-done.22.refs_8_ = bf16[144,1024]{1,0:T(8,128)(2,1)} collective-permute-done((bf16[144,1024]{1,0:T(8,128)(2,1)}, bf16[144,1024]{1,0:T(8,128)(2,1)}, u32[]{:S(2)}, u32[]{:S(2)}) %collective-permute-start.22) | collective-permute-done | bytes 294944 | tf_op jit(solution)/shard_map/ppermute | solution.py:82
  107.5 4.8 %expert_kernel.4 = (bf16[288,1024]{1,0:T(8,128)(2,1)}, bf16[144,1024]{1,0:T(8,128)(2,1)S(1)}, bf16[144,1024]{1,0:T(8,128)(2,1)S(1)}, bf16[144,1024]{1,0:T(8,128)...) custom-call(bf16[1024,128]{1,0:T(8,128)(2,1)S(1)} %get-tuple-element.137.refs_3_.refs_0_.refs_6_, ...), custom_call_target="tpu_custom_call" | custom-call | tf_op jit(solution)/shard_map/expert_kernel/pallas_call | solution.py:323
  115.3 4.9 %expert_kernel.5 = (bf16[288,1024]{1,0:T(8,128)(2,1)}, bf16[144,1024]{1,0:T(8,128)(2,1)S(1)}, bf16[144,1024]{1,0:T(8,128)(2,1)S(1)}, bf16[144,1024]{1,0:T(8,128)...) custom-call(bf16[1024,128]{1,0:T(8,128)(2,1)S(1)} %get-tuple-element.137.refs_3_.refs_0_.refs_6_, ...), custom_call_target="tpu_custom_call" | custom-call | tf_op jit(solution)/shard_map/expert_kernel/pallas_call | solution.py:323
  123.0 4.9 %expert_kernel.6 = (bf16[288,1024]{1,0:T(8,128)(2,1)}, bf16[144,1024]{1,0:T(8,128)(2,1)S(1)}, bf16[144,1024]{1,0:T(8,128)(2,1)S(1)}, bf16[144,1024]{1,0:T(8,128)...) custom-call(bf16[1024,128]{1,0:T(8,128)(2,1)S(1)} %get-tuple-element.137.refs_3_.refs_0_.refs_6_, ...), custom_call_target="tpu_custom_call" | custom-call | tf_op jit(solution)/shard_map/expert_kernel/pallas_call | solution.py:323
  127.9 5.9 %expert_kernel.7 = (bf16[288,1024]{1,0:T(8,128)(2,1)}, bf16[144,1024]{1,0:T(8,128)(2,1)S(1)}, bf16[144,1024]{1,0:T(8,128)(2,1)S(1)}, bf16[144,1024]{1,0:T(8,128)...) custom-call(bf16[1024,128]{1,0:T(8,128)(2,1)S(1)} %get-tuple-element.137.refs_3_.refs_0_.refs_6_, ...), custom_call_target="tpu_custom_call" | custom-call | tf_op jit(solution)/shard_map/expert_kernel/pallas_call | solution.py:323
  136.0 7.3 %expert_grad_kernel.1 = (f32[1024,1024]{1,0:T(8,128)}, f32[1024,1024]{1,0:T(8,128)}, f32[1,1024]{1,0:T(1,128)}, f32[1,256]{1,0:T(1,128)}) custom-call(bf16[144,1024]{1,0:T(8,128)(2,1)S(1)} %get-tuple-element.150.refs_0_, bf16[144,1024]{1,0:T(8,128)(2,1)S(1)} %get-tuple-element.161.refs_1_, bf16[144,1024]{1,0:T(8,128)(2,1)S(1)} %get-tuple-element.162.refs_2_, ...), custom_call_target="tpu_custom_call" | custom-call | tf_op jit(solution)/shard_map/expert_grad_kernel/pallas_call | solution.py:376
  143.3 7.5 %collective-permute-done.27.refs_3_ = bf16[288,1024]{1,0:T(8,128)(2,1)S(1)} collective-permute-done((bf16[288,1024]{1,0:T(8,128)(2,1)}, bf16[288,1024]{1,0:T(8,128)(2,1)S(1)}, u32[]{:S(2)}, u32[]{:S(2)}) %collective-permute-start.27) | collective-permute-done | bytes 589856 | tf_op jit(solution)/shard_map/ppermute | solution.py:71
  150.7 15.4 %collective-permute-done.26.refs_2_ = bf16[288,1024]{1,0:T(8,128)(2,1)S(1)} collective-permute-done((bf16[288,1024]{1,0:T(8,128)(2,1)}, bf16[288,1024]{1,0:T(8,128)(2,1)S(1)}, u32[]{:S(2)}, u32[]{:S(2)}) %collective-permute-start.26) | collective-permute-done | bytes 589856 | tf_op jit(solution)/shard_map/ppermute | solution.py:71
  168.5 14.9 %all_to_all.40 = bf16[8,40,1024]{2,1,0:T(8,128)(2,1)S(1)} all-to-all(bf16[8,40,1024]{2,1,0:T(8,128)(2,1)} %bitcast.32), channel_id=1, replica_groups=mesh['dp'=4,'expert'=8] {'expert'}, dimensions={0} | all-to-all | bytes 1310720 | tf_op jit(solution)/shard_map/all_to_all | solution.py:62
  183.4 4.4 %combine_kernel.1 = (bf16[128,1024]{1,0:T(8,128)(2,1)}, f32[128,1024]{1,0:T(8,128)}, bf16[128,1024]{1,0:T(8,128)(2,1)S(1)}, bf16[4,128,256]{2,1,0:T(8,128)(2,1)}...) custom-call(bf16[320,1024]{1,0:T(8,128)(2,1)S(1)} %bitcast.27, s32[128,1]{1,0:T(8,128)} %get-tuple-element.192.refs_1_, ...), custom_call_target="tpu_custom_call" | custom-call | tf_op jit(solution)/shard_map/combine_kernel/pallas_call | solution.py:40
  190.6 10.9 %all-to-all-start.6 = ((bf16[4,128,256]{2,1,0:T(8,128)(2,1)}), bf16[4,128,256]{2,1,0:T(8,128)(2,1)S(1)}, u32[]{:S(2)}, u32[]{:S(2)}) async-start(bf16[4,128,256]{2,1,0:T(8,128)(2,1)} %get-tuple-element.198), calls=%async_computation.6 | async-start | bytes 524288 | tf_op jit(solution)/shard_map/all_to_all | solution.py:62
  202.5 8.5 %all-to-all-done.6.refs_0_ = bf16[4,128,256]{2,1,0:T(8,128)(2,1)S(1)} async-done(((bf16[4,128,256]{2,1,0:T(8,128)(2,1)}), bf16[4,128,256]{2,1,0:T(8,128)(2,1)S(1)}, u32[]{:S(2)}, u32[]{:S(2)}) %all-to-all-start.6) | async-done | bytes 262176 | tf_op jit(solution)/shard_map/all_to_all | solution.py:62
  214.5 8.4 %attend_back_kernel.1 = (bf16[512,768]{1,0:T(8,128)(2,1)S(1)}, bf16[4,128,1024]{2,1,0:T(8,128)(2,1)}) custom-call(bf16[4,128,256]{2,1,0:T(8,128)(2,1)S(1)} %all-to-all-done.6.refs_0_, bf16[4,512,512]{2,1,0:T(8,128)(2,1)} %get-tuple-element.207.refs_1_, bf16[512,768]{1,0:T(8,128)(2,1)} %get-tuple-element.208.refs_2_, bf16[4,32,896]{2,1,0:T(8,128)(2,1)} %copy-done.14, ...), custom_call_target="tpu_custom_call" | custom-call | tf_op jit(solution)/shard_map/attend_back_kernel/pallas_call | solution.py:40
  223.6 4.0 %qkv_grad_kernel.1 = (bf16[4,4,32,896]{3,2,1,0:T(8,128)(2,1)}, bf16[4,4,32,896]{3,2,1,0:T(8,128)(2,1)S(1)}) custom-call(bf16[512,1024]{1,0:T(8,128)(2,1)} %get-tuple-element.197.refs_0_, f32[8,1024]{1,0:T(8,128)S(1)} %get-tuple-element.138.refs_4_.refs_7_.refs_1_.refs_2_, bf16[512,768]{1,0:T(8,128)(2,1)S(1)} %get-tuple-element.214.refs_2_, ...), custom_call_target="tpu_custom_call" | custom-call | tf_op jit(solution)/shard_map/qkv_grad_kernel/pallas_call | solution.py:40
  227.6 4.4 %all-to-all-start.7 = ((bf16[4,128,1024]{2,1,0:T(8,128)(2,1)}), bf16[4,128,1024]{2,1,0:T(8,128)(2,1)S(1)}, u32[]{:S(2)}, u32[]{:S(2)}) async-start(bf16[4,128,1024]{2,1,0:T(8,128)(2,1)} %get-tuple-element.220.refs_3_), calls=%async_computation.7 | async-start | bytes 2097152 | tf_op jit(solution)/shard_map/all_to_all | solution.py:62
  239.1 5.2 %collective-permute-done.34.refs_1_ = bf16[4,32,896]{2,1,0:T(8,128)(2,1)S(1)} collective-permute-done((bf16[4,32,896]{2,1,0:T(8,128)(2,1)}, bf16[4,32,896]{2,1,0:T(8,128)(2,1)S(1)}, u32[]{:S(2)}, u32[]{:S(2)}) %collective-permute-start.34) | collective-permute-done | bytes 229408 | tf_op jit(solution)/shard_map/ppermute | solution.py:58
  244.3 5.3 %collective-permute-done.35.refs_2_ = bf16[4,32,896]{2,1,0:T(8,128)(2,1)S(1)} collective-permute-done((bf16[4,32,896]{2,1,0:T(8,128)(2,1)}, bf16[4,32,896]{2,1,0:T(8,128)(2,1)S(1)}, u32[]{:S(2)}, u32[]{:S(2)}) %collective-permute-start.35) | collective-permute-done | bytes 229408 | tf_op jit(solution)/shard_map/ppermute | solution.py:58
  259.0 3.9 %all-to-all-done.7.refs_0_ = bf16[4,128,1024]{2,1,0:T(8,128)(2,1)S(1)} async-done(((bf16[4,128,1024]{2,1,0:T(8,128)(2,1)}), bf16[4,128,1024]{2,1,0:T(8,128)(2,1)S(1)}, u32[]{:S(2)}, u32[]{:S(2)}) %all-to-all-start.7) | async-done | bytes 1048608 | tf_op jit(solution)/shard_map/all_to_all | solution.py:62
  (133 shorter events, 67.9 us)
Async XLA Ops:
  2.4 14.5 %all-to-all-start.1 = ((bf16[4,32,896]{2,1,0:T(8,128)(2,1)}), bf16[4,32,896]{2,1,0:T(8,128)(2,1)S(1)}, u32[]{:S(2)}, u32[]{:S(2)}) async-start(bf16[4,32,896]{2,1,0:T(8,128)(2,1)} %get-tuple-element.132), calls=%async_computation.1 | async-start | bytes 458752 | tf_op jit(solution)/shard_map/all_to_all | solution.py:62
  17.0 26.8 %all-to-all-start = ((bf16[8,24,1024]{2,1,0:T(8,128)(2,1)}), bf16[8,24,1024]{2,1,0:T(8,128)(2,1)S(1)}, u32[]{:S(2)}, u32[]{:S(2)}) async-start(bf16[8,24,1024]{2,1,0:T(8,128)(2,1)} %bitcast.42), calls=%async_computation | async-start | bytes 786432 | tf_op jit(solution)/shard_map/all_to_all | solution.py:62
  21.4 21.1 %collective-permute-start.8 = (bf16[128,1024]{1,0:T(8,128)(2,1)}, bf16[128,1024]{1,0:T(8,128)(2,1)S(1)}, u32[]{:S(2)}, u32[]{:S(2)}) collective-permute-start(bf16[128,1024]{1,0:T(8,128)(2,1)} %bitcast.34), channel_id=1, source_target_pairs={{0,16},{8,24},{16,0},{24,8},{1,17},{9,25},{17,1},{25,9},{2,18},{10... | collective-permute-start | bytes 786440 | tf_op jit(solution)/shard_map/ppermute | solution.py:71
  24.5 23.3 %collective-permute-start.7 = (bf16[128,1024]{1,0:T(8,128)(2,1)}, bf16[128,1024]{1,0:T(8,128)(2,1)S(1)}, u32[]{:S(2)}, u32[]{:S(2)}) collective-permute-start(bf16[128,1024]{1,0:T(8,128)(2,1)} %bitcast.35), channel_id=1, source_target_pairs={{0,8},{8,0},{16,24},{24,16},{1,9},{9,1},{17,25},{25,17},{2,10},{10... | collective-permute-start | bytes 786440 | tf_op jit(solution)/shard_map/ppermute | solution.py:71
  24.5 24.0 %collective-permute-start.5 = (bf16[4,32,896]{2,1,0:T(8,128)(2,1)S(1)}, bf16[4,32,896]{2,1,0:T(8,128)(2,1)S(1)}, u32[]{:S(2)}, u32[]{:S(2)}) collective-permute-start(bf16[4,32,896]{2,1,0:T(8,128)(2,1)S(1)} %all-to-all-done.1.refs_1_.refs_3_), channel_id=1, source_target_pairs={{0,6},{1,7},{2,4},{3,5},{4,2},{5,3},{6,0},{7,1},{8,14},{9,15},{10,... | collective-permute-start | bytes 688136 | tf_op jit(solution)/shard_map/ppermute | solution.py:58
  27.4 21.1 %collective-permute-start.3 = (bf16[4,32,896]{2,1,0:T(8,128)(2,1)S(1)}, bf16[4,32,896]{2,1,0:T(8,128)(2,1)S(1)}, u32[]{:S(2)}, u32[]{:S(2)}) collective-permute-start(bf16[4,32,896]{2,1,0:T(8,128)(2,1)S(1)} %all-to-all-done.1.refs_1_.refs_3_), channel_id=1, source_target_pairs={{0,4},{1,5},{2,6},{3,7},{4,0},{5,1},{6,2},{7,3},{8,12},{9,13},{10,... | collective-permute-start | bytes 688136 | tf_op jit(solution)/shard_map/ppermute | solution.py:58
  28.0 21.0 %collective-permute-start.1 = (bf16[4,32,896]{2,1,0:T(8,128)(2,1)S(1)}, bf16[4,32,896]{2,1,0:T(8,128)(2,1)S(1)}, u32[]{:S(2)}, u32[]{:S(2)}) collective-permute-start(bf16[4,32,896]{2,1,0:T(8,128)(2,1)S(1)} %all-to-all-done.1.refs_1_.refs_3_), channel_id=1, source_target_pairs={{0,2},{1,3},{2,0},{3,1},{4,6},{5,7},{6,4},{7,5},{8,10},{9,11},{10,... | collective-permute-start | bytes 688136 | tf_op jit(solution)/shard_map/ppermute | solution.py:58
  42.5 12.9 %collective-permute-start.10 = (bf16[128,1024]{1,0:T(8,128)(2,1)S(1)}, bf16[128,1024]{1,0:T(8,128)(2,1)S(1)}, u32[]{:S(2)}, u32[]{:S(2)}) collective-permute-start(bf16[128,1024]{1,0:T(8,128)(2,1)S(1)} %collective-permute-done.8.refs_11_), channel_id=1, source_target_pairs={{8,0},{16,24},{9,1},{17,25},{10,2},{18,26},{11,3},{19,27},{12,4},{... | collective-permute-start | bytes 786440 | tf_op jit(solution)/shard_map/ppermute | solution.py:82
  43.8 13.3 %all-to-all-start.3 = ((bf16[4,32,1024]{2,1,0:T(8,128)(2,1)}), bf16[4,32,1024]{2,1,0:T(8,128)(2,1)S(1)}, u32[]{:S(2)}, u32[]{:S(2)}) async-start(bf16[4,32,1024]{2,1,0:T(8,128)(2,1)} %get-tuple-element.136), calls=%async_computation.3 | async-start | bytes 524288 | tf_op jit(solution)/shard_map/all_to_all | solution.py:62
  55.4 13.6 %collective-permute-start.12 = (bf16[144,1024]{1,0:T(8,128)(2,1)}, bf16[144,1024]{1,0:T(8,128)(2,1)S(1)}, u32[]{:S(2)}, u32[]{:S(2)}) collective-permute-start(bf16[144,1024]{1,0:T(8,128)(2,1)} %pack_kernel.2.refs_6_), channel_id=1, source_target_pairs={{0,16},{8,24},{16,0},{24,8},{1,17},{9,25},{17,1},{25,9},{2,18},{10... | collective-permute-start | bytes 884744 | tf_op jit(solution)/shard_map/ppermute | solution.py:71
  55.5 13.7 %collective-permute-start.11 = (bf16[144,1024]{1,0:T(8,128)(2,1)}, bf16[144,1024]{1,0:T(8,128)(2,1)S(1)}, u32[]{:S(2)}, u32[]{:S(2)}) collective-permute-start(bf16[144,1024]{1,0:T(8,128)(2,1)} %pack_kernel.2.refs_6_), channel_id=1, source_target_pairs={{0,8},{8,0},{16,24},{24,16},{1,9},{9,1},{17,25},{25,17},{2,10},{10... | collective-permute-start | bytes 884744 | tf_op jit(solution)/shard_map/ppermute | solution.py:71
  57.1 15.9 %collective-permute-start.18 = (bf16[4,32,1024]{2,1,0:T(8,128)(2,1)S(1)}, bf16[4,32,1024]{2,1,0:T(8,128)(2,1)S(1)}, u32[]{:S(2)}, u32[]{:S(2)}) collective-permute-start(bf16[4,32,1024]{2,1,0:T(8,128)(2,1)S(1)} %all-to-all-done.3.refs_0_), channel_id=1, source_target_pairs={{0,6},{1,7},{2,4},{3,5},{4,2},{5,3},{6,0},{7,1},{8,14},{9,15},{10,... | collective-permute-start | bytes 786440 | tf_op jit(solution)/shard_map/ppermute | solution.py:58
  59.6 13.9 %collective-permute-start.16 = (bf16[4,32,1024]{2,1,0:T(8,128)(2,1)S(1)}, bf16[4,32,1024]{2,1,0:T(8,128)(2,1)S(1)}, u32[]{:S(2)}, u32[]{:S(2)}) collective-permute-start(bf16[4,32,1024]{2,1,0:T(8,128)(2,1)S(1)} %all-to-all-done.3.refs_0_), channel_id=1, source_target_pairs={{0,4},{1,5},{2,6},{3,7},{4,0},{5,1},{6,2},{7,3},{8,12},{9,13},{10,... | collective-permute-start | bytes 786440 | tf_op jit(solution)/shard_map/ppermute | solution.py:58
  60.2 13.4 %collective-permute-start.14 = (bf16[4,32,1024]{2,1,0:T(8,128)(2,1)S(1)}, bf16[4,32,1024]{2,1,0:T(8,128)(2,1)S(1)}, u32[]{:S(2)}, u32[]{:S(2)}) collective-permute-start(bf16[4,32,1024]{2,1,0:T(8,128)(2,1)S(1)} %all-to-all-done.3.refs_0_), channel_id=1, source_target_pairs={{0,2},{1,3},{2,0},{3,1},{4,6},{5,7},{6,4},{7,5},{8,10},{9,11},{10,... | collective-permute-start | bytes 786440 | tf_op jit(solution)/shard_map/ppermute | solution.py:58
  69.2 12.7 %all-to-all-start.2 = ((bf16[4,128,256]{2,1,0:T(8,128)(2,1)}), bf16[4,128,256]{2,1,0:T(8,128)(2,1)S(1)}, u32[]{:S(2)}, u32[]{:S(2)}) async-start(bf16[4,128,256]{2,1,0:T(8,128)(2,1)} %get-tuple-element.135), calls=%async_computation.2 | async-start | bytes 524288 | tf_op jit(solution)/shard_map/all_to_all | solution.py:62
  85.4 12.2 %all-to-all-start.4 = ((bf16[8,24,1024]{2,1,0:T(8,128)(2,1)}), bf16[8,24,1024]{2,1,0:T(8,128)(2,1)S(1)}, u32[]{:S(2)}, u32[]{:S(2)}) async-start(bf16[8,24,1024]{2,1,0:T(8,128)(2,1)} %bitcast.43), calls=%async_computation.4 | async-start | bytes 786432 | tf_op jit(solution)/shard_map/all_to_all | solution.py:62
  90.6 11.7 %collective-permute-start.22 = (bf16[144,1024]{1,0:T(8,128)(2,1)}, bf16[144,1024]{1,0:T(8,128)(2,1)}, u32[]{:S(2)}, u32[]{:S(2)}) collective-permute-start(bf16[144,1024]{1,0:T(8,128)(2,1)} %copy-done.8), channel_id=1, source_target_pairs={{8,0},{16,24},{9,1},{17,25},{10,2},{18,26},{11,3},{19,27},{12,4},{... | collective-permute-start | bytes 884744 | tf_op jit(solution)/shard_map/ppermute | solution.py:82
  99.4 14.2 %collective-permute-start.20 = (bf16[144,1024]{1,0:T(8,128)(2,1)}, bf16[144,1024]{1,0:T(8,128)(2,1)S(1)}, u32[]{:S(2)}, u32[]{:S(2)}) collective-permute-start(bf16[144,1024]{1,0:T(8,128)(2,1)} %pack_kernel.3.refs_5_), channel_id=1, source_target_pairs={{0,16},{8,24},{16,0},{24,8},{1,17},{9,25},{17,1},{25,9},{2,18},{10... | collective-permute-start | bytes 884744 | tf_op jit(solution)/shard_map/ppermute | solution.py:71
  102.3 25.5 %collective-permute-start.24 = (bf16[144,1024]{1,0:T(8,128)(2,1)}, bf16[144,1024]{1,0:T(8,128)(2,1)S(1)}, u32[]{:S(2)}, u32[]{:S(2)}) collective-permute-start(bf16[144,1024]{1,0:T(8,128)(2,1)} %pack_kernel.3.refs_5_), channel_id=1, source_target_pairs={{8,16},{16,8},{9,17},{17,9},{10,18},{18,10},{11,19},{19,11},{12,20... | collective-permute-start | bytes 884744 | tf_op jit(solution)/shard_map/ppermute | solution.py:79
  103.0 20.0 %collective-permute-start.23 = (bf16[144,1024]{1,0:T(8,128)(2,1)}, bf16[144,1024]{1,0:T(8,128)(2,1)S(1)}, u32[]{:S(2)}, u32[]{:S(2)}) collective-permute-start(bf16[144,1024]{1,0:T(8,128)(2,1)} %pack_kernel.3.refs_5_), channel_id=1, source_target_pairs={{0,8},{8,0},{16,24},{24,16},{1,9},{9,1},{17,25},{25,17},{2,10},{10... | collective-permute-start | bytes 884744 | tf_op jit(solution)/shard_map/ppermute | solution.py:71
  113.6 14.2 %collective-permute-start.25 = (bf16[144,1024]{1,0:T(8,128)(2,1)S(1)}, bf16[144,1024]{1,0:T(8,128)(2,1)S(1)}, u32[]{:S(2)}, u32[]{:S(2)}) collective-permute-start(bf16[144,1024]{1,0:T(8,128)(2,1)S(1)} %collective-permute-done.20.refs_5_), channel_id=1, source_target_pairs={{8,0},{16,24},{9,1},{17,25},{10,2},{18,26},{11,3},{19,27},{12,4},{... | collective-permute-start | bytes 884744 | tf_op jit(solution)/shard_map/ppermute | solution.py:82
  120.2 30.6 %collective-permute-start.27 = (bf16[288,1024]{1,0:T(8,128)(2,1)}, bf16[288,1024]{1,0:T(8,128)(2,1)S(1)}, u32[]{:S(2)}, u32[]{:S(2)}) collective-permute-start(bf16[288,1024]{1,0:T(8,128)(2,1)} %get-tuple-element.153), channel_id=1, source_target_pairs={{0,16},{8,24},{16,0},{24,8},{1,17},{9,25},{17,1},{25,9},{2,18},{10... | collective-permute-start | bytes 1769480 | tf_op jit(solution)/shard_map/ppermute | solution.py:71
  127.9 38.2 %collective-permute-start.26 = (bf16[288,1024]{1,0:T(8,128)(2,1)}, bf16[288,1024]{1,0:T(8,128)(2,1)S(1)}, u32[]{:S(2)}, u32[]{:S(2)}) collective-permute-start(bf16[288,1024]{1,0:T(8,128)(2,1)} %get-tuple-element.186), channel_id=1, source_target_pairs={{0,8},{8,0},{16,24},{24,16},{1,9},{9,1},{17,25},{25,17},{2,10},{10... | collective-permute-start | bytes 1769480 | tf_op jit(solution)/shard_map/ppermute | solution.py:71
  133.8 32.3 %collective-permute-start.28 = (bf16[288,1024]{1,0:T(8,128)(2,1)}, bf16[288,1024]{1,0:T(8,128)(2,1)S(1)}, u32[]{:S(2)}, u32[]{:S(2)}) collective-permute-start(bf16[288,1024]{1,0:T(8,128)(2,1)} %get-tuple-element.187), channel_id=1, source_target_pairs={{0,24},{8,16},{16,8},{24,0},{1,25},{9,17},{17,9},{25,1},{2,26},{10... | collective-permute-start | bytes 1769480 | tf_op jit(solution)/shard_map/ppermute | solution.py:71
  190.6 20.5 %all-to-all-start.6 = ((bf16[4,128,256]{2,1,0:T(8,128)(2,1)}), bf16[4,128,256]{2,1,0:T(8,128)(2,1)S(1)}, u32[]{:S(2)}, u32[]{:S(2)}) async-start(bf16[4,128,256]{2,1,0:T(8,128)(2,1)} %get-tuple-element.198), calls=%async_computation.6 | async-start | bytes 524288 | tf_op jit(solution)/shard_map/all_to_all | solution.py:62
  211.0 11.9 %collective-permute-start.30 = (bf16[4,32,1024]{2,1,0:T(8,128)(2,1)}, bf16[4,32,1024]{2,1,0:T(8,128)(2,1)S(1)}, u32[]{:S(2)}, u32[]{:S(2)}) collective-permute-start(bf16[4,32,1024]{2,1,0:T(8,128)(2,1)} %get-tuple-element.211), channel_id=1, source_target_pairs={{0,2},{1,3},{2,0},{3,1},{4,6},{5,7},{6,4},{7,5},{8,10},{9,11},{10,... | collective-permute-start | bytes 786440 | tf_op jit(solution)/shard_map/ppermute | solution.py:58
  211.6 12.0 %collective-permute-start.31 = (bf16[4,32,1024]{2,1,0:T(8,128)(2,1)}, bf16[4,32,1024]{2,1,0:T(8,128)(2,1)S(1)}, u32[]{:S(2)}, u32[]{:S(2)}) collective-permute-start(bf16[4,32,1024]{2,1,0:T(8,128)(2,1)} %get-tuple-element.212), channel_id=1, source_target_pairs={{0,4},{1,5},{2,6},{3,7},{4,0},{5,1},{6,2},{7,3},{8,12},{9,13},{10,... | collective-permute-start | bytes 786440 | tf_op jit(solution)/shard_map/ppermute | solution.py:58
  212.2 11.4 %collective-permute-start.32 = (bf16[4,32,1024]{2,1,0:T(8,128)(2,1)}, bf16[4,32,1024]{2,1,0:T(8,128)(2,1)S(1)}, u32[]{:S(2)}, u32[]{:S(2)}) collective-permute-start(bf16[4,32,1024]{2,1,0:T(8,128)(2,1)} %get-tuple-element.213), channel_id=1, source_target_pairs={{0,6},{1,7},{2,4},{3,5},{4,2},{5,3},{6,0},{7,1},{8,14},{9,15},{10,... | collective-permute-start | bytes 786440 | tf_op jit(solution)/shard_map/ppermute | solution.py:58
  227.6 35.2 %all-to-all-start.7 = ((bf16[4,128,1024]{2,1,0:T(8,128)(2,1)}), bf16[4,128,1024]{2,1,0:T(8,128)(2,1)S(1)}, u32[]{:S(2)}, u32[]{:S(2)}) async-start(bf16[4,128,1024]{2,1,0:T(8,128)(2,1)} %get-tuple-element.220.refs_3_), calls=%async_computation.7 | async-start | bytes 2097152 | tf_op jit(solution)/shard_map/all_to_all | solution.py:62
  237.1 12.5 %collective-permute-start.35 = (bf16[4,32,896]{2,1,0:T(8,128)(2,1)}, bf16[4,32,896]{2,1,0:T(8,128)(2,1)S(1)}, u32[]{:S(2)}, u32[]{:S(2)}) collective-permute-start(bf16[4,32,896]{2,1,0:T(8,128)(2,1)} %get-tuple-element.225), channel_id=1, source_target_pairs={{0,4},{1,5},{2,6},{3,7},{4,0},{5,1},{6,2},{7,3},{8,12},{9,13},{10,... | collective-permute-start | bytes 688136 | tf_op jit(solution)/shard_map/ppermute | solution.py:58
  237.7 11.9 %collective-permute-start.36 = (bf16[4,32,896]{2,1,0:T(8,128)(2,1)}, bf16[4,32,896]{2,1,0:T(8,128)(2,1)S(1)}, u32[]{:S(2)}, u32[]{:S(2)}) collective-permute-start(bf16[4,32,896]{2,1,0:T(8,128)(2,1)} %get-tuple-element.226), channel_id=1, source_target_pairs={{0,6},{1,7},{2,4},{3,5},{4,2},{5,3},{6,0},{7,1},{8,14},{9,15},{10,... | collective-permute-start | bytes 688136 | tf_op jit(solution)/shard_map/ppermute | solution.py:58
  252.8 12.6 %collective-permute-start.38 = (bf16[32,1920]{1,0:T(8,128)(2,1)}, bf16[32,1920]{1,0:T(8,128)(2,1)S(1)}, u32[]{:S(2)}, u32[]{:S(2)}) collective-permute-start(bf16[32,1920]{1,0:T(8,128)(2,1)} %get-tuple-element.236), channel_id=1, source_target_pairs={{0,16},{8,24},{16,0},{24,8},{1,17},{9,25},{17,1},{25,9},{2,18},{10... | collective-permute-start | bytes 368648 | tf_op jit(solution)/shard_map/ppermute | solution.py:53
  (39 other events, 394.1 us)
